TPU v7x, 256 devices: a whole 4x4x8 slice. The times are simulated.
256 devices in a mesh: gx: 4 (over y_hi, core), gy: 8 (over y_lo, x), gz: 8 (over z).
Axes of the slice: x: 4, y: 4 (y_hi: 2, y_lo: 2; y = y_hi * 2 + y_lo), z: 8, core: 2. Of those that a mesh axis runs over, the one named last changes fastest.
Arguments:
- positions: float32 [3, 4, 8, 8, 512], P(None, 'gx', 'gy', 'gz'), may hold values from 0 to 16, as said below
- charges: float32 [4, 8, 8, 512], P('gx', 'gy', 'gz'), may hold values from -4 to 4
- atom_types: int32 [4, 8, 8, 512], P('gx', 'gy', 'gz'), may hold values from 0 to 7
- type_table: float32 [3, 8], replicated, may hold values from 0.5 to 2
- live_count: int32 [4, 8, 8], P('gx', 'gy', 'gz'), may hold values from 358 to 512, as said below
- exp_map: float32 [64, 128, 128], P('gx', 'gy', 'gz'), may hold values from -6 to 6
Outputs:
- displacement: float32 [3, 4, 8, 8, 512], P(None, 'gx', 'gy', 'gz')
- last_force: float32 [3, 4, 8, 8, 512], P(None, 'gx', 'gy', 'gz')
- evolved: float32 [64, 128, 128], P('gx', 'gy', 'gz')
Inputs may be any that keep to these rules, and one draw needn't show every extreme that they name: `positions`: each coordinate lies within its cell's brick: 0 to 16, 16, 16 along x, y, z. The live atoms of a cell are its first live_count slots; some cell has all 512 slots live.
All inputs are finite; a program needn't handle non-finite values.
Results may differ from a plain program's by a relative error of at most 0.0003.
Values sent between devices are 32-bit elements; how exact they have to be, the bound alone decides.
No kernel may reach another device: no remote copies, remote signals or barrier semaphores. Data moves between devices by JAX's collectives and lax.ppermute only.
A program may use at most 128 MiB of HBM per device.

v0:
```python
import functools
import math

import jax
import jax.numpy as jnp
from jax import lax
from jax.sharding import Mesh
from jax.sharding import PartitionSpec as P

SPLAT_MARGIN = 3
BLUR_REACH = 2
STEPS = 2
GX_GY_GZ = ("gx_0", "gx_1", "gy_0", "gy_1", "gz")
GX = ("gx_0", "gx_1")
GY = ("gy_0", "gy_1")


CUTOFF = 10.0
EPSILON = 1e-06
STEP_SIZE = 1.0
FIT_GAIN = 0.2


def one_axis_at_a_time(x, axes):
    return functools.reduce(lax.psum, axes, x)


def padded(cells, sides, width):
    for axis, dim in sides:
        count = lax.axis_size(axis)
        ends = count - 1
        head = lax.slice_in_dim(cells, 0, width, axis=dim)
        tail = lax.slice_in_dim(cells, cells.shape[dim] - width, cells.shape[dim], axis=dim)
        cells = jnp.concatenate(
            [
                lax.ppermute(tail, axis, [(i, (i + 1) % count) for i in range(ends)]),
                cells,
                lax.ppermute(head, axis, [((i + 1) % count, i) for i in range(ends)]),
            ],
            axis=dim,
        )
    return cells


def pack_atoms(positions, charges, atom_types, type_table, live_count):
    type_total = type_table.shape[1]
    onehot = (atom_types[..., None] == jnp.arange(type_total, dtype=jnp.int32)).astype(jnp.float32)
    props = jnp.sum(onehot[None] * type_table[:, None, None, None, None, :], axis=-1)
    slots = lax.broadcasted_iota(jnp.int32, charges.shape, 3)
    living = (slots < live_count[..., None]).astype(jnp.float32)
    return jnp.concatenate([positions, charges[None], props, living[None]], axis=0)


def block_list(nearby, brick_dims):
    channels = nearby.shape[0]
    slot_count = nearby.shape[-1]
    blocks = jnp.transpose(nearby.reshape(channels, 27, slot_count), (1, 0, 2))
    number = jnp.arange(27, dtype=jnp.int32)
    sides = jnp.stack([number // 9 - 1, number // 3 % 3 - 1, number % 3 - 1], axis=1).astype(
        jnp.float32
    )
    offsets = sides * jnp.array(brick_dims, jnp.float32)[None, :]
    centre = (number == 13).astype(jnp.float32)
    return (blocks, offsets, centre)


def geometry(own_atoms, block, offset):
    separation = own_atoms[0:3, :, None] - (block[0:3, None, :] + offset[:, None, None])
    squared = jnp.sum(separation * separation, axis=0)
    smooth_cut = jnp.maximum(1.0 - squared / (CUTOFF * CUTOFF), 0.0)
    return (separation, squared, smooth_cut)


def born_radius(own_atoms, nearby, brick_dims):
    blocks, offsets, centre = block_list(nearby, brick_dims)
    slot_count = own_atoms.shape[1]
    identity_mask = jnp.eye(slot_count, dtype=jnp.float32)

    def born_visit(summed, element):
        block, offset, middle = element
        separation, squared, smooth_cut = geometry(own_atoms, block, offset)
        keep_mask = 1.0 - middle * identity_mask
        weight_term = (
            jnp.exp(-squared / 8.0)
            * smooth_cut
            * smooth_cut
            * keep_mask
            * (block[5] * block[7])[None, :]
        )
        return (summed + jnp.sum(weight_term, axis=1), None)

    summed, unused = lax.scan(
        born_visit, jnp.zeros((slot_count,), jnp.float32), (blocks, offsets, centre)
    )
    return own_atoms[4] + summed


def gb_forces(own_atoms, own_radius, nearby, near_radius, brick_dims):
    blocks, offsets, centre = block_list(nearby, brick_dims)
    slot_count = own_atoms.shape[1]
    identity_mask = jnp.eye(slot_count, dtype=jnp.float32)
    radii = near_radius.reshape(27, slot_count)

    def gb_visit(summed, element):
        block, radius_block, offset, middle = element
        separation, squared, smooth_cut = geometry(own_atoms, block, offset)
        product = own_radius[:, None] * radius_block[None, :]
        fading = jnp.exp(-squared / (4.0 * product))
        inverse = lax.rsqrt(squared + product * fading)
        charge_pair = (
            (own_atoms[3] * own_atoms[7])[:, None]
            * (block[3] * block[7])[None, :]
            * (1.0 - middle * identity_mask)
        )
        slope = (
            -0.5
            * charge_pair
            * (
                -2.0 * smooth_cut / (CUTOFF * CUTOFF) * inverse
                - 0.5
                * smooth_cut
                * smooth_cut
                * inverse
                * inverse
                * inverse
                * (1.0 - 0.25 * fading)
            )
        )
        return (summed - 2.0 * jnp.sum(slope[None] * separation, axis=2), None)

    summed, unused = lax.scan(
        gb_visit, jnp.zeros((3, slot_count), jnp.float32), (blocks, radii, offsets, centre)
    )
    return summed


def profile(coord, start, stop, shift):
    points = jnp.arange(start, stop, dtype=jnp.float32)
    gap = points[None, :] - (coord[:, None] + shift)
    return (jnp.exp(-0.5 * gap * gap), gap)


def window_range(side, length, reach):
    lower = max(side * length - SPLAT_MARGIN, -reach)
    upper = min(side * length + length + SPLAT_MARGIN, length + reach)
    return (lower, upper)


def splat_window(nearby, brick_dims, reach):
    extent = tuple((length + 2 * reach for length in brick_dims))
    density = jnp.zeros(extent, jnp.float32)
    slot_count = nearby.shape[-1]
    for side_x in (-1, 0, 1):
        for side_y in (-1, 0, 1):
            for side_z in (-1, 0, 1):
                block = nearby[:, side_x + 1, side_y + 1, side_z + 1, :]
                low_x, high_x = window_range(side_x, brick_dims[0], reach)
                low_y, high_y = window_range(side_y, brick_dims[1], reach)
                low_z, high_z = window_range(side_z, brick_dims[2], reach)
                profile_x = profile(block[0], low_x, high_x, float(side_x * brick_dims[0]))[0]
                profile_y = profile(block[1], low_y, high_y, float(side_y * brick_dims[1]))[0]
                profile_z = profile(block[2], low_z, high_z, float(side_z * brick_dims[2]))[0]
                mass = block[6] * block[7]
                plane = ((profile_x * mass[:, None])[:, :, None] * profile_y[:, None, :]).reshape(
                    slot_count, -1
                )
                placed = jnp.dot(plane.T, profile_z, precision=lax.Precision.HIGHEST)
                placed = placed.reshape(high_x - low_x, high_y - low_y, high_z - low_z)
                density = density.at[
                    low_x + reach : high_x + reach,
                    low_y + reach : high_y + reach,
                    low_z + reach : high_z + reach,
                ].add(placed)
    return density


def kernel_weights(reach):
    values = [math.exp(-0.5 * (index - reach) ** 2) for index in range(2 * reach + 1)]
    whole = sum(values)
    return [value / whole for value in values]


def blur_trim(widened, reach):
    weights = kernel_weights(BLUR_REACH)
    result = widened
    for axis in range(3):
        length = result.shape[axis] - 2 * reach
        summed = jnp.zeros(result.shape[:axis] + (length,) + result.shape[axis + 1 :], jnp.float32)
        for index in range(len(weights)):
            start = reach - BLUR_REACH + index
            summed = summed + weights[index] * lax.slice_in_dim(
                result, start, start + length, axis=axis
            )
        result = summed
    return result


def correlate(evolved, exp_map):
    return (
        one_axis_at_a_time(jnp.sum(evolved * evolved), GX_GY_GZ),
        one_axis_at_a_time(jnp.sum(evolved * exp_map), GX_GY_GZ),
        one_axis_at_a_time(jnp.sum(exp_map * exp_map), GX_GY_GZ),
    )


def correlation_slope(evolved, exp_map, sums):
    squares, cross_sum, target = sums
    norm_value = jnp.sqrt((squares + EPSILON) * (target + EPSILON))
    score = cross_sum / norm_value
    return exp_map / norm_value - score * evolved / (squares + EPSILON)


def fit_force(grad_ext, own_atoms, brick_dims, scale):
    margin = SPLAT_MARGIN
    slot_count = own_atoms.shape[1]
    profile_x, gap_x = profile(own_atoms[0], -margin, brick_dims[0] + margin, 0.0)
    profile_y, gap_y = profile(own_atoms[1], -margin, brick_dims[1] + margin, 0.0)
    profile_z, gap_z = profile(own_atoms[2], -margin, brick_dims[2] + margin, 0.0)
    stacked = jnp.concatenate([profile_z, gap_z * profile_z], axis=0)
    inner = jnp.dot(
        grad_ext.reshape(-1, grad_ext.shape[2]), stacked.T, precision=lax.Precision.HIGHEST
    )
    inner = inner.reshape(grad_ext.shape[0], grad_ext.shape[1], 2 * slot_count)
    plain_z = inner[:, :, :slot_count]
    slope_z = inner[:, :, slot_count:]
    plain_y = jnp.einsum("ija,aj->ia", plain_z, profile_y, precision=lax.Precision.HIGHEST)
    turned_y = jnp.einsum("ija,aj->ia", plain_z, gap_y * profile_y, precision=lax.Precision.HIGHEST)
    turned_z = jnp.einsum("ija,aj->ia", slope_z, profile_y, precision=lax.Precision.HIGHEST)
    force = jnp.stack(
        [
            jnp.sum(gap_x * profile_x * plain_y.T, axis=1),
            jnp.sum(profile_x * turned_y.T, axis=1),
            jnp.sum(profile_x * turned_z.T, axis=1),
        ]
    )
    return scale * (own_atoms[6] * own_atoms[7])[None, :] * force


def inside_window(brick_dims, reach):
    extents = (lax.axis_size(GX), lax.axis_size(GY), lax.axis_size("gz"))
    places = (lax.axis_index(GX), lax.axis_index(GY), lax.axis_index("gz"))
    factors = []
    for axis in range(3):
        coords = places[axis] * brick_dims[axis] + jnp.arange(
            -reach, brick_dims[axis] + reach, dtype=jnp.int32
        )
        factors.append(
            ((coords >= 0) & (coords < brick_dims[axis] * extents[axis])).astype(jnp.float32)
        )
    return factors[0][:, None, None] * factors[1][None, :, None] * factors[2][None, None, :]


def on_device(positions, charges, atom_types, type_table, live_count, exp_map):
    brick_dims = exp_map.shape
    packed = pack_atoms(positions, charges, atom_types, type_table, live_count)
    grid_points = (
        brick_dims[0]
        * brick_dims[1]
        * brick_dims[2]
        * lax.axis_size(GX)
        * lax.axis_size(GY)
        * lax.axis_size("gz")
    )
    scale = FIT_GAIN * float(grid_points)
    frame_reach = BLUR_REACH + SPLAT_MARGIN
    current = positions
    force = jnp.zeros((3, positions.shape[-1]), jnp.float32)
    evolved = jnp.zeros_like(exp_map)
    for step_index in range(STEPS):
        packed = jnp.concatenate([current, packed[3:]], axis=0)
        nearby = padded(packed, ((GX, 1), (GY, 2), ("gz", 3)), 1)
        own_atoms = packed[:, 0, 0, 0, :]
        radius = born_radius(own_atoms, nearby, brick_dims)
        near_radius = padded(radius.reshape(1, 1, 1, -1), ((GX, 0), (GY, 1), ("gz", 2)), 1)
        gb_part = gb_forces(own_atoms, radius, nearby, near_radius, brick_dims)
        density = splat_window(nearby, brick_dims, 0)
        widened = padded(density, ((GX, 0), (GY, 1), ("gz", 2)), BLUR_REACH)
        evolved = blur_trim(widened, BLUR_REACH)
        sums = correlate(evolved, exp_map)
        sensitivity = correlation_slope(evolved, exp_map, sums)
        deeper = padded(sensitivity, ((GX, 0), (GY, 1), ("gz", 2)), frame_reach)
        grad_ext = blur_trim(deeper, BLUR_REACH) * inside_window(brick_dims, SPLAT_MARGIN)
        fit_part = fit_force(grad_ext, own_atoms, brick_dims, scale)
        force = gb_part + fit_part
        current = current + STEP_SIZE * (own_atoms[7][None, :] * force).reshape(current.shape)
    return (current - positions, force.reshape(current.shape), evolved)


def solution(mesh):
    torus = Mesh(
        mesh.devices.reshape(2, 2, 2, 4, mesh.shape["gz"]), ("gx_0", "gx_1", "gy_0", "gy_1", "gz")
    )
    placed = (
        P(None, GX, GY, "gz", None),
        P(GX, GY, "gz", None),
        P(GX, GY, "gz", None),
        P(),
        P(GX, GY, "gz"),
        P(GX, GY, "gz"),
    )
    return jax.shard_map(
        on_device,
        mesh=torus,
        in_specs=placed,
        out_specs=(P(None, GX, GY, "gz", None), P(None, GX, GY, "gz", None), P(GX, GY, "gz")),
        check_vma=False,
    )
```

profile of v0, /device:TPU:56, one launch (start us, length us, event | category | flops | bytes accessed | tf_op | source)
XLA Modules:
  0.0 688.7 jit_solution(10770645709486071541)
XLA Ops:
  4.1 2.6 collective-permute-start.1
  12.4 2.7 and_reduce_fusion.2
  15.9 4.7 collective-permute-start.3
  22.6 6.0 collective-permute-done.2
  29.3 2.0 collective-permute-start.5
  31.4 3.8 collective-permute-start.4
  43.8 2.2 fusion.46
  48.5 2.0 fusion.49
  56.3 6.3 scatter-add.191
  64.8 2.5 scatter-add.195
  69.4 5.0 scatter-add.200
  83.0 5.1 collective-permute-start.13
  91.5 6.0 collective-permute-start.15
  99.2 3.8 collective-permute-start.16
  103.0 2.0 collective-permute-start.17
  105.0 59.3 %while.104 = (s32[]{:T(128)}, f32[512]{0:T(512)S(1)}, f32[8,512]{1,0:T(8,128)S(1)}, f32[27,8,512]{2,1,0:T(8,128)S(1)}, f32[27,3]{1,0:T(8,128)S(1)}, /*index=5*/f32[27]{0:T(128)S(1)}, s32[]{:T(128)}, s32[]{:T(128)}, s32[]{}, s32[]{}) while((s32[]{:T(128)}, f32[512]{0:T(512)S(1)}, f32[8,512]{1,0:T(8,128)S(1)}, ...), condition=%wide.region_4.5_spmd.clone, body=%wide.region_1.4_spmd.clone.sunk | while | flops 5507589 | bytes 2150615 | solution.py:92
  164.4 3.7 collective-permute-start.7
  168.1 2.1 collective-permute-start.6
  171.6 7.1 %all-reduce.11 = (f32[]{:T(128)}, f32[]{:T(128)}, f32[]{:T(128)}) all-reduce(f32[]{:T(128)} %get-tuple-element.1175, f32[]{:T(128)} %get-tuple-element.1174, f32[]{:T(128)} %get-tuple-element.1173), channel_id=1, replica_groups=mesh['gx_0'=2,'gx_1'=2,'gy_0'=2,'gy_1'=4,'gz'=8] {'gx_0'}, use_global_device_ids=true, to_apply=%region_13.14 | all-reduce | flops 3 | bytes 24 | tf_op jit(solution)/shard_map/psum | solution.py:25
  178.7 3.2 all-reduce.9
  181.8 5.6 all-reduce.7
  187.4 10.4 %all-reduce.5 = (f32[]{:T(128)}, f32[]{:T(128)}, f32[]{:T(128)}) all-reduce(f32[]{:T(128)} %get-tuple-element.1256, f32[]{:T(128)} %get-tuple-element.1257, f32[]{:T(128)} %get-tuple-element.1258), channel_id=1, replica_groups=mesh['gx_0'=2,'gx_1'=2,'gy_0'=2,'gy_1'=4,'gz'=8] {'gy_1'}, use_global_device_ids=true, to_apply=%region_16.17 | all-reduce | flops 3 | bytes 24 | tf_op jit(solution)/shard_map/psum | solution.py:25
  197.8 19.6 %all-reduce.3 = (f32[]{:T(128)}, f32[]{:T(128)}, f32[]{:T(128)}) all-reduce(f32[]{:T(128)} %get-tuple-element.1251, f32[]{:T(128)} %get-tuple-element.1252, f32[]{:T(128)} %get-tuple-element.1253), channel_id=1, replica_groups=mesh['gx_0'=2,'gx_1'=2,'gy_0'=2,'gy_1'=4,'gz'=8] {'gz'}, use_global_device_ids=true, to_apply=%region_17.18 | all-reduce | flops 3 | bytes 24 | tf_op jit(solution)/shard_map/psum | solution.py:25
  221.3 5.1 collective-permute-start.19
  226.4 3.1 collective-permute-start.9
  229.6 2.7 collective-permute-start.8
  234.3 6.0 collective-permute-start.21
  240.4 3.8 collective-permute-start.11
  244.2 2.0 collective-permute-start.10
  246.5 3.1 collective-permute-start.22
  249.7 2.7 collective-permute-start.23
  252.5 92.6 %while.105 = (s32[]{:T(128)}, f32[3,512]{1,0:T(4,128)S(1)}, f32[512,1]{0,1:T(1,128)S(1)}, f32[27,8,512]{2,1,0:T(8,128)S(1)}, f32[27]{0:T(128)S(1)}, /*index=5*/f...) while((s32[]{:T(128)}, f32[3,512]{1,0:T(4,128)S(1)}, ...), condition=%wide.region_8.9_spmd.clone, body=%wide.region_5.8_spmd.clone.sunk | while | flops 11539461 | bytes 4286707 | solution.py:131
  345.8 2.1 fusion.86
  350.6 2.4 collective-permute-start.24
  353.1 4.1 collective-permute-done.24
  357.2 3.1 collective-permute-start.27
  360.3 2.7 collective-permute-start.26
  363.1 5.3 collective-permute-done.26
  370.3 4.3 collective-permute-start.28
  384.0 2.2 fusion.44
  388.7 2.0 fusion.48
  396.5 6.3 scatter-add.235
  405.0 2.5 scatter-add.239
  408.7 5.0 scatter-add.244
  422.3 5.1 collective-permute-start.37
  430.8 6.0 collective-permute-start.39
  438.5 4.3 collective-permute-start.40
  444.7 59.0 %while.106 = (s32[]{:T(128)}, f32[512]{0:T(512)S(1)}, f32[8,512]{1,0:T(8,128)S(1)}, f32[27,8,512]{2,1,0:T(8,128)S(1)}, f32[27,3]{1,0:T(8,128)S(1)}, /*index=5*/f32[27]{0:T(128)S(1)}, s32[]{:T(128)}, s32[]{:T(128)}, s32[]{}, s32[]{}) while((s32[]{:T(128)}, f32[512]{0:T(512)S(1)}, f32[8,512]{1,0:T(8,128)S(1)}, ...), condition=%wide.region_36.37_spmd.clone, body=%wide.region_33.36_spmd.clone.sunk | while | flops 5507589 | bytes 2150615 | solution.py:92
  503.8 3.7 collective-permute-start.31
  510.7 7.2 %all-reduce.10 = (f32[]{:T(128)}, f32[]{:T(128)}) all-reduce(f32[]{:T(128)} %get-tuple-element.1172, f32[]{:T(128)} %get-tuple-element.1171), channel_id=1, replica_groups=mesh['gx_0'=2,'gx_1'=2,'gy_0'=2,'gy_1'=4,'gz'=8] {'gx_0'}, use_global_device_ids=true, to_apply=%region_42.43 | all-reduce | flops 2 | bytes 16 | tf_op jit(solution)/shard_map/psum | solution.py:25
  517.9 3.1 all-reduce.8
  521.0 5.6 all-reduce.6
  526.5 10.4 %all-reduce.4 = (f32[]{:T(128)}, f32[]{:T(128)}) all-reduce(f32[]{:T(128)} %get-tuple-element.1254, f32[]{:T(128)} %get-tuple-element.1255), channel_id=1, replica_groups=mesh['gx_0'=2,'gx_1'=2,'gy_0'=2,'gy_1'=4,'gz'=8] {'gy_1'}, use_global_device_ids=true, to_apply=%region_45.46 | all-reduce | flops 2 | bytes 16 | tf_op jit(solution)/shard_map/psum | solution.py:25
  536.9 19.7 %all-reduce.2 = (f32[]{:T(128)}, f32[]{:T(128)}) all-reduce(f32[]{:T(128)} %get-tuple-element.1249, f32[]{:T(128)} %get-tuple-element.1250), channel_id=1, replica_groups=mesh['gx_0'=2,'gx_1'=2,'gy_0'=2,'gy_1'=4,'gz'=8] {'gz'}, use_global_device_ids=true, to_apply=%region_46.47 | all-reduce | flops 2 | bytes 16 | tf_op jit(solution)/shard_map/psum | solution.py:25
  560.0 5.1 collective-permute-start.43
  565.1 3.1 collective-permute-start.33
  568.3 2.7 collective-permute-start.32
  573.0 6.0 collective-permute-start.45
  579.1 2.2 collective-permute-start.35
  581.3 3.6 collective-permute-start.34
  585.2 3.1 collective-permute-start.46
  588.4 2.7 collective-permute-start.47
  591.3 92.6 %while.107 = (s32[]{:T(128)}, f32[3,512]{1,0:T(4,128)S(1)}, f32[512,1]{0,1:T(1,128)S(1)}, f32[27,8,512]{2,1,0:T(8,128)S(1)}, f32[27]{0:T(128)S(1)}, /*index=5*/f...) while((s32[]{:T(128)}, f32[3,512]{1,0:T(4,128)S(1)}, ...), condition=%wide.region_40.41_spmd.clone, body=%wide.region_37.40_spmd.clone.sunk | while | flops 11539461 | bytes 4286707 | solution.py:131
  684.5 2.1 fusion.87
  (1439 shorter events, 401.5 us)
Async XLA Ops:
  4.1 11.0 %collective-permute-start.1 = (f32[8,1,1,1,512]{4,0,3,2,1:T(8,128)S(1)}, f32[8,1,1,1,512]{4,0,3,2,1:T(8,128)S(1)}, u32[]{:S(2)}, u32[]{:S(2)}) collective-permute-start(f32[8,1,1,1,512]{4,0,3,2,1:T(8,128)S(1)} %pad_maximum_fusion.31), channel_id=1, source_target_pairs={{64,0},{128,64},{192,128},{65,1},{129,65},{193,129},{66,2},{130,66... | collective-permute-start | bytes 49160 | tf_op jit(solution)/shard_map/ppermute | solution.py:38
  6.7 8.4 %collective-permute-start = (f32[8,1,1,1,512]{4,0,3,2,1:T(8,128)S(1)}, f32[8,1,1,1,512]{4,0,3,2,1:T(8,128)S(1)}, u32[]{:S(2)}, u32[]{:S(2)}) collective-permute-start(f32[8,1,1,1,512]{4,0,3,2,1:T(8,128)S(1)} %pad_maximum_fusion.31), channel_id=1, source_target_pairs={{0,64},{64,128},{128,192},{1,65},{65,129},{129,193},{2,66},{66,130... | collective-permute-start | bytes 49160 | tf_op jit(solution)/shard_map/ppermute | solution.py:36
  15.9 6.7 collective-permute-start.3
  20.5 8.1 %collective-permute-start.2 = (f32[8,3,1,1,512]{4,0,3,2,1:T(8,128)S(1)}, f32[8,3,1,1,512]{4,0,3,2,1:T(8,128)S(1)}, u32[]{:S(2)}, u32[]{:S(2)}) collective-permute-start(f32[8,3,1,1,512]{4,0,3,2,1:T(8,128)S(1)} %fusion.219), channel_id=1, source_target_pairs={{0,8},{8,16},{16,24},{24,32},{32,40},{40,48},{48,56},{1,9},{9,17},... | collective-permute-start | bytes 147464 | tf_op jit(solution)/shard_map/ppermute | solution.py:36
  29.3 7.0 %collective-permute-start.5 = (f32[8,3,3,1,512]{4,0,3,2,1:T(8,128)S(1)}, f32[8,3,3,1,512]{4,0,3,2,1:T(8,128)S(1)}, u32[]{:S(2)}, u32[]{:S(2)}) collective-permute-start(f32[8,3,3,1,512]{4,0,3,2,1:T(8,128)S(1)} %fusion.135), channel_id=1, source_target_pairs={{1,0},{2,1},{3,2},{4,3},{5,4},{6,5},{7,6},{9,8},{10,9},{11,10},{12... | collective-permute-start | bytes 442376 | tf_op jit(solution)/shard_map/ppermute | solution.py:38
  31.4 7.0 %collective-permute-start.4 = (f32[8,3,3,1,512]{4,0,3,2,1:T(8,128)S(1)}, f32[8,3,3,1,512]{4,0,3,2,1:T(8,128)S(1)}, u32[]{:S(2)}, u32[]{:S(2)}) collective-permute-start(f32[8,3,3,1,512]{4,0,3,2,1:T(8,128)S(1)} %fusion.135), channel_id=1, source_target_pairs={{0,1},{1,2},{2,3},{3,4},{4,5},{5,6},{6,7},{8,9},{9,10},{10,11},{11... | collective-permute-start | bytes 442376 | tf_op jit(solution)/shard_map/ppermute | solution.py:36
  63.6 33.9 %copy-start.2 = (f32[1,1,1,512]{3,2,1,0:T(1,128)S(1)}, f32[1,1,1,512]{3,2,1,0:T(1,128)}, u32[]{:S(2)}) copy-start(f32[1,1,1,512]{3,2,1,0:T(1,128)} %param.131) | copy-start | bytes 6148
  81.0 7.2 %collective-permute-start.12 = (f32[2,16,16]{2,1,0:T(8,128)S(1)}, f32[2,16,16]{2,1,0:T(8,128)S(1)}, u32[]{:S(2)}, u32[]{:S(2)}) collective-permute-start(f32[2,16,16]{2,1,0:T(8,128)S(1)} %get-tuple-element.1437), channel_id=1, source_target_pairs={{0,64},{64,128},{128,192},{1,65},{65,129},{129,193},{2,66},{66,130... | collective-permute-start | bytes 6152 | tf_op jit(solution)/shard_map/ppermute | solution.py:36
  83.0 6.6 collective-permute-start.13
  89.6 8.0 %collective-permute-start.14 = (f32[20,2,16]{2,1,0:T(2,128)S(1)}, f32[20,2,16]{2,1,0:T(2,128)S(1)}, u32[]{:S(2)}, u32[]{:S(2)}) collective-permute-start(f32[20,2,16]{2,1,0:T(2,128)S(1)} %get-tuple-element.1285), channel_id=1, source_target_pairs={{0,8},{8,16},{16,24},{24,32},{32,40},{40,48},{48,56},{1,9},{9,17},... | collective-permute-start | bytes 7688 | tf_op jit(solution)/shard_map/ppermute | solution.py:36
  91.5 7.5 %collective-permute-start.15 = (f32[20,2,16]{2,1,0:T(2,128)S(1)}, f32[20,2,16]{2,1,0:T(2,128)S(1)}, u32[]{:S(2)}, u32[]{:S(2)}) collective-permute-start(f32[20,2,16]{2,1,0:T(2,128)S(1)} %get-tuple-element.1286), channel_id=1, source_target_pairs={{8,0},{16,8},{24,16},{32,24},{40,32},{48,40},{56,48},{9,1},{17,9},... | collective-permute-start | bytes 7688 | tf_op jit(solution)/shard_map/ppermute | solution.py:38
  99.2 71.1 %collective-permute-start.16 = (f32[20,20,2]{2,1,0:T(8,128)S(1)}, f32[20,20,2]{2,1,0:T(8,128)S(1)}, u32[]{:S(2)}, u32[]{:S(2)}) collective-permute-start(f32[20,20,2]{2,1,0:T(8,128)S(1)} %get-tuple-element.1277), channel_id=1, source_target_pairs={{0,1},{1,2},{2,3},{3,4},{4,5},{5,6},{6,7},{8,9},{9,10},{10,11},{11... | collective-permute-start | bytes 9608 | tf_op jit(solution)/shard_map/ppermute | solution.py:36
  103.0 67.3 %collective-permute-start.17 = (f32[20,20,2]{2,1,0:T(8,128)S(1)}, f32[20,20,2]{2,1,0:T(8,128)S(1)}, u32[]{:S(2)}, u32[]{:S(2)}) collective-permute-start(f32[20,20,2]{2,1,0:T(8,128)S(1)} %get-tuple-element.1278), channel_id=1, source_target_pairs={{1,0},{2,1},{3,2},{4,3},{5,4},{6,5},{7,6},{9,8},{10,9},{11,10},{12... | collective-permute-start | bytes 9608 | tf_op jit(solution)/shard_map/ppermute | solution.py:38
  164.3 6.3 copy-start
  164.4 62.0 %collective-permute-start.7 = (f32[1,1,1,512]{3,2,1,0:T(1,128)S(1)}, f32[1,1,1,512]{3,2,1,0:T(1,128)S(1)}, u32[]{:S(2)}, u32[]{:S(2)}) collective-permute-start(f32[1,1,1,512]{3,2,1,0:T(1,128)S(1)} %bitcast.816), channel_id=1, source_target_pairs={{64,0},{128,64},{192,128},{65,1},{129,65},{193,129},{66,2},{130,66... | collective-permute-start | bytes 6152 | tf_op jit(solution)/shard_map/ppermute | solution.py:38
  168.1 58.3 %collective-permute-start.6 = (f32[1,1,1,512]{3,2,1,0:T(1,128)S(1)}, f32[1,1,1,512]{3,2,1,0:T(1,128)S(1)}, u32[]{:S(2)}, u32[]{:S(2)}) collective-permute-start(f32[1,1,1,512]{3,2,1,0:T(1,128)S(1)} %bitcast.817), channel_id=1, source_target_pairs={{0,64},{64,128},{128,192},{1,65},{65,129},{129,193},{2,66},{66,130... | collective-permute-start | bytes 6152 | tf_op jit(solution)/shard_map/ppermute | solution.py:36
  219.3 13.0 %collective-permute-start.18 = (f32[5,16,16]{2,1,0:T(8,128)S(1)}, f32[5,16,16]{2,1,0:T(8,128)S(1)}, u32[]{:S(2)}, u32[]{:S(2)}) collective-permute-start(f32[5,16,16]{2,1,0:T(8,128)S(1)} %get-tuple-element.1435), channel_id=1, source_target_pairs={{0,64},{64,128},{128,192},{1,65},{65,129},{129,193},{2,66},{66,130... | collective-permute-start | bytes 15368 | tf_op jit(solution)/shard_map/ppermute | solution.py:36
  221.3 11.1 %collective-permute-start.19 = (f32[5,16,16]{2,1,0:T(8,128)S(1)}, f32[5,16,16]{2,1,0:T(8,128)S(1)}, u32[]{:S(2)}, u32[]{:S(2)}) collective-permute-start(f32[5,16,16]{2,1,0:T(8,128)S(1)} %get-tuple-element.1436), channel_id=1, source_target_pairs={{64,0},{128,64},{192,128},{65,1},{129,65},{193,129},{66,2},{130,66... | collective-permute-start | bytes 15368 | tf_op jit(solution)/shard_map/ppermute | solution.py:38
  226.4 13.9 %collective-permute-start.9 = (f32[3,1,1,512]{3,2,1,0:T(1,128)S(1)}, f32[3,1,1,512]{3,2,1,0:T(1,128)S(1)}, u32[]{:S(2)}, u32[]{:S(2)}) collective-permute-start(f32[3,1,1,512]{3,2,1,0:T(1,128)S(1)} %pad_maximum_fusion.44), channel_id=1, source_target_pairs={{8,0},{16,8},{24,16},{32,24},{40,32},{48,40},{56,48},{9,1},{17,9},... | collective-permute-start | bytes 18440 | tf_op jit(solution)/shard_map/ppermute | solution.py:38
  229.6 10.8 %collective-permute-start.8 = (f32[3,1,1,512]{3,2,1,0:T(1,128)S(1)}, f32[3,1,1,512]{3,2,1,0:T(1,128)S(1)}, u32[]{:S(2)}, u32[]{:S(2)}) collective-permute-start(f32[3,1,1,512]{3,2,1,0:T(1,128)S(1)} %pad_maximum_fusion.44), channel_id=1, source_target_pairs={{0,8},{8,16},{16,24},{24,32},{32,40},{40,48},{48,56},{1,9},{9,17},... | collective-permute-start | bytes 18440 | tf_op jit(solution)/shard_map/ppermute | solution.py:36
  232.4 13.9 %collective-permute-start.20 = (f32[26,5,16]{2,1,0:T(8,128)S(1)}, f32[26,5,16]{2,1,0:T(8,128)S(1)}, u32[]{:S(2)}, u32[]{:S(2)}) collective-permute-start(f32[26,5,16]{2,1,0:T(8,128)S(1)} %get-tuple-element.1281), channel_id=1, source_target_pairs={{0,8},{8,16},{16,24},{24,32},{32,40},{40,48},{48,56},{1,9},{9,17},... | collective-permute-start | bytes 24968 | tf_op jit(solution)/shard_map/ppermute | solution.py:36
  234.3 12.0 %collective-permute-start.21 = (f32[26,5,16]{2,1,0:T(8,128)S(1)}, f32[26,5,16]{2,1,0:T(8,128)S(1)}, u32[]{:S(2)}, u32[]{:S(2)}) collective-permute-start(f32[26,5,16]{2,1,0:T(8,128)S(1)} %get-tuple-element.1282), channel_id=1, source_target_pairs={{8,0},{16,8},{24,16},{32,24},{40,32},{48,40},{56,48},{9,1},{17,9},... | collective-permute-start | bytes 24968 | tf_op jit(solution)/shard_map/ppermute | solution.py:38
  240.4 12.0 %collective-permute-start.11 = (f32[3,3,1,512]{3,2,1,0:T(1,128)S(1)}, f32[3,3,1,512]{3,2,1,0:T(1,128)S(1)}, u32[]{:S(2)}, u32[]{:S(2)}) collective-permute-start(f32[3,3,1,512]{3,2,1,0:T(1,128)S(1)} %pad_maximum_fusion.42), channel_id=1, source_target_pairs={{1,0},{2,1},{3,2},{4,3},{5,4},{6,5},{7,6},{9,8},{10,9},{11,10},{12... | collective-permute-start | bytes 55304 | tf_op jit(solution)/shard_map/ppermute | solution.py:38
  244.2 8.2 %collective-permute-start.10 = (f32[3,3,1,512]{3,2,1,0:T(1,128)S(1)}, f32[3,3,1,512]{3,2,1,0:T(1,128)S(1)}, u32[]{:S(2)}, u32[]{:S(2)}) collective-permute-start(f32[3,3,1,512]{3,2,1,0:T(1,128)S(1)} %pad_maximum_fusion.42), channel_id=1, source_target_pairs={{0,1},{1,2},{2,3},{3,4},{4,5},{5,6},{6,7},{8,9},{9,10},{10,11},{11... | collective-permute-start | bytes 55304 | tf_op jit(solution)/shard_map/ppermute | solution.py:36
  246.5 98.6 %collective-permute-start.22 = (f32[26,26,5]{2,1,0:T(8,128)S(1)}, f32[26,26,5]{2,1,0:T(8,128)S(1)}, u32[]{:S(2)}, u32[]{:S(2)}) collective-permute-start(f32[26,26,5]{2,1,0:T(8,128)S(1)} %get-tuple-element.1273), channel_id=1, source_target_pairs={{0,1},{1,2},{2,3},{3,4},{4,5},{5,6},{6,7},{8,9},{9,10},{10,11},{11... | collective-permute-start | bytes 40568 | tf_op jit(solution)/shard_map/ppermute | solution.py:36
  249.7 95.5 %collective-permute-start.23 = (f32[26,26,5]{2,1,0:T(8,128)S(1)}, f32[26,26,5]{2,1,0:T(8,128)S(1)}, u32[]{:S(2)}, u32[]{:S(2)}) collective-permute-start(f32[26,26,5]{2,1,0:T(8,128)S(1)} %get-tuple-element.1274), channel_id=1, source_target_pairs={{1,0},{2,1},{3,2},{4,3},{5,4},{6,5},{7,6},{9,8},{10,9},{11,10},{12... | collective-permute-start | bytes 40568 | tf_op jit(solution)/shard_map/ppermute | solution.py:38
  345.8 2.8 copy-start.3
  348.7 4.4 collective-permute-start.25
  350.6 6.6 collective-permute-start.24
  357.2 6.0 collective-permute-start.27
  360.3 8.1 %collective-permute-start.26 = (f32[8,3,1,1,512]{4,0,3,2,1:T(8,128)S(1)}, f32[8,3,1,1,512]{4,0,3,2,1:T(8,128)S(1)}, u32[]{:S(2)}, u32[]{:S(2)}) collective-permute-start(f32[8,3,1,1,512]{4,0,3,2,1:T(8,128)S(1)} %fusion.221), channel_id=1, source_target_pairs={{0,8},{8,16},{16,24},{24,32},{32,40},{40,48},{48,56},{1,9},{9,17},... | collective-permute-start | bytes 147464 | tf_op jit(solution)/shard_map/ppermute | solution.py:36
  368.4 7.4 %collective-permute-start.29 = (f32[8,3,3,1,512]{4,0,3,2,1:T(8,128)S(1)}, f32[8,3,3,1,512]{4,0,3,2,1:T(8,128)S(1)}, u32[]{:S(2)}, u32[]{:S(2)}) collective-permute-start(f32[8,3,3,1,512]{4,0,3,2,1:T(8,128)S(1)} %fusion.139), channel_id=1, source_target_pairs={{1,0},{2,1},{3,2},{4,3},{5,4},{6,5},{7,6},{9,8},{10,9},{11,10},{12... | collective-permute-start | bytes 442376 | tf_op jit(solution)/shard_map/ppermute | solution.py:38
  370.3 7.0 %collective-permute-start.28 = (f32[8,3,3,1,512]{4,0,3,2,1:T(8,128)S(1)}, f32[8,3,3,1,512]{4,0,3,2,1:T(8,128)S(1)}, u32[]{:S(2)}, u32[]{:S(2)}) collective-permute-start(f32[8,3,3,1,512]{4,0,3,2,1:T(8,128)S(1)} %fusion.139), channel_id=1, source_target_pairs={{0,1},{1,2},{2,3},{3,4},{4,5},{5,6},{6,7},{8,9},{9,10},{10,11},{11... | collective-permute-start | bytes 442376 | tf_op jit(solution)/shard_map/ppermute | solution.py:36
  420.3 7.2 %collective-permute-start.36 = (f32[2,16,16]{2,1,0:T(8,128)S(1)}, f32[2,16,16]{2,1,0:T(8,128)S(1)}, u32[]{:S(2)}, u32[]{:S(2)}) collective-permute-start(f32[2,16,16]{2,1,0:T(8,128)S(1)} %get-tuple-element.1433), channel_id=1, source_target_pairs={{0,64},{64,128},{128,192},{1,65},{65,129},{129,193},{2,66},{66,130... | collective-permute-start | bytes 6152 | tf_op jit(solution)/shard_map/ppermute | solution.py:36
  422.3 6.6 collective-permute-start.37
  428.9 8.0 %collective-permute-start.38 = (f32[20,2,16]{2,1,0:T(2,128)S(1)}, f32[20,2,16]{2,1,0:T(2,128)S(1)}, u32[]{:S(2)}, u32[]{:S(2)}) collective-permute-start(f32[20,2,16]{2,1,0:T(2,128)S(1)} %get-tuple-element.1283), channel_id=1, source_target_pairs={{0,8},{8,16},{16,24},{24,32},{32,40},{40,48},{48,56},{1,9},{9,17},... | collective-permute-start | bytes 7688 | tf_op jit(solution)/shard_map/ppermute | solution.py:36
  430.8 7.5 %collective-permute-start.39 = (f32[20,2,16]{2,1,0:T(2,128)S(1)}, f32[20,2,16]{2,1,0:T(2,128)S(1)}, u32[]{:S(2)}, u32[]{:S(2)}) collective-permute-start(f32[20,2,16]{2,1,0:T(2,128)S(1)} %get-tuple-element.1284), channel_id=1, source_target_pairs={{8,0},{16,8},{24,16},{32,24},{40,32},{48,40},{56,48},{9,1},{17,9},... | collective-permute-start | bytes 7688 | tf_op jit(solution)/shard_map/ppermute | solution.py:38
  438.5 71.0 %collective-permute-start.40 = (f32[20,20,2]{2,1,0:T(8,128)S(1)}, f32[20,20,2]{2,1,0:T(8,128)S(1)}, u32[]{:S(2)}, u32[]{:S(2)}) collective-permute-start(f32[20,20,2]{2,1,0:T(8,128)S(1)} %get-tuple-element.1275), channel_id=1, source_target_pairs={{0,1},{1,2},{2,3},{3,4},{4,5},{5,6},{6,7},{8,9},{9,10},{10,11},{11... | collective-permute-start | bytes 9608 | tf_op jit(solution)/shard_map/ppermute | solution.py:36
  442.8 66.7 %collective-permute-start.41 = (f32[20,20,2]{2,1,0:T(8,128)S(1)}, f32[20,20,2]{2,1,0:T(8,128)S(1)}, u32[]{:S(2)}, u32[]{:S(2)}) collective-permute-start(f32[20,20,2]{2,1,0:T(8,128)S(1)} %get-tuple-element.1276), channel_id=1, source_target_pairs={{1,0},{2,1},{3,2},{4,3},{5,4},{6,5},{7,6},{9,8},{10,9},{11,10},{12... | collective-permute-start | bytes 9608 | tf_op jit(solution)/shard_map/ppermute | solution.py:38
  503.8 61.3 %collective-permute-start.31 = (f32[1,1,1,512]{3,2,1,0:T(1,128)S(1)}, f32[1,1,1,512]{3,2,1,0:T(1,128)S(1)}, u32[]{:S(2)}, u32[]{:S(2)}) collective-permute-start(f32[1,1,1,512]{3,2,1,0:T(1,128)S(1)} %bitcast.821), channel_id=1, source_target_pairs={{64,0},{128,64},{192,128},{65,1},{129,65},{193,129},{66,2},{130,66... | collective-permute-start | bytes 6152 | tf_op jit(solution)/shard_map/ppermute | solution.py:38
  507.5 57.6 %collective-permute-start.30 = (f32[1,1,1,512]{3,2,1,0:T(1,128)S(1)}, f32[1,1,1,512]{3,2,1,0:T(1,128)S(1)}, u32[]{:S(2)}, u32[]{:S(2)}) collective-permute-start(f32[1,1,1,512]{3,2,1,0:T(1,128)S(1)} %bitcast.822), channel_id=1, source_target_pairs={{0,64},{64,128},{128,192},{1,65},{65,129},{129,193},{2,66},{66,130... | collective-permute-start | bytes 6152 | tf_op jit(solution)/shard_map/ppermute | solution.py:36
  510.7 80.6 %copy-start.1 = (f32[16,16,16]{2,1,0:T(8,128)}, f32[16,16,16]{2,1,0:T(8,128)S(1)}, u32[]{:S(2)}) copy-start(f32[16,16,16]{2,1,0:T(8,128)S(1)} %get-tuple-element.1269) | copy-start | bytes 49156
  558.0 13.0 %collective-permute-start.42 = (f32[5,16,16]{2,1,0:T(8,128)S(1)}, f32[5,16,16]{2,1,0:T(8,128)S(1)}, u32[]{:S(2)}, u32[]{:S(2)}) collective-permute-start(f32[5,16,16]{2,1,0:T(8,128)S(1)} %get-tuple-element.1431), channel_id=1, source_target_pairs={{0,64},{64,128},{128,192},{1,65},{65,129},{129,193},{2,66},{66,130... | collective-permute-start | bytes 15368 | tf_op jit(solution)/shard_map/ppermute | solution.py:36
  560.0 11.1 %collective-permute-start.43 = (f32[5,16,16]{2,1,0:T(8,128)S(1)}, f32[5,16,16]{2,1,0:T(8,128)S(1)}, u32[]{:S(2)}, u32[]{:S(2)}) collective-permute-start(f32[5,16,16]{2,1,0:T(8,128)S(1)} %get-tuple-element.1432), channel_id=1, source_target_pairs={{64,0},{128,64},{192,128},{65,1},{129,65},{193,129},{66,2},{130,66... | collective-permute-start | bytes 15368 | tf_op jit(solution)/shard_map/ppermute | solution.py:38
  565.1 13.9 %collective-permute-start.33 = (f32[3,1,1,512]{3,2,1,0:T(1,128)S(1)}, f32[3,1,1,512]{3,2,1,0:T(1,128)S(1)}, u32[]{:S(2)}, u32[]{:S(2)}) collective-permute-start(f32[3,1,1,512]{3,2,1,0:T(1,128)S(1)} %pad_maximum_fusion.45), channel_id=1, source_target_pairs={{8,0},{16,8},{24,16},{32,24},{40,32},{48,40},{56,48},{9,1},{17,9},... | collective-permute-start | bytes 18440 | tf_op jit(solution)/shard_map/ppermute | solution.py:38
  568.3 10.8 %collective-permute-start.32 = (f32[3,1,1,512]{3,2,1,0:T(1,128)S(1)}, f32[3,1,1,512]{3,2,1,0:T(1,128)S(1)}, u32[]{:S(2)}, u32[]{:S(2)}) collective-permute-start(f32[3,1,1,512]{3,2,1,0:T(1,128)S(1)} %pad_maximum_fusion.45), channel_id=1, source_target_pairs={{0,8},{8,16},{16,24},{24,32},{32,40},{40,48},{48,56},{1,9},{9,17},... | collective-permute-start | bytes 18440 | tf_op jit(solution)/shard_map/ppermute | solution.py:36
  571.1 13.9 %collective-permute-start.44 = (f32[26,5,16]{2,1,0:T(8,128)S(1)}, f32[26,5,16]{2,1,0:T(8,128)S(1)}, u32[]{:S(2)}, u32[]{:S(2)}) collective-permute-start(f32[26,5,16]{2,1,0:T(8,128)S(1)} %get-tuple-element.1279), channel_id=1, source_target_pairs={{0,8},{8,16},{16,24},{24,32},{32,40},{40,48},{48,56},{1,9},{9,17},... | collective-permute-start | bytes 24968 | tf_op jit(solution)/shard_map/ppermute | solution.py:36
  573.0 12.0 %collective-permute-start.45 = (f32[26,5,16]{2,1,0:T(8,128)S(1)}, f32[26,5,16]{2,1,0:T(8,128)S(1)}, u32[]{:S(2)}, u32[]{:S(2)}) collective-permute-start(f32[26,5,16]{2,1,0:T(8,128)S(1)} %get-tuple-element.1280), channel_id=1, source_target_pairs={{8,0},{16,8},{24,16},{32,24},{40,32},{48,40},{56,48},{9,1},{17,9},... | collective-permute-start | bytes 24968 | tf_op jit(solution)/shard_map/ppermute | solution.py:38
  579.1 12.0 %collective-permute-start.35 = (f32[3,3,1,512]{3,2,1,0:T(1,128)S(1)}, f32[3,3,1,512]{3,2,1,0:T(1,128)S(1)}, u32[]{:S(2)}, u32[]{:S(2)}) collective-permute-start(f32[3,3,1,512]{3,2,1,0:T(1,128)S(1)} %pad_maximum_fusion.43), channel_id=1, source_target_pairs={{1,0},{2,1},{3,2},{4,3},{5,4},{6,5},{7,6},{9,8},{10,9},{11,10},{12... | collective-permute-start | bytes 55304 | tf_op jit(solution)/shard_map/ppermute | solution.py:38
  581.3 9.8 %collective-permute-start.34 = (f32[3,3,1,512]{3,2,1,0:T(1,128)S(1)}, f32[3,3,1,512]{3,2,1,0:T(1,128)S(1)}, u32[]{:S(2)}, u32[]{:S(2)}) collective-permute-start(f32[3,3,1,512]{3,2,1,0:T(1,128)S(1)} %pad_maximum_fusion.43), channel_id=1, source_target_pairs={{0,1},{1,2},{2,3},{3,4},{4,5},{5,6},{6,7},{8,9},{9,10},{10,11},{11... | collective-permute-start | bytes 55304 | tf_op jit(solution)/shard_map/ppermute | solution.py:36
  585.2 98.7 %collective-permute-start.46 = (f32[26,26,5]{2,1,0:T(8,128)S(1)}, f32[26,26,5]{2,1,0:T(8,128)S(1)}, u32[]{:S(2)}, u32[]{:S(2)}) collective-permute-start(f32[26,26,5]{2,1,0:T(8,128)S(1)} %get-tuple-element.1271), channel_id=1, source_target_pairs={{0,1},{1,2},{2,3},{3,4},{4,5},{5,6},{6,7},{8,9},{9,10},{10,11},{11... | collective-permute-start | bytes 40568 | tf_op jit(solution)/shard_map/ppermute | solution.py:36
  588.4 95.5 %collective-permute-start.47 = (f32[26,26,5]{2,1,0:T(8,128)S(1)}, f32[26,26,5]{2,1,0:T(8,128)S(1)}, u32[]{:S(2)}, u32[]{:S(2)}) collective-permute-start(f32[26,26,5]{2,1,0:T(8,128)S(1)} %get-tuple-element.1272), channel_id=1, source_target_pairs={{1,0},{2,1},{3,2},{4,3},{5,4},{6,5},{7,6},{9,8},{10,9},{11,10},{12... | collective-permute-start | bytes 40568 | tf_op jit(solution)/shard_map/ppermute | solution.py:38
where the time goes:
time: 696 us; the launch traced here: 689 us
  other arithmetic  256 us (37%)
  starting transfers between devices  152 us (22%)
  local copies, waits for them, and re-layouts  126 us (18%)
  blocking collectives  91.8 us (13%)
  matrix products  28.1 us (4%)
  waiting for transfers between devices  22.9 us (3%)
  between operations  7.8 us (1%)
    mul x54, other arithmetic, gb_visit(): -0.5 * charge_pair  92.2 us
    psum x10, blocking collectives, one_axis_at_a_time(): return functools.reduce(lax.psum, axes, x)  91.8 us
    ppermute x24, starting transfers between devices, padded(): lax.ppermute(head, axis, [((i + 1) % count, i) for i in range(ends)])  90.2 us
    dynamic_slice x108, local copies, waits for them, and re-layouts, born_radius(): lax.scan(born_visit, jnp.zeros((slot_count,), jnp.float32), (blocks, offs...  63.9 us
    ppermute x24, starting transfers between devices, padded(): lax.ppermute(tail, axis, [(i, (i + 1) % count) for i in range(ends)])  62 us
    reduce_sum x54, other arithmetic, born_visit(): return (summed + jnp.sum(weight_term, axis=1), None)  59.4 us
    scatter-add x50, local copies, waits for them, and re-layouts, splat_window(): density = density.at[low_x + reach:high_x + reach, low_y + reach:high_y +...  53.7 us
    reduce_sum x108, other arithmetic, geometry(): squared = jnp.sum(separation * separation, axis=0)  39.2 us
  transfers between devices with their start and end apart: 48, of which 11 were waited for; matrix products, arithmetic and copies ran while one was open for 45% of the time, Pallas kernels for 0%

commit v1 on v0

v1 whole, which is shorter than its diff:
```python
import functools
import math

import jax
import jax.numpy as jnp
from jax import lax
from jax.experimental import pallas as pl
from jax.experimental.pallas import tpu as pltpu
from jax.sharding import PartitionSpec as P

SPLAT_MARGIN = 3
BLUR_REACH = 2
STEPS = 2
CUTOFF = 10.0
EPSILON = 1e-06
STEP_SIZE = 1.0
FIT_GAIN = 0.2

AXES = ("gx", "gy", "gz")
SLOTS = 512
LANES = 128
TILES = SLOTS // LANES
ROWS = 64
BRICK = 16
PLANES = 26
PAD = 8
WIDE = 32
INTERPRET = False


def call(kernel, out_shape, cost, scratch=(), smem=0, n_in=0, vmem=48):
    specs = [pl.BlockSpec(memory_space=pltpu.SMEM)] * smem
    specs += [pl.BlockSpec(memory_space=pltpu.VMEM)] * (n_in - smem)
    many = isinstance(out_shape, (tuple, list))
    out_spec = pl.BlockSpec(memory_space=pltpu.VMEM)
    return pl.pallas_call(
        kernel,
        out_shape=out_shape,
        in_specs=specs,
        out_specs=[out_spec] * len(out_shape) if many else out_spec,
        scratch_shapes=list(scratch),
        cost_estimate=pl.CostEstimate(flops=cost, bytes_accessed=1 << 18, transcendentals=0),
        compiler_params=pltpu.CompilerParams(vmem_limit_bytes=vmem << 20),
        interpret=INTERPRET,
    )


def spread(row):
    return jnp.transpose(jnp.broadcast_to(row, (LANES, LANES)))


def gather_rows(acc):
    return jnp.sum(jnp.transpose(acc), axis=0, keepdims=True)


def cell_sides(number, fixed_y, fixed_z):
    side_x = lax.rem(number, 3) - 1
    side_y = number // 3 - 1 if fixed_y is None else fixed_y
    return side_x, side_y, fixed_z


def born_kernel(groups, *refs):
    own = refs[0]
    cells = refs[1 : 1 + 2 * len(groups)]
    out, col, acc = refs[1 + 2 * len(groups) :]
    for channel in range(3):
        for tile in range(TILES):
            row = own[4 * channel + tile : 4 * channel + tile + 1, :] * (1.0 / CUTOFF)
            col[channel, tile * LANES : (tile + 1) * LANES, :] = spread(row)
    acc[...] = jnp.zeros_like(acc)
    for index, (count, fixed_y, fixed_z) in enumerate(groups):
        pos, aux = cells[2 * index], cells[2 * index + 1]

        def visit(number, carry, pos=pos, aux=aux, fixed_y=fixed_y, fixed_z=fixed_z):
            sides = cell_sides(number, fixed_y, fixed_z)
            shift = [side * float(BRICK) if isinstance(side, int) else side.astype(jnp.float32) * float(BRICK) for side in sides]
            rows = []
            for tile in range(TILES):
                coords = [
                    (pos[number, 4 * d + tile : 4 * d + tile + 1, :] + shift[d]) * (1.0 / CUTOFF)
                    for d in range(3)
                ]
                rows.append(coords + [aux[number, 16 + tile : 17 + tile, :]])

            def block(ib, inner):
                at = pl.ds(pl.multiple_of(ib * ROWS, ROWS), ROWS)
                xi, yi, zi = col[0, at, :], col[1, at, :], col[2, at, :]
                total = acc[at, :]
                for xj, yj, zj, wj in rows:
                    dx, dy, dz = xi - xj, yi - yj, zi - zj
                    u = dx * dx + dy * dy + dz * dz
                    s = jnp.maximum(1.0 - u, 0.0)
                    e = jnp.exp(u * (-CUTOFF * CUTOFF / 8.0))
                    total = total + e * s * (s * wj)
                acc[at, :] = total
                return inner

            return lax.fori_loop(0, SLOTS // ROWS, block, carry)

        lax.fori_loop(0, count, visit, 0)
    for tile in range(TILES):
        out[tile : tile + 1, :] = gather_rows(acc[tile * LANES : (tile + 1) * LANES, :])


def gb_kernel(groups, *refs):
    own, own_radius = refs[:2]
    cells = refs[2 : 2 + 3 * len(groups)]
    out, col, acc = refs[2 + 3 * len(groups) :]
    for tile in range(TILES):
        at = slice(tile * LANES, (tile + 1) * LANES)
        for channel in range(3):
            row = own[4 * channel + tile : 4 * channel + tile + 1, :] * (1.0 / CUTOFF)
            col[channel, at, :] = spread(row)
        radius = spread(own_radius[tile : tile + 1, :] * (1.0 / CUTOFF))
        col[3, at, :] = radius
        col[4, at, :] = -0.5 / radius
    acc[...] = jnp.zeros_like(acc)
    for index, (count, fixed_y, fixed_z) in enumerate(groups):
        pos, aux, rad = cells[3 * index : 3 * index + 3]

        def visit(number, carry, pos=pos, aux=aux, rad=rad, fixed_y=fixed_y, fixed_z=fixed_z):
            sides = cell_sides(number, fixed_y, fixed_z)
            shift = [side * float(BRICK) if isinstance(side, int) else side.astype(jnp.float32) * float(BRICK) for side in sides]
            rows = []
            for tile in range(TILES):
                coords = [
                    (pos[number, 4 * d + tile : 4 * d + tile + 1, :] + shift[d]) * (1.0 / CUTOFF)
                    for d in range(3)
                ]
                radius = jnp.maximum(rad[number, tile : tile + 1, :], 0.5) * (1.0 / CUTOFF)
                rows.append(coords + [aux[number, 12 + tile : 13 + tile, :], radius, 0.5 / radius])

            def block(ib, inner):
                at = pl.ds(pl.multiple_of(ib * ROWS, ROWS), ROWS)
                xi, yi, zi = col[0, at, :], col[1, at, :], col[2, at, :]
                ri, ai = col[3, at, :], col[4, at, :]
                fx, fy, fz = acc[0, at, :], acc[1, at, :], acc[2, at, :]
                for xj, yj, zj, qj, rj, aj in rows:
                    dx, dy, dz = xi - xj, yi - yj, zi - zj
                    u = dx * dx + dy * dy + dz * dz
                    s = jnp.maximum(1.0 - u, 0.0)
                    e = jnp.exp(u * (ai * aj))
                    inv = lax.rsqrt(u + (ri * rj) * e)
                    t = s * inv
                    m = (qj * t) * (1.0 + (t * inv) * (0.25 - 0.0625 * e))
                    fx = fx + m * dx
                    fy = fy + m * dy
                    fz = fz + m * dz
                acc[0, at, :] = fx
                acc[1, at, :] = fy
                acc[2, at, :] = fz
                return inner

            return lax.fori_loop(0, SLOTS // ROWS, block, carry)

        lax.fori_loop(0, count, visit, 0)
    for channel in range(3):
        for tile in range(TILES):
            total = gather_rows(acc[channel, tile * LANES : (tile + 1) * LANES, :])
            out[4 * channel + tile : 4 * channel + tile + 1, :] = total


def kernel_weights(reach):
    values = [math.exp(-0.5 * (index - reach) ** 2) for index in range(2 * reach + 1)]
    whole = sum(values)
    return [value / whole for value in values]


TAPS = kernel_weights(BLUR_REACH)


def blurred(values):
    rows = values.shape[0]
    near = pltpu.roll(values, 1, 0) + pltpu.roll(values, rows - 1, 0)
    far = pltpu.roll(values, 2, 0) + pltpu.roll(values, rows - 2, 0)
    return TAPS[2] * values + TAPS[1] * near + TAPS[0] * far


def profiles(row, side, base, rows, low, high, slope):
    number = lax.broadcasted_iota(jnp.int32, (rows, LANES), 0) + base
    shift = side * BRICK
    inside = (number >= low) & (number < high)
    window = inside & (number >= shift - SPLAT_MARGIN) & (number < shift + BRICK + SPLAT_MARGIN)
    moved = row + (float(shift) if isinstance(shift, int) else shift.astype(jnp.float32))
    gap = number.astype(jnp.float32) - moved
    plain = jnp.where(window, jnp.exp(-0.5 * gap * gap), 0.0)
    margin = SPLAT_MARGIN + BLUR_REACH
    reached = inside & (number >= shift - margin) & (number < shift + BRICK + margin)
    first = jnp.where(reached, blurred(plain), 0.0)
    if not slope:
        return first
    return first, jnp.where(reached, blurred(gap * plain), 0.0)


def split(values):
    high = values.astype(jnp.bfloat16)
    return high, (values - high.astype(jnp.float32)).astype(jnp.bfloat16)


def evolve_kernel(bounds, pos, aux, exp_ext, out, sums, px, left_hi, left_lo, right):
    out[...] = jnp.zeros_like(out)

    def splat(number, wide_x, wide_y):
        side_x = lax.rem(number, 3) - 1
        side_y = lax.rem(number // 3, 3) - 1
        side_z = number // 9 - 1
        if wide_x:
            side_x, base_x, rows_x, planes, first = 0, -PAD, WIDE, PLANES, 0
        else:
            base_x, rows_x, planes = side_x * 8, BRICK, 10
            base_x = jnp.where(side_x < 0, -PAD, PAD)
            first = jnp.where(side_x < 0, 0, BRICK)
        if wide_y:
            side_y, base_y, rows_y, start = 0, -PAD, WIDE, 0
        else:
            base_y, rows_y = jnp.where(side_y < 0, -PAD, PAD), BRICK
            start = pl.multiple_of(jnp.where(side_y < 0, 0, BRICK), BRICK)
        for tile in range(TILES):
            lanes = slice(tile * LANES, (tile + 1) * LANES)
            z = profiles(pos[number, 8 + tile : 9 + tile, :], side_z, -PAD, WIDE, bounds[4], bounds[5], False)
            z_hi, z_lo = split(z)
            right[0:WIDE, lanes] = z_hi
            right[WIDE : 2 * WIDE, lanes] = z_lo
            x = profiles(pos[number, tile : tile + 1, :], side_x, base_x, rows_x, bounds[0], bounds[1], False)
            px[0:rows_x, :] = x * aux[number, 20 + tile : 21 + tile, :]
            y = profiles(pos[number, 4 + tile : 5 + tile, :], side_y, base_y, rows_y, bounds[2], bounds[3], False)
            for plane in range(planes):
                rows = slice(plane * rows_y, (plane + 1) * rows_y)
                hi, lo = split(px[plane + 3 : plane + 4, :] * y)
                left_hi[rows, lanes] = hi
                left_lo[rows, lanes] = lo
        weights = right[...]
        dims = (((1,), (1,)), ((), ()))
        total = planes * rows_y
        placed = lax.dot_general(left_hi[0:total, :], weights, dims, preferred_element_type=jnp.float32)
        placed = placed + lax.dot_general(left_lo[0:total, :], weights, dims, preferred_element_type=jnp.float32)
        placed = placed.reshape(planes, rows_y, 2 * WIDE)
        at = pl.ds(first, planes)
        out[at, pl.ds(start, rows_y), 0 : 2 * WIDE] = out[at, pl.ds(start, rows_y), 0 : 2 * WIDE] + placed

    def both(k, carry):
        splat(9 * k + 4, True, True)
        return carry

    def only_x(k, carry):
        splat(9 * (k // 2) + 1 + 6 * lax.rem(k, 2), True, False)
        return carry

    def only_y(k, carry):
        splat(9 * (k // 2) + 3 + 2 * lax.rem(k, 2), False, True)
        return carry

    def neither(k, carry):
        splat(9 * (k // 4) + 2 * lax.rem(k, 2) + 6 * lax.rem(k // 2, 2), False, False)
        return carry

    lax.fori_loop(0, 3, both, 0)
    lax.fori_loop(0, 6, only_x, 0)
    lax.fori_loop(0, 6, only_y, 0)
    lax.fori_loop(0, 12, neither, 0)
    lane = lax.broadcasted_iota(jnp.int32, (WIDE, LANES), 1)
    row = lax.broadcasted_iota(jnp.int32, (WIDE, LANES), 0)
    own = (lane >= PAD) & (lane < PAD + BRICK) & (row >= PAD) & (row < PAD + BRICK)
    squares = jnp.zeros((WIDE, LANES), jnp.float32)
    cross = squares
    target = squares
    for plane in range(PLANES):
        raw = out[plane]
        value = jnp.where(lane < WIDE, raw + pltpu.roll(raw, LANES - WIDE, 1), 0.0)
        out[plane] = value
        if 5 <= plane < 5 + BRICK:
            value = jnp.where(own, value, 0.0)
            given = jnp.where(own, exp_ext[plane], 0.0)
            squares = squares + value * value
            cross = cross + value * given
            target = target + given * given
    sums[...] = jnp.zeros_like(sums)
    sums[0:1, :] = jnp.sum(squares, axis=0, keepdims=True)
    sums[1:2, :] = jnp.sum(cross, axis=0, keepdims=True)
    sums[2:3, :] = jnp.sum(target, axis=0, keepdims=True)


def fit_kernel(scale, parts, bounds, *refs):
    own, aux, extra, evolved, exp_ext, sums = refs[:6]
    gb = refs[6 : 6 + parts]
    moved, force, left, right, inner, px, pxs = refs[6 + parts :]
    squares = jnp.sum(sums[0:1, :], axis=1, keepdims=True)
    cross = jnp.sum(sums[1:2, :], axis=1, keepdims=True)
    target = jnp.sum(sums[2:3, :], axis=1, keepdims=True)
    norm = jnp.sqrt((squares + EPSILON) * (target + EPSILON))
    given_part = 1.0 / norm
    model_part = (cross / norm) / (squares + EPSILON)
    for plane in range(PLANES):
        s = exp_ext[plane] * given_part - evolved[plane] * model_part
        hi = s.astype(jnp.bfloat16).astype(jnp.float32)
        lo = (s - hi).astype(jnp.bfloat16).astype(jnp.float32)
        packed = hi + pltpu.roll(lo, WIDE, 1) + pltpu.roll(hi, 2 * WIDE, 1)
        left[plane * WIDE : (plane + 1) * WIDE, :] = packed.astype(jnp.bfloat16)
    right[...] = jnp.zeros_like(right)
    for tile in range(TILES):
        z, zs = profiles(own[8 + tile : 9 + tile, :], 0, -PAD, WIDE, bounds[4], bounds[5], True)
        for part, values in enumerate((z, zs)):
            lanes = slice(part * LANES, (part + 1) * LANES)
            hi, lo = split(values)
            right[0:WIDE, lanes] = hi
            right[WIDE : 2 * WIDE, lanes] = hi
            right[2 * WIDE : 3 * WIDE, lanes] = lo
        inner[...] = jnp.dot(left[...], right[...], preferred_element_type=jnp.float32)
        x, xs = profiles(own[tile : tile + 1, :], 0, -PAD, WIDE, bounds[0], bounds[1], True)
        y, ys = profiles(own[4 + tile : 5 + tile, :], 0, -PAD, WIDE, bounds[2], bounds[3], True)
        px[...] = x
        pxs[...] = xs
        turned_x = jnp.zeros((WIDE, LANES), jnp.float32)
        plain = turned_x
        turned_z = turned_x
        for plane in range(PLANES):
            rows = slice(plane * WIDE, (plane + 1) * WIDE)
            at_x = px[plane + 3 : plane + 4, :]
            part = inner[rows, 0:LANES]
            turned_x = turned_x + pxs[plane + 3 : plane + 4, :] * part
            plain = plain + at_x * part
            turned_z = turned_z + at_x * inner[rows, LANES : 2 * LANES]
        weight = scale * aux[20 + tile : 21 + tile, :]
        charge = -2.0 / (CUTOFF * CUTOFF) * aux[12 + tile : 13 + tile, :]
        sides = (turned_x * y, plain * ys, turned_z * y)
        for channel in range(3):
            at = slice(4 * channel + tile, 4 * channel + tile + 1)
            pair = gb[0][at, :]
            for other in gb[1:]:
                pair = pair + other[at, :]
            total = charge * pair + weight * jnp.sum(sides[channel], axis=0, keepdims=True)
            force[at, :] = total
            moved[at, :] = own[at, :] + STEP_SIZE * (extra[4 + tile : 5 + tile, :] * total)


def shifted(block, axis, step):
    count = lax.axis_size(axis)
    pairs = [(i, i + step) for i in range(count) if 0 <= i + step < count]
    return lax.ppermute(block, axis, pairs)


def both_sides(block, axis):
    return shifted(block, axis, 1), shifted(block, axis, -1)


def total_over_devices(values):
    for axis in AXES:
        count = lax.axis_size(axis)
        if count & (count - 1):
            values = lax.psum(values, axis)
            continue
        step = 1
        while step < count:
            pairs = [(i, i ^ step) for i in range(count)]
            values = values + lax.ppermute(values, axis, pairs)
            step *= 2
    return values


def widened(field, width):
    for dim, axis in enumerate(AXES):
        size = field.shape[dim]
        head = lax.slice_in_dim(field, 0, width, axis=dim)
        tail = lax.slice_in_dim(field, size - width, size, axis=dim)
        field = jnp.concatenate([shifted(tail, axis, 1), field, shifted(head, axis, -1)], axis=dim)
    return field


def f32(*shape):
    return jax.ShapeDtypeStruct(shape, jnp.float32)


def born_part(own, pieces, groups):
    cells = sum(count for count, _, _ in groups)
    args = [own] + [array for piece in pieces for array in piece]
    return call(
        functools.partial(born_kernel, groups),
        f32(TILES, LANES),
        cells * SLOTS * SLOTS * 20,
        scratch=[pltpu.VMEM((3, SLOTS, LANES), jnp.float32), pltpu.VMEM((SLOTS, LANES), jnp.float32)],
        n_in=len(args),
    )(*args)


def gb_part(own, radius, pieces, groups):
    cells = sum(count for count, _, _ in groups)
    args = [own, radius] + [array for piece in pieces for array in piece]
    return call(
        functools.partial(gb_kernel, groups),
        f32(3 * TILES, LANES),
        cells * SLOTS * SLOTS * 40,
        scratch=[pltpu.VMEM((5, SLOTS, LANES), jnp.float32), pltpu.VMEM((3, SLOTS, LANES), jnp.float32)],
        n_in=len(args),
    )(*args)


def gathered(block):
    line = jnp.stack([*(shifted(block, "gx", 1)[None]), block, *(shifted(block, "gx", -1)[None])])
    before_y, after_y = both_sides(line, "gy")
    plane = jnp.concatenate([before_y, line, after_y])
    before_z, after_z = both_sides(plane, "gz")
    return line, (before_y, after_y), plane, (before_z, after_z)


GROUPS_X = ((3, 0, 0),)
GROUPS_Y = ((3, -1, 0), (3, 1, 0))
GROUPS_Z = ((9, None, -1), (9, None, 1))


def on_device(positions, charges, atom_types, type_table, live_count, exp_map):
    sizes = [lax.axis_size(axis) for axis in AXES]
    places = [lax.axis_index(axis) for axis in AXES]
    bounds = []
    for size, place in zip(sizes, places):
        bounds += [-place * BRICK, (size - place) * BRICK]
    bounds = jnp.stack(bounds).astype(jnp.int32)
    scale = FIT_GAIN * float(BRICK**3 * sizes[0] * sizes[1] * sizes[2])

    onehot = (atom_types.reshape(SLOTS, 1) == jnp.arange(type_table.shape[1], dtype=jnp.int32)).astype(jnp.float32)
    props = jnp.sum(onehot[None] * type_table[:, None, :], axis=-1)
    living = (lax.iota(jnp.int32, SLOTS) < live_count.reshape(())).astype(jnp.float32)
    start = positions.reshape(3 * TILES, LANES)
    rest = jnp.stack([charges.reshape(SLOTS) * living, props[1] * living, props[2] * living])
    packed = jnp.concatenate([start, rest.reshape(3 * TILES, LANES)])
    extra = jnp.stack([props[0], living]).reshape(2 * TILES, LANES)

    exp_wide = widened(exp_map, BLUR_REACH + SPLAT_MARGIN)
    exp_ext = jnp.pad(exp_wide, ((0, 0), (3, 3), (3, LANES - PLANES - 3)))

    fixed = None
    moved = packed
    for step in range(STEPS):
        line, sides_y, plane, sides_z = gathered(moved)
        if fixed is None:
            fixed = (line, sides_y, plane, sides_z)
        partial = [
            born_part(moved, [(line, fixed[0])], GROUPS_X),
            born_part(moved, list(zip(sides_y, fixed[1])), GROUPS_Y),
            born_part(moved, list(zip(sides_z, fixed[3])), GROUPS_Z),
        ]
        radius = extra[:TILES] + (partial[0] + partial[1] + partial[2] - packed[16:20])
        near = gathered(radius)
        pairs = [
            gb_part(moved, radius, [(line, fixed[0], near[0])], GROUPS_X),
            gb_part(moved, radius, list(zip(sides_y, fixed[1], near[1])), GROUPS_Y),
            gb_part(moved, radius, list(zip(sides_z, fixed[3], near[3])), GROUPS_Z),
        ]
        every = jnp.concatenate([sides_z[0], plane, sides_z[1]])
        if step == 0:
            every_fixed = every
        evolved, sums = call(
            evolve_kernel,
            (f32(PLANES, WIDE, LANES), f32(8, LANES)),
            1 << 33,
            scratch=[
                pltpu.VMEM((WIDE, LANES), jnp.float32),
                pltpu.VMEM((PLANES * WIDE, SLOTS), jnp.bfloat16),
                pltpu.VMEM((PLANES * WIDE, SLOTS), jnp.bfloat16),
                pltpu.VMEM((2 * WIDE, SLOTS), jnp.bfloat16),
            ],
            smem=1,
            n_in=4,
        )(bounds, every, every_fixed, exp_ext)
        sums = total_over_devices(sums)
        moved, force = call(
            functools.partial(fit_kernel, scale, len(pairs)),
            (f32(3 * TILES, LANES), f32(3 * TILES, LANES)),
            1 << 30,
            scratch=[
                pltpu.VMEM((PLANES * WIDE, LANES), jnp.bfloat16),
                pltpu.VMEM((LANES, 2 * LANES), jnp.bfloat16),
                pltpu.VMEM((PLANES * WIDE, 2 * LANES), jnp.float32),
                pltpu.VMEM((WIDE, LANES), jnp.float32),
                pltpu.VMEM((WIDE, LANES), jnp.float32),
            ],
            smem=1,
            n_in=7 + len(pairs),
        )(bounds, moved, packed, extra, evolved, exp_ext, sums, *pairs)
    own = evolved[5 : 5 + BRICK, PAD : PAD + BRICK, PAD : PAD + BRICK]
    return (moved - start).reshape(positions.shape), force.reshape(positions.shape), own


def solution(mesh):
    placed = (
        P(None, *AXES, None),
        P(*AXES, None),
        P(*AXES, None),
        P(),
        P(*AXES),
        P(*AXES),
    )
    return jax.shard_map(
        on_device,
        mesh=mesh,
        in_specs=placed,
        out_specs=(placed[0], placed[0], P(*AXES)),
        check_vma=False,
    )
```

time: 696 us -> 305 us (0.44)
  other arithmetic: 256 us -> 0.79 us
  Pallas kernels: 0 us -> 146 us
  local copies, waits for them, and re-layouts: 126 us -> 3.89 us
  blocking collectives: 91.8 us -> 0 us
  matrix products: 28.1 us -> 0 us
  starting transfers between devices: 152 us -> 125 us
    pallas_call x0 -> x16, Pallas kernels: none -> 146 us  [the longest x6 68.9 us: gb_part(): call(functools.partial(gb_kernel, groups), f32(3 * TILES, LANES), cells *...]
    reduce_sum x221 -> x1, other arithmetic: 134 us -> 0.09 us  [on_device(): props = jnp.sum(onehot[None] * type_table[:, None, :], axis=-1)]
    mul x242 -> x0, other arithmetic: 95.7 us -> none  [the longest x54 92.2 us: gb_visit(): -0.5 * charge_pair]
    psum x10 -> x0, blocking collectives: 91.8 us -> none  [one_axis_at_a_time(): return functools.reduce(lax.psum, axes, x)]
    dynamic_slice x162 -> x0, local copies, waits for them, and re-layouts: 64.6 us -> none  [the longest x108 63.9 us: born_radius(): lax.scan(born_visit, jnp.zeros((slot_count,), jnp.float32), (blocks, offs...]
    scatter-add x50 -> x0, local copies, waits for them, and re-layouts: 53.7 us -> none  [splat_window(): density = density.at[low_x + reach:high_x + reach, low_y + reach:high_y +...]
    dot_general x56 -> x0, matrix products: 28.1 us -> none  [the longest x54 24 us: splat_window(): placed = jnp.dot(plane.T, profile_z, precision=lax.Precision.HIGHEST)]
    ppermute x48 -> x46, starting transfers between devices: 152 us -> 125 us  [the longest x30 98.9 us: shifted(): return lax.ppermute(block, axis, pairs)]
  transfers between devices with their start and end apart: 48 -> 46, of which waited for: 11 -> 9; matrix products, arithmetic and copies ran while one was open for 45% -> 1% of each run, Pallas kernels for 0% -> 39%
where the time goes in v1:
time: 305 us; the launch traced here: 300 us
  Pallas kernels  146 us (48%)
  starting transfers between devices  125 us (41%)
  waiting for transfers between devices  21.6 us (7%)
  local copies, waits for them, and re-layouts  3.89 us (1%)
    ppermute x30, starting transfers between devices, shifted(): return lax.ppermute(block, axis, pairs)  98.9 us
    pallas_call x6, Pallas kernels, gb_part(): call(functools.partial(gb_kernel, groups), f32(3 * TILES, LANES), cells *...  68.9 us
    pallas_call x6, Pallas kernels, born_part(): call(functools.partial(born_kernel, groups), f32(TILES, LANES), cells * S...  40.1 us
    pallas_call x2, Pallas kernels, on_device(): call(evolve_kernel, (f32(PLANES, WIDE, LANES), f32(8, LANES)), 1 << 33, s...  33.5 us
    ppermute x16, starting transfers between devices, total_over_devices(): values = values + lax.ppermute(values, axis, pairs)  26.2 us
    ppermute x16, waiting for transfers between devices, total_over_devices(): values = values + lax.ppermute(values, axis, pairs)  13.8 us
    ppermute x30, waiting for transfers between devices, shifted(): return lax.ppermute(block, axis, pairs)  7.78 us
  transfers between devices with their start and end apart: 46, of which 9 were waited for; matrix products, arithmetic and copies ran while one was open for 1% of the time, Pallas kernels for 39%

profile of v1, /device:TPU:56, one launch (start us, length us, event | category | flops | bytes accessed | tf_op | source)
XLA Modules:
  0.0 300.2 jit_solution(3996767816749716683)
XLA Ops:
  0.6 0.8 fusion.9
  1.4 2.0 collective-permute-start.6
  5.0 5.1 %collective-permute-start.1 = (f32[24,128]{1,0:T(8,128)S(1)}, f32[24,128]{1,0:T(8,128)S(1)}, u32[]{:S(2)}, u32[]{:S(2)}) collective-permute-start(f32[24,128]{1,0:T(8,128)S(1)} %pad_maximum_fusion.3.refs_0_.refs_1_), channel_id=1, source_target_pairs={{64,0},{128,64},{192,128},{65,1},{129,65},{193,129},{66,2},{130,66... | collective-permute-start | bytes 36872 | tf_op jit(solution)/shard_map/ppermute | solution.py:339
  10.1 1.9 collective-permute-start
  12.1 5.1 %collective-permute-start.7 = (f32[5,16,16]{2,1,0:T(8,128)S(1)}, f32[5,16,16]{2,1,0:T(8,128)S(1)}, u32[]{:S(2)}, u32[]{:S(2)}) collective-permute-start(f32[5,16,16]{2,1,0:T(8,128)S(1)} %get-tuple-element.30), channel_id=1, source_target_pairs={{64,0},{128,64},{192,128},{65,1},{129,65},{193,129},{66,2},{130,66... | collective-permute-start | bytes 15368 | tf_op jit(solution)/shard_map/ppermute | solution.py:339
  17.4 1.5 collective-permute-done.7
  18.9 4.8 %collective-permute-start.9 = (f32[26,5,16]{2,1,0:T(8,128)S(1)}, f32[26,5,16]{2,1,0:T(8,128)S(1)}, u32[]{:S(2)}, u32[]{:S(2)}) collective-permute-start(f32[26,5,16]{2,1,0:T(8,128)S(1)} %get-tuple-element.29), channel_id=1, source_target_pairs={{8,0},{16,8},{24,16},{32,24},{40,32},{48,40},{56,48},{9,1},{17,9},... | collective-permute-start | bytes 24968 | tf_op jit(solution)/shard_map/ppermute | solution.py:339
  23.8 1.9 collective-permute-start.8
  25.7 2.5 collective-permute-start.2
  28.2 5.5 %collective-permute-start.3 = (f32[3,24,128]{2,1,0:T(8,128)S(1)}, f32[3,24,128]{2,1,0:T(8,128)S(1)}, u32[]{:S(2)}, u32[]{:S(2)}) collective-permute-start(f32[3,24,128]{2,1,0:T(8,128)S(1)} %pad_maximum_fusion.1.refs_1_.refs_2_.refs_3_), channel_id=1, source_target_pairs={{8,0},{16,8},{24,16},{32,24},{40,32},{48,40},{56,48},{9,1},{17,9},... | collective-permute-start | bytes 110600 | tf_op jit(solution)/shard_map/ppermute | solution.py:339
  33.7 2.5 shard_map.86
  36.5 2.0 collective-permute-start.11
  38.5 3.8 %collective-permute-start.10 = (f32[26,26,5]{2,1,0:T(8,128)S(1)}, f32[26,26,5]{2,1,0:T(8,128)S(1)}, u32[]{:S(2)}, u32[]{:S(2)}) collective-permute-start(f32[26,26,5]{2,1,0:T(8,128)S(1)} %get-tuple-element.26), channel_id=1, source_target_pairs={{0,1},{1,2},{2,3},{3,4},{4,5},{5,6},{6,7},{8,9},{9,10},{10,11},{11... | collective-permute-start | bytes 40568 | tf_op jit(solution)/shard_map/ppermute | solution.py:339
  42.4 3.8 %collective-permute-start.4 = (f32[9,24,128]{2,1,0:T(8,128)S(1)}, f32[9,24,128]{2,1,0:T(8,128)S(1)}, u32[]{:S(2)}, u32[]{:S(2)}) collective-permute-start(f32[9,24,128]{2,1,0:T(8,128)S(1)} %constant_dynamic-update-slice_fusion), channel_id=1, source_target_pairs={{0,1},{1,2},{2,3},{3,4},{4,5},{5,6},{6,7},{8,9},{9,10},{10,11},{11... | collective-permute-start | bytes 331784 | tf_op jit(solution)/shard_map/ppermute | solution.py:339
  46.3 2.0 collective-permute-start.5
  49.3 4.6 %shard_map.87 = f32[4,128]{1,0:T(4,128)S(1)} custom-call(f32[24,128]{1,0:T(8,128)S(1)} %pad_maximum_fusion.3.refs_0_.refs_1_, f32[3,24,128]{2,1,0:T(8,128)S(1)} %collective-permute-done.2.refs_1_.refs_2_.refs_3_, f32[3,24,128]{2,1,0:T(8,128)S(1)} %collective-permute-done.2.refs_1_.refs_2_.refs_3_, ...), custom_call_target="tpu_custom_call" | custom-call | flops 31457280 | bytes 262144 | tf_op jit(solution)/shard_map/pallas_call | solution.py:376
  54.0 13.0 %shard_map.88 = f32[4,128]{1,0:T(4,128)S(1)} custom-call(f32[24,128]{1,0:T(8,128)S(1)} %pad_maximum_fusion.3.refs_0_.refs_1_, f32[9,24,128]{2,1,0:T(8,128)S(1)} %collective-permute-done.4.refs_1_.refs_2_.refs_3_, f32[9,24,128]{2,1,0:T(8,128)S(1)} %collective-permute-done.4.refs_1_.refs_2_.refs_3_, ...), custom_call_target="tpu_custom_call" | custom-call | flops 94371840 | bytes 262144 | tf_op jit(solution)/shard_map/pallas_call | solution.py:376
  67.0 6.7 %collective-permute-start.21 = (f32[4,128]{1,0:T(4,128)S(1)}, f32[4,128]{1,0:T(4,128)S(1)}, u32[]{:S(2)}, u32[]{:S(2)}) collective-permute-start(f32[4,128]{1,0:T(4,128)S(1)} %subtract_add_fusion.1.refs_1_), channel_id=1, source_target_pairs={{64,0},{128,64},{192,128},{65,1},{129,65},{193,129},{66,2},{130,66... | collective-permute-start | bytes 6152 | tf_op jit(solution)/shard_map/ppermute | solution.py:339
  73.7 1.9 collective-permute-start.20
  75.8 16.8 %shard_map.85 = (f32[26,32,128]{2,1,0:T(8,128)S(1)}, f32[8,128]{1,0:T(8,128)S(1)}) custom-call(s32[6]{0:T(128)S(1)} %stack.61.bounds, f32[27,24,128]{2,1,0:T(8,128)S(1)} %constant_dynamic-update-slice_fusion.5.pos.aux, f32[27,24,128]{2,1,0:T(8,128)S(1)} %constant_dynamic-update-slice_fusion.5.pos.aux, f32[26,32,128]{2,1,0:T(8,128)S(1)} %select_maximum_fusion.exp_ext.refs_4_), custom_call_target="tpu_custom_call" | custom-call | flops 8589934592 | bytes 262144 | tf_op jit(solution)/shard_map/pallas_call | solution.py:451
  92.7 1.9 collective-permute-start.22
  94.6 3.7 %collective-permute-start.13 = (f32[8,128]{1,0:T(8,128)S(1)}, f32[8,128]{1,0:T(8,128)S(1)}, u32[]{:S(2)}, u32[]{:S(2)}) collective-permute-start(f32[8,128]{1,0:T(8,128)S(1)} %add.69), channel_id=1, source_target_pairs={{0,128},{64,192},{128,0},{192,64},{1,129},{65,193},{129,1},{193,65... | collective-permute-start | bytes 12296 | tf_op jit(solution)/shard_map/ppermute | solution.py:355
  98.3 5.4 %collective-permute-start.23 = (f32[3,4,128]{2,1,0:T(4,128)S(1)}, f32[3,4,128]{2,1,0:T(4,128)S(1)}, u32[]{:S(2)}, u32[]{:S(2)}) collective-permute-start(f32[3,4,128]{2,1,0:T(4,128)S(1)} %pad_maximum_fusion.5.refs_4_), channel_id=1, source_target_pairs={{8,0},{16,8},{24,16},{32,24},{40,32},{48,40},{56,48},{9,1},{17,9},... | collective-permute-start | bytes 18440 | tf_op jit(solution)/shard_map/ppermute | solution.py:339
  103.9 3.5 %collective-permute-done.14 = f32[8,128]{1,0:T(8,128)S(1)} collective-permute-done((f32[8,128]{1,0:T(8,128)S(1)}, f32[8,128]{1,0:T(8,128)S(1)}, u32[]{:S(2)}, u32[]{:S(2)}) %collective-permute-start.14) | collective-permute-done | bytes 4128 | tf_op jit(solution)/shard_map/ppermute | solution.py:355
  107.5 5.1 %collective-permute-done.15 = f32[8,128]{1,0:T(8,128)S(1)} collective-permute-done((f32[8,128]{1,0:T(8,128)S(1)}, f32[8,128]{1,0:T(8,128)S(1)}, u32[]{:S(2)}, u32[]{:S(2)}) %collective-permute-start.15) | collective-permute-done | bytes 4128 | tf_op jit(solution)/shard_map/ppermute | solution.py:355
  112.6 3.9 %collective-permute-start.24 = (f32[9,4,128]{2,1,0:T(4,128)S(1)}, f32[9,4,128]{2,1,0:T(4,128)S(1)}, u32[]{:S(2)}, u32[]{:S(2)}) collective-permute-start(f32[9,4,128]{2,1,0:T(4,128)S(1)} %constant_dynamic-update-slice_fusion.15), channel_id=1, source_target_pairs={{0,1},{1,2},{2,3},{3,4},{4,5},{5,6},{6,7},{8,9},{9,10},{10,11},{11... | collective-permute-start | bytes 55304 | tf_op jit(solution)/shard_map/ppermute | solution.py:339
  116.5 1.9 collective-permute-start.25
  118.6 4.2 %shard_map.89.refs_6_ = f32[12,128]{1,0:T(8,128)S(1)} custom-call(f32[24,128]{1,0:T(8,128)S(1)} %pad_maximum_fusion.3.refs_0_.refs_1_, f32[4,128]{1,0:T(4,128)S(1)} %subtract_add_fusion.1.refs_1_, f32[3,24,128]{2,1,0:T(8,128)S(1)} %pad_maximum_fusion.1.refs_1_.refs_2_.refs_3_, f32[3,24,128]{2,1,0:T(8,128)S(1)} %pad_maximum_fusion.1.refs_1_.refs_2_.refs_3_, ...), custom_call_target="tpu_custom_call" | custom-call | flops 31457280 | bytes 262144 | tf_op jit(solution)/shard_map/pallas_call | solution.py:388
  122.9 5.7 %collective-permute-start.18 = (f32[8,128]{1,0:T(8,128)S(1)}, f32[8,128]{1,0:T(8,128)S(1)}, u32[]{:S(2)}, u32[]{:S(2)}) collective-permute-start(f32[8,128]{1,0:T(8,128)S(1)} %add.74), channel_id=1, source_target_pairs={{0,2},{1,3},{2,0},{3,1},{4,6},{5,7},{6,4},{7,5},{8,10},{9,11},{10,... | collective-permute-start | bytes 12296 | tf_op jit(solution)/shard_map/ppermute | solution.py:355
  128.5 7.8 %shard_map.90.refs_7_ = f32[12,128]{1,0:T(8,128)S(1)} custom-call(f32[24,128]{1,0:T(8,128)S(1)} %pad_maximum_fusion.3.refs_0_.refs_1_, f32[4,128]{1,0:T(4,128)S(1)} %subtract_add_fusion.1.refs_1_, f32[3,24,128]{2,1,0:T(8,128)S(1)} %collective-permute-done.2.refs_1_.refs_2_.refs_3_, f32[3,24,128]{2,1,0:T(8,128)S(1)} %collective-permute-done.2.refs_1_.refs_2_.refs_3_, ...), custom_call_target="tpu_custom_call" | custom-call | flops 62914560 | bytes 262144 | tf_op jit(solution)/shard_map/pallas_call | solution.py:388
  136.4 4.4 %collective-permute-start.19 = (f32[8,128]{1,0:T(8,128)S(1)}, f32[8,128]{1,0:T(8,128)S(1)}, u32[]{:S(2)}, u32[]{:S(2)}) collective-permute-start(f32[8,128]{1,0:T(8,128)S(1)} %add.75), channel_id=1, source_target_pairs={{0,4},{1,5},{2,6},{3,7},{4,0},{5,1},{6,2},{7,3},{8,12},{9,13},{10,... | collective-permute-start | bytes 12296 | tf_op jit(solution)/shard_map/ppermute | solution.py:355
  140.8 22.3 %shard_map.91.refs_8_ = f32[12,128]{1,0:T(8,128)S(1)} custom-call(f32[24,128]{1,0:T(8,128)S(1)} %pad_maximum_fusion.3.refs_0_.refs_1_, f32[4,128]{1,0:T(4,128)S(1)} %subtract_add_fusion.1.refs_1_, f32[9,24,128]{2,1,0:T(8,128)S(1)} %collective-permute-done.4.refs_1_.refs_2_.refs_3_, f32[9,24,128]{2,1,0:T(8,128)S(1)} %collective-permute-done.4.refs_1_.refs_2_.refs_3_, ...), custom_call_target="tpu_custom_call" | custom-call | flops 188743680 | bytes 262144 | tf_op jit(solution)/shard_map/pallas_call | solution.py:388
  163.2 2.2 shard_map.92
  165.4 1.9 collective-permute-start.27
  167.3 2.4 collective-permute-start.26
  169.7 4.1 %collective-permute-done.26 = f32[12,128]{1,0:T(8,128)S(1)} collective-permute-done((f32[12,128]{1,0:T(8,128)S(1)}, f32[12,128]{1,0:T(8,128)S(1)}, u32[]{:S(2)}, u32[]{:S(2)}) %collective-permute-start.26) | collective-permute-done | bytes 6176 | tf_op jit(solution)/shard_map/ppermute | solution.py:339
  173.8 1.9 collective-permute-start.28
  175.7 6.0 %collective-permute-start.29 = (f32[3,12,128]{2,1,0:T(8,128)S(1)}, f32[3,12,128]{2,1,0:T(8,128)S(1)}, u32[]{:S(2)}, u32[]{:S(2)}) collective-permute-start(f32[3,12,128]{2,1,0:T(8,128)S(1)} %pad_maximum_fusion.2.refs_1_.refs_2_), channel_id=1, source_target_pairs={{8,0},{16,8},{24,16},{32,24},{40,32},{48,40},{56,48},{9,1},{17,9},... | collective-permute-start | bytes 55304 | tf_op jit(solution)/shard_map/ppermute | solution.py:339
  181.8 1.4 collective-permute-done.29.refs_3_.refs_5_
  183.3 3.4 %collective-permute-start.30 = (f32[9,12,128]{2,1,0:T(8,128)S(1)}, f32[9,12,128]{2,1,0:T(8,128)S(1)}, u32[]{:S(2)}, u32[]{:S(2)}) collective-permute-start(f32[9,12,128]{2,1,0:T(8,128)S(1)} %constant_dynamic-update-slice_fusion.20), channel_id=1, source_target_pairs={{0,1},{1,2},{2,3},{3,4},{4,5},{5,6},{6,7},{8,9},{9,10},{10,11},{11... | collective-permute-start | bytes 165896 | tf_op jit(solution)/shard_map/ppermute | solution.py:339
  186.6 2.5 collective-permute-start.31
  189.1 2.5 shard_map.94
  191.6 4.6 %shard_map.95 = f32[4,128]{1,0:T(4,128)S(1)} custom-call(f32[12,128]{1,0:T(8,128)S(1)} %get-tuple-element.12.refs_0_, f32[3,12,128]{2,1,0:T(8,128)S(1)} %collective-permute-done.28.refs_1_.refs_2_, f32[3,24,128]{2,1,0:T(8,128)S(1)} %collective-permute-done.2.refs_1_.refs_2_.refs_3_, f32[3,12,128]{2,1,0:T(8,128)S(1)} %collective-permute-done.29.refs_3_.refs_5_, ...), custom_call_target="tpu_custom_call" | custom-call | flops 31457280 | bytes 262144 | tf_op jit(solution)/shard_map/pallas_call | solution.py:376
  196.2 13.0 %shard_map.96 = f32[4,128]{1,0:T(4,128)S(1)} custom-call(f32[12,128]{1,0:T(8,128)S(1)} %get-tuple-element.12.refs_0_, f32[9,12,128]{2,1,0:T(8,128)S(1)} %collective-permute-done.30.refs_1_.refs_2_, f32[9,24,128]{2,1,0:T(8,128)S(1)} %collective-permute-done.4.refs_1_.refs_2_.refs_3_, f32[9,12,128]{2,1,0:T(8,128)S(1)} %collective-permute-done.31.refs_3_.refs_5_, ...), custom_call_target="tpu_custom_call" | custom-call | flops 94371840 | bytes 262144 | tf_op jit(solution)/shard_map/pallas_call | solution.py:376
  209.2 1.9 collective-permute-start.41
  211.1 2.4 collective-permute-start.40
  213.6 16.8 %shard_map.93 = (f32[26,32,128]{2,1,0:T(8,128)S(1)}, f32[8,128]{1,0:T(8,128)S(1)}) custom-call(s32[6]{0:T(128)S(1)} %stack.61.bounds, f32[27,12,128]{2,1,0:T(8,128)S(1)} %constant_dynamic-update-slice_fusion.25.pos, f32[27,24,128]{2,1,0:T(8,128)S(1)} %constant_dynamic-update-slice_fusion.5.pos.aux, f32[26,32,128]{2,1,0:T(8,128)S(1)} %select_maximum_fusion.exp_ext.refs_4_), custom_call_target="tpu_custom_call" | custom-call | flops 8589934592 | bytes 262144 | tf_op jit(solution)/shard_map/pallas_call | solution.py:451
  230.6 1.9 collective-permute-start.42
  232.5 3.2 %collective-permute-start.33 = (f32[8,128]{1,0:T(8,128)S(1)}, f32[8,128]{1,0:T(8,128)S(1)}, u32[]{:S(2)}, u32[]{:S(2)}) collective-permute-start(f32[8,128]{1,0:T(8,128)S(1)} %add.80), channel_id=1, source_target_pairs={{0,128},{64,192},{128,0},{192,64},{1,129},{65,193},{129,1},{193,65... | collective-permute-start | bytes 12296 | tf_op jit(solution)/shard_map/ppermute | solution.py:355
  235.7 6.3 %collective-permute-start.43 = (f32[3,4,128]{2,1,0:T(4,128)S(1)}, f32[3,4,128]{2,1,0:T(4,128)S(1)}, u32[]{:S(2)}, u32[]{:S(2)}) collective-permute-start(f32[3,4,128]{2,1,0:T(4,128)S(1)} %pad_maximum_fusion.6.refs_4_), channel_id=1, source_target_pairs={{8,0},{16,8},{24,16},{32,24},{40,32},{48,40},{56,48},{9,1},{17,9},... | collective-permute-start | bytes 18440 | tf_op jit(solution)/shard_map/ppermute | solution.py:339
  242.2 3.5 %collective-permute-done.34 = f32[8,128]{1,0:T(8,128)S(1)} collective-permute-done((f32[8,128]{1,0:T(8,128)S(1)}, f32[8,128]{1,0:T(8,128)S(1)}, u32[]{:S(2)}, u32[]{:S(2)}) %collective-permute-start.34) | collective-permute-done | bytes 4128 | tf_op jit(solution)/shard_map/ppermute | solution.py:355
  245.8 3.4 %collective-permute-start.44 = (f32[9,4,128]{2,1,0:T(4,128)S(1)}, f32[9,4,128]{2,1,0:T(4,128)S(1)}, u32[]{:S(2)}, u32[]{:S(2)}) collective-permute-start(f32[9,4,128]{2,1,0:T(4,128)S(1)} %constant_dynamic-update-slice_fusion.32), channel_id=1, source_target_pairs={{0,1},{1,2},{2,3},{3,4},{4,5},{5,6},{6,7},{8,9},{9,10},{10,11},{11... | collective-permute-start | bytes 55304 | tf_op jit(solution)/shard_map/ppermute | solution.py:339
  249.2 2.5 collective-permute-start.45
  251.7 2.1 collective-permute-start.36
  253.8 1.6 collective-permute-done.36
  255.4 0.8 slice.48
  256.1 4.2 %shard_map.97.refs_6_ = f32[12,128]{1,0:T(8,128)S(1)} custom-call(f32[12,128]{1,0:T(8,128)S(1)} %get-tuple-element.12.refs_0_, f32[4,128]{1,0:T(4,128)S(1)} %subtract_add_fusion.refs_1_, f32[3,12,128]{2,1,0:T(8,128)S(1)} %pad_maximum_fusion.2.refs_1_.refs_2_, f32[3,24,128]{2,1,0:T(8,128)S(1)} %pad_maximum_fusion.1.refs_1_.refs_2_.refs_3_, ...), custom_call_target="tpu_custom_call" | custom-call | flops 31457280 | bytes 262144 | tf_op jit(solution)/shard_map/pallas_call | solution.py:388
  260.4 3.2 %collective-permute-start.38 = (f32[8,128]{1,0:T(8,128)S(1)}, f32[8,128]{1,0:T(8,128)S(1)}, u32[]{:S(2)}, u32[]{:S(2)}) collective-permute-start(f32[8,128]{1,0:T(8,128)S(1)} %add.85), channel_id=1, source_target_pairs={{0,2},{1,3},{2,0},{3,1},{4,6},{5,7},{6,4},{7,5},{8,10},{9,11},{10,... | collective-permute-start | bytes 12296 | tf_op jit(solution)/shard_map/ppermute | solution.py:355
  263.6 7.9 %shard_map.98.refs_7_ = f32[12,128]{1,0:T(8,128)S(1)} custom-call(f32[12,128]{1,0:T(8,128)S(1)} %get-tuple-element.12.refs_0_, f32[4,128]{1,0:T(4,128)S(1)} %subtract_add_fusion.refs_1_, f32[3,12,128]{2,1,0:T(8,128)S(1)} %collective-permute-done.28.refs_1_.refs_2_, f32[3,24,128]{2,1,0:T(8,128)S(1)} %collective-permute-done.2.refs_1_.refs_2_.refs_3_, ...), custom_call_target="tpu_custom_call" | custom-call | flops 62914560 | bytes 262144 | tf_op jit(solution)/shard_map/pallas_call | solution.py:388
  271.5 3.4 %collective-permute-start.39 = (f32[8,128]{1,0:T(8,128)S(1)}, f32[8,128]{1,0:T(8,128)S(1)}, u32[]{:S(2)}, u32[]{:S(2)}) collective-permute-start(f32[8,128]{1,0:T(8,128)S(1)} %add.86), channel_id=1, source_target_pairs={{0,4},{1,5},{2,6},{3,7},{4,0},{5,1},{6,2},{7,3},{8,12},{9,13},{10,... | collective-permute-start | bytes 12296 | tf_op jit(solution)/shard_map/ppermute | solution.py:355
  275.0 22.3 %shard_map.99.refs_8_ = f32[12,128]{1,0:T(8,128)S(1)} custom-call(f32[12,128]{1,0:T(8,128)S(1)} %get-tuple-element.12.refs_0_, f32[4,128]{1,0:T(4,128)S(1)} %subtract_add_fusion.refs_1_, f32[9,12,128]{2,1,0:T(8,128)S(1)} %collective-permute-done.30.refs_1_.refs_2_, f32[9,24,128]{2,1,0:T(8,128)S(1)} %collective-permute-done.4.refs_1_.refs_2_.refs_3_, ...), custom_call_target="tpu_custom_call" | custom-call | flops 188743680 | bytes 262144 | tf_op jit(solution)/shard_map/pallas_call | solution.py:388
  297.3 1.6 shard_map.100
  299.0 0.6 reshape.86
  299.6 0.6 reshape.87
  (134 shorter events, 3.2 us)
Async XLA Ops:
  1.4 2.1 copy-start.2
  1.4 15.9 %collective-permute-start.6 = (f32[5,16,16]{2,1,0:T(8,128)S(1)}, f32[5,16,16]{2,1,0:T(8,128)S(1)}, u32[]{:S(2)}, u32[]{:S(2)}) collective-permute-start(f32[5,16,16]{2,1,0:T(8,128)S(1)} %get-tuple-element.31), channel_id=1, source_target_pairs={{0,64},{64,128},{128,192},{1,65},{65,129},{129,193},{2,66},{66,130... | collective-permute-start | bytes 15368 | tf_op jit(solution)/shard_map/ppermute | solution.py:339
  3.5 0.7 copy-start.4
  4.2 0.7 copy-start.3
  4.2 0.7 copy-start.1
  4.3 13.0 %copy-start = (f32[16,16,16]{2,1,0:T(8,128)S(1)}, f32[16,16,16]{2,1,0:T(8,128)}, u32[]{:S(2)}) copy-start(f32[16,16,16]{2,1,0:T(8,128)} %param.11) | copy-start | bytes 49156
  5.0 20.7 %collective-permute-start.1 = (f32[24,128]{1,0:T(8,128)S(1)}, f32[24,128]{1,0:T(8,128)S(1)}, u32[]{:S(2)}, u32[]{:S(2)}) collective-permute-start(f32[24,128]{1,0:T(8,128)S(1)} %pad_maximum_fusion.3.refs_0_.refs_1_), channel_id=1, source_target_pairs={{64,0},{128,64},{192,128},{65,1},{129,65},{193,129},{66,2},{130,66... | collective-permute-start | bytes 36872 | tf_op jit(solution)/shard_map/ppermute | solution.py:339
  10.1 15.6 %collective-permute-start = (f32[24,128]{1,0:T(8,128)S(1)}, f32[24,128]{1,0:T(8,128)S(1)}, u32[]{:S(2)}, u32[]{:S(2)}) collective-permute-start(f32[24,128]{1,0:T(8,128)S(1)} %pad_maximum_fusion.3.refs_0_.refs_1_), channel_id=1, source_target_pairs={{0,64},{64,128},{128,192},{1,65},{65,129},{129,193},{2,66},{66,130... | collective-permute-start | bytes 36872 | tf_op jit(solution)/shard_map/ppermute | solution.py:339
  12.1 6.8 %collective-permute-start.7 = (f32[5,16,16]{2,1,0:T(8,128)S(1)}, f32[5,16,16]{2,1,0:T(8,128)S(1)}, u32[]{:S(2)}, u32[]{:S(2)}) collective-permute-start(f32[5,16,16]{2,1,0:T(8,128)S(1)} %get-tuple-element.30), channel_id=1, source_target_pairs={{64,0},{128,64},{192,128},{65,1},{129,65},{193,129},{66,2},{130,66... | collective-permute-start | bytes 15368 | tf_op jit(solution)/shard_map/ppermute | solution.py:339
  18.9 17.3 %collective-permute-start.9 = (f32[26,5,16]{2,1,0:T(8,128)S(1)}, f32[26,5,16]{2,1,0:T(8,128)S(1)}, u32[]{:S(2)}, u32[]{:S(2)}) collective-permute-start(f32[26,5,16]{2,1,0:T(8,128)S(1)} %get-tuple-element.29), channel_id=1, source_target_pairs={{8,0},{16,8},{24,16},{32,24},{40,32},{48,40},{56,48},{9,1},{17,9},... | collective-permute-start | bytes 24968 | tf_op jit(solution)/shard_map/ppermute | solution.py:339
  23.8 12.5 %collective-permute-start.8 = (f32[26,5,16]{2,1,0:T(8,128)S(1)}, f32[26,5,16]{2,1,0:T(8,128)S(1)}, u32[]{:S(2)}, u32[]{:S(2)}) collective-permute-start(f32[26,5,16]{2,1,0:T(8,128)S(1)} %get-tuple-element.28), channel_id=1, source_target_pairs={{0,8},{8,16},{16,24},{24,32},{32,40},{40,48},{48,56},{1,9},{9,17},... | collective-permute-start | bytes 24968 | tf_op jit(solution)/shard_map/ppermute | solution.py:339
  25.7 16.6 %collective-permute-start.2 = (f32[3,24,128]{2,1,0:T(8,128)S(1)}, f32[3,24,128]{2,1,0:T(8,128)S(1)}, u32[]{:S(2)}, u32[]{:S(2)}) collective-permute-start(f32[3,24,128]{2,1,0:T(8,128)S(1)} %pad_maximum_fusion.1.refs_1_.refs_2_.refs_3_), channel_id=1, source_target_pairs={{0,8},{8,16},{16,24},{24,32},{32,40},{40,48},{48,56},{1,9},{9,17},... | collective-permute-start | bytes 110600 | tf_op jit(solution)/shard_map/ppermute | solution.py:339
  28.2 14.2 %collective-permute-start.3 = (f32[3,24,128]{2,1,0:T(8,128)S(1)}, f32[3,24,128]{2,1,0:T(8,128)S(1)}, u32[]{:S(2)}, u32[]{:S(2)}) collective-permute-start(f32[3,24,128]{2,1,0:T(8,128)S(1)} %pad_maximum_fusion.1.refs_1_.refs_2_.refs_3_), channel_id=1, source_target_pairs={{8,0},{16,8},{24,16},{32,24},{40,32},{48,40},{56,48},{9,1},{17,9},... | collective-permute-start | bytes 110600 | tf_op jit(solution)/shard_map/ppermute | solution.py:339
  36.5 11.8 %collective-permute-start.11 = (f32[26,26,5]{2,1,0:T(8,128)S(1)}, f32[26,26,5]{2,1,0:T(8,128)S(1)}, u32[]{:S(2)}, u32[]{:S(2)}) collective-permute-start(f32[26,26,5]{2,1,0:T(8,128)S(1)} %get-tuple-element.27), channel_id=1, source_target_pairs={{1,0},{2,1},{3,2},{4,3},{5,4},{6,5},{7,6},{9,8},{10,9},{11,10},{12... | collective-permute-start | bytes 40568 | tf_op jit(solution)/shard_map/ppermute | solution.py:339
  38.5 10.3 %collective-permute-start.10 = (f32[26,26,5]{2,1,0:T(8,128)S(1)}, f32[26,26,5]{2,1,0:T(8,128)S(1)}, u32[]{:S(2)}, u32[]{:S(2)}) collective-permute-start(f32[26,26,5]{2,1,0:T(8,128)S(1)} %get-tuple-element.26), channel_id=1, source_target_pairs={{0,1},{1,2},{2,3},{3,4},{4,5},{5,6},{6,7},{8,9},{9,10},{10,11},{11... | collective-permute-start | bytes 40568 | tf_op jit(solution)/shard_map/ppermute | solution.py:339
  42.4 11.4 %collective-permute-start.4 = (f32[9,24,128]{2,1,0:T(8,128)S(1)}, f32[9,24,128]{2,1,0:T(8,128)S(1)}, u32[]{:S(2)}, u32[]{:S(2)}) collective-permute-start(f32[9,24,128]{2,1,0:T(8,128)S(1)} %constant_dynamic-update-slice_fusion), channel_id=1, source_target_pairs={{0,1},{1,2},{2,3},{3,4},{4,5},{5,6},{6,7},{8,9},{9,10},{10,11},{11... | collective-permute-start | bytes 331784 | tf_op jit(solution)/shard_map/ppermute | solution.py:339
  46.3 7.7 %collective-permute-start.5 = (f32[9,24,128]{2,1,0:T(8,128)S(1)}, f32[9,24,128]{2,1,0:T(8,128)S(1)}, u32[]{:S(2)}, u32[]{:S(2)}) collective-permute-start(f32[9,24,128]{2,1,0:T(8,128)S(1)} %constant_dynamic-update-slice_fusion), channel_id=1, source_target_pairs={{1,0},{2,1},{3,2},{4,3},{5,4},{6,5},{7,6},{9,8},{10,9},{11,10},{12... | collective-permute-start | bytes 331784 | tf_op jit(solution)/shard_map/ppermute | solution.py:339
  67.0 25.6 %collective-permute-start.21 = (f32[4,128]{1,0:T(4,128)S(1)}, f32[4,128]{1,0:T(4,128)S(1)}, u32[]{:S(2)}, u32[]{:S(2)}) collective-permute-start(f32[4,128]{1,0:T(4,128)S(1)} %subtract_add_fusion.1.refs_1_), channel_id=1, source_target_pairs={{64,0},{128,64},{192,128},{65,1},{129,65},{193,129},{66,2},{130,66... | collective-permute-start | bytes 6152 | tf_op jit(solution)/shard_map/ppermute | solution.py:339
  73.7 18.9 %collective-permute-start.20 = (f32[4,128]{1,0:T(4,128)S(1)}, f32[4,128]{1,0:T(4,128)S(1)}, u32[]{:S(2)}, u32[]{:S(2)}) collective-permute-start(f32[4,128]{1,0:T(4,128)S(1)} %subtract_add_fusion.1.refs_1_), channel_id=1, source_target_pairs={{0,64},{64,128},{128,192},{1,65},{65,129},{129,193},{2,66},{66,130... | collective-permute-start | bytes 6152 | tf_op jit(solution)/shard_map/ppermute | solution.py:339
  92.5 2.1 collective-permute-start.12
  92.7 11.2 %collective-permute-start.22 = (f32[3,4,128]{2,1,0:T(4,128)S(1)}, f32[3,4,128]{2,1,0:T(4,128)S(1)}, u32[]{:S(2)}, u32[]{:S(2)}) collective-permute-start(f32[3,4,128]{2,1,0:T(4,128)S(1)} %pad_maximum_fusion.5.refs_4_), channel_id=1, source_target_pairs={{0,8},{8,16},{16,24},{24,32},{32,40},{40,48},{48,56},{1,9},{9,17},... | collective-permute-start | bytes 18440 | tf_op jit(solution)/shard_map/ppermute | solution.py:339
  94.6 9.1 %collective-permute-start.13 = (f32[8,128]{1,0:T(8,128)S(1)}, f32[8,128]{1,0:T(8,128)S(1)}, u32[]{:S(2)}, u32[]{:S(2)}) collective-permute-start(f32[8,128]{1,0:T(8,128)S(1)} %add.69), channel_id=1, source_target_pairs={{0,128},{64,192},{128,0},{192,64},{1,129},{65,193},{129,1},{193,65... | collective-permute-start | bytes 12296 | tf_op jit(solution)/shard_map/ppermute | solution.py:355
  98.3 14.3 %collective-permute-start.23 = (f32[3,4,128]{2,1,0:T(4,128)S(1)}, f32[3,4,128]{2,1,0:T(4,128)S(1)}, u32[]{:S(2)}, u32[]{:S(2)}) collective-permute-start(f32[3,4,128]{2,1,0:T(4,128)S(1)} %pad_maximum_fusion.5.refs_4_), channel_id=1, source_target_pairs={{8,0},{16,8},{24,16},{32,24},{40,32},{48,40},{56,48},{9,1},{17,9},... | collective-permute-start | bytes 18440 | tf_op jit(solution)/shard_map/ppermute | solution.py:339
  103.8 3.7 %collective-permute-start.14 = (f32[8,128]{1,0:T(8,128)S(1)}, f32[8,128]{1,0:T(8,128)S(1)}, u32[]{:S(2)}, u32[]{:S(2)}) collective-permute-start(f32[8,128]{1,0:T(8,128)S(1)} %add.70), channel_id=1, source_target_pairs={{0,8},{8,0},{16,24},{24,16},{32,40},{40,32},{48,56},{56,48},{1,9},... | collective-permute-start | bytes 12296 | tf_op jit(solution)/shard_map/ppermute | solution.py:355
  107.5 5.1 %collective-permute-start.15 = (f32[8,128]{1,0:T(8,128)S(1)}, f32[8,128]{1,0:T(8,128)S(1)}, u32[]{:S(2)}, u32[]{:S(2)}) collective-permute-start(f32[8,128]{1,0:T(8,128)S(1)} %add.71), channel_id=1, source_target_pairs={{0,16},{8,24},{16,0},{24,8},{32,48},{40,56},{48,32},{56,40},{1,17}... | collective-permute-start | bytes 12296 | tf_op jit(solution)/shard_map/ppermute | solution.py:355
  112.6 5.9 %collective-permute-start.16 = (f32[8,128]{1,0:T(8,128)S(1)}, f32[8,128]{1,0:T(8,128)S(1)}, u32[]{:S(2)}, u32[]{:S(2)}) collective-permute-start(f32[8,128]{1,0:T(8,128)S(1)} %add.72), channel_id=1, source_target_pairs={{0,32},{8,40},{16,48},{24,56},{32,0},{40,8},{48,16},{56,24},{1,33}... | collective-permute-start | bytes 12296 | tf_op jit(solution)/shard_map/ppermute | solution.py:355
  112.6 28.2 %collective-permute-start.24 = (f32[9,4,128]{2,1,0:T(4,128)S(1)}, f32[9,4,128]{2,1,0:T(4,128)S(1)}, u32[]{:S(2)}, u32[]{:S(2)}) collective-permute-start(f32[9,4,128]{2,1,0:T(4,128)S(1)} %constant_dynamic-update-slice_fusion.15), channel_id=1, source_target_pairs={{0,1},{1,2},{2,3},{3,4},{4,5},{5,6},{6,7},{8,9},{9,10},{10,11},{11... | collective-permute-start | bytes 55304 | tf_op jit(solution)/shard_map/ppermute | solution.py:339
  116.5 24.3 %collective-permute-start.25 = (f32[9,4,128]{2,1,0:T(4,128)S(1)}, f32[9,4,128]{2,1,0:T(4,128)S(1)}, u32[]{:S(2)}, u32[]{:S(2)}) collective-permute-start(f32[9,4,128]{2,1,0:T(4,128)S(1)} %constant_dynamic-update-slice_fusion.15), channel_id=1, source_target_pairs={{1,0},{2,1},{3,2},{4,3},{5,4},{6,5},{7,6},{9,8},{10,9},{11,10},{12... | collective-permute-start | bytes 55304 | tf_op jit(solution)/shard_map/ppermute | solution.py:339
  118.5 4.4 %collective-permute-start.17 = (f32[8,128]{1,0:T(8,128)S(1)}, f32[8,128]{1,0:T(8,128)S(1)}, u32[]{:S(2)}, u32[]{:S(2)}) collective-permute-start(f32[8,128]{1,0:T(8,128)S(1)} %add.73), channel_id=1, source_target_pairs={{0,1},{1,0},{2,3},{3,2},{4,5},{5,4},{6,7},{7,6},{8,9},{9,8},{10,11... | collective-permute-start | bytes 12296 | tf_op jit(solution)/shard_map/ppermute | solution.py:355
  122.9 13.5 %collective-permute-start.18 = (f32[8,128]{1,0:T(8,128)S(1)}, f32[8,128]{1,0:T(8,128)S(1)}, u32[]{:S(2)}, u32[]{:S(2)}) collective-permute-start(f32[8,128]{1,0:T(8,128)S(1)} %add.74), channel_id=1, source_target_pairs={{0,2},{1,3},{2,0},{3,1},{4,6},{5,7},{6,4},{7,5},{8,10},{9,11},{10,... | collective-permute-start | bytes 12296 | tf_op jit(solution)/shard_map/ppermute | solution.py:355
  136.4 26.7 %collective-permute-start.19 = (f32[8,128]{1,0:T(8,128)S(1)}, f32[8,128]{1,0:T(8,128)S(1)}, u32[]{:S(2)}, u32[]{:S(2)}) collective-permute-start(f32[8,128]{1,0:T(8,128)S(1)} %add.75), channel_id=1, source_target_pairs={{0,4},{1,5},{2,6},{3,7},{4,0},{5,1},{6,2},{7,3},{8,12},{9,13},{10,... | collective-permute-start | bytes 12296 | tf_op jit(solution)/shard_map/ppermute | solution.py:355
  165.4 4.3 %collective-permute-start.27 = (f32[12,128]{1,0:T(8,128)S(1)}, f32[12,128]{1,0:T(8,128)S(1)}, u32[]{:S(2)}, u32[]{:S(2)}) collective-permute-start(f32[12,128]{1,0:T(8,128)S(1)} %get-tuple-element.12.refs_0_), channel_id=1, source_target_pairs={{64,0},{128,64},{192,128},{65,1},{129,65},{193,129},{66,2},{130,66... | collective-permute-start | bytes 18440 | tf_op jit(solution)/shard_map/ppermute | solution.py:339
  167.3 6.5 %collective-permute-start.26 = (f32[12,128]{1,0:T(8,128)S(1)}, f32[12,128]{1,0:T(8,128)S(1)}, u32[]{:S(2)}, u32[]{:S(2)}) collective-permute-start(f32[12,128]{1,0:T(8,128)S(1)} %get-tuple-element.12.refs_0_), channel_id=1, source_target_pairs={{0,64},{64,128},{128,192},{1,65},{65,129},{129,193},{2,66},{66,130... | collective-permute-start | bytes 18440 | tf_op jit(solution)/shard_map/ppermute | solution.py:339
  173.8 8.0 %collective-permute-start.28 = (f32[3,12,128]{2,1,0:T(8,128)S(1)}, f32[3,12,128]{2,1,0:T(8,128)S(1)}, u32[]{:S(2)}, u32[]{:S(2)}) collective-permute-start(f32[3,12,128]{2,1,0:T(8,128)S(1)} %pad_maximum_fusion.2.refs_1_.refs_2_), channel_id=1, source_target_pairs={{0,8},{8,16},{16,24},{24,32},{32,40},{40,48},{48,56},{1,9},{9,17},... | collective-permute-start | bytes 55304 | tf_op jit(solution)/shard_map/ppermute | solution.py:339
  175.7 7.5 %collective-permute-start.29 = (f32[3,12,128]{2,1,0:T(8,128)S(1)}, f32[3,12,128]{2,1,0:T(8,128)S(1)}, u32[]{:S(2)}, u32[]{:S(2)}) collective-permute-start(f32[3,12,128]{2,1,0:T(8,128)S(1)} %pad_maximum_fusion.2.refs_1_.refs_2_), channel_id=1, source_target_pairs={{8,0},{16,8},{24,16},{32,24},{40,32},{48,40},{56,48},{9,1},{17,9},... | collective-permute-start | bytes 55304 | tf_op jit(solution)/shard_map/ppermute | solution.py:339
  183.3 12.9 %collective-permute-start.30 = (f32[9,12,128]{2,1,0:T(8,128)S(1)}, f32[9,12,128]{2,1,0:T(8,128)S(1)}, u32[]{:S(2)}, u32[]{:S(2)}) collective-permute-start(f32[9,12,128]{2,1,0:T(8,128)S(1)} %constant_dynamic-update-slice_fusion.20), channel_id=1, source_target_pairs={{0,1},{1,2},{2,3},{3,4},{4,5},{5,6},{6,7},{8,9},{9,10},{10,11},{11... | collective-permute-start | bytes 165896 | tf_op jit(solution)/shard_map/ppermute | solution.py:339
  186.6 9.6 %collective-permute-start.31 = (f32[9,12,128]{2,1,0:T(8,128)S(1)}, f32[9,12,128]{2,1,0:T(8,128)S(1)}, u32[]{:S(2)}, u32[]{:S(2)}) collective-permute-start(f32[9,12,128]{2,1,0:T(8,128)S(1)} %constant_dynamic-update-slice_fusion.20), channel_id=1, source_target_pairs={{1,0},{2,1},{3,2},{4,3},{5,4},{6,5},{7,6},{9,8},{10,9},{11,10},{12... | collective-permute-start | bytes 165896 | tf_op jit(solution)/shard_map/ppermute | solution.py:339
  209.2 21.3 %collective-permute-start.41 = (f32[4,128]{1,0:T(4,128)S(1)}, f32[4,128]{1,0:T(4,128)S(1)}, u32[]{:S(2)}, u32[]{:S(2)}) collective-permute-start(f32[4,128]{1,0:T(4,128)S(1)} %subtract_add_fusion.refs_1_), channel_id=1, source_target_pairs={{64,0},{128,64},{192,128},{65,1},{129,65},{193,129},{66,2},{130,66... | collective-permute-start | bytes 6152 | tf_op jit(solution)/shard_map/ppermute | solution.py:339
  211.1 19.4 %collective-permute-start.40 = (f32[4,128]{1,0:T(4,128)S(1)}, f32[4,128]{1,0:T(4,128)S(1)}, u32[]{:S(2)}, u32[]{:S(2)}) collective-permute-start(f32[4,128]{1,0:T(4,128)S(1)} %subtract_add_fusion.refs_1_), channel_id=1, source_target_pairs={{0,64},{64,128},{128,192},{1,65},{65,129},{129,193},{2,66},{66,130... | collective-permute-start | bytes 6152 | tf_op jit(solution)/shard_map/ppermute | solution.py:339
  230.4 2.1 collective-permute-start.32
  230.6 11.6 %collective-permute-start.42 = (f32[3,4,128]{2,1,0:T(4,128)S(1)}, f32[3,4,128]{2,1,0:T(4,128)S(1)}, u32[]{:S(2)}, u32[]{:S(2)}) collective-permute-start(f32[3,4,128]{2,1,0:T(4,128)S(1)} %pad_maximum_fusion.6.refs_4_), channel_id=1, source_target_pairs={{0,8},{8,16},{16,24},{24,32},{32,40},{40,48},{48,56},{1,9},{9,17},... | collective-permute-start | bytes 18440 | tf_op jit(solution)/shard_map/ppermute | solution.py:339
  232.5 9.5 %collective-permute-start.33 = (f32[8,128]{1,0:T(8,128)S(1)}, f32[8,128]{1,0:T(8,128)S(1)}, u32[]{:S(2)}, u32[]{:S(2)}) collective-permute-start(f32[8,128]{1,0:T(8,128)S(1)} %add.80), channel_id=1, source_target_pairs={{0,128},{64,192},{128,0},{192,64},{1,129},{65,193},{129,1},{193,65... | collective-permute-start | bytes 12296 | tf_op jit(solution)/shard_map/ppermute | solution.py:355
  235.7 10.0 %collective-permute-start.43 = (f32[3,4,128]{2,1,0:T(4,128)S(1)}, f32[3,4,128]{2,1,0:T(4,128)S(1)}, u32[]{:S(2)}, u32[]{:S(2)}) collective-permute-start(f32[3,4,128]{2,1,0:T(4,128)S(1)} %pad_maximum_fusion.6.refs_4_), channel_id=1, source_target_pairs={{8,0},{16,8},{24,16},{32,24},{40,32},{48,40},{56,48},{9,1},{17,9},... | collective-permute-start | bytes 18440 | tf_op jit(solution)/shard_map/ppermute | solution.py:339
  242.1 3.7 %collective-permute-start.34 = (f32[8,128]{1,0:T(8,128)S(1)}, f32[8,128]{1,0:T(8,128)S(1)}, u32[]{:S(2)}, u32[]{:S(2)}) collective-permute-start(f32[8,128]{1,0:T(8,128)S(1)} %add.81), channel_id=1, source_target_pairs={{0,8},{8,0},{16,24},{24,16},{32,40},{40,32},{48,56},{56,48},{1,9},... | collective-permute-start | bytes 12296 | tf_op jit(solution)/shard_map/ppermute | solution.py:355
  245.8 5.9 %collective-permute-start.35 = (f32[8,128]{1,0:T(8,128)S(1)}, f32[8,128]{1,0:T(8,128)S(1)}, u32[]{:S(2)}, u32[]{:S(2)}) collective-permute-start(f32[8,128]{1,0:T(8,128)S(1)} %add.82), channel_id=1, source_target_pairs={{0,16},{8,24},{16,0},{24,8},{32,48},{40,56},{48,32},{56,40},{1,17}... | collective-permute-start | bytes 12296 | tf_op jit(solution)/shard_map/ppermute | solution.py:355
  245.8 29.2 %collective-permute-start.44 = (f32[9,4,128]{2,1,0:T(4,128)S(1)}, f32[9,4,128]{2,1,0:T(4,128)S(1)}, u32[]{:S(2)}, u32[]{:S(2)}) collective-permute-start(f32[9,4,128]{2,1,0:T(4,128)S(1)} %constant_dynamic-update-slice_fusion.32), channel_id=1, source_target_pairs={{0,1},{1,2},{2,3},{3,4},{4,5},{5,6},{6,7},{8,9},{9,10},{10,11},{11... | collective-permute-start | bytes 55304 | tf_op jit(solution)/shard_map/ppermute | solution.py:339
  249.2 25.8 %collective-permute-start.45 = (f32[9,4,128]{2,1,0:T(4,128)S(1)}, f32[9,4,128]{2,1,0:T(4,128)S(1)}, u32[]{:S(2)}, u32[]{:S(2)}) collective-permute-start(f32[9,4,128]{2,1,0:T(4,128)S(1)} %constant_dynamic-update-slice_fusion.32), channel_id=1, source_target_pairs={{1,0},{2,1},{3,2},{4,3},{5,4},{6,5},{7,6},{9,8},{10,9},{11,10},{12... | collective-permute-start | bytes 55304 | tf_op jit(solution)/shard_map/ppermute | solution.py:339
  251.7 3.7 %collective-permute-start.36 = (f32[8,128]{1,0:T(8,128)S(1)}, f32[8,128]{1,0:T(8,128)S(1)}, u32[]{:S(2)}, u32[]{:S(2)}) collective-permute-start(f32[8,128]{1,0:T(8,128)S(1)} %add.83), channel_id=1, source_target_pairs={{0,32},{8,40},{16,48},{24,56},{32,0},{40,8},{48,16},{56,24},{1,33}... | collective-permute-start | bytes 12296 | tf_op jit(solution)/shard_map/ppermute | solution.py:355
  255.4 5.0 %collective-permute-start.37 = (f32[8,128]{1,0:T(8,128)S(1)}, f32[8,128]{1,0:T(8,128)S(1)}, u32[]{:S(2)}, u32[]{:S(2)}) collective-permute-start(f32[8,128]{1,0:T(8,128)S(1)} %add.84), channel_id=1, source_target_pairs={{0,1},{1,0},{2,3},{3,2},{4,5},{5,4},{6,7},{7,6},{8,9},{9,8},{10,11... | collective-permute-start | bytes 12296 | tf_op jit(solution)/shard_map/ppermute | solution.py:355
  260.4 11.1 %collective-permute-start.38 = (f32[8,128]{1,0:T(8,128)S(1)}, f32[8,128]{1,0:T(8,128)S(1)}, u32[]{:S(2)}, u32[]{:S(2)}) collective-permute-start(f32[8,128]{1,0:T(8,128)S(1)} %add.85), channel_id=1, source_target_pairs={{0,2},{1,3},{2,0},{3,1},{4,6},{5,7},{6,4},{7,5},{8,10},{9,11},{10,... | collective-permute-start | bytes 12296 | tf_op jit(solution)/shard_map/ppermute | solution.py:355
  271.5 25.8 %collective-permute-start.39 = (f32[8,128]{1,0:T(8,128)S(1)}, f32[8,128]{1,0:T(8,128)S(1)}, u32[]{:S(2)}, u32[]{:S(2)}) collective-permute-start(f32[8,128]{1,0:T(8,128)S(1)} %add.86), channel_id=1, source_target_pairs={{0,4},{1,5},{2,6},{3,7},{4,0},{5,1},{6,2},{7,3},{8,12},{9,13},{10,... | collective-permute-start | bytes 12296 | tf_op jit(solution)/shard_map/ppermute | solution.py:355

commit v2 on v1

--- a/solution.py
+++ b/solution.py
@@ -20,7 +20,6 @@
 SLOTS = 512
 LANES = 128
 TILES = SLOTS // LANES
-ROWS = 64
 BRICK = 16
 PLANES = 26
 PAD = 8
@@ -53,59 +52,180 @@
     return jnp.sum(jnp.transpose(acc), axis=0, keepdims=True)
 
 
-def cell_sides(number, fixed_y, fixed_z):
-    side_x = lax.rem(number, 3) - 1
-    side_y = number // 3 - 1 if fixed_y is None else fixed_y
-    return side_x, side_y, fixed_z
-
-
-def born_kernel(groups, *refs):
-    own = refs[0]
-    cells = refs[1 : 1 + 2 * len(groups)]
-    out, col, acc = refs[1 + 2 * len(groups) :]
+BLOCK = 32
+BLOCKS = SLOTS // BLOCK
+UNROLL = 8
+CELLS = 27
+EMPTY = CELLS * TILES
+ROOM = EMPTY + 4
+FAR = 1e9
+
+
+def three_parts(values):
+    high = values.astype(jnp.bfloat16)
+    rest = values - high.astype(jnp.float32)
+    middle = rest.astype(jnp.bfloat16)
+    return high, middle, (rest - middle.astype(jnp.float32)).astype(jnp.bfloat16)
+
+
+def arrange_kernel(table, live_count, pos, charges, types, out, order, col, left):
+    count = live_count[0]
+    slot = lax.broadcasted_iota(jnp.int32, (TILES, LANES), 0) * LANES
+    slot = slot + lax.broadcasted_iota(jnp.int32, (TILES, LANES), 1)
+    living = slot < count
+    alive = jnp.where(living, 1.0, 0.0)
+    kinds = types[...]
+    props = []
+    for row in range(3):
+        value = jnp.zeros((TILES, LANES), jnp.float32)
+        for kind in range(table.shape[1]):
+            value = jnp.where(kinds == kind, table[row, kind], value)
+        props.append(value)
+    group = jnp.zeros((TILES, LANES), jnp.float32)
+    sub = lax.broadcasted_iota(jnp.int32, (SLOTS, LANES), 0)
+    lane = lax.broadcasted_iota(jnp.int32, (SLOTS, LANES), 1)
+    for dim, size in ((0, 256), (1, 128), (2, 64), (0, 32)):
+        key = group * 64.0 + jnp.where(living, pos[4 * dim : 4 * dim + 4, :], 40.0)
+        for tile in range(TILES):
+            col[tile * LANES : (tile + 1) * LANES, :] = spread(key[tile : tile + 1, :])
+        ranks = []
+        for tile in range(TILES):
+            row = key[tile : tile + 1, :]
+            other = col[...]
+            ahead = (other < row) | ((other == row) & (sub < lane + tile * LANES))
+            ranks.append(jnp.sum(jnp.where(ahead, 1.0, 0.0), axis=0, keepdims=True))
+        rank = jnp.concatenate(ranks, axis=0)
+        group = jnp.floor(rank * (1.0 / size))
+    order[...] = rank
+    values = [pos[0:4, :], pos[4:8, :], pos[8:12, :], charges[...] * alive]
+    values += [props[1] * alive, props[2] * alive, props[0], alive]
+    total = jnp.zeros((3 * len(values), SLOTS), jnp.float32)
+    for tile in range(TILES):
+        block = jnp.concatenate([value[tile : tile + 1, :] for value in values], axis=0)
+        for part, piece in enumerate(three_parts(block)):
+            left[8 * part : 8 * part + 8, :] = piece.astype(jnp.float32)
+        hot = jnp.where(rank[tile : tile + 1, :] == sub.astype(jnp.float32), 1.0, 0.0).astype(jnp.bfloat16)
+        dims = (((1,), (1,)), ((), ()))
+        total = total + lax.dot_general(left[...].astype(jnp.bfloat16), hot, dims, preferred_element_type=jnp.float32)
+    total = total[0:8] + total[8:16] + total[16:24]
+    for channel in range(8):
+        for tile in range(TILES):
+            at = slice(4 * channel + tile, 4 * channel + tile + 1)
+            out[at, :] = total[channel : channel + 1, tile * LANES : (tile + 1) * LANES]
+
+
+def restore_kernel(order, moved, start, force, out, left):
+    values = [moved[4 * d : 4 * d + 4, :] - start[4 * d : 4 * d + 4, :] for d in range(3)]
+    values += [force[4 * d : 4 * d + 4, :] for d in range(3)]
+    values += [jnp.zeros((TILES, LANES), jnp.float32)] * 2
+    sub = lax.broadcasted_iota(jnp.int32, (LANES, LANES), 0).astype(jnp.float32)
+    totals = [jnp.zeros((24, LANES), jnp.float32) for _ in range(TILES)]
+    for source in range(TILES):
+        block = jnp.concatenate([value[source : source + 1, :] for value in values], axis=0)
+        for part, piece in enumerate(three_parts(block)):
+            left[8 * part : 8 * part + 8, :] = piece.astype(jnp.float32)
+        parts = left[...].astype(jnp.bfloat16)
+        for tile in range(TILES):
+            hot = jnp.where(order[tile : tile + 1, :] == sub + float(source * LANES), 1.0, 0.0)
+            totals[tile] = totals[tile] + jnp.dot(parts, hot.astype(jnp.bfloat16), preferred_element_type=jnp.float32)
+    for tile in range(TILES):
+        total = totals[tile][0:8] + totals[tile][8:16] + totals[tile][16:24]
+        for channel in range(6):
+            at = slice(4 * channel + tile, 4 * channel + tile + 1)
+            out[at, :] = total[channel : channel + 1, :]
+
+
+def plan_kernel(pos, aux, listed, tiles, active):
+    own, own_aux = pos[13], aux[13]
+    low, high = [], []
+    for dim in range(3):
+        living = own_aux[16:20, :] > 0.0
+        value = own[4 * dim : 4 * dim + 4, :]
+        lo, hi = jnp.where(living, value, FAR), jnp.where(living, value, -FAR)
+        for step in (1, 2, 4, 8, 16):
+            lo = jnp.minimum(lo, pltpu.roll(lo, LANES - step, 1))
+            hi = jnp.maximum(hi, pltpu.roll(hi, LANES - step, 1))
+        low.append(lo)
+        high.append(hi)
+    active[...] = jnp.zeros_like(active)
+    tiles[EMPTY:ROOM] = jnp.zeros((ROOM - EMPTY, 8, LANES), jnp.float32)
+
+    def visit(number, carry):
+        sides = (lax.rem(number, 3) - 1, lax.rem(number // 3, 3) - 1, number // 9 - 1)
+        living = aux[number, 16:20, :] > 0.0
+        near_low, near_high = [], []
+        for dim in range(3):
+            moved = pos[number, 4 * dim : 4 * dim + 4, :] + sides[dim].astype(jnp.float32) * float(BRICK)
+            near_low.append(jnp.min(jnp.where(living, moved, FAR), axis=1, keepdims=True))
+            near_high.append(jnp.max(jnp.where(living, moved, -FAR), axis=1, keepdims=True))
+            scaled = moved * (1.0 / CUTOFF)
+            for tile in range(TILES):
+                tiles[4 * number + tile, dim : dim + 1, :] = scaled[tile : tile + 1, :]
+        for tile in range(TILES):
+            tiles[4 * number + tile, 3:4, :] = aux[number, 16 + tile : 17 + tile, :]
+            tiles[4 * number + tile, 4:5, :] = aux[number, 12 + tile : 13 + tile, :]
+        for tile in range(TILES):
+            apart = jnp.zeros((TILES, LANES), jnp.float32)
+            for dim in range(3):
+                lo, hi = low[dim][tile : tile + 1, :], high[dim][tile : tile + 1, :]
+                gap = jnp.maximum(jnp.maximum(near_low[dim] - hi, lo - near_high[dim]), 0.0)
+                apart = apart + gap * gap
+            near = jnp.where(apart < CUTOFF * CUTOFF * 1.0001, 1.0, 0.0)
+            active[tile, pl.ds(4 * number, TILES), :] = near
+        return carry
+
+    lax.fori_loop(0, CELLS, visit, 0)
+    row = lax.broadcasted_iota(jnp.int32, (LANES, LANES), 0)
+    lane = lax.broadcasted_iota(jnp.int32, (LANES, LANES), 1)
+    before = jnp.where(lane < row, 1.0, 0.0).astype(jnp.bfloat16)
+    for tile in range(TILES):
+        flags = active[tile]
+        ranks = jnp.dot(before, flags.astype(jnp.bfloat16), preferred_element_type=jnp.float32)
+        for part in range(LANES // BLOCK):
+            at = slice(part * BLOCK, part * BLOCK + 1)
+            chosen = jnp.broadcast_to(flags[:, at], (LANES, LANES)) > 0.0
+            place = jnp.broadcast_to(ranks[:, at], (LANES, LANES)).astype(jnp.int32)
+            total = jnp.sum(jnp.where(chosen, 1, 0), axis=0, keepdims=True)
+            entry = jnp.sum(jnp.where(chosen & (place == lane), row, 0), axis=0, keepdims=True)
+            spot = lane[0:1, :]
+            entry = jnp.where(spot < total, entry, EMPTY)
+            block = tile * (LANES // BLOCK) + part
+            listed[block : block + 1, :] = jnp.where(spot == LANES - 1, total, entry)
+
+
+def born_kernel(listed, tiles, own, out, col, acc):
     for channel in range(3):
         for tile in range(TILES):
             row = own[4 * channel + tile : 4 * channel + tile + 1, :] * (1.0 / CUTOFF)
             col[channel, tile * LANES : (tile + 1) * LANES, :] = spread(row)
-    acc[...] = jnp.zeros_like(acc)
-    for index, (count, fixed_y, fixed_z) in enumerate(groups):
-        pos, aux = cells[2 * index], cells[2 * index + 1]
-
-        def visit(number, carry, pos=pos, aux=aux, fixed_y=fixed_y, fixed_z=fixed_z):
-            sides = cell_sides(number, fixed_y, fixed_z)
-            shift = [side * float(BRICK) if isinstance(side, int) else side.astype(jnp.float32) * float(BRICK) for side in sides]
-            rows = []
-            for tile in range(TILES):
-                coords = [
-                    (pos[number, 4 * d + tile : 4 * d + tile + 1, :] + shift[d]) * (1.0 / CUTOFF)
-                    for d in range(3)
-                ]
-                rows.append(coords + [aux[number, 16 + tile : 17 + tile, :]])
-
-            def block(ib, inner):
-                at = pl.ds(pl.multiple_of(ib * ROWS, ROWS), ROWS)
-                xi, yi, zi = col[0, at, :], col[1, at, :], col[2, at, :]
-                total = acc[at, :]
-                for xj, yj, zj, wj in rows:
-                    dx, dy, dz = xi - xj, yi - yj, zi - zj
-                    u = dx * dx + dy * dy + dz * dz
-                    s = jnp.maximum(1.0 - u, 0.0)
-                    e = jnp.exp(u * (-CUTOFF * CUTOFF / 8.0))
-                    total = total + e * s * (s * wj)
-                acc[at, :] = total
-                return inner
-
-            return lax.fori_loop(0, SLOTS // ROWS, block, carry)
-
-        lax.fori_loop(0, count, visit, 0)
+
+    def block(ib, carry):
+        at = pl.ds(pl.multiple_of(ib * BLOCK, BLOCK), BLOCK)
+        xi, yi, zi = col[0, at, :], col[1, at, :], col[2, at, :]
+
+        def some(chunk, total):
+            for k in range(UNROLL):
+                tile = listed[ib, chunk * UNROLL + k]
+                dx = xi - tiles[tile, 0:1, :]
+                dy = yi - tiles[tile, 1:2, :]
+                dz = zi - tiles[tile, 2:3, :]
+                u = dx * dx + dy * dy + dz * dz
+                s = jnp.maximum(1.0 - u, 0.0)
+                e = jnp.exp(u * (-CUTOFF * CUTOFF / 8.0))
+                total = total + (e * s) * (s * tiles[tile, 3:4, :])
+            return total
+
+        chunks = (listed[ib, LANES - 1] + UNROLL - 1) // UNROLL
+        acc[at, :] = lax.fori_loop(0, chunks, some, jnp.zeros((BLOCK, LANES), jnp.float32))
+        return carry
+
+    lax.fori_loop(0, BLOCKS, block, 0)
     for tile in range(TILES):
-        out[tile : tile + 1, :] = gather_rows(acc[tile * LANES : (tile + 1) * LANES, :])
-
-
-def gb_kernel(groups, *refs):
-    own, own_radius = refs[:2]
-    cells = refs[2 : 2 + 3 * len(groups)]
-    out, col, acc = refs[2 + 3 * len(groups) :]
+        total = gather_rows(acc[tile * LANES : (tile + 1) * LANES, :]) - own[16 + tile : 17 + tile, :]
+        out[tile : tile + 1, :] = own[24 + tile : 25 + tile, :] + total
+
+
+def gb_kernel(listed, tiles, own, own_radius, radii, out, col, acc, rows):
     for tile in range(TILES):
         at = slice(tile * LANES, (tile + 1) * LANES)
         for channel in range(3):
@@ -114,46 +234,49 @@
         radius = spread(own_radius[tile : tile + 1, :] * (1.0 / CUTOFF))
         col[3, at, :] = radius
         col[4, at, :] = -0.5 / radius
-    acc[...] = jnp.zeros_like(acc)
-    for index, (count, fixed_y, fixed_z) in enumerate(groups):
-        pos, aux, rad = cells[3 * index : 3 * index + 3]
-
-        def visit(number, carry, pos=pos, aux=aux, rad=rad, fixed_y=fixed_y, fixed_z=fixed_z):
-            sides = cell_sides(number, fixed_y, fixed_z)
-            shift = [side * float(BRICK) if isinstance(side, int) else side.astype(jnp.float32) * float(BRICK) for side in sides]
-            rows = []
-            for tile in range(TILES):
-                coords = [
-                    (pos[number, 4 * d + tile : 4 * d + tile + 1, :] + shift[d]) * (1.0 / CUTOFF)
-                    for d in range(3)
-                ]
-                radius = jnp.maximum(rad[number, tile : tile + 1, :], 0.5) * (1.0 / CUTOFF)
-                rows.append(coords + [aux[number, 12 + tile : 13 + tile, :], radius, 0.5 / radius])
-
-            def block(ib, inner):
-                at = pl.ds(pl.multiple_of(ib * ROWS, ROWS), ROWS)
-                xi, yi, zi = col[0, at, :], col[1, at, :], col[2, at, :]
-                ri, ai = col[3, at, :], col[4, at, :]
-                fx, fy, fz = acc[0, at, :], acc[1, at, :], acc[2, at, :]
-                for xj, yj, zj, qj, rj, aj in rows:
-                    dx, dy, dz = xi - xj, yi - yj, zi - zj
-                    u = dx * dx + dy * dy + dz * dz
-                    s = jnp.maximum(1.0 - u, 0.0)
-                    e = jnp.exp(u * (ai * aj))
-                    inv = lax.rsqrt(u + (ri * rj) * e)
-                    t = s * inv
-                    m = (qj * t) * (1.0 + (t * inv) * (0.25 - 0.0625 * e))
-                    fx = fx + m * dx
-                    fy = fy + m * dy
-                    fz = fz + m * dz
-                acc[0, at, :] = fx
-                acc[1, at, :] = fy
-                acc[2, at, :] = fz
-                return inner
-
-            return lax.fori_loop(0, SLOTS // ROWS, block, carry)
-
-        lax.fori_loop(0, count, visit, 0)
+    rows[EMPTY:ROOM] = jnp.ones((ROOM - EMPTY, 2, LANES), jnp.float32)
+
+    def ready(number, carry):
+        radius = jnp.maximum(radii[number], 0.5) * (1.0 / CUTOFF)
+        half = 0.5 / radius
+        for tile in range(TILES):
+            rows[4 * number + tile, 0:1, :] = radius[tile : tile + 1, :]
+            rows[4 * number + tile, 1:2, :] = half[tile : tile + 1, :]
+        return carry
+
+    lax.fori_loop(0, CELLS, ready, 0)
+
+    def block(ib, carry):
+        at = pl.ds(pl.multiple_of(ib * BLOCK, BLOCK), BLOCK)
+        xi, yi, zi = col[0, at, :], col[1, at, :], col[2, at, :]
+        ri, ai = col[3, at, :], col[4, at, :]
+
+        def some(chunk, force):
+            fx, fy, fz = force
+            for k in range(UNROLL):
+                tile = listed[ib, chunk * UNROLL + k]
+                dx = xi - tiles[tile, 0:1, :]
+                dy = yi - tiles[tile, 1:2, :]
+                dz = zi - tiles[tile, 2:3, :]
+                u = dx * dx + dy * dy + dz * dz
+                s = jnp.maximum(1.0 - u, 0.0)
+                e = jnp.exp(u * (ai * rows[tile, 1:2, :]))
+                inv = lax.rsqrt(u + (ri * rows[tile, 0:1, :]) * e)
+                t = s * inv
+                m = (tiles[tile, 4:5, :] * t) * (1.0 + (t * inv) * (0.25 - 0.0625 * e))
+                fx = fx + m * dx
+                fy = fy + m * dy
+                fz = fz + m * dz
+            return fx, fy, fz
+
+        chunks = (listed[ib, LANES - 1] + UNROLL - 1) // UNROLL
+        zero = jnp.zeros((BLOCK, LANES), jnp.float32)
+        force = lax.fori_loop(0, chunks, some, (zero, zero, zero))
+        for channel in range(3):
+            acc[channel, at, :] = force[channel]
+        return carry
+
+    lax.fori_loop(0, BLOCKS, block, 0)
     for channel in range(3):
         for tile in range(TILES):
             total = gather_rows(acc[channel, tile * LANES : (tile + 1) * LANES, :])
@@ -281,9 +404,9 @@
 
 
 def fit_kernel(scale, parts, bounds, *refs):
-    own, aux, extra, evolved, exp_ext, sums = refs[:6]
-    gb = refs[6 : 6 + parts]
-    moved, force, left, right, inner, px, pxs = refs[6 + parts :]
+    own, evolved, exp_ext, sums = refs[:4]
+    gb = refs[4 : 4 + parts]
+    moved, force, left, right, inner, px, pxs = refs[4 + parts :]
     squares = jnp.sum(sums[0:1, :], axis=1, keepdims=True)
     cross = jnp.sum(sums[1:2, :], axis=1, keepdims=True)
     target = jnp.sum(sums[2:3, :], axis=1, keepdims=True)
@@ -320,8 +443,8 @@
             turned_x = turned_x + pxs[plane + 3 : plane + 4, :] * part
             plain = plain + at_x * part
             turned_z = turned_z + at_x * inner[rows, LANES : 2 * LANES]
-        weight = scale * aux[20 + tile : 21 + tile, :]
-        charge = -2.0 / (CUTOFF * CUTOFF) * aux[12 + tile : 13 + tile, :]
+        weight = scale * own[20 + tile : 21 + tile, :]
+        charge = -2.0 / (CUTOFF * CUTOFF) * own[12 + tile : 13 + tile, :]
         sides = (turned_x * y, plain * ys, turned_z * y)
         for channel in range(3):
             at = slice(4 * channel + tile, 4 * channel + tile + 1)
@@ -330,7 +453,7 @@
                 pair = pair + other[at, :]
             total = charge * pair + weight * jnp.sum(sides[channel], axis=0, keepdims=True)
             force[at, :] = total
-            moved[at, :] = own[at, :] + STEP_SIZE * (extra[4 + tile : 5 + tile, :] * total)
+            moved[at, :] = own[at, :] + STEP_SIZE * (own[28 + tile : 29 + tile, :] * total)
 
 
 def shifted(block, axis, step):
@@ -370,41 +493,12 @@
     return jax.ShapeDtypeStruct(shape, jnp.float32)
 
 
-def born_part(own, pieces, groups):
-    cells = sum(count for count, _, _ in groups)
-    args = [own] + [array for piece in pieces for array in piece]
-    return call(
-        functools.partial(born_kernel, groups),
-        f32(TILES, LANES),
-        cells * SLOTS * SLOTS * 20,
-        scratch=[pltpu.VMEM((3, SLOTS, LANES), jnp.float32), pltpu.VMEM((SLOTS, LANES), jnp.float32)],
-        n_in=len(args),
-    )(*args)
-
-
-def gb_part(own, radius, pieces, groups):
-    cells = sum(count for count, _, _ in groups)
-    args = [own, radius] + [array for piece in pieces for array in piece]
-    return call(
-        functools.partial(gb_kernel, groups),
-        f32(3 * TILES, LANES),
-        cells * SLOTS * SLOTS * 40,
-        scratch=[pltpu.VMEM((5, SLOTS, LANES), jnp.float32), pltpu.VMEM((3, SLOTS, LANES), jnp.float32)],
-        n_in=len(args),
-    )(*args)
-
-
 def gathered(block):
     line = jnp.stack([*(shifted(block, "gx", 1)[None]), block, *(shifted(block, "gx", -1)[None])])
     before_y, after_y = both_sides(line, "gy")
     plane = jnp.concatenate([before_y, line, after_y])
     before_z, after_z = both_sides(plane, "gz")
     return line, (before_y, after_y), plane, (before_z, after_z)
-
-
-GROUPS_X = ((3, 0, 0),)
-GROUPS_Y = ((3, -1, 0), (3, 1, 0))
-GROUPS_Z = ((9, None, -1), (9, None, 1))
 
 
 def on_device(positions, charges, atom_types, type_table, live_count, exp_map):
@@ -416,38 +510,63 @@
     bounds = jnp.stack(bounds).astype(jnp.int32)
     scale = FIT_GAIN * float(BRICK**3 * sizes[0] * sizes[1] * sizes[2])
 
-    onehot = (atom_types.reshape(SLOTS, 1) == jnp.arange(type_table.shape[1], dtype=jnp.int32)).astype(jnp.float32)
-    props = jnp.sum(onehot[None] * type_table[:, None, :], axis=-1)
-    living = (lax.iota(jnp.int32, SLOTS) < live_count.reshape(())).astype(jnp.float32)
-    start = positions.reshape(3 * TILES, LANES)
-    rest = jnp.stack([charges.reshape(SLOTS) * living, props[1] * living, props[2] * living])
-    packed = jnp.concatenate([start, rest.reshape(3 * TILES, LANES)])
-    extra = jnp.stack([props[0], living]).reshape(2 * TILES, LANES)
+    atoms, order = call(
+        arrange_kernel,
+        (f32(32, LANES), f32(TILES, LANES)),
+        1 << 22,
+        scratch=[pltpu.VMEM((SLOTS, LANES), jnp.float32), pltpu.VMEM((24, LANES), jnp.float32)],
+        smem=2,
+        n_in=5,
+    )(
+        type_table,
+        live_count.reshape(1),
+        positions.reshape(3 * TILES, LANES),
+        charges.reshape(TILES, LANES),
+        atom_types.reshape(TILES, LANES),
+    )
 
     exp_wide = widened(exp_map, BLUR_REACH + SPLAT_MARGIN)
     exp_ext = jnp.pad(exp_wide, ((0, 0), (3, 3), (3, LANES - PLANES - 3)))
 
     fixed = None
-    moved = packed
+    moved = atoms
     for step in range(STEPS):
-        line, sides_y, plane, sides_z = gathered(moved)
+        line, sides_y, plane, sides_z = gathered(moved[:24] if step == 0 else moved)
+        every = jnp.concatenate([sides_z[0], plane, sides_z[1]])
         if fixed is None:
-            fixed = (line, sides_y, plane, sides_z)
-        partial = [
-            born_part(moved, [(line, fixed[0])], GROUPS_X),
-            born_part(moved, list(zip(sides_y, fixed[1])), GROUPS_Y),
-            born_part(moved, list(zip(sides_z, fixed[3])), GROUPS_Z),
+            fixed = every
+        listed, tiles = call(
+            plan_kernel,
+            (jax.ShapeDtypeStruct((BLOCKS, LANES), jnp.int32), f32(ROOM, 8, LANES)),
+            1 << 22,
+            scratch=[pltpu.VMEM((TILES, LANES, LANES), jnp.float32)],
+            n_in=2,
+        )(every, fixed)
+        own = atoms if step == 0 else jnp.concatenate([moved, atoms[12:]])
+        radius = call(
+            born_kernel,
+            f32(TILES, LANES),
+            1 << 27,
+            scratch=[pltpu.VMEM((3, SLOTS, LANES), jnp.float32), pltpu.VMEM((SLOTS, LANES), jnp.float32)],
+            smem=1,
+            n_in=3,
+        )(listed, tiles, own)
+        near = gathered(radius)
+        radii = jnp.concatenate([near[3][0], near[2], near[3][1]])
+        pairs = [
+            call(
+                gb_kernel,
+                f32(3 * TILES, LANES),
+                1 << 28,
+                scratch=[
+                    pltpu.VMEM((5, SLOTS, LANES), jnp.float32),
+                    pltpu.VMEM((3, SLOTS, LANES), jnp.float32),
+                    pltpu.VMEM((ROOM, 2, LANES), jnp.float32),
+                ],
+                smem=1,
+                n_in=5,
+            )(listed, tiles, own, radius, radii)
         ]
-        radius = extra[:TILES] + (partial[0] + partial[1] + partial[2] - packed[16:20])
-        near = gathered(radius)
-        pairs = [
-            gb_part(moved, radius, [(line, fixed[0], near[0])], GROUPS_X),
-            gb_part(moved, radius, list(zip(sides_y, fixed[1], near[1])), GROUPS_Y),
-            gb_part(moved, radius, list(zip(sides_z, fixed[3], near[3])), GROUPS_Z),
-        ]
-        every = jnp.concatenate([sides_z[0], plane, sides_z[1]])
-        if step == 0:
-            every_fixed = every
         evolved, sums = call(
             evolve_kernel,
             (f32(PLANES, WIDE, LANES), f32(8, LANES)),
@@ -460,7 +579,7 @@
             ],
             smem=1,
             n_in=4,
-        )(bounds, every, every_fixed, exp_ext)
+        )(bounds, every, fixed, exp_ext)
         sums = total_over_devices(sums)
         moved, force = call(
             functools.partial(fit_kernel, scale, len(pairs)),
@@ -474,10 +593,18 @@
                 pltpu.VMEM((WIDE, LANES), jnp.float32),
             ],
             smem=1,
-            n_in=7 + len(pairs),
-        )(bounds, moved, packed, extra, evolved, exp_ext, sums, *pairs)
+            n_in=5 + len(pairs),
+        )(bounds, own, evolved, exp_ext, sums, *pairs)
+    results = call(
+        restore_kernel,
+        f32(6 * TILES, LANES),
+        1 << 20,
+        scratch=[pltpu.VMEM((24, LANES), jnp.float32)],
+        n_in=4,
+    )(order, moved, atoms, force)
     own = evolved[5 : 5 + BRICK, PAD : PAD + BRICK, PAD : PAD + BRICK]
-    return (moved - start).reshape(positions.shape), force.reshape(positions.shape), own
+    results = results.reshape((2,) + positions.shape)
+    return results[0], results[1], own
 
 
 def solution(mesh):

time: 305 us -> 273 us (0.90); the launches traced: 300 us -> 271 us
  Pallas kernels: 146 us -> 85.3 us
  waiting for transfers between devices: 21.6 us -> 50.4 us
  starting transfers between devices: 125 us -> 129 us
    pallas_call x12 -> x8, Pallas kernels: 109 us -> 47.9 us  [the longest x2 24 us: on_device(): call(gb_kernel, f32(3 * TILES, LANES), 1 << 28, scratch=[pltpu.VMEM((5, S...]
    ppermute x16, waiting for transfers between devices: 13.8 us -> 28.4 us  [total_over_devices(): values = values + lax.ppermute(values, axis, pairs)]
    ppermute x30, waiting for transfers between devices: 7.78 us -> 22 us  [shifted(): return lax.ppermute(block, axis, pairs)]
    ppermute x30, starting transfers between devices: 98.9 us -> 109 us  [shifted(): return lax.ppermute(block, axis, pairs)]
    ppermute x16, starting transfers between devices: 26.2 us -> 19.3 us  [total_over_devices(): values = values + lax.ppermute(values, axis, pairs)]
  transfers between devices with their start and end apart: 46 -> 46, of which waited for: 9 -> 18; matrix products, arithmetic and copies ran while one was open for 1% -> 1% of each run, Pallas kernels for 39% -> 26%
where the time goes in v2:
time: 273 us; the launch traced here: 271 us
  starting transfers between devices  129 us (47%)
  Pallas kernels  85.3 us (31%)
  waiting for transfers between devices  50.4 us (18%)
  local copies, waits for them, and re-layouts  4.11 us (2%)
    ppermute x30, starting transfers between devices, shifted(): return lax.ppermute(block, axis, pairs)  109 us
    pallas_call x2, Pallas kernels, on_device(): call(evolve_kernel, (f32(PLANES, WIDE, LANES), f32(8, LANES)), 1 << 33, s...  33.6 us
    ppermute x16, waiting for transfers between devices, total_over_devices(): values = values + lax.ppermute(values, axis, pairs)  28.4 us
    pallas_call x2, Pallas kernels, on_device(): call(gb_kernel, f32(3 * TILES, LANES), 1 << 28, scratch=[pltpu.VMEM((5, S...  24 us
    ppermute x30, waiting for transfers between devices, shifted(): return lax.ppermute(block, axis, pairs)  22 us
    ppermute x16, starting transfers between devices, total_over_devices(): values = values + lax.ppermute(values, axis, pairs)  19.3 us
    pallas_call x2, Pallas kernels, on_device(): call(born_kernel, f32(TILES, LANES), 1 << 27, scratch=[pltpu.VMEM((3, SLO...  14 us
    pallas_call x2, Pallas kernels, on_device(): call(plan_kernel, (jax.ShapeDtypeStruct((BLOCKS, LANES), jnp.int32), f32(...  7.87 us
  transfers between devices with their start and end apart: 46, of which 18 were waited for; matrix products, arithmetic and copies ran while one was open for 1% of the time, Pallas kernels for 26%

profile of v2, /device:TPU:56, one launch (start us, length us, event | category | flops | bytes accessed | tf_op | source)
XLA Modules:
  0.0 271.4 jit_solution(17591197729563057365)
XLA Ops:
  1.5 1.9 collective-permute-start.6
  4.8 1.8 shard_map.85
  6.7 5.1 %collective-permute-start.1 = (f32[24,128]{1,0:T(8,128)S(1)}, f32[24,128]{1,0:T(8,128)S(1)}, u32[]{:S(2)}, u32[]{:S(2)}) collective-permute-start(f32[24,128]{1,0:T(8,128)S(1)} %get-tuple-element.42), channel_id=1, source_target_pairs={{64,0},{128,64},{192,128},{65,1},{129,65},{193,129},{66,2},{130,66... | collective-permute-start | bytes 36872 | tf_op jit(solution)/shard_map/ppermute | solution.py:462
  11.8 1.9 collective-permute-start
  13.8 5.1 %collective-permute-start.7 = (f32[5,16,16]{2,1,0:T(8,128)S(1)}, f32[5,16,16]{2,1,0:T(8,128)S(1)}, u32[]{:S(2)}, u32[]{:S(2)}) collective-permute-start(f32[5,16,16]{2,1,0:T(8,128)S(1)} %get-tuple-element.39), channel_id=1, source_target_pairs={{64,0},{128,64},{192,128},{65,1},{129,65},{193,129},{66,2},{130,66... | collective-permute-start | bytes 15368 | tf_op jit(solution)/shard_map/ppermute | solution.py:462
  19.1 1.5 collective-permute-done.7
  20.6 3.4 %collective-permute-start.8 = (f32[26,5,16]{2,1,0:T(8,128)S(1)}, f32[26,5,16]{2,1,0:T(8,128)S(1)}, u32[]{:S(2)}, u32[]{:S(2)}) collective-permute-start(f32[26,5,16]{2,1,0:T(8,128)S(1)} %get-tuple-element.37), channel_id=1, source_target_pairs={{0,8},{8,16},{16,24},{24,32},{32,40},{40,48},{48,56},{1,9},{9,17},... | collective-permute-start | bytes 24968 | tf_op jit(solution)/shard_map/ppermute | solution.py:462
  24.0 4.6 %collective-permute-start.9 = (f32[26,5,16]{2,1,0:T(8,128)S(1)}, f32[26,5,16]{2,1,0:T(8,128)S(1)}, u32[]{:S(2)}, u32[]{:S(2)}) collective-permute-start(f32[26,5,16]{2,1,0:T(8,128)S(1)} %get-tuple-element.38), channel_id=1, source_target_pairs={{8,0},{16,8},{24,16},{32,24},{40,32},{48,40},{56,48},{9,1},{17,9},... | collective-permute-start | bytes 24968 | tf_op jit(solution)/shard_map/ppermute | solution.py:462
  28.6 1.9 collective-permute-start.2
  30.5 6.0 %collective-permute-start.3 = (f32[3,24,128]{2,1,0:T(8,128)S(1)}, f32[3,24,128]{2,1,0:T(8,128)S(1)}, u32[]{:S(2)}, u32[]{:S(2)}) collective-permute-start(f32[3,24,128]{2,1,0:T(8,128)S(1)} %pad_maximum_fusion.1), channel_id=1, source_target_pairs={{8,0},{16,8},{24,16},{32,24},{40,32},{48,40},{56,48},{9,1},{17,9},... | collective-permute-start | bytes 110600 | tf_op jit(solution)/shard_map/ppermute | solution.py:462
  36.7 1.5 collective-permute-done.3
  38.2 3.8 %collective-permute-start.4 = (f32[9,24,128]{2,1,0:T(8,128)S(1)}, f32[9,24,128]{2,1,0:T(8,128)S(1)}, u32[]{:S(2)}, u32[]{:S(2)}) collective-permute-start(f32[9,24,128]{2,1,0:T(8,128)S(1)} %constant_dynamic-update-slice_fusion), channel_id=1, source_target_pairs={{0,1},{1,2},{2,3},{3,4},{4,5},{5,6},{6,7},{8,9},{9,10},{10,11},{11... | collective-permute-start | bytes 331784 | tf_op jit(solution)/shard_map/ppermute | solution.py:462
  42.2 3.8 %collective-permute-start.10 = (f32[26,26,5]{2,1,0:T(8,128)S(1)}, f32[26,26,5]{2,1,0:T(8,128)S(1)}, u32[]{:S(2)}, u32[]{:S(2)}) collective-permute-start(f32[26,26,5]{2,1,0:T(8,128)S(1)} %get-tuple-element.35), channel_id=1, source_target_pairs={{0,1},{1,2},{2,3},{3,4},{4,5},{5,6},{6,7},{8,9},{9,10},{10,11},{11... | collective-permute-start | bytes 40568 | tf_op jit(solution)/shard_map/ppermute | solution.py:462
  46.0 2.0 collective-permute-start.11
  48.1 1.9 collective-permute-start.5
  50.1 8.3 %collective-permute-done.5 = f32[9,24,128]{2,1,0:T(8,128)S(1)} collective-permute-done((f32[9,24,128]{2,1,0:T(8,128)S(1)}, f32[9,24,128]{2,1,0:T(8,128)S(1)}, u32[]{:S(2)}, u32[]{:S(2)}) %collective-permute-start.5) | collective-permute-done | bytes 110624 | tf_op jit(solution)/shard_map/ppermute | solution.py:462
  58.4 3.9 %shard_map.87 = (s32[16,128]{1,0:T(8,128)S(1)}, f32[112,8,128]{2,1,0:T(8,128)S(1)}) custom-call(f32[27,24,128]{2,1,0:T(8,128)S(1)} %constant_dynamic-update-slice_fusion.5.pos.aux, f32[27,24,128]{2,1,0:T(8,128)S(1)} %constant_dynamic-update-slice_fusion.5.pos.aux), custom_call_target="tpu_custom_call" | custom-call | flops 4194304 | bytes 262144 | tf_op jit(solution)/shard_map/pallas_call | solution.py:538
  62.3 6.9 %shard_map.88.own_radius = f32[4,128]{1,0:T(4,128)S(1)} custom-call(s32[16,128]{1,0:T(8,128)S(1)} %get-tuple-element.20.listed, f32[112,8,128]{2,1,0:T(8,128)S(1)} %get-tuple-element.21.tiles, f32[32,128]{1,0:T(8,128)S(1)} %get-tuple-element.17.own.refs_0_.start), custom_call_target="tpu_custom_call" | custom-call | flops 134217728 | bytes 262144 | tf_op jit(solution)/shard_map/pallas_call | solution.py:546
  69.2 1.9 collective-permute-start.20
  71.1 7.7 %collective-permute-start.21 = (f32[4,128]{1,0:T(4,128)S(1)}, f32[4,128]{1,0:T(4,128)S(1)}, u32[]{:S(2)}, u32[]{:S(2)}) collective-permute-start(f32[4,128]{1,0:T(4,128)S(1)} %shard_map.88.own_radius), channel_id=1, source_target_pairs={{64,0},{128,64},{192,128},{65,1},{129,65},{193,129},{66,2},{130,66... | collective-permute-start | bytes 6152 | tf_op jit(solution)/shard_map/ppermute | solution.py:462
  80.1 1.9 collective-permute-start.22
  82.0 16.8 %shard_map.86 = (f32[26,32,128]{2,1,0:T(8,128)S(1)}, f32[8,128]{1,0:T(8,128)S(1)}) custom-call(s32[6]{0:T(128)S(1)} %stack.51.bounds, f32[27,24,128]{2,1,0:T(8,128)S(1)} %constant_dynamic-update-slice_fusion.5.pos.aux, f32[27,24,128]{2,1,0:T(8,128)S(1)} %constant_dynamic-update-slice_fusion.5.pos.aux, f32[26,32,128]{2,1,0:T(8,128)S(1)} %select_maximum_fusion.exp_ext.refs_2_), custom_call_target="tpu_custom_call" | custom-call | flops 8589934592 | bytes 262144 | tf_op jit(solution)/shard_map/pallas_call | solution.py:570
  98.9 6.0 %collective-permute-start.23 = (f32[3,4,128]{2,1,0:T(4,128)S(1)}, f32[3,4,128]{2,1,0:T(4,128)S(1)}, u32[]{:S(2)}, u32[]{:S(2)}) collective-permute-start(f32[3,4,128]{2,1,0:T(4,128)S(1)} %pad_maximum_fusion.4), channel_id=1, source_target_pairs={{8,0},{16,8},{24,16},{32,24},{40,32},{48,40},{56,48},{9,1},{17,9},... | collective-permute-start | bytes 18440 | tf_op jit(solution)/shard_map/ppermute | solution.py:462
  105.0 3.4 %collective-permute-start.13 = (f32[8,128]{1,0:T(8,128)S(1)}, f32[8,128]{1,0:T(8,128)S(1)}, u32[]{:S(2)}, u32[]{:S(2)}) collective-permute-start(f32[8,128]{1,0:T(8,128)S(1)} %add.50), channel_id=1, source_target_pairs={{0,128},{64,192},{128,0},{192,64},{1,129},{65,193},{129,1},{193,65... | collective-permute-start | bytes 12296 | tf_op jit(solution)/shard_map/ppermute | solution.py:478
  108.4 4.1 %collective-permute-start.24 = (f32[9,4,128]{2,1,0:T(4,128)S(1)}, f32[9,4,128]{2,1,0:T(4,128)S(1)}, u32[]{:S(2)}, u32[]{:S(2)}) collective-permute-start(f32[9,4,128]{2,1,0:T(4,128)S(1)} %constant_dynamic-update-slice_fusion.15), channel_id=1, source_target_pairs={{0,1},{1,2},{2,3},{3,4},{4,5},{5,6},{6,7},{8,9},{9,10},{10,11},{11... | collective-permute-start | bytes 55304 | tf_op jit(solution)/shard_map/ppermute | solution.py:462
  112.6 3.6 %collective-permute-done.14 = f32[8,128]{1,0:T(8,128)S(1)} collective-permute-done((f32[8,128]{1,0:T(8,128)S(1)}, f32[8,128]{1,0:T(8,128)S(1)}, u32[]{:S(2)}, u32[]{:S(2)}) %collective-permute-start.14) | collective-permute-done | bytes 4128 | tf_op jit(solution)/shard_map/ppermute | solution.py:478
  116.2 5.1 %collective-permute-done.15 = f32[8,128]{1,0:T(8,128)S(1)} collective-permute-done((f32[8,128]{1,0:T(8,128)S(1)}, f32[8,128]{1,0:T(8,128)S(1)}, u32[]{:S(2)}, u32[]{:S(2)}) %collective-permute-start.15) | collective-permute-done | bytes 4128 | tf_op jit(solution)/shard_map/ppermute | solution.py:478
  121.4 3.6 %collective-permute-done.16 = f32[8,128]{1,0:T(8,128)S(1)} collective-permute-done((f32[8,128]{1,0:T(8,128)S(1)}, f32[8,128]{1,0:T(8,128)S(1)}, u32[]{:S(2)}, u32[]{:S(2)}) %collective-permute-start.16) | collective-permute-done | bytes 4128 | tf_op jit(solution)/shard_map/ppermute | solution.py:478
  125.0 3.9 %collective-permute-start.25 = (f32[9,4,128]{2,1,0:T(4,128)S(1)}, f32[9,4,128]{2,1,0:T(4,128)S(1)}, u32[]{:S(2)}, u32[]{:S(2)}) collective-permute-start(f32[9,4,128]{2,1,0:T(4,128)S(1)} %constant_dynamic-update-slice_fusion.15), channel_id=1, source_target_pairs={{1,0},{2,1},{3,2},{4,3},{5,4},{6,5},{7,6},{9,8},{10,9},{11,10},{12... | collective-permute-start | bytes 55304 | tf_op jit(solution)/shard_map/ppermute | solution.py:462
  128.9 1.4 collective-permute-start.18
  130.6 2.9 %collective-permute-done.18 = f32[8,128]{1,0:T(8,128)S(1)} collective-permute-done((f32[8,128]{1,0:T(8,128)S(1)}, f32[8,128]{1,0:T(8,128)S(1)}, u32[]{:S(2)}, u32[]{:S(2)}) %collective-permute-start.18) | collective-permute-done | bytes 4128 | tf_op jit(solution)/shard_map/ppermute | solution.py:478
  133.5 1.1 collective-permute-start.19
  134.6 11.8 %shard_map.89.refs_4_ = f32[12,128]{1,0:T(8,128)S(1)} custom-call(s32[16,128]{1,0:T(8,128)S(1)} %get-tuple-element.20.listed, f32[112,8,128]{2,1,0:T(8,128)S(1)} %get-tuple-element.21.tiles, f32[32,128]{1,0:T(8,128)S(1)} %get-tuple-element.17.own.refs_0_.start, f32[4,128]{1,0:T(4,128)S(1)} %shard_map.88.own_radius, ...), custom_call_target="tpu_custom_call" | custom-call | flops 268435456 | bytes 262144 | tf_op jit(solution)/shard_map/pallas_call | solution.py:557
  146.5 2.2 shard_map.90
  148.8 1.9 collective-permute-start.26
  150.7 5.1 %collective-permute-start.27 = (f32[12,128]{1,0:T(8,128)S(1)}, f32[12,128]{1,0:T(8,128)S(1)}, u32[]{:S(2)}, u32[]{:S(2)}) collective-permute-start(f32[12,128]{1,0:T(8,128)S(1)} %get-tuple-element.22), channel_id=1, source_target_pairs={{64,0},{128,64},{192,128},{65,1},{129,65},{193,129},{66,2},{130,66... | collective-permute-start | bytes 18440 | tf_op jit(solution)/shard_map/ppermute | solution.py:462
  155.8 1.3 collective-permute-done.27
  157.2 3.0 %collective-permute-start.28 = (f32[3,12,128]{2,1,0:T(8,128)S(1)}, f32[3,12,128]{2,1,0:T(8,128)S(1)}, u32[]{:S(2)}, u32[]{:S(2)}) collective-permute-start(f32[3,12,128]{2,1,0:T(8,128)S(1)} %pad_maximum_fusion.2), channel_id=1, source_target_pairs={{0,8},{8,16},{16,24},{24,32},{32,40},{40,48},{48,56},{1,9},{9,17},... | collective-permute-start | bytes 55304 | tf_op jit(solution)/shard_map/ppermute | solution.py:462
  160.1 5.0 %collective-permute-start.29 = (f32[3,12,128]{2,1,0:T(8,128)S(1)}, f32[3,12,128]{2,1,0:T(8,128)S(1)}, u32[]{:S(2)}, u32[]{:S(2)}) collective-permute-start(f32[3,12,128]{2,1,0:T(8,128)S(1)} %pad_maximum_fusion.2), channel_id=1, source_target_pairs={{8,0},{16,8},{24,16},{32,24},{40,32},{48,40},{56,48},{9,1},{17,9},... | collective-permute-start | bytes 55304 | tf_op jit(solution)/shard_map/ppermute | solution.py:462
  165.2 1.4 collective-permute-done.29
  166.6 5.5 %collective-permute-start.30 = (f32[9,12,128]{2,1,0:T(8,128)S(1)}, f32[9,12,128]{2,1,0:T(8,128)S(1)}, u32[]{:S(2)}, u32[]{:S(2)}) collective-permute-start(f32[9,12,128]{2,1,0:T(8,128)S(1)} %constant_dynamic-update-slice_fusion.27), channel_id=1, source_target_pairs={{0,1},{1,2},{2,3},{3,4},{4,5},{5,6},{6,7},{8,9},{9,10},{10,11},{11... | collective-permute-start | bytes 165896 | tf_op jit(solution)/shard_map/ppermute | solution.py:462
  172.2 1.9 collective-permute-start.31
  174.2 4.2 %collective-permute-done.31 = f32[9,12,128]{2,1,0:T(8,128)S(1)} collective-permute-done((f32[9,12,128]{2,1,0:T(8,128)S(1)}, f32[9,12,128]{2,1,0:T(8,128)S(1)}, u32[]{:S(2)}, u32[]{:S(2)}) %collective-permute-start.31) | collective-permute-done | bytes 55328 | tf_op jit(solution)/shard_map/ppermute | solution.py:462
  178.4 3.9 %shard_map.92 = (s32[16,128]{1,0:T(8,128)S(1)}, f32[112,8,128]{2,1,0:T(8,128)S(1)}) custom-call(f32[27,12,128]{2,1,0:T(8,128)S(1)} %constant_dynamic-update-slice_fusion.32.pos, f32[27,24,128]{2,1,0:T(8,128)S(1)} %constant_dynamic-update-slice_fusion.5.pos.aux), custom_call_target="tpu_custom_call" | custom-call | flops 4194304 | bytes 262144 | tf_op jit(solution)/shard_map/pallas_call | solution.py:538
  182.4 7.1 %shard_map.93.own_radius = f32[4,128]{1,0:T(4,128)S(1)} custom-call(s32[16,128]{1,0:T(8,128)S(1)} %get-tuple-element.25.listed, f32[112,8,128]{2,1,0:T(8,128)S(1)} %get-tuple-element.26.tiles, f32[32,128]{1,0:T(8,128)S(1)} %pad_maximum_fusion.3.own.refs_0_), custom_call_target="tpu_custom_call" | custom-call | flops 134217728 | bytes 262144 | tf_op jit(solution)/shard_map/pallas_call | solution.py:546
  189.4 1.9 collective-permute-start.40
  191.4 5.1 %collective-permute-start.41 = (f32[4,128]{1,0:T(4,128)S(1)}, f32[4,128]{1,0:T(4,128)S(1)}, u32[]{:S(2)}, u32[]{:S(2)}) collective-permute-start(f32[4,128]{1,0:T(4,128)S(1)} %shard_map.93.own_radius), channel_id=1, source_target_pairs={{64,0},{128,64},{192,128},{65,1},{129,65},{193,129},{66,2},{130,66... | collective-permute-start | bytes 6152 | tf_op jit(solution)/shard_map/ppermute | solution.py:462
  196.5 1.3 collective-permute-done.41
  197.8 1.9 collective-permute-start.42
  199.7 16.8 %shard_map.91 = (f32[26,32,128]{2,1,0:T(8,128)S(1)}, f32[8,128]{1,0:T(8,128)S(1)}) custom-call(s32[6]{0:T(128)S(1)} %stack.51.bounds, f32[27,12,128]{2,1,0:T(8,128)S(1)} %constant_dynamic-update-slice_fusion.32.pos, f32[27,24,128]{2,1,0:T(8,128)S(1)} %constant_dynamic-update-slice_fusion.5.pos.aux, f32[26,32,128]{2,1,0:T(8,128)S(1)} %select_maximum_fusion.exp_ext.refs_2_), custom_call_target="tpu_custom_call" | custom-call | flops 8589934592 | bytes 262144 | tf_op jit(solution)/shard_map/pallas_call | solution.py:570
  216.6 7.0 %collective-permute-start.43 = (f32[3,4,128]{2,1,0:T(4,128)S(1)}, f32[3,4,128]{2,1,0:T(4,128)S(1)}, u32[]{:S(2)}, u32[]{:S(2)}) collective-permute-start(f32[3,4,128]{2,1,0:T(4,128)S(1)} %pad_maximum_fusion.5), channel_id=1, source_target_pairs={{8,0},{16,8},{24,16},{32,24},{40,32},{48,40},{56,48},{9,1},{17,9},... | collective-permute-start | bytes 18440 | tf_op jit(solution)/shard_map/ppermute | solution.py:462
  223.7 4.3 %collective-permute-start.33 = (f32[8,128]{1,0:T(8,128)S(1)}, f32[8,128]{1,0:T(8,128)S(1)}, u32[]{:S(2)}, u32[]{:S(2)}) collective-permute-start(f32[8,128]{1,0:T(8,128)S(1)} %add.58), channel_id=1, source_target_pairs={{0,128},{64,192},{128,0},{192,64},{1,129},{65,193},{129,1},{193,65... | collective-permute-start | bytes 12296 | tf_op jit(solution)/shard_map/ppermute | solution.py:478
  228.0 1.9 collective-permute-start.44
  230.0 3.6 %collective-permute-done.34 = f32[8,128]{1,0:T(8,128)S(1)} collective-permute-done((f32[8,128]{1,0:T(8,128)S(1)}, f32[8,128]{1,0:T(8,128)S(1)}, u32[]{:S(2)}, u32[]{:S(2)}) %collective-permute-start.34) | collective-permute-done | bytes 4128 | tf_op jit(solution)/shard_map/ppermute | solution.py:478
  233.6 5.1 %collective-permute-done.35 = f32[8,128]{1,0:T(8,128)S(1)} collective-permute-done((f32[8,128]{1,0:T(8,128)S(1)}, f32[8,128]{1,0:T(8,128)S(1)}, u32[]{:S(2)}, u32[]{:S(2)}) %collective-permute-start.35) | collective-permute-done | bytes 4128 | tf_op jit(solution)/shard_map/ppermute | solution.py:478
  238.7 3.6 %collective-permute-done.36 = f32[8,128]{1,0:T(8,128)S(1)} collective-permute-done((f32[8,128]{1,0:T(8,128)S(1)}, f32[8,128]{1,0:T(8,128)S(1)}, u32[]{:S(2)}, u32[]{:S(2)}) %collective-permute-start.36) | collective-permute-done | bytes 4128 | tf_op jit(solution)/shard_map/ppermute | solution.py:478
  242.4 2.0 collective-permute-start.37
  245.1 1.9 collective-permute-start.45
  247.1 2.2 collective-permute-start.38
  249.4 1.4 collective-permute-done.45
  250.8 0.9 collective-permute-done.38
  251.7 4.4 %collective-permute-start.39 = (f32[8,128]{1,0:T(8,128)S(1)}, f32[8,128]{1,0:T(8,128)S(1)}, u32[]{:S(2)}, u32[]{:S(2)}) collective-permute-start(f32[8,128]{1,0:T(8,128)S(1)} %add.64), channel_id=1, source_target_pairs={{0,4},{1,5},{2,6},{3,7},{4,0},{5,1},{6,2},{7,3},{8,12},{9,13},{10,... | collective-permute-start | bytes 12296 | tf_op jit(solution)/shard_map/ppermute | solution.py:478
  256.1 12.2 %shard_map.94.refs_4_ = f32[12,128]{1,0:T(8,128)S(1)} custom-call(s32[16,128]{1,0:T(8,128)S(1)} %get-tuple-element.25.listed, f32[112,8,128]{2,1,0:T(8,128)S(1)} %get-tuple-element.26.tiles, f32[32,128]{1,0:T(8,128)S(1)} %pad_maximum_fusion.3.own.refs_0_, f32[4,128]{1,0:T(4,128)S(1)} %shard_map.93.own_radius, ...), custom_call_target="tpu_custom_call" | custom-call | flops 268435456 | bytes 262144 | tf_op jit(solution)/shard_map/pallas_call | solution.py:557
  268.3 1.6 shard_map.95
  (136 shorter events, 6.5 us)
Async XLA Ops:
  0.6 2.8 %copy-start.4 = (f32[3,1,1,1,512]{4,3,2,1,0:T(1,128)S(1)}, f32[3,1,1,1,512]{4,3,2,1,0:T(1,128)}, u32[]{:S(2)}) copy-start(f32[3,1,1,1,512]{4,3,2,1,0:T(1,128)} %param.6) | copy-start | bytes 18436
  0.6 18.4 %copy-start.3 = (f32[16,16,16]{2,1,0:T(8,128)S(1)}, f32[16,16,16]{2,1,0:T(8,128)}, u32[]{:S(2)}) copy-start(f32[16,16,16]{2,1,0:T(8,128)} %param.11) | copy-start | bytes 49156
  1.5 17.5 %collective-permute-start.6 = (f32[5,16,16]{2,1,0:T(8,128)S(1)}, f32[5,16,16]{2,1,0:T(8,128)S(1)}, u32[]{:S(2)}, u32[]{:S(2)}) collective-permute-start(f32[5,16,16]{2,1,0:T(8,128)S(1)} %get-tuple-element.40), channel_id=1, source_target_pairs={{0,64},{64,128},{128,192},{1,65},{65,129},{129,193},{2,66},{66,130... | collective-permute-start | bytes 15368 | tf_op jit(solution)/shard_map/ppermute | solution.py:462
  3.5 0.7 copy-start.1
  3.5 0.7 copy-start.2
  4.2 0.7 copy-start
  6.7 21.9 %collective-permute-start.1 = (f32[24,128]{1,0:T(8,128)S(1)}, f32[24,128]{1,0:T(8,128)S(1)}, u32[]{:S(2)}, u32[]{:S(2)}) collective-permute-start(f32[24,128]{1,0:T(8,128)S(1)} %get-tuple-element.42), channel_id=1, source_target_pairs={{64,0},{128,64},{192,128},{65,1},{129,65},{193,129},{66,2},{130,66... | collective-permute-start | bytes 36872 | tf_op jit(solution)/shard_map/ppermute | solution.py:462
  11.8 16.7 %collective-permute-start = (f32[24,128]{1,0:T(8,128)S(1)}, f32[24,128]{1,0:T(8,128)S(1)}, u32[]{:S(2)}, u32[]{:S(2)}) collective-permute-start(f32[24,128]{1,0:T(8,128)S(1)} %get-tuple-element.42), channel_id=1, source_target_pairs={{0,64},{64,128},{128,192},{1,65},{65,129},{129,193},{2,66},{66,130... | collective-permute-start | bytes 36872 | tf_op jit(solution)/shard_map/ppermute | solution.py:462
  13.8 6.8 %collective-permute-start.7 = (f32[5,16,16]{2,1,0:T(8,128)S(1)}, f32[5,16,16]{2,1,0:T(8,128)S(1)}, u32[]{:S(2)}, u32[]{:S(2)}) collective-permute-start(f32[5,16,16]{2,1,0:T(8,128)S(1)} %get-tuple-element.39), channel_id=1, source_target_pairs={{64,0},{128,64},{192,128},{65,1},{129,65},{193,129},{66,2},{130,66... | collective-permute-start | bytes 15368 | tf_op jit(solution)/shard_map/ppermute | solution.py:462
  20.6 16.0 %collective-permute-start.8 = (f32[26,5,16]{2,1,0:T(8,128)S(1)}, f32[26,5,16]{2,1,0:T(8,128)S(1)}, u32[]{:S(2)}, u32[]{:S(2)}) collective-permute-start(f32[26,5,16]{2,1,0:T(8,128)S(1)} %get-tuple-element.37), channel_id=1, source_target_pairs={{0,8},{8,16},{16,24},{24,32},{32,40},{40,48},{48,56},{1,9},{9,17},... | collective-permute-start | bytes 24968 | tf_op jit(solution)/shard_map/ppermute | solution.py:462
  24.0 12.6 %collective-permute-start.9 = (f32[26,5,16]{2,1,0:T(8,128)S(1)}, f32[26,5,16]{2,1,0:T(8,128)S(1)}, u32[]{:S(2)}, u32[]{:S(2)}) collective-permute-start(f32[26,5,16]{2,1,0:T(8,128)S(1)} %get-tuple-element.38), channel_id=1, source_target_pairs={{8,0},{16,8},{24,16},{32,24},{40,32},{48,40},{56,48},{9,1},{17,9},... | collective-permute-start | bytes 24968 | tf_op jit(solution)/shard_map/ppermute | solution.py:462
  28.6 8.1 %collective-permute-start.2 = (f32[3,24,128]{2,1,0:T(8,128)S(1)}, f32[3,24,128]{2,1,0:T(8,128)S(1)}, u32[]{:S(2)}, u32[]{:S(2)}) collective-permute-start(f32[3,24,128]{2,1,0:T(8,128)S(1)} %pad_maximum_fusion.1), channel_id=1, source_target_pairs={{0,8},{8,16},{16,24},{24,32},{32,40},{40,48},{48,56},{1,9},{9,17},... | collective-permute-start | bytes 110600 | tf_op jit(solution)/shard_map/ppermute | solution.py:462
  30.5 7.7 %collective-permute-start.3 = (f32[3,24,128]{2,1,0:T(8,128)S(1)}, f32[3,24,128]{2,1,0:T(8,128)S(1)}, u32[]{:S(2)}, u32[]{:S(2)}) collective-permute-start(f32[3,24,128]{2,1,0:T(8,128)S(1)} %pad_maximum_fusion.1), channel_id=1, source_target_pairs={{8,0},{16,8},{24,16},{32,24},{40,32},{48,40},{56,48},{9,1},{17,9},... | collective-permute-start | bytes 110600 | tf_op jit(solution)/shard_map/ppermute | solution.py:462
  38.2 11.8 %collective-permute-start.4 = (f32[9,24,128]{2,1,0:T(8,128)S(1)}, f32[9,24,128]{2,1,0:T(8,128)S(1)}, u32[]{:S(2)}, u32[]{:S(2)}) collective-permute-start(f32[9,24,128]{2,1,0:T(8,128)S(1)} %constant_dynamic-update-slice_fusion), channel_id=1, source_target_pairs={{0,1},{1,2},{2,3},{3,4},{4,5},{5,6},{6,7},{8,9},{9,10},{10,11},{11... | collective-permute-start | bytes 331784 | tf_op jit(solution)/shard_map/ppermute | solution.py:462
  42.2 36.6 %collective-permute-start.10 = (f32[26,26,5]{2,1,0:T(8,128)S(1)}, f32[26,26,5]{2,1,0:T(8,128)S(1)}, u32[]{:S(2)}, u32[]{:S(2)}) collective-permute-start(f32[26,26,5]{2,1,0:T(8,128)S(1)} %get-tuple-element.35), channel_id=1, source_target_pairs={{0,1},{1,2},{2,3},{3,4},{4,5},{5,6},{6,7},{8,9},{9,10},{10,11},{11... | collective-permute-start | bytes 40568 | tf_op jit(solution)/shard_map/ppermute | solution.py:462
  46.0 32.8 %collective-permute-start.11 = (f32[26,26,5]{2,1,0:T(8,128)S(1)}, f32[26,26,5]{2,1,0:T(8,128)S(1)}, u32[]{:S(2)}, u32[]{:S(2)}) collective-permute-start(f32[26,26,5]{2,1,0:T(8,128)S(1)} %get-tuple-element.36), channel_id=1, source_target_pairs={{1,0},{2,1},{3,2},{4,3},{5,4},{6,5},{7,6},{9,8},{10,9},{11,10},{12... | collective-permute-start | bytes 40568 | tf_op jit(solution)/shard_map/ppermute | solution.py:462
  48.1 10.3 %collective-permute-start.5 = (f32[9,24,128]{2,1,0:T(8,128)S(1)}, f32[9,24,128]{2,1,0:T(8,128)S(1)}, u32[]{:S(2)}, u32[]{:S(2)}) collective-permute-start(f32[9,24,128]{2,1,0:T(8,128)S(1)} %constant_dynamic-update-slice_fusion), channel_id=1, source_target_pairs={{1,0},{2,1},{3,2},{4,3},{5,4},{6,5},{7,6},{9,8},{10,9},{11,10},{12... | collective-permute-start | bytes 331784 | tf_op jit(solution)/shard_map/ppermute | solution.py:462
  69.2 10.1 %collective-permute-start.20 = (f32[4,128]{1,0:T(4,128)S(1)}, f32[4,128]{1,0:T(4,128)S(1)}, u32[]{:S(2)}, u32[]{:S(2)}) collective-permute-start(f32[4,128]{1,0:T(4,128)S(1)} %shard_map.88.own_radius), channel_id=1, source_target_pairs={{0,64},{64,128},{128,192},{1,65},{65,129},{129,193},{2,66},{66,130... | collective-permute-start | bytes 6152 | tf_op jit(solution)/shard_map/ppermute | solution.py:462
  71.1 9.0 %collective-permute-start.21 = (f32[4,128]{1,0:T(4,128)S(1)}, f32[4,128]{1,0:T(4,128)S(1)}, u32[]{:S(2)}, u32[]{:S(2)}) collective-permute-start(f32[4,128]{1,0:T(4,128)S(1)} %shard_map.88.own_radius), channel_id=1, source_target_pairs={{64,0},{128,64},{192,128},{65,1},{129,65},{193,129},{66,2},{130,66... | collective-permute-start | bytes 6152 | tf_op jit(solution)/shard_map/ppermute | solution.py:462
  80.1 28.2 %collective-permute-start.22 = (f32[3,4,128]{2,1,0:T(4,128)S(1)}, f32[3,4,128]{2,1,0:T(4,128)S(1)}, u32[]{:S(2)}, u32[]{:S(2)}) collective-permute-start(f32[3,4,128]{2,1,0:T(4,128)S(1)} %pad_maximum_fusion.4), channel_id=1, source_target_pairs={{0,8},{8,16},{16,24},{24,32},{32,40},{40,48},{48,56},{1,9},{9,17},... | collective-permute-start | bytes 18440 | tf_op jit(solution)/shard_map/ppermute | solution.py:462
  98.8 6.1 %collective-permute-start.12 = (f32[8,128]{1,0:T(8,128)S(1)}, f32[8,128]{1,0:T(8,128)S(1)}, u32[]{:S(2)}, u32[]{:S(2)}) collective-permute-start(f32[8,128]{1,0:T(8,128)S(1)} %get-tuple-element.19), channel_id=1, source_target_pairs={{0,64},{64,0},{128,192},{192,128},{1,65},{65,1},{129,193},{193,129... | collective-permute-start | bytes 12296 | tf_op jit(solution)/shard_map/ppermute | solution.py:478
  98.9 9.5 %collective-permute-start.23 = (f32[3,4,128]{2,1,0:T(4,128)S(1)}, f32[3,4,128]{2,1,0:T(4,128)S(1)}, u32[]{:S(2)}, u32[]{:S(2)}) collective-permute-start(f32[3,4,128]{2,1,0:T(4,128)S(1)} %pad_maximum_fusion.4), channel_id=1, source_target_pairs={{8,0},{16,8},{24,16},{32,24},{40,32},{48,40},{56,48},{9,1},{17,9},... | collective-permute-start | bytes 18440 | tf_op jit(solution)/shard_map/ppermute | solution.py:462
  105.0 7.5 %collective-permute-start.13 = (f32[8,128]{1,0:T(8,128)S(1)}, f32[8,128]{1,0:T(8,128)S(1)}, u32[]{:S(2)}, u32[]{:S(2)}) collective-permute-start(f32[8,128]{1,0:T(8,128)S(1)} %add.50), channel_id=1, source_target_pairs={{0,128},{64,192},{128,0},{192,64},{1,129},{65,193},{129,1},{193,65... | collective-permute-start | bytes 12296 | tf_op jit(solution)/shard_map/ppermute | solution.py:478
  108.4 21.9 %collective-permute-start.24 = (f32[9,4,128]{2,1,0:T(4,128)S(1)}, f32[9,4,128]{2,1,0:T(4,128)S(1)}, u32[]{:S(2)}, u32[]{:S(2)}) collective-permute-start(f32[9,4,128]{2,1,0:T(4,128)S(1)} %constant_dynamic-update-slice_fusion.15), channel_id=1, source_target_pairs={{0,1},{1,2},{2,3},{3,4},{4,5},{5,6},{6,7},{8,9},{9,10},{10,11},{11... | collective-permute-start | bytes 55304 | tf_op jit(solution)/shard_map/ppermute | solution.py:462
  112.5 3.7 %collective-permute-start.14 = (f32[8,128]{1,0:T(8,128)S(1)}, f32[8,128]{1,0:T(8,128)S(1)}, u32[]{:S(2)}, u32[]{:S(2)}) collective-permute-start(f32[8,128]{1,0:T(8,128)S(1)} %add.51), channel_id=1, source_target_pairs={{0,8},{8,0},{16,24},{24,16},{32,40},{40,32},{48,56},{56,48},{1,9},... | collective-permute-start | bytes 12296 | tf_op jit(solution)/shard_map/ppermute | solution.py:478
  116.2 5.1 %collective-permute-start.15 = (f32[8,128]{1,0:T(8,128)S(1)}, f32[8,128]{1,0:T(8,128)S(1)}, u32[]{:S(2)}, u32[]{:S(2)}) collective-permute-start(f32[8,128]{1,0:T(8,128)S(1)} %add.52), channel_id=1, source_target_pairs={{0,16},{8,24},{16,0},{24,8},{32,48},{40,56},{48,32},{56,40},{1,17}... | collective-permute-start | bytes 12296 | tf_op jit(solution)/shard_map/ppermute | solution.py:478
  121.3 3.6 %collective-permute-start.16 = (f32[8,128]{1,0:T(8,128)S(1)}, f32[8,128]{1,0:T(8,128)S(1)}, u32[]{:S(2)}, u32[]{:S(2)}) collective-permute-start(f32[8,128]{1,0:T(8,128)S(1)} %add.53), channel_id=1, source_target_pairs={{0,32},{8,40},{16,48},{24,56},{32,0},{40,8},{48,16},{56,24},{1,33}... | collective-permute-start | bytes 12296 | tf_op jit(solution)/shard_map/ppermute | solution.py:478
  125.0 3.9 %collective-permute-start.17 = (f32[8,128]{1,0:T(8,128)S(1)}, f32[8,128]{1,0:T(8,128)S(1)}, u32[]{:S(2)}, u32[]{:S(2)}) collective-permute-start(f32[8,128]{1,0:T(8,128)S(1)} %add.54), channel_id=1, source_target_pairs={{0,1},{1,0},{2,3},{3,2},{4,5},{5,4},{6,7},{7,6},{8,9},{9,8},{10,11... | collective-permute-start | bytes 12296 | tf_op jit(solution)/shard_map/ppermute | solution.py:478
  125.0 5.6 %collective-permute-start.25 = (f32[9,4,128]{2,1,0:T(4,128)S(1)}, f32[9,4,128]{2,1,0:T(4,128)S(1)}, u32[]{:S(2)}, u32[]{:S(2)}) collective-permute-start(f32[9,4,128]{2,1,0:T(4,128)S(1)} %constant_dynamic-update-slice_fusion.15), channel_id=1, source_target_pairs={{1,0},{2,1},{3,2},{4,3},{5,4},{6,5},{7,6},{9,8},{10,9},{11,10},{12... | collective-permute-start | bytes 55304 | tf_op jit(solution)/shard_map/ppermute | solution.py:462
  128.9 4.6 %collective-permute-start.18 = (f32[8,128]{1,0:T(8,128)S(1)}, f32[8,128]{1,0:T(8,128)S(1)}, u32[]{:S(2)}, u32[]{:S(2)}) collective-permute-start(f32[8,128]{1,0:T(8,128)S(1)} %add.55), channel_id=1, source_target_pairs={{0,2},{1,3},{2,0},{3,1},{4,6},{5,7},{6,4},{7,5},{8,10},{9,11},{10,... | collective-permute-start | bytes 12296 | tf_op jit(solution)/shard_map/ppermute | solution.py:478
  133.5 13.0 %collective-permute-start.19 = (f32[8,128]{1,0:T(8,128)S(1)}, f32[8,128]{1,0:T(8,128)S(1)}, u32[]{:S(2)}, u32[]{:S(2)}) collective-permute-start(f32[8,128]{1,0:T(8,128)S(1)} %add.56), channel_id=1, source_target_pairs={{0,4},{1,5},{2,6},{3,7},{4,0},{5,1},{6,2},{7,3},{8,12},{9,13},{10,... | collective-permute-start | bytes 12296 | tf_op jit(solution)/shard_map/ppermute | solution.py:478
  148.8 7.1 %collective-permute-start.26 = (f32[12,128]{1,0:T(8,128)S(1)}, f32[12,128]{1,0:T(8,128)S(1)}, u32[]{:S(2)}, u32[]{:S(2)}) collective-permute-start(f32[12,128]{1,0:T(8,128)S(1)} %get-tuple-element.22), channel_id=1, source_target_pairs={{0,64},{64,128},{128,192},{1,65},{65,129},{129,193},{2,66},{66,130... | collective-permute-start | bytes 18440 | tf_op jit(solution)/shard_map/ppermute | solution.py:462
  150.7 6.5 %collective-permute-start.27 = (f32[12,128]{1,0:T(8,128)S(1)}, f32[12,128]{1,0:T(8,128)S(1)}, u32[]{:S(2)}, u32[]{:S(2)}) collective-permute-start(f32[12,128]{1,0:T(8,128)S(1)} %get-tuple-element.22), channel_id=1, source_target_pairs={{64,0},{128,64},{192,128},{65,1},{129,65},{193,129},{66,2},{130,66... | collective-permute-start | bytes 18440 | tf_op jit(solution)/shard_map/ppermute | solution.py:462
  157.2 8.0 %collective-permute-start.28 = (f32[3,12,128]{2,1,0:T(8,128)S(1)}, f32[3,12,128]{2,1,0:T(8,128)S(1)}, u32[]{:S(2)}, u32[]{:S(2)}) collective-permute-start(f32[3,12,128]{2,1,0:T(8,128)S(1)} %pad_maximum_fusion.2), channel_id=1, source_target_pairs={{0,8},{8,16},{16,24},{24,32},{32,40},{40,48},{48,56},{1,9},{9,17},... | collective-permute-start | bytes 55304 | tf_op jit(solution)/shard_map/ppermute | solution.py:462
  160.1 6.5 %collective-permute-start.29 = (f32[3,12,128]{2,1,0:T(8,128)S(1)}, f32[3,12,128]{2,1,0:T(8,128)S(1)}, u32[]{:S(2)}, u32[]{:S(2)}) collective-permute-start(f32[3,12,128]{2,1,0:T(8,128)S(1)} %pad_maximum_fusion.2), channel_id=1, source_target_pairs={{8,0},{16,8},{24,16},{32,24},{40,32},{48,40},{56,48},{9,1},{17,9},... | collective-permute-start | bytes 55304 | tf_op jit(solution)/shard_map/ppermute | solution.py:462
  166.6 7.5 %collective-permute-start.30 = (f32[9,12,128]{2,1,0:T(8,128)S(1)}, f32[9,12,128]{2,1,0:T(8,128)S(1)}, u32[]{:S(2)}, u32[]{:S(2)}) collective-permute-start(f32[9,12,128]{2,1,0:T(8,128)S(1)} %constant_dynamic-update-slice_fusion.27), channel_id=1, source_target_pairs={{0,1},{1,2},{2,3},{3,4},{4,5},{5,6},{6,7},{8,9},{9,10},{10,11},{11... | collective-permute-start | bytes 165896 | tf_op jit(solution)/shard_map/ppermute | solution.py:462
  172.2 6.2 %collective-permute-start.31 = (f32[9,12,128]{2,1,0:T(8,128)S(1)}, f32[9,12,128]{2,1,0:T(8,128)S(1)}, u32[]{:S(2)}, u32[]{:S(2)}) collective-permute-start(f32[9,12,128]{2,1,0:T(8,128)S(1)} %constant_dynamic-update-slice_fusion.27), channel_id=1, source_target_pairs={{1,0},{2,1},{3,2},{4,3},{5,4},{6,5},{7,6},{9,8},{10,9},{11,10},{12... | collective-permute-start | bytes 165896 | tf_op jit(solution)/shard_map/ppermute | solution.py:462
  189.4 7.1 %collective-permute-start.40 = (f32[4,128]{1,0:T(4,128)S(1)}, f32[4,128]{1,0:T(4,128)S(1)}, u32[]{:S(2)}, u32[]{:S(2)}) collective-permute-start(f32[4,128]{1,0:T(4,128)S(1)} %shard_map.93.own_radius), channel_id=1, source_target_pairs={{0,64},{64,128},{128,192},{1,65},{65,129},{129,193},{2,66},{66,130... | collective-permute-start | bytes 6152 | tf_op jit(solution)/shard_map/ppermute | solution.py:462
  191.4 6.4 %collective-permute-start.41 = (f32[4,128]{1,0:T(4,128)S(1)}, f32[4,128]{1,0:T(4,128)S(1)}, u32[]{:S(2)}, u32[]{:S(2)}) collective-permute-start(f32[4,128]{1,0:T(4,128)S(1)} %shard_map.93.own_radius), channel_id=1, source_target_pairs={{64,0},{128,64},{192,128},{65,1},{129,65},{193,129},{66,2},{130,66... | collective-permute-start | bytes 6152 | tf_op jit(solution)/shard_map/ppermute | solution.py:462
  197.8 30.1 %collective-permute-start.42 = (f32[3,4,128]{2,1,0:T(4,128)S(1)}, f32[3,4,128]{2,1,0:T(4,128)S(1)}, u32[]{:S(2)}, u32[]{:S(2)}) collective-permute-start(f32[3,4,128]{2,1,0:T(4,128)S(1)} %pad_maximum_fusion.5), channel_id=1, source_target_pairs={{0,8},{8,16},{16,24},{24,32},{32,40},{40,48},{48,56},{1,9},{9,17},... | collective-permute-start | bytes 18440 | tf_op jit(solution)/shard_map/ppermute | solution.py:462
  216.5 7.1 %collective-permute-start.32 = (f32[8,128]{1,0:T(8,128)S(1)}, f32[8,128]{1,0:T(8,128)S(1)}, u32[]{:S(2)}, u32[]{:S(2)}) collective-permute-start(f32[8,128]{1,0:T(8,128)S(1)} %get-tuple-element.24), channel_id=1, source_target_pairs={{0,64},{64,0},{128,192},{192,128},{1,65},{65,1},{129,193},{193,129... | collective-permute-start | bytes 12296 | tf_op jit(solution)/shard_map/ppermute | solution.py:478
  216.6 11.3 %collective-permute-start.43 = (f32[3,4,128]{2,1,0:T(4,128)S(1)}, f32[3,4,128]{2,1,0:T(4,128)S(1)}, u32[]{:S(2)}, u32[]{:S(2)}) collective-permute-start(f32[3,4,128]{2,1,0:T(4,128)S(1)} %pad_maximum_fusion.5), channel_id=1, source_target_pairs={{8,0},{16,8},{24,16},{32,24},{40,32},{48,40},{56,48},{9,1},{17,9},... | collective-permute-start | bytes 18440 | tf_op jit(solution)/shard_map/ppermute | solution.py:462
  223.7 6.3 %collective-permute-start.33 = (f32[8,128]{1,0:T(8,128)S(1)}, f32[8,128]{1,0:T(8,128)S(1)}, u32[]{:S(2)}, u32[]{:S(2)}) collective-permute-start(f32[8,128]{1,0:T(8,128)S(1)} %add.58), channel_id=1, source_target_pairs={{0,128},{64,192},{128,0},{192,64},{1,129},{65,193},{129,1},{193,65... | collective-permute-start | bytes 12296 | tf_op jit(solution)/shard_map/ppermute | solution.py:478
  228.0 21.3 %collective-permute-start.44 = (f32[9,4,128]{2,1,0:T(4,128)S(1)}, f32[9,4,128]{2,1,0:T(4,128)S(1)}, u32[]{:S(2)}, u32[]{:S(2)}) collective-permute-start(f32[9,4,128]{2,1,0:T(4,128)S(1)} %constant_dynamic-update-slice_fusion.39), channel_id=1, source_target_pairs={{0,1},{1,2},{2,3},{3,4},{4,5},{5,6},{6,7},{8,9},{9,10},{10,11},{11... | collective-permute-start | bytes 55304 | tf_op jit(solution)/shard_map/ppermute | solution.py:462
  229.9 3.7 %collective-permute-start.34 = (f32[8,128]{1,0:T(8,128)S(1)}, f32[8,128]{1,0:T(8,128)S(1)}, u32[]{:S(2)}, u32[]{:S(2)}) collective-permute-start(f32[8,128]{1,0:T(8,128)S(1)} %add.59), channel_id=1, source_target_pairs={{0,8},{8,0},{16,24},{24,16},{32,40},{40,32},{48,56},{56,48},{1,9},... | collective-permute-start | bytes 12296 | tf_op jit(solution)/shard_map/ppermute | solution.py:478
  233.6 5.1 %collective-permute-start.35 = (f32[8,128]{1,0:T(8,128)S(1)}, f32[8,128]{1,0:T(8,128)S(1)}, u32[]{:S(2)}, u32[]{:S(2)}) collective-permute-start(f32[8,128]{1,0:T(8,128)S(1)} %add.60), channel_id=1, source_target_pairs={{0,16},{8,24},{16,0},{24,8},{32,48},{40,56},{48,32},{56,40},{1,17}... | collective-permute-start | bytes 12296 | tf_op jit(solution)/shard_map/ppermute | solution.py:478
  238.7 3.6 %collective-permute-start.36 = (f32[8,128]{1,0:T(8,128)S(1)}, f32[8,128]{1,0:T(8,128)S(1)}, u32[]{:S(2)}, u32[]{:S(2)}) collective-permute-start(f32[8,128]{1,0:T(8,128)S(1)} %add.61), channel_id=1, source_target_pairs={{0,32},{8,40},{16,48},{24,56},{32,0},{40,8},{48,16},{56,24},{1,33}... | collective-permute-start | bytes 12296 | tf_op jit(solution)/shard_map/ppermute | solution.py:478
  242.4 4.7 %collective-permute-start.37 = (f32[8,128]{1,0:T(8,128)S(1)}, f32[8,128]{1,0:T(8,128)S(1)}, u32[]{:S(2)}, u32[]{:S(2)}) collective-permute-start(f32[8,128]{1,0:T(8,128)S(1)} %add.62), channel_id=1, source_target_pairs={{0,1},{1,0},{2,3},{3,2},{4,5},{5,4},{6,7},{7,6},{8,9},{9,8},{10,11... | collective-permute-start | bytes 12296 | tf_op jit(solution)/shard_map/ppermute | solution.py:478
  245.1 5.6 %collective-permute-start.45 = (f32[9,4,128]{2,1,0:T(4,128)S(1)}, f32[9,4,128]{2,1,0:T(4,128)S(1)}, u32[]{:S(2)}, u32[]{:S(2)}) collective-permute-start(f32[9,4,128]{2,1,0:T(4,128)S(1)} %constant_dynamic-update-slice_fusion.39), channel_id=1, source_target_pairs={{1,0},{2,1},{3,2},{4,3},{5,4},{6,5},{7,6},{9,8},{10,9},{11,10},{12... | collective-permute-start | bytes 55304 | tf_op jit(solution)/shard_map/ppermute | solution.py:462
  247.1 4.6 %collective-permute-start.38 = (f32[8,128]{1,0:T(8,128)S(1)}, f32[8,128]{1,0:T(8,128)S(1)}, u32[]{:S(2)}, u32[]{:S(2)}) collective-permute-start(f32[8,128]{1,0:T(8,128)S(1)} %add.63), channel_id=1, source_target_pairs={{0,2},{1,3},{2,0},{3,1},{4,6},{5,7},{6,4},{7,5},{8,10},{9,11},{10,... | collective-permute-start | bytes 12296 | tf_op jit(solution)/shard_map/ppermute | solution.py:478
  251.7 16.6 %collective-permute-start.39 = (f32[8,128]{1,0:T(8,128)S(1)}, f32[8,128]{1,0:T(8,128)S(1)}, u32[]{:S(2)}, u32[]{:S(2)}) collective-permute-start(f32[8,128]{1,0:T(8,128)S(1)} %add.64), channel_id=1, source_target_pairs={{0,4},{1,5},{2,6},{3,7},{4,0},{5,1},{6,2},{7,3},{8,12},{9,13},{10,... | collective-permute-start | bytes 12296 | tf_op jit(solution)/shard_map/ppermute | solution.py:478

commit v3 on v2

--- a/solution.py
+++ b/solution.py
@@ -135,11 +135,19 @@
             out[at, :] = total[channel : channel + 1, :]
 
 
-def plan_kernel(pos, aux, listed, tiles, active):
-    own, own_aux = pos[13], aux[13]
+def plan_kernel(rows, fields, *refs):
+    info, own = refs[:2]
+    sources = refs[2:5]
+    if fields == 2:
+        known = ()
+        listed, tiles, evolved, given, sums, active = refs[5:]
+    else:
+        known = refs[5:6]
+        given = refs[6]
+        listed, tiles, evolved, sums, active = refs[7:]
     low, high = [], []
     for dim in range(3):
-        living = own_aux[16:20, :] > 0.0
+        living = own[28:32, :] > 0.0
         value = own[4 * dim : 4 * dim + 4, :]
         lo, hi = jnp.where(living, value, FAR), jnp.where(living, value, -FAR)
         for step in (1, 2, 4, 8, 16):
@@ -149,32 +157,48 @@
         high.append(hi)
     active[...] = jnp.zeros_like(active)
     tiles[EMPTY:ROOM] = jnp.zeros((ROOM - EMPTY, 8, LANES), jnp.float32)
-
-    def visit(number, carry):
-        sides = (lax.rem(number, 3) - 1, lax.rem(number // 3, 3) - 1, number // 9 - 1)
-        living = aux[number, 16:20, :] > 0.0
-        near_low, near_high = [], []
-        for dim in range(3):
-            moved = pos[number, 4 * dim : 4 * dim + 4, :] + sides[dim].astype(jnp.float32) * float(BRICK)
-            near_low.append(jnp.min(jnp.where(living, moved, FAR), axis=1, keepdims=True))
-            near_high.append(jnp.max(jnp.where(living, moved, -FAR), axis=1, keepdims=True))
-            scaled = moved * (1.0 / CUTOFF)
+    after_first, valid = arrivals(info, 2)
+    slots = (1, jnp.where(after_first, 2, 0), jnp.where(after_first, 0, 2))
+    for source, slot, ok in zip(sources, slots, (None,) + valid):
+
+        def visit(cell, carry, source=source, slot=slot, ok=ok):
+            number = slot * 9 + cell
+            sides = (lax.rem(cell, 3) - 1, cell // 3 - 1, slot - 1)
+            block = source[pl.ds(pl.multiple_of(cell * rows, 8), rows), :]
+            if ok is not None:
+                block = block * ok
+            if known:
+                charge = [known[0][4 * number + tile, 4:5, :] for tile in range(TILES)]
+                screen = [known[0][4 * number + tile, 3:4, :] for tile in range(TILES)]
+                living = jnp.concatenate(screen, axis=0) > 0.0
+            else:
+                charge = [block[12 + tile : 13 + tile] for tile in range(TILES)]
+                screen = [block[16 + tile : 17 + tile] for tile in range(TILES)]
+                living = block[16:20] > 0.0
+            near_low, near_high = [], []
+            for dim in range(3):
+                side = sides[dim]
+                shift = float(side * BRICK) if isinstance(side, int) else side.astype(jnp.float32) * float(BRICK)
+                moved = block[4 * dim : 4 * dim + 4] + shift
+                near_low.append(jnp.min(jnp.where(living, moved, FAR), axis=1, keepdims=True))
+                near_high.append(jnp.max(jnp.where(living, moved, -FAR), axis=1, keepdims=True))
+                scaled = moved * (1.0 / CUTOFF)
+                for tile in range(TILES):
+                    tiles[4 * number + tile, dim : dim + 1, :] = scaled[tile : tile + 1, :]
             for tile in range(TILES):
-                tiles[4 * number + tile, dim : dim + 1, :] = scaled[tile : tile + 1, :]
-        for tile in range(TILES):
-            tiles[4 * number + tile, 3:4, :] = aux[number, 16 + tile : 17 + tile, :]
-            tiles[4 * number + tile, 4:5, :] = aux[number, 12 + tile : 13 + tile, :]
-        for tile in range(TILES):
-            apart = jnp.zeros((TILES, LANES), jnp.float32)
-            for dim in range(3):
-                lo, hi = low[dim][tile : tile + 1, :], high[dim][tile : tile + 1, :]
-                gap = jnp.maximum(jnp.maximum(near_low[dim] - hi, lo - near_high[dim]), 0.0)
-                apart = apart + gap * gap
-            near = jnp.where(apart < CUTOFF * CUTOFF * 1.0001, 1.0, 0.0)
-            active[tile, pl.ds(4 * number, TILES), :] = near
-        return carry
-
-    lax.fori_loop(0, CELLS, visit, 0)
+                tiles[4 * number + tile, 3:4, :] = screen[tile]
+                tiles[4 * number + tile, 4:5, :] = charge[tile]
+            for tile in range(TILES):
+                apart = jnp.zeros((TILES, LANES), jnp.float32)
+                for dim in range(3):
+                    lo, hi = low[dim][tile : tile + 1, :], high[dim][tile : tile + 1, :]
+                    gap = jnp.maximum(jnp.maximum(near_low[dim] - hi, lo - near_high[dim]), 0.0)
+                    apart = apart + gap * gap
+                near = jnp.where(apart < CUTOFF * CUTOFF * 1.0001, 1.0, 0.0)
+                active[tile, pl.ds(4 * number, TILES), :] = near
+            return carry
+
+        lax.fori_loop(0, 9, visit, 0)
     row = lax.broadcasted_iota(jnp.int32, (LANES, LANES), 0)
     lane = lax.broadcasted_iota(jnp.int32, (LANES, LANES), 1)
     before = jnp.where(lane < row, 1.0, 0.0).astype(jnp.bfloat16)
@@ -191,9 +215,100 @@
             entry = jnp.where(spot < total, entry, EMPTY)
             block = tile * (LANES // BLOCK) + part
             listed[block : block + 1, :] = jnp.where(spot == LANES - 1, total, entry)
-
-
-def born_kernel(listed, tiles, own, out, col, acc):
+    lane = lax.broadcasted_iota(jnp.int32, (8, LANES), 1)
+    sub = lane & (WIDE - 1)
+    own_points = (lane >= WIDE) & (lane < 3 * WIDE) & (sub >= PAD) & (sub < PAD + BRICK)
+    squares = jnp.zeros((8, LANES), jnp.float32)
+    cross = squares
+    target = squares
+    adds = shift_masks(info, 2)
+    for plane in range(PLANES):
+        at = slice(9 * rows + 8 * plane, 9 * rows + 8 * plane + 8)
+        value = received(2, adds, sources, at)
+        evolved[plane] = value
+        if fields == 2:
+            at = slice(9 * rows + 8 * (PLANES + plane), 9 * rows + 8 * (PLANES + plane) + 8)
+            given[plane] = received(2, adds, sources, at)
+        if 5 <= plane < 5 + BRICK:
+            value = jnp.where(own_points, value, 0.0)
+            wanted = jnp.where(own_points, given[plane], 0.0)
+            squares = squares + value * value
+            cross = cross + value * wanted
+            target = target + wanted * wanted
+    sums[...] = jnp.zeros_like(sums)
+    sums[0:1, :] = jnp.sum(squares, axis=0, keepdims=True)
+    sums[1:2, :] = jnp.sum(cross, axis=0, keepdims=True)
+    sums[2:3, :] = jnp.sum(target, axis=0, keepdims=True)
+
+
+def arrivals(info, axis):
+    after_first = info[6 + 2 * axis] == 0
+    return after_first, (1.0, jnp.where(info[7 + 2 * axis] > 0, 1.0, 0.0))
+
+
+def shift_masks(info, axis):
+    lane = lax.broadcasted_iota(jnp.int32, (8, LANES), 1)
+    upper = (lane >= 64) if axis == 1 else ((lane & (WIDE - 1)) >= BRICK)
+    after_first, valid = arrivals(info, axis)
+    after_one = jnp.where(after_first, 1.0, 0.0)
+    masks = []
+    for after, ok in zip((after_one, 1.0 - after_one), valid):
+        masks.append((jnp.where(upper, after * ok, 0.0), jnp.where(upper, 0.0, (1.0 - after) * ok)))
+    return masks
+
+
+def received(axis, masks, sources, at):
+    value = sources[0][at, :]
+    for (from_after, from_before), source in zip(masks, sources[1:]):
+        other = source[at, :]
+        if axis == 1:
+            value = value + pltpu.roll(other, 64, 1) * (from_after + from_before)
+        else:
+            value = value + pltpu.roll(other, BRICK, 1) * from_after
+            value = value + pltpu.roll(other, LANES - BRICK, 1) * from_before
+    return value
+
+
+def merge_kernel(axis, count, rows, fields, info, mine, first, second, out):
+    after_first, valid = arrivals(info, axis)
+    span = count * rows
+    out[span : 2 * span, :] = mine[0:span, :]
+    slots = (jnp.where(after_first, 2 * span, 0), jnp.where(after_first, 0, 2 * span))
+    for source, slot, ok in zip((first, second), slots, valid):
+        out[pl.ds(pl.multiple_of(slot, 8), span), :] = source[0:span, :] * ok
+    if axis == 0:
+        for field in range(fields):
+            base = 3 * span + field * 8 * PLANES
+            mine_base = span + field * 8 * PLANES
+            out[base : base + 8 * PLANES, :] = mine[mine_base : mine_base + 8 * PLANES, :]
+            for source, slot, ok in zip((first, second), slots, valid):
+                to = pl.multiple_of(jnp.where(slot > 0, 8 * BRICK, 0), 8)
+                into = pl.ds(pl.multiple_of(base + to, 8), 80)
+                off = pl.ds(pl.multiple_of(mine_base + 8 * BRICK - to, 8), 80)
+                out[into, :] = out[into, :] + source[off, :] * ok
+        return
+    masks = shift_masks(info, axis)
+    for plane in range(PLANES * fields):
+        at = slice(span + 8 * plane, span + 8 * plane + 8)
+        out[3 * span + 8 * plane : 3 * span + 8 * plane + 8, :] = received(axis, masks, (mine, first, second), at)
+
+
+def radius_merge_kernel(axis, count, extra, info, mine, first, second, *refs):
+    others, out = refs[:extra], refs[extra]
+    after_first, valid = arrivals(info, axis)
+    span = count * TILES
+    out[span : 2 * span, :] = mine[0:span, :]
+    slots = (jnp.where(after_first, 2 * span, 0), jnp.where(after_first, 0, 2 * span))
+    for source, slot in zip((first, second), slots):
+        out[pl.ds(pl.multiple_of(slot, 8), span), :] = source[0:span, :]
+    total = mine[span : span + 8, :] + first[span : span + 8, :]
+    for other in others:
+        total = total + other[...]
+    out[3 * span : 3 * span + 8, :] = total
+
+
+def born_kernel(listed, tiles, own, sums, out, col, acc):
+    out[TILES : TILES + 8, :] = sums[...]
     for channel in range(3):
         for tile in range(TILES):
             row = own[4 * channel + tile : 4 * channel + tile + 1, :] * (1.0 / CUTOFF)
@@ -225,7 +340,7 @@
         out[tile : tile + 1, :] = own[24 + tile : 25 + tile, :] + total
 
 
-def gb_kernel(listed, tiles, own, own_radius, radii, out, col, acc, rows):
+def gb_kernel(info, listed, tiles, own, own_radius, mine, first, second, out, col, acc, rows):
     for tile in range(TILES):
         at = slice(tile * LANES, (tile + 1) * LANES)
         for channel in range(3):
@@ -236,15 +351,15 @@
         col[4, at, :] = -0.5 / radius
     rows[EMPTY:ROOM] = jnp.ones((ROOM - EMPTY, 2, LANES), jnp.float32)
 
-    def ready(number, carry):
-        radius = jnp.maximum(radii[number], 0.5) * (1.0 / CUTOFF)
-        half = 0.5 / radius
-        for tile in range(TILES):
-            rows[4 * number + tile, 0:1, :] = radius[tile : tile + 1, :]
-            rows[4 * number + tile, 1:2, :] = half[tile : tile + 1, :]
-        return carry
-
-    lax.fori_loop(0, CELLS, ready, 0)
+    after_first, _ = arrivals(info, 2)
+    slots = (1, jnp.where(after_first, 2, 0), jnp.where(after_first, 0, 2))
+    for source, slot in zip((mine, first, second), slots):
+        for cell in range(9):
+            radius = source[TILES * cell : TILES * cell + TILES, :] * (1.0 / CUTOFF)
+            half = 0.5 / radius
+            for tile in range(TILES):
+                rows[slot * 36 + 4 * cell + tile, 0:1, :] = radius[tile : tile + 1, :]
+                rows[slot * 36 + 4 * cell + tile, 1:2, :] = half[tile : tile + 1, :]
 
     def block(ib, carry):
         at = pl.ds(pl.multiple_of(ib * BLOCK, BLOCK), BLOCK)
@@ -320,87 +435,40 @@
     return high, (values - high.astype(jnp.float32)).astype(jnp.bfloat16)
 
 
-def evolve_kernel(bounds, pos, aux, exp_ext, out, sums, px, left_hi, left_lo, right):
-    out[...] = jnp.zeros_like(out)
-
-    def splat(number, wide_x, wide_y):
-        side_x = lax.rem(number, 3) - 1
-        side_y = lax.rem(number // 3, 3) - 1
-        side_z = number // 9 - 1
-        if wide_x:
-            side_x, base_x, rows_x, planes, first = 0, -PAD, WIDE, PLANES, 0
-        else:
-            base_x, rows_x, planes = side_x * 8, BRICK, 10
-            base_x = jnp.where(side_x < 0, -PAD, PAD)
-            first = jnp.where(side_x < 0, 0, BRICK)
-        if wide_y:
-            side_y, base_y, rows_y, start = 0, -PAD, WIDE, 0
-        else:
-            base_y, rows_y = jnp.where(side_y < 0, -PAD, PAD), BRICK
-            start = pl.multiple_of(jnp.where(side_y < 0, 0, BRICK), BRICK)
-        for tile in range(TILES):
-            lanes = slice(tile * LANES, (tile + 1) * LANES)
-            z = profiles(pos[number, 8 + tile : 9 + tile, :], side_z, -PAD, WIDE, bounds[4], bounds[5], False)
-            z_hi, z_lo = split(z)
-            right[0:WIDE, lanes] = z_hi
-            right[WIDE : 2 * WIDE, lanes] = z_lo
-            x = profiles(pos[number, tile : tile + 1, :], side_x, base_x, rows_x, bounds[0], bounds[1], False)
-            px[0:rows_x, :] = x * aux[number, 20 + tile : 21 + tile, :]
-            y = profiles(pos[number, 4 + tile : 5 + tile, :], side_y, base_y, rows_y, bounds[2], bounds[3], False)
-            for plane in range(planes):
-                rows = slice(plane * rows_y, (plane + 1) * rows_y)
-                hi, lo = split(px[plane + 3 : plane + 4, :] * y)
-                left_hi[rows, lanes] = hi
-                left_lo[rows, lanes] = lo
-        weights = right[...]
-        dims = (((1,), (1,)), ((), ()))
-        total = planes * rows_y
-        placed = lax.dot_general(left_hi[0:total, :], weights, dims, preferred_element_type=jnp.float32)
-        placed = placed + lax.dot_general(left_lo[0:total, :], weights, dims, preferred_element_type=jnp.float32)
-        placed = placed.reshape(planes, rows_y, 2 * WIDE)
-        at = pl.ds(first, planes)
-        out[at, pl.ds(start, rows_y), 0 : 2 * WIDE] = out[at, pl.ds(start, rows_y), 0 : 2 * WIDE] + placed
-
-    def both(k, carry):
-        splat(9 * k + 4, True, True)
-        return carry
-
-    def only_x(k, carry):
-        splat(9 * (k // 2) + 1 + 6 * lax.rem(k, 2), True, False)
-        return carry
-
-    def only_y(k, carry):
-        splat(9 * (k // 2) + 3 + 2 * lax.rem(k, 2), False, True)
-        return carry
-
-    def neither(k, carry):
-        splat(9 * (k // 4) + 2 * lax.rem(k, 2) + 6 * lax.rem(k // 2, 2), False, False)
-        return carry
-
-    lax.fori_loop(0, 3, both, 0)
-    lax.fori_loop(0, 6, only_x, 0)
-    lax.fori_loop(0, 6, only_y, 0)
-    lax.fori_loop(0, 12, neither, 0)
-    lane = lax.broadcasted_iota(jnp.int32, (WIDE, LANES), 1)
-    row = lax.broadcasted_iota(jnp.int32, (WIDE, LANES), 0)
-    own = (lane >= PAD) & (lane < PAD + BRICK) & (row >= PAD) & (row < PAD + BRICK)
-    squares = jnp.zeros((WIDE, LANES), jnp.float32)
-    cross = squares
-    target = squares
+def splat_kernel(fields, rows, bounds, own, *refs):
+    if fields == 2:
+        given = refs[0]
+    out, px, left_hi, left_lo, right = refs[fields - 1 :]
+    out[0:rows, :] = own[0:rows, :]
+    for tile in range(TILES):
+        lanes = slice(tile * LANES, (tile + 1) * LANES)
+        z = profiles(own[8 + tile : 9 + tile, :], 0, -PAD, WIDE, bounds[4], bounds[5], False)
+        z_hi, z_lo = split(z)
+        right[0:WIDE, lanes] = z_hi
+        right[WIDE : 2 * WIDE, lanes] = z_lo
+        x = profiles(own[tile : tile + 1, :], 0, -PAD, WIDE, bounds[0], bounds[1], False)
+        px[...] = x * own[20 + tile : 21 + tile, :]
+        y = profiles(own[4 + tile : 5 + tile, :], 0, -PAD, WIDE, bounds[2], bounds[3], False)
+        for plane in range(PLANES):
+            at = slice(plane * WIDE, (plane + 1) * WIDE)
+            hi, lo = split(px[plane + 3 : plane + 4, :] * y)
+            left_hi[at, lanes] = hi
+            left_lo[at, lanes] = lo
+    weights = right[...]
+    dims = (((1,), (1,)), ((), ()))
+    placed = lax.dot_general(left_hi[...], weights, dims, preferred_element_type=jnp.float32)
+    placed = placed + lax.dot_general(left_lo[...], weights, dims, preferred_element_type=jnp.float32)
+    placed = placed[:, 0:WIDE] + placed[:, WIDE : 2 * WIDE]
+    placed = placed.reshape(PLANES, 4, 8, WIDE)
     for plane in range(PLANES):
-        raw = out[plane]
-        value = jnp.where(lane < WIDE, raw + pltpu.roll(raw, LANES - WIDE, 1), 0.0)
-        out[plane] = value
-        if 5 <= plane < 5 + BRICK:
-            value = jnp.where(own, value, 0.0)
-            given = jnp.where(own, exp_ext[plane], 0.0)
-            squares = squares + value * value
-            cross = cross + value * given
-            target = target + given * given
-    sums[...] = jnp.zeros_like(sums)
-    sums[0:1, :] = jnp.sum(squares, axis=0, keepdims=True)
-    sums[1:2, :] = jnp.sum(cross, axis=0, keepdims=True)
-    sums[2:3, :] = jnp.sum(target, axis=0, keepdims=True)
+        parts = [placed[plane, k] for k in range(4)]
+        out[rows + 8 * plane : rows + 8 * plane + 8, :] = jnp.concatenate(parts, axis=1)
+    if fields == 2:
+        base = rows + 8 * PLANES
+        out[base : base + 8 * PLANES, :] = jnp.zeros((8 * PLANES, LANES), jnp.float32)
+        for plane in range(BRICK):
+            value = pltpu.roll(given[plane, 0:8, :], WIDE + PAD, 1) + pltpu.roll(given[plane, 8:16, :], 2 * WIDE + PAD, 1)
+            out[base + 8 * (plane + 5) : base + 8 * (plane + 6), :] = value
 
 
 def fit_kernel(scale, parts, bounds, *refs):
@@ -415,10 +483,14 @@
     model_part = (cross / norm) / (squares + EPSILON)
     for plane in range(PLANES):
         s = exp_ext[plane] * given_part - evolved[plane] * model_part
+        blocks = [s] + [pltpu.roll(s, LANES - WIDE * k, 1) for k in (1, 2, 3)]
+        s = jnp.concatenate(blocks, axis=0)
+        s = jnp.where(lax.broadcasted_iota(jnp.int32, (WIDE, LANES), 1) < WIDE, s, 0.0)
         hi = s.astype(jnp.bfloat16).astype(jnp.float32)
         lo = (s - hi).astype(jnp.bfloat16).astype(jnp.float32)
         packed = hi + pltpu.roll(lo, WIDE, 1) + pltpu.roll(hi, 2 * WIDE, 1)
         left[plane * WIDE : (plane + 1) * WIDE, :] = packed.astype(jnp.bfloat16)
+    moved[3 * TILES :, :] = own[3 * TILES :, :]
     right[...] = jnp.zeros_like(right)
     for tile in range(TILES):
         z, zs = profiles(own[8 + tile : 9 + tile, :], 0, -PAD, WIDE, bounds[4], bounds[5], True)
@@ -456,58 +528,36 @@
             moved[at, :] = own[at, :] + STEP_SIZE * (own[28 + tile : 29 + tile, :] * total)
 
 
-def shifted(block, axis, step):
+def partners(axis):
     count = lax.axis_size(axis)
-    pairs = [(i, i + step) for i in range(count) if 0 <= i + step < count]
-    return lax.ppermute(block, axis, pairs)
+    even = [(i, i ^ 1) for i in range(count)]
+    odd = [(i, (i + 1 if i % 2 else i - 1) % count) for i in range(count)]
+    return even, odd
 
 
 def both_sides(block, axis):
-    return shifted(block, axis, 1), shifted(block, axis, -1)
-
-
-def total_over_devices(values):
-    for axis in AXES:
-        count = lax.axis_size(axis)
-        if count & (count - 1):
-            values = lax.psum(values, axis)
-            continue
-        step = 1
-        while step < count:
-            pairs = [(i, i ^ step) for i in range(count)]
-            values = values + lax.ppermute(values, axis, pairs)
-            step *= 2
-    return values
-
-
-def widened(field, width):
-    for dim, axis in enumerate(AXES):
-        size = field.shape[dim]
-        head = lax.slice_in_dim(field, 0, width, axis=dim)
-        tail = lax.slice_in_dim(field, size - width, size, axis=dim)
-        field = jnp.concatenate([shifted(tail, axis, 1), field, shifted(head, axis, -1)], axis=dim)
-    return field
+    even, odd = partners(axis)
+    return lax.ppermute(block, axis, even), lax.ppermute(block, axis, odd)
+
+
+def across(block, axis, flip):
+    return lax.ppermute(block, axis, [(i, i ^ flip) for i in range(lax.axis_size(axis))])
 
 
 def f32(*shape):
     return jax.ShapeDtypeStruct(shape, jnp.float32)
-
-
-def gathered(block):
-    line = jnp.stack([*(shifted(block, "gx", 1)[None]), block, *(shifted(block, "gx", -1)[None])])
-    before_y, after_y = both_sides(line, "gy")
-    plane = jnp.concatenate([before_y, line, after_y])
-    before_z, after_z = both_sides(plane, "gz")
-    return line, (before_y, after_y), plane, (before_z, after_z)
 
 
 def on_device(positions, charges, atom_types, type_table, live_count, exp_map):
     sizes = [lax.axis_size(axis) for axis in AXES]
     places = [lax.axis_index(axis) for axis in AXES]
-    bounds = []
+    info = []
     for size, place in zip(sizes, places):
-        bounds += [-place * BRICK, (size - place) * BRICK]
-    bounds = jnp.stack(bounds).astype(jnp.int32)
+        info += [-place * BRICK, (size - place) * BRICK]
+    for size, place in zip(sizes, places):
+        odd = place % 2
+        info += [odd, jnp.where(odd == 0, place > 0, place < size - 1).astype(jnp.int32)]
+    info = jnp.stack(info).astype(jnp.int32)
     scale = FIT_GAIN * float(BRICK**3 * sizes[0] * sizes[1] * sizes[2])
 
     atoms, order = call(
@@ -524,53 +574,15 @@
         charges.reshape(TILES, LANES),
         atom_types.reshape(TILES, LANES),
     )
-
-    exp_wide = widened(exp_map, BLUR_REACH + SPLAT_MARGIN)
-    exp_ext = jnp.pad(exp_wide, ((0, 0), (3, 3), (3, LANES - PLANES - 3)))
-
-    fixed = None
-    moved = atoms
+    given = jnp.pad(exp_map, ((0, 0), (0, 0), (0, LANES - BRICK)))
+    own = atoms
     for step in range(STEPS):
-        line, sides_y, plane, sides_z = gathered(moved[:24] if step == 0 else moved)
-        every = jnp.concatenate([sides_z[0], plane, sides_z[1]])
-        if fixed is None:
-            fixed = every
-        listed, tiles = call(
-            plan_kernel,
-            (jax.ShapeDtypeStruct((BLOCKS, LANES), jnp.int32), f32(ROOM, 8, LANES)),
-            1 << 22,
-            scratch=[pltpu.VMEM((TILES, LANES, LANES), jnp.float32)],
-            n_in=2,
-        )(every, fixed)
-        own = atoms if step == 0 else jnp.concatenate([moved, atoms[12:]])
-        radius = call(
-            born_kernel,
-            f32(TILES, LANES),
-            1 << 27,
-            scratch=[pltpu.VMEM((3, SLOTS, LANES), jnp.float32), pltpu.VMEM((SLOTS, LANES), jnp.float32)],
-            smem=1,
-            n_in=3,
-        )(listed, tiles, own)
-        near = gathered(radius)
-        radii = jnp.concatenate([near[3][0], near[2], near[3][1]])
-        pairs = [
-            call(
-                gb_kernel,
-                f32(3 * TILES, LANES),
-                1 << 28,
-                scratch=[
-                    pltpu.VMEM((5, SLOTS, LANES), jnp.float32),
-                    pltpu.VMEM((3, SLOTS, LANES), jnp.float32),
-                    pltpu.VMEM((ROOM, 2, LANES), jnp.float32),
-                ],
-                smem=1,
-                n_in=5,
-            )(listed, tiles, own, radius, radii)
-        ]
-        evolved, sums = call(
-            evolve_kernel,
-            (f32(PLANES, WIDE, LANES), f32(8, LANES)),
-            1 << 33,
+        fields, rows = (2, 24) if step == 0 else (1, 16)
+        planes = 8 * PLANES * fields
+        message = call(
+            functools.partial(splat_kernel, fields, rows),
+            f32(rows + planes, LANES),
+            1 << 26,
             scratch=[
                 pltpu.VMEM((WIDE, LANES), jnp.float32),
                 pltpu.VMEM((PLANES * WIDE, SLOTS), jnp.bfloat16),
@@ -578,13 +590,79 @@
                 pltpu.VMEM((2 * WIDE, SLOTS), jnp.bfloat16),
             ],
             smem=1,
+            n_in=1 + fields,
+        )(*((info, own, given) if step == 0 else (info, own)))
+        for number, axis in enumerate(AXES[:2]):
+            count = 3**number
+            message = call(
+                functools.partial(merge_kernel, number, count, rows, fields),
+                f32(3 * count * rows + planes, LANES),
+                1 << 20,
+                smem=1,
+                n_in=4,
+            )(info, message, *both_sides(message, axis))
+        before = () if step == 0 else (tiles, exp_ext)
+        planned = call(
+            functools.partial(plan_kernel, rows, fields),
+            (jax.ShapeDtypeStruct((BLOCKS, LANES), jnp.int32), f32(ROOM, 8, LANES))
+            + (f32(PLANES, 8, LANES),) * fields
+            + (f32(8, LANES),),
+            1 << 22,
+            scratch=[pltpu.VMEM((TILES, LANES, LANES), jnp.float32)],
+            smem=1,
+            n_in=5 + len(before),
+        )(info, own, message, *both_sides(message, AXES[2]), *before)
+        if step == 0:
+            listed, tiles, evolved, exp_ext, sums = planned
+        else:
+            listed, tiles, evolved, sums = planned
+        if sizes[0] >= 4:
+            sums = sums + across(sums, AXES[0], 2)
+        radius = call(
+            born_kernel,
+            f32(TILES + 8, LANES),
+            1 << 27,
+            scratch=[pltpu.VMEM((3, SLOTS, LANES), jnp.float32), pltpu.VMEM((SLOTS, LANES), jnp.float32)],
+            smem=1,
             n_in=4,
-        )(bounds, every, fixed, exp_ext)
-        sums = total_over_devices(sums)
-        moved, force = call(
-            functools.partial(fit_kernel, scale, len(pairs)),
-            (f32(3 * TILES, LANES), f32(3 * TILES, LANES)),
-            1 << 30,
+        )(listed, tiles, own, sums)
+        line = radius
+        for number, axis in enumerate(AXES):
+            count = 3**number
+            span = count * TILES
+            flips = (2, 3) if number and sizes[number] >= 4 else ()
+            here = line[span:]
+            others = [across(here, axis, flip) for flip in flips]
+            near = both_sides(line, axis)
+            if number == 2:
+                sums = here + near[0][span:]
+                for other in others:
+                    sums = sums + other
+                break
+            line = call(
+                functools.partial(radius_merge_kernel, number, count, len(others)),
+                f32(3 * span + 8, LANES),
+                1 << 20,
+                smem=1,
+                n_in=4 + len(others),
+            )(info, line, *near, *others)
+        pair = call(
+            gb_kernel,
+            f32(3 * TILES, LANES),
+            1 << 28,
+            scratch=[
+                pltpu.VMEM((5, SLOTS, LANES), jnp.float32),
+                pltpu.VMEM((3, SLOTS, LANES), jnp.float32),
+                pltpu.VMEM((ROOM, 2, LANES), jnp.float32),
+            ],
+            smem=2,
+            n_in=8,
+        )(info, listed, tiles, own, radius, line, *near)
+        sums = finished(sums, sizes)
+        own, force = call(
+            functools.partial(fit_kernel, scale, 1),
+            (f32(32, LANES), f32(3 * TILES, LANES)),
+            1 << 26,
             scratch=[
                 pltpu.VMEM((PLANES * WIDE, LANES), jnp.bfloat16),
                 pltpu.VMEM((LANES, 2 * LANES), jnp.bfloat16),
@@ -593,18 +671,40 @@
                 pltpu.VMEM((WIDE, LANES), jnp.float32),
             ],
             smem=1,
-            n_in=5 + len(pairs),
-        )(bounds, own, evolved, exp_ext, sums, *pairs)
+            n_in=6,
+        )(info, own, evolved, exp_ext, sums, pair)
     results = call(
         restore_kernel,
         f32(6 * TILES, LANES),
         1 << 20,
         scratch=[pltpu.VMEM((24, LANES), jnp.float32)],
         n_in=4,
-    )(order, moved, atoms, force)
-    own = evolved[5 : 5 + BRICK, PAD : PAD + BRICK, PAD : PAD + BRICK]
+    )(order, own, atoms, force)
+    model = evolved[5 : 5 + BRICK].reshape(BRICK, 8, 4, WIDE).transpose(0, 2, 1, 3).reshape(BRICK, WIDE, WIDE)
+    model = model[:, PAD : PAD + BRICK, PAD : PAD + BRICK]
     results = results.reshape((2,) + positions.shape)
-    return results[0], results[1], own
+    return results[0], results[1], model
+
+
+def finished(sums, sizes):
+    assert sizes[0] in (2, 4) and all(size in (2, 4, 8) for size in sizes)
+    far = [axis for axis, size in zip(AXES, sizes) if size == 8]
+    if not far:
+        return sums
+    counts = [lax.axis_size(axis) for axis in far]
+    total = sums
+    for choice in range(1, 1 << len(far)):
+        flips = [4 if choice >> k & 1 else 0 for k in range(len(far))]
+        pairs = []
+        for source in range(math.prod(counts)):
+            target, rest, unit = 0, source, 1
+            for count, flip in reversed(list(zip(counts, flips))):
+                target += (rest % count ^ flip) * unit
+                rest //= count
+                unit *= count
+            pairs.append((source, target))
+        total = total + lax.ppermute(sums, tuple(far), pairs)
+    return total
 
 
 def solution(mesh):

time: 273 us -> 187 us (0.68)
  starting transfers between devices: 129 us -> 57.5 us
  Pallas kernels: 85.3 us -> 64.4 us
  waiting for transfers between devices: 50.4 us -> 59.4 us
    ppermute x46 -> x40, starting transfers between devices: 129 us -> 57.5 us  [the longest x24 24.6 us: both_sides(): return (lax.ppermute(block, axis, even), lax.ppermute(block, axis, odd))]
    pallas_call x8 -> x16, Pallas kernels: 59.2 us -> 36.3 us  [the longest x2 15.4 us: on_device(): call(born_kernel, f32(TILES + 8, LANES), 1 << 27, scratch=[pltpu.VMEM((3,...]
    ppermute x46 -> x40, waiting for transfers between devices: 50.4 us -> 59.4 us  [the longest x24 44.5 us: both_sides(): return (lax.ppermute(block, axis, even), lax.ppermute(block, axis, odd))]
  transfers between devices with their start and end apart: 46 -> 40, of which waited for: 18 -> 19; matrix products, arithmetic and copies ran while one was open for 1% -> 1% of each run, Pallas kernels for 26% -> 14%
where the time goes in v3:
time: 187 us
  Pallas kernels  64.4 us (34%)
  waiting for transfers between devices  59.4 us (32%)
  starting transfers between devices  57.5 us (31%)
  local copies, waits for them, and re-layouts  2.98 us (2%)
    ppermute x24, waiting for transfers between devices, both_sides(): return (lax.ppermute(block, axis, even), lax.ppermute(block, axis, odd))  44.5 us
    pallas_call x2, Pallas kernels, on_device(): call(gb_kernel, f32(3 * TILES, LANES), 1 << 28, scratch=[pltpu.VMEM((5, S...  26 us
    ppermute x24, starting transfers between devices, both_sides(): return (lax.ppermute(block, axis, even), lax.ppermute(block, axis, odd))  24.6 us
    ppermute x10, starting transfers between devices, across(): lax.ppermute(block, axis, [(i, i ^ flip) for i in range(lax.axis_size(axi...  17.9 us
    pallas_call x2, Pallas kernels, on_device(): call(born_kernel, f32(TILES + 8, LANES), 1 << 27, scratch=[pltpu.VMEM((3,...  15.4 us
    ppermute x6, starting transfers between devices, finished(): total = total + lax.ppermute(sums, tuple(far), pairs)  15 us
    ppermute x10, waiting for transfers between devices, across(): lax.ppermute(block, axis, [(i, i ^ flip) for i in range(lax.axis_size(axi...  14.8 us
    pallas_call x2, Pallas kernels, on_device(): call(functools.partial(plan_kernel, rows, fields), (jax.ShapeDtypeStruct(...  9.07 us
  transfers between devices with their start and end apart: 40, of which 19 were waited for; matrix products, arithmetic and copies ran while one was open for 1% of the time, Pallas kernels for 14%

profile of v3, /device:TPU:56, one launch (start us, length us, event | category | flops | bytes accessed | tf_op | source)
XLA Modules:
  0.0 186.7 jit_solution(11974083254840870450)
XLA Ops:
  1.3 0.7 reduce
  2.1 0.6 copy-done.1
  2.8 1.8 shard_map.85
  4.7 1.5 shard_map.86.mine
  6.2 0.8 collective-permute-start.1
  7.0 0.7 collective-permute-start
  7.6 8.0 %collective-permute-done.1.second = f32[440,128]{1,0:T(8,128)S(1)} collective-permute-done((f32[440,128]{1,0:T(8,128)S(1)}, f32[440,128]{1,0:T(8,128)S(1)}, u32[]{:S(2)}, u32[]{:S(2)}) %collective-permute-start.1) | collective-permute-done | bytes 225312 | tf_op jit(solution)/shard_map/ppermute | solution.py:540
  15.6 0.6 shard_map.87.mine
  16.2 3.0 %collective-permute-start.3 = (f32[488,128]{1,0:T(8,128)S(1)}, f32[488,128]{1,0:T(8,128)S(1)}, u32[]{:S(2)}, u32[]{:S(2)}) collective-permute-start(f32[488,128]{1,0:T(8,128)S(1)} %shard_map.87.mine), channel_id=1, source_target_pairs={{0,56},{8,16},{16,8},{24,32},{32,24},{40,48},{48,40},{56,0},{1,57}... | collective-permute-start | bytes 749576 | tf_op jit(solution)/shard_map/ppermute | solution.py:540
  19.3 7.2 %collective-permute-done.3.second = f32[488,128]{1,0:T(8,128)S(1)} collective-permute-done((f32[488,128]{1,0:T(8,128)S(1)}, f32[488,128]{1,0:T(8,128)S(1)}, u32[]{:S(2)}, u32[]{:S(2)}) %collective-permute-start.3) | collective-permute-done | bytes 249888 | tf_op jit(solution)/shard_map/ppermute | solution.py:540
  27.0 0.7 shard_map.88.refs_2_
  27.7 2.0 %collective-permute-start.5 = (f32[632,128]{1,0:T(8,128)S(1)}, f32[632,128]{1,0:T(8,128)S(1)}, u32[]{:S(2)}, u32[]{:S(2)}) collective-permute-start(f32[632,128]{1,0:T(8,128)S(1)} %shard_map.88.refs_2_), channel_id=1, source_target_pairs={{0,7},{1,2},{2,1},{3,4},{4,3},{5,6},{6,5},{7,0},{8,15},{9,10},{10,... | collective-permute-start | bytes 970760 | tf_op jit(solution)/shard_map/ppermute | solution.py:540
  29.7 4.0 %collective-permute-start.4 = (f32[632,128]{1,0:T(8,128)S(1)}, f32[632,128]{1,0:T(8,128)S(1)}, u32[]{:S(2)}, u32[]{:S(2)}) collective-permute-start(f32[632,128]{1,0:T(8,128)S(1)} %shard_map.88.refs_2_), channel_id=1, source_target_pairs={{0,1},{1,0},{2,3},{3,2},{4,5},{5,4},{6,7},{7,6},{8,9},{9,8},{10,11... | collective-permute-start | bytes 970760 | tf_op jit(solution)/shard_map/ppermute | solution.py:540
  33.8 2.7 %collective-permute-done.5.refs_4_ = f32[632,128]{1,0:T(8,128)S(1)} collective-permute-done((f32[632,128]{1,0:T(8,128)S(1)}, f32[632,128]{1,0:T(8,128)S(1)}, u32[]{:S(2)}, u32[]{:S(2)}) %collective-permute-start.5) | collective-permute-done | bytes 323616 | tf_op jit(solution)/shard_map/ppermute | solution.py:540
  36.5 3.8 %collective-permute-done.4.refs_3_ = f32[632,128]{1,0:T(8,128)S(1)} collective-permute-done((f32[632,128]{1,0:T(8,128)S(1)}, f32[632,128]{1,0:T(8,128)S(1)}, u32[]{:S(2)}, u32[]{:S(2)}) %collective-permute-start.4) | collective-permute-done | bytes 323616 | tf_op jit(solution)/shard_map/ppermute | solution.py:540
  40.2 4.6 %shard_map.89 = (s32[16,128]{1,0:T(8,128)S(1)}, f32[112,8,128]{2,1,0:T(8,128)S(1)}, f32[26,8,128]{2,1,0:T(8,128)S(1)}, f32[26,8,128]{2,1,0:T(8,128)S(1)}, f32[8,128]{1,0:T(8,128)S(1)}) custom-call(s32[12]{0:T(128)S(1)} %stack.63.bounds.info.refs_0_, f32[32,128]{1,0:T(8,128)S(1)} %get-tuple-element.18.own.refs_1_.refs_0_.start, ...), custom_call_target="tpu_custom_call" | custom-call | flops 4194304 | bytes 262144 | tf_op jit(solution)/shard_map/pallas_call | solution.py:605
  44.8 1.1 collective-permute-start.6
  45.9 4.1 %collective-permute-done.6 = f32[8,128]{1,0:T(8,128)S(1)} collective-permute-done((f32[8,128]{1,0:T(8,128)S(1)}, f32[8,128]{1,0:T(8,128)S(1)}, u32[]{:S(2)}, u32[]{:S(2)}) %collective-permute-start.6) | collective-permute-done | bytes 4128 | tf_op jit(solution)/shard_map/ppermute | solution.py:544
  50.0 7.6 %shard_map.90.mine.own_radius = f32[12,128]{1,0:T(8,128)S(1)} custom-call(s32[16,128]{1,0:T(8,128)S(1)} %get-tuple-element.21.listed, f32[112,8,128]{2,1,0:T(8,128)S(1)} %get-tuple-element.22.tiles.refs_5_, f32[32,128]{1,0:T(8,128)S(1)} %get-tuple-element.18.own.refs_1_.refs_0_.start, f32[8,128]{1,0:T(8,128)S(1)} %add.57.sums), custom_call_target="tpu_custom_call" | custom-call | flops 134217728 | bytes 262144 | tf_op jit(solution)/shard_map/pallas_call | solution.py:621
  57.9 4.5 %collective-permute-done.8.second = f32[12,128]{1,0:T(8,128)S(1)} collective-permute-done((f32[12,128]{1,0:T(8,128)S(1)}, f32[12,128]{1,0:T(8,128)S(1)}, u32[]{:S(2)}, u32[]{:S(2)}) %collective-permute-start.8) | collective-permute-done | bytes 6176 | tf_op jit(solution)/shard_map/ppermute | solution.py:540
  62.9 2.5 %collective-permute-start.10 = (f32[20,128]{1,0:T(8,128)S(1)}, f32[20,128]{1,0:T(8,128)S(1)}, u32[]{:S(2)}, u32[]{:S(2)}) collective-permute-start(f32[20,128]{1,0:T(8,128)S(1)} %shard_map.91.mine), channel_id=1, source_target_pairs={{0,56},{8,16},{16,8},{24,32},{32,24},{40,48},{48,40},{56,0},{1,57}... | collective-permute-start | bytes 30728 | tf_op jit(solution)/shard_map/ppermute | solution.py:540
  65.8 3.7 %collective-permute-start.11 = (f32[8,128]{1,0:T(8,128)S(1)}, f32[8,128]{1,0:T(8,128)S(1)}, u32[]{:S(2)}, u32[]{:S(2)}) collective-permute-start(f32[8,128]{1,0:T(8,128)S(1)} %slice.42), channel_id=1, source_target_pairs={{0,16},{8,24},{16,0},{24,8},{32,48},{40,56},{48,32},{56,40},{1,17}... | collective-permute-start | bytes 12296 | tf_op jit(solution)/shard_map/ppermute | solution.py:544
  69.5 0.7 collective-permute-done.12.refs_1_
  70.2 0.9 collective-permute-done.11.refs_0_
  71.1 0.5 shard_map.92.mine
  72.1 2.5 %collective-permute-start.14 = (f32[8,128]{1,0:T(8,128)S(1)}, f32[8,128]{1,0:T(8,128)S(1)}, u32[]{:S(2)}, u32[]{:S(2)}) collective-permute-start(f32[8,128]{1,0:T(8,128)S(1)} %slice.43), channel_id=1, source_target_pairs={{0,2},{1,3},{2,0},{3,1},{4,6},{5,7},{6,4},{7,5},{8,10},{9,11},{10,... | collective-permute-start | bytes 12296 | tf_op jit(solution)/shard_map/ppermute | solution.py:544
  75.2 1.5 collective-permute-start.19
  76.7 1.6 collective-permute-done.15
  78.3 4.4 %collective-permute-start.18 = (f32[8,128]{1,0:T(8,128)S(1)}, f32[8,128]{1,0:T(8,128)S(1)}, u32[]{:S(2)}, u32[]{:S(2)}) collective-permute-start(f32[8,128]{1,0:T(8,128)S(1)} %fusion.3), channel_id=1, source_target_pairs={{0,36},{1,37},{2,38},{3,39},{4,32},{5,33},{6,34},{7,35},{8,44},{9,... | collective-permute-start | bytes 12296 | tf_op jit(solution)/shard_map/ppermute | solution.py:706
  82.7 2.2 %collective-permute-start.17 = (f32[8,128]{1,0:T(8,128)S(1)}, f32[8,128]{1,0:T(8,128)S(1)}, u32[]{:S(2)}, u32[]{:S(2)}) collective-permute-start(f32[8,128]{1,0:T(8,128)S(1)} %fusion.3), channel_id=1, source_target_pairs={{0,4},{1,5},{2,6},{3,7},{4,0},{5,1},{6,2},{7,3},{8,12},{9,13},{10,... | collective-permute-start | bytes 12296 | tf_op jit(solution)/shard_map/ppermute | solution.py:706
  84.8 0.9 collective-permute-start.16
  85.7 12.9 %shard_map.93.refs_4_ = f32[12,128]{1,0:T(8,128)S(1)} custom-call(s32[12]{0:T(128)S(1)} %stack.63.bounds.info.refs_0_, s32[16,128]{1,0:T(8,128)S(1)} %get-tuple-element.21.listed, f32[112,8,128]{2,1,0:T(8,128)S(1)} %get-tuple-element.22.tiles.refs_5_, f32[32,128]{1,0:T(8,128)S(1)} %get-tuple-element.18.own.refs_1_.refs_0_.start, ...), custom_call_target="tpu_custom_call" | custom-call | flops 268435456 | bytes 262144 | tf_op jit(solution)/shard_map/pallas_call | solution.py:649
  98.7 2.4 %shard_map.94 = (f32[32,128]{1,0:T(8,128)S(1)}, f32[12,128]{1,0:T(8,128)}) custom-call(s32[12]{0:T(128)S(1)} %stack.63.bounds.info.refs_0_, f32[32,128]{1,0:T(8,128)S(1)} %get-tuple-element.18.own.refs_1_.refs_0_.start, f32[26,8,128]{2,1,0:T(8,128)S(1)} %get-tuple-element.19.refs_1_, f32[26,8,128]{2,1,0:T(8,128)S(1)} %get-tuple-element.20.refs_2_.refs_6_, ...), custom_call_target="tpu_custom_call" | custom-call | flops 67108864 | bytes 262144 | tf_op jit(solution)/shard_map/pallas_call | solution.py:662
  101.1 1.5 shard_map.95.mine
  102.8 5.6 %collective-permute-done.21.second = f32[224,128]{1,0:T(8,128)S(1)} collective-permute-done((f32[224,128]{1,0:T(8,128)S(1)}, f32[224,128]{1,0:T(8,128)S(1)}, u32[]{:S(2)}, u32[]{:S(2)}) %collective-permute-start.21) | collective-permute-done | bytes 114720 | tf_op jit(solution)/shard_map/ppermute | solution.py:540
  108.4 0.6 shard_map.96.mine
  109.0 1.6 collective-permute-start.23
  110.6 1.0 collective-permute-start.22
  111.6 4.6 %collective-permute-done.23.second = f32[256,128]{1,0:T(8,128)S(1)} collective-permute-done((f32[256,128]{1,0:T(8,128)S(1)}, f32[256,128]{1,0:T(8,128)S(1)}, u32[]{:S(2)}, u32[]{:S(2)}) %collective-permute-start.23) | collective-permute-done | bytes 131104 | tf_op jit(solution)/shard_map/ppermute | solution.py:540
  116.2 0.7 shard_map.97.refs_2_
  116.8 0.7 collective-permute-start.25
  117.5 1.9 %collective-permute-start.24 = (f32[352,128]{1,0:T(8,128)S(1)}, f32[352,128]{1,0:T(8,128)S(1)}, u32[]{:S(2)}, u32[]{:S(2)}) collective-permute-start(f32[352,128]{1,0:T(8,128)S(1)} %shard_map.97.refs_2_), channel_id=1, source_target_pairs={{0,1},{1,0},{2,3},{3,2},{4,5},{5,4},{6,7},{7,6},{8,9},{9,8},{10,11... | collective-permute-start | bytes 540680 | tf_op jit(solution)/shard_map/ppermute | solution.py:540
  119.4 3.0 %collective-permute-done.25.refs_4_ = f32[352,128]{1,0:T(8,128)S(1)} collective-permute-done((f32[352,128]{1,0:T(8,128)S(1)}, f32[352,128]{1,0:T(8,128)S(1)}, u32[]{:S(2)}, u32[]{:S(2)}) %collective-permute-start.25) | collective-permute-done | bytes 180256 | tf_op jit(solution)/shard_map/ppermute | solution.py:540
  122.4 0.6 collective-permute-done.24.refs_3_
  123.0 4.5 %shard_map.98 = (s32[16,128]{1,0:T(8,128)S(1)}, f32[112,8,128]{2,1,0:T(8,128)S(1)}, f32[26,8,128]{2,1,0:T(8,128)S(1)}, f32[8,128]{1,0:T(8,128)S(1)}) custom-call(s32[12]{0:T(128)S(1)} %stack.63.bounds.info.refs_0_, f32[32,128]{1,0:T(8,128)S(1)} %get-tuple-element.24.own.refs_1_.refs_0_, f32[352,128]{1,0:T(8,128)S(1)} %shard_map.97.refs_2_, ...), custom_call_target="tpu_custom_call" | custom-call | flops 4194304 | bytes 262144 | tf_op jit(solution)/shard_map/pallas_call | solution.py:605
  127.5 1.7 collective-permute-start.26
  129.1 3.5 %collective-permute-done.26 = f32[8,128]{1,0:T(8,128)S(1)} collective-permute-done((f32[8,128]{1,0:T(8,128)S(1)}, f32[8,128]{1,0:T(8,128)S(1)}, u32[]{:S(2)}, u32[]{:S(2)}) %collective-permute-start.26) | collective-permute-done | bytes 4128 | tf_op jit(solution)/shard_map/ppermute | solution.py:544
  132.7 7.7 %shard_map.99.mine.own_radius = f32[12,128]{1,0:T(8,128)S(1)} custom-call(s32[16,128]{1,0:T(8,128)S(1)} %get-tuple-element.26.listed, f32[112,8,128]{2,1,0:T(8,128)S(1)} %get-tuple-element.27.tiles, f32[32,128]{1,0:T(8,128)S(1)} %get-tuple-element.24.own.refs_1_.refs_0_, f32[8,128]{1,0:T(8,128)S(1)} %add.64.sums), custom_call_target="tpu_custom_call" | custom-call | flops 134217728 | bytes 262144 | tf_op jit(solution)/shard_map/pallas_call | solution.py:621
  141.0 4.1 %collective-permute-done.28.second = f32[12,128]{1,0:T(8,128)S(1)} collective-permute-done((f32[12,128]{1,0:T(8,128)S(1)}, f32[12,128]{1,0:T(8,128)S(1)}, u32[]{:S(2)}, u32[]{:S(2)}) %collective-permute-start.28) | collective-permute-done | bytes 6176 | tf_op jit(solution)/shard_map/ppermute | solution.py:540
  145.6 1.8 collective-permute-start.30
  147.5 2.3 %collective-permute-start.32 = (f32[8,128]{1,0:T(8,128)S(1)}, f32[8,128]{1,0:T(8,128)S(1)}, u32[]{:S(2)}, u32[]{:S(2)}) collective-permute-start(f32[8,128]{1,0:T(8,128)S(1)} %slice.45), channel_id=1, source_target_pairs={{0,24},{8,16},{16,8},{24,0},{32,56},{40,48},{48,40},{56,32},{1,25}... | collective-permute-start | bytes 12296 | tf_op jit(solution)/shard_map/ppermute | solution.py:544
  149.8 1.7 collective-permute-start.31
  151.5 0.8 collective-permute-done.32.refs_1_
  152.3 2.6 %collective-permute-done.31.refs_0_ = f32[8,128]{1,0:T(8,128)S(1)} collective-permute-done((f32[8,128]{1,0:T(8,128)S(1)}, f32[8,128]{1,0:T(8,128)S(1)}, u32[]{:S(2)}, u32[]{:S(2)}) %collective-permute-start.31) | collective-permute-done | bytes 4128 | tf_op jit(solution)/shard_map/ppermute | solution.py:544
  155.6 3.5 %collective-permute-start.34 = (f32[8,128]{1,0:T(8,128)S(1)}, f32[8,128]{1,0:T(8,128)S(1)}, u32[]{:S(2)}, u32[]{:S(2)}) collective-permute-start(f32[8,128]{1,0:T(8,128)S(1)} %slice.46), channel_id=1, source_target_pairs={{0,2},{1,3},{2,0},{3,1},{4,6},{5,7},{6,4},{7,5},{8,10},{9,11},{10,... | collective-permute-start | bytes 12296 | tf_op jit(solution)/shard_map/ppermute | solution.py:544
  159.8 0.8 slice.50
  160.6 1.6 collective-permute-start.39
  162.2 0.6 collective-permute-done.35
  162.8 5.6 %collective-permute-start.38 = (f32[8,128]{1,0:T(8,128)S(1)}, f32[8,128]{1,0:T(8,128)S(1)}, u32[]{:S(2)}, u32[]{:S(2)}) collective-permute-start(f32[8,128]{1,0:T(8,128)S(1)} %fusion.1), channel_id=1, source_target_pairs={{0,36},{1,37},{2,38},{3,39},{4,32},{5,33},{6,34},{7,35},{8,44},{9,... | collective-permute-start | bytes 12296 | tf_op jit(solution)/shard_map/ppermute | solution.py:706
  168.5 1.8 collective-permute-start.36
  170.3 13.1 %shard_map.102.refs_4_ = f32[12,128]{1,0:T(8,128)S(1)} custom-call(s32[12]{0:T(128)S(1)} %stack.63.bounds.info.refs_0_, s32[16,128]{1,0:T(8,128)S(1)} %get-tuple-element.26.listed, f32[112,8,128]{2,1,0:T(8,128)S(1)} %get-tuple-element.27.tiles, f32[32,128]{1,0:T(8,128)S(1)} %get-tuple-element.24.own.refs_1_.refs_0_, ...), custom_call_target="tpu_custom_call" | custom-call | flops 268435456 | bytes 262144 | tf_op jit(solution)/shard_map/pallas_call | solution.py:649
  183.4 1.8 shard_map.103
  185.5 0.6 squeeze.9
  186.1 0.6 squeeze.8
  (65 shorter events, 6.2 us)
Async XLA Ops:
  0.6 1.5 copy-start.3
  2.1 0.7 copy-start.1
  2.1 0.7 copy-start.2
  2.1 0.7 copy-start
  6.2 9.4 %collective-permute-start.1 = (f32[440,128]{1,0:T(8,128)S(1)}, f32[440,128]{1,0:T(8,128)S(1)}, u32[]{:S(2)}, u32[]{:S(2)}) collective-permute-start(f32[440,128]{1,0:T(8,128)S(1)} %shard_map.86.mine), channel_id=1, source_target_pairs={{0,192},{64,128},{128,64},{192,0},{1,193},{65,129},{129,65},{193,1... | collective-permute-start | bytes 675848 | tf_op jit(solution)/shard_map/ppermute | solution.py:540
  7.0 8.6 %collective-permute-start = (f32[440,128]{1,0:T(8,128)S(1)}, f32[440,128]{1,0:T(8,128)S(1)}, u32[]{:S(2)}, u32[]{:S(2)}) collective-permute-start(f32[440,128]{1,0:T(8,128)S(1)} %shard_map.86.mine), channel_id=1, source_target_pairs={{0,64},{64,0},{128,192},{192,128},{1,65},{65,1},{129,193},{193,129... | collective-permute-start | bytes 675848 | tf_op jit(solution)/shard_map/ppermute | solution.py:540
  16.2 10.3 %collective-permute-start.3 = (f32[488,128]{1,0:T(8,128)S(1)}, f32[488,128]{1,0:T(8,128)S(1)}, u32[]{:S(2)}, u32[]{:S(2)}) collective-permute-start(f32[488,128]{1,0:T(8,128)S(1)} %shard_map.87.mine), channel_id=1, source_target_pairs={{0,56},{8,16},{16,8},{24,32},{32,24},{40,48},{48,40},{56,0},{1,57}... | collective-permute-start | bytes 749576 | tf_op jit(solution)/shard_map/ppermute | solution.py:540
  19.2 7.8 %collective-permute-start.2 = (f32[488,128]{1,0:T(8,128)S(1)}, f32[488,128]{1,0:T(8,128)S(1)}, u32[]{:S(2)}, u32[]{:S(2)}) collective-permute-start(f32[488,128]{1,0:T(8,128)S(1)} %shard_map.87.mine), channel_id=1, source_target_pairs={{0,8},{8,0},{16,24},{24,16},{32,40},{40,32},{48,56},{56,48},{1,9},... | collective-permute-start | bytes 749576 | tf_op jit(solution)/shard_map/ppermute | solution.py:540
  27.7 8.8 %collective-permute-start.5 = (f32[632,128]{1,0:T(8,128)S(1)}, f32[632,128]{1,0:T(8,128)S(1)}, u32[]{:S(2)}, u32[]{:S(2)}) collective-permute-start(f32[632,128]{1,0:T(8,128)S(1)} %shard_map.88.refs_2_), channel_id=1, source_target_pairs={{0,7},{1,2},{2,1},{3,4},{4,3},{5,6},{6,5},{7,0},{8,15},{9,10},{10,... | collective-permute-start | bytes 970760 | tf_op jit(solution)/shard_map/ppermute | solution.py:540
  29.7 10.5 %collective-permute-start.4 = (f32[632,128]{1,0:T(8,128)S(1)}, f32[632,128]{1,0:T(8,128)S(1)}, u32[]{:S(2)}, u32[]{:S(2)}) collective-permute-start(f32[632,128]{1,0:T(8,128)S(1)} %shard_map.88.refs_2_), channel_id=1, source_target_pairs={{0,1},{1,0},{2,3},{3,2},{4,5},{5,4},{6,7},{7,6},{8,9},{9,8},{10,11... | collective-permute-start | bytes 970760 | tf_op jit(solution)/shard_map/ppermute | solution.py:540
  44.8 5.2 %collective-permute-start.6 = (f32[8,128]{1,0:T(8,128)S(1)}, f32[8,128]{1,0:T(8,128)S(1)}, u32[]{:S(2)}, u32[]{:S(2)}) collective-permute-start(f32[8,128]{1,0:T(8,128)S(1)} %get-tuple-element.23), channel_id=1, source_target_pairs={{0,128},{64,192},{128,0},{192,64},{1,129},{65,193},{129,1},{193,65... | collective-permute-start | bytes 12296 | tf_op jit(solution)/shard_map/ppermute | solution.py:544
  57.7 4.7 %collective-permute-start.8 = (f32[12,128]{1,0:T(8,128)S(1)}, f32[12,128]{1,0:T(8,128)S(1)}, u32[]{:S(2)}, u32[]{:S(2)}) collective-permute-start(f32[12,128]{1,0:T(8,128)S(1)} %shard_map.90.mine.own_radius), channel_id=1, source_target_pairs={{0,192},{64,128},{128,64},{192,0},{1,193},{65,129},{129,65},{193,1... | collective-permute-start | bytes 18440 | tf_op jit(solution)/shard_map/ppermute | solution.py:540
  57.8 4.6 %collective-permute-start.7 = (f32[12,128]{1,0:T(8,128)S(1)}, f32[12,128]{1,0:T(8,128)S(1)}, u32[]{:S(2)}, u32[]{:S(2)}) collective-permute-start(f32[12,128]{1,0:T(8,128)S(1)} %shard_map.90.mine.own_radius), channel_id=1, source_target_pairs={{0,64},{64,0},{128,192},{192,128},{1,65},{65,1},{129,193},{193,129... | collective-permute-start | bytes 18440 | tf_op jit(solution)/shard_map/ppermute | solution.py:540
  62.9 8.2 %collective-permute-start.10 = (f32[20,128]{1,0:T(8,128)S(1)}, f32[20,128]{1,0:T(8,128)S(1)}, u32[]{:S(2)}, u32[]{:S(2)}) collective-permute-start(f32[20,128]{1,0:T(8,128)S(1)} %shard_map.91.mine), channel_id=1, source_target_pairs={{0,56},{8,16},{16,8},{24,32},{32,24},{40,48},{48,40},{56,0},{1,57}... | collective-permute-start | bytes 30728 | tf_op jit(solution)/shard_map/ppermute | solution.py:540
  65.4 5.7 %collective-permute-start.9 = (f32[20,128]{1,0:T(8,128)S(1)}, f32[20,128]{1,0:T(8,128)S(1)}, u32[]{:S(2)}, u32[]{:S(2)}) collective-permute-start(f32[20,128]{1,0:T(8,128)S(1)} %shard_map.91.mine), channel_id=1, source_target_pairs={{0,8},{8,0},{16,24},{24,16},{32,40},{40,32},{48,56},{56,48},{1,9},... | collective-permute-start | bytes 30728 | tf_op jit(solution)/shard_map/ppermute | solution.py:540
  65.4 4.8 %collective-permute-start.12 = (f32[8,128]{1,0:T(8,128)S(1)}, f32[8,128]{1,0:T(8,128)S(1)}, u32[]{:S(2)}, u32[]{:S(2)}) collective-permute-start(f32[8,128]{1,0:T(8,128)S(1)} %slice.42), channel_id=1, source_target_pairs={{0,24},{8,16},{16,8},{24,0},{32,56},{40,48},{48,40},{56,32},{1,25}... | collective-permute-start | bytes 12296 | tf_op jit(solution)/shard_map/ppermute | solution.py:544
  65.8 5.3 %collective-permute-start.11 = (f32[8,128]{1,0:T(8,128)S(1)}, f32[8,128]{1,0:T(8,128)S(1)}, u32[]{:S(2)}, u32[]{:S(2)}) collective-permute-start(f32[8,128]{1,0:T(8,128)S(1)} %slice.42), channel_id=1, source_target_pairs={{0,16},{8,24},{16,0},{24,8},{32,48},{40,56},{48,32},{56,40},{1,17}... | collective-permute-start | bytes 12296 | tf_op jit(solution)/shard_map/ppermute | solution.py:544
  71.6 6.6 %collective-permute-start.13 = (f32[44,128]{1,0:T(8,128)S(1)}, f32[44,128]{1,0:T(8,128)S(1)}, u32[]{:S(2)}, u32[]{:S(2)}) collective-permute-start(f32[44,128]{1,0:T(8,128)S(1)} %shard_map.92.mine), channel_id=1, source_target_pairs={{0,1},{1,0},{2,3},{3,2},{4,5},{5,4},{6,7},{7,6},{8,9},{9,8},{10,11... | collective-permute-start | bytes 67592 | tf_op jit(solution)/shard_map/ppermute | solution.py:540
  72.1 4.6 %collective-permute-start.14 = (f32[8,128]{1,0:T(8,128)S(1)}, f32[8,128]{1,0:T(8,128)S(1)}, u32[]{:S(2)}, u32[]{:S(2)}) collective-permute-start(f32[8,128]{1,0:T(8,128)S(1)} %slice.43), channel_id=1, source_target_pairs={{0,2},{1,3},{2,0},{3,1},{4,6},{5,7},{6,4},{7,5},{8,10},{9,11},{10,... | collective-permute-start | bytes 12296 | tf_op jit(solution)/shard_map/ppermute | solution.py:544
  74.6 3.6 %collective-permute-start.15 = (f32[8,128]{1,0:T(8,128)S(1)}, f32[8,128]{1,0:T(8,128)S(1)}, u32[]{:S(2)}, u32[]{:S(2)}) collective-permute-start(f32[8,128]{1,0:T(8,128)S(1)} %slice.43), channel_id=1, source_target_pairs={{0,3},{1,2},{2,1},{3,0},{4,7},{5,6},{6,5},{7,4},{8,11},{9,10},{10,... | collective-permute-start | bytes 12296 | tf_op jit(solution)/shard_map/ppermute | solution.py:544
  75.2 10.6 %collective-permute-start.19 = (f32[44,128]{1,0:T(8,128)S(1)}, f32[44,128]{1,0:T(8,128)S(1)}, u32[]{:S(2)}, u32[]{:S(2)}) collective-permute-start(f32[44,128]{1,0:T(8,128)S(1)} %shard_map.92.mine), channel_id=1, source_target_pairs={{0,7},{1,2},{2,1},{3,4},{4,3},{5,6},{6,5},{7,0},{8,15},{9,10},{10,... | collective-permute-start | bytes 67592 | tf_op jit(solution)/shard_map/ppermute | solution.py:540
  78.3 20.4 %collective-permute-start.18 = (f32[8,128]{1,0:T(8,128)S(1)}, f32[8,128]{1,0:T(8,128)S(1)}, u32[]{:S(2)}, u32[]{:S(2)}) collective-permute-start(f32[8,128]{1,0:T(8,128)S(1)} %fusion.3), channel_id=1, source_target_pairs={{0,36},{1,37},{2,38},{3,39},{4,32},{5,33},{6,34},{7,35},{8,44},{9,... | collective-permute-start | bytes 12296 | tf_op jit(solution)/shard_map/ppermute | solution.py:706
  82.7 16.0 %collective-permute-start.17 = (f32[8,128]{1,0:T(8,128)S(1)}, f32[8,128]{1,0:T(8,128)S(1)}, u32[]{:S(2)}, u32[]{:S(2)}) collective-permute-start(f32[8,128]{1,0:T(8,128)S(1)} %fusion.3), channel_id=1, source_target_pairs={{0,4},{1,5},{2,6},{3,7},{4,0},{5,1},{6,2},{7,3},{8,12},{9,13},{10,... | collective-permute-start | bytes 12296 | tf_op jit(solution)/shard_map/ppermute | solution.py:706
  84.8 13.9 %collective-permute-start.16 = (f32[8,128]{1,0:T(8,128)S(1)}, f32[8,128]{1,0:T(8,128)S(1)}, u32[]{:S(2)}, u32[]{:S(2)}) collective-permute-start(f32[8,128]{1,0:T(8,128)S(1)} %fusion.3), channel_id=1, source_target_pairs={{0,32},{1,33},{2,34},{3,35},{4,36},{5,37},{6,38},{7,39},{8,40},{9,... | collective-permute-start | bytes 12296 | tf_op jit(solution)/shard_map/ppermute | solution.py:706
  102.6 5.8 %collective-permute-start.21 = (f32[224,128]{1,0:T(8,128)S(1)}, f32[224,128]{1,0:T(8,128)S(1)}, u32[]{:S(2)}, u32[]{:S(2)}) collective-permute-start(f32[224,128]{1,0:T(8,128)S(1)} %shard_map.95.mine), channel_id=1, source_target_pairs={{0,192},{64,128},{128,64},{192,0},{1,193},{65,129},{129,65},{193,1... | collective-permute-start | bytes 344072 | tf_op jit(solution)/shard_map/ppermute | solution.py:540
  102.7 5.7 %collective-permute-start.20 = (f32[224,128]{1,0:T(8,128)S(1)}, f32[224,128]{1,0:T(8,128)S(1)}, u32[]{:S(2)}, u32[]{:S(2)}) collective-permute-start(f32[224,128]{1,0:T(8,128)S(1)} %shard_map.95.mine), channel_id=1, source_target_pairs={{0,64},{64,0},{128,192},{192,128},{1,65},{65,1},{129,193},{193,129... | collective-permute-start | bytes 344072 | tf_op jit(solution)/shard_map/ppermute | solution.py:540
  109.0 7.2 %collective-permute-start.23 = (f32[256,128]{1,0:T(8,128)S(1)}, f32[256,128]{1,0:T(8,128)S(1)}, u32[]{:S(2)}, u32[]{:S(2)}) collective-permute-start(f32[256,128]{1,0:T(8,128)S(1)} %shard_map.96.mine), channel_id=1, source_target_pairs={{0,56},{8,16},{16,8},{24,32},{32,24},{40,48},{48,40},{56,0},{1,57}... | collective-permute-start | bytes 393224 | tf_op jit(solution)/shard_map/ppermute | solution.py:540
  110.6 5.6 %collective-permute-start.22 = (f32[256,128]{1,0:T(8,128)S(1)}, f32[256,128]{1,0:T(8,128)S(1)}, u32[]{:S(2)}, u32[]{:S(2)}) collective-permute-start(f32[256,128]{1,0:T(8,128)S(1)} %shard_map.96.mine), channel_id=1, source_target_pairs={{0,8},{8,0},{16,24},{24,16},{32,40},{40,32},{48,56},{56,48},{1,9},... | collective-permute-start | bytes 393224 | tf_op jit(solution)/shard_map/ppermute | solution.py:540
  116.8 5.6 %collective-permute-start.25 = (f32[352,128]{1,0:T(8,128)S(1)}, f32[352,128]{1,0:T(8,128)S(1)}, u32[]{:S(2)}, u32[]{:S(2)}) collective-permute-start(f32[352,128]{1,0:T(8,128)S(1)} %shard_map.97.refs_2_), channel_id=1, source_target_pairs={{0,7},{1,2},{2,1},{3,4},{4,3},{5,6},{6,5},{7,0},{8,15},{9,10},{10,... | collective-permute-start | bytes 540680 | tf_op jit(solution)/shard_map/ppermute | solution.py:540
  117.5 5.5 %collective-permute-start.24 = (f32[352,128]{1,0:T(8,128)S(1)}, f32[352,128]{1,0:T(8,128)S(1)}, u32[]{:S(2)}, u32[]{:S(2)}) collective-permute-start(f32[352,128]{1,0:T(8,128)S(1)} %shard_map.97.refs_2_), channel_id=1, source_target_pairs={{0,1},{1,0},{2,3},{3,2},{4,5},{5,4},{6,7},{7,6},{8,9},{9,8},{10,11... | collective-permute-start | bytes 540680 | tf_op jit(solution)/shard_map/ppermute | solution.py:540
  127.5 5.2 %collective-permute-start.26 = (f32[8,128]{1,0:T(8,128)S(1)}, f32[8,128]{1,0:T(8,128)S(1)}, u32[]{:S(2)}, u32[]{:S(2)}) collective-permute-start(f32[8,128]{1,0:T(8,128)S(1)} %get-tuple-element.28), channel_id=1, source_target_pairs={{0,128},{64,192},{128,0},{192,64},{1,129},{65,193},{129,1},{193,65... | collective-permute-start | bytes 12296 | tf_op jit(solution)/shard_map/ppermute | solution.py:544
  140.4 4.7 %collective-permute-start.28 = (f32[12,128]{1,0:T(8,128)S(1)}, f32[12,128]{1,0:T(8,128)S(1)}, u32[]{:S(2)}, u32[]{:S(2)}) collective-permute-start(f32[12,128]{1,0:T(8,128)S(1)} %shard_map.99.mine.own_radius), channel_id=1, source_target_pairs={{0,192},{64,128},{128,64},{192,0},{1,193},{65,129},{129,65},{193,1... | collective-permute-start | bytes 18440 | tf_op jit(solution)/shard_map/ppermute | solution.py:540
  140.5 4.6 %collective-permute-start.27 = (f32[12,128]{1,0:T(8,128)S(1)}, f32[12,128]{1,0:T(8,128)S(1)}, u32[]{:S(2)}, u32[]{:S(2)}) collective-permute-start(f32[12,128]{1,0:T(8,128)S(1)} %shard_map.99.mine.own_radius), channel_id=1, source_target_pairs={{0,64},{64,0},{128,192},{192,128},{1,65},{65,1},{129,193},{193,129... | collective-permute-start | bytes 18440 | tf_op jit(solution)/shard_map/ppermute | solution.py:540
  145.6 9.3 %collective-permute-start.30 = (f32[20,128]{1,0:T(8,128)S(1)}, f32[20,128]{1,0:T(8,128)S(1)}, u32[]{:S(2)}, u32[]{:S(2)}) collective-permute-start(f32[20,128]{1,0:T(8,128)S(1)} %shard_map.100.mine), channel_id=1, source_target_pairs={{0,56},{8,16},{16,8},{24,32},{32,24},{40,48},{48,40},{56,0},{1,57}... | collective-permute-start | bytes 30728 | tf_op jit(solution)/shard_map/ppermute | solution.py:540
  147.4 7.5 %collective-permute-start.29 = (f32[20,128]{1,0:T(8,128)S(1)}, f32[20,128]{1,0:T(8,128)S(1)}, u32[]{:S(2)}, u32[]{:S(2)}) collective-permute-start(f32[20,128]{1,0:T(8,128)S(1)} %shard_map.100.mine), channel_id=1, source_target_pairs={{0,8},{8,0},{16,24},{24,16},{32,40},{40,32},{48,56},{56,48},{1,9},... | collective-permute-start | bytes 30728 | tf_op jit(solution)/shard_map/ppermute | solution.py:540
  147.5 4.8 %collective-permute-start.32 = (f32[8,128]{1,0:T(8,128)S(1)}, f32[8,128]{1,0:T(8,128)S(1)}, u32[]{:S(2)}, u32[]{:S(2)}) collective-permute-start(f32[8,128]{1,0:T(8,128)S(1)} %slice.45), channel_id=1, source_target_pairs={{0,24},{8,16},{16,8},{24,0},{32,56},{40,48},{48,40},{56,32},{1,25}... | collective-permute-start | bytes 12296 | tf_op jit(solution)/shard_map/ppermute | solution.py:544
  149.8 5.1 %collective-permute-start.31 = (f32[8,128]{1,0:T(8,128)S(1)}, f32[8,128]{1,0:T(8,128)S(1)}, u32[]{:S(2)}, u32[]{:S(2)}) collective-permute-start(f32[8,128]{1,0:T(8,128)S(1)} %slice.45), channel_id=1, source_target_pairs={{0,16},{8,24},{16,0},{24,8},{32,48},{40,56},{48,32},{56,40},{1,17}... | collective-permute-start | bytes 12296 | tf_op jit(solution)/shard_map/ppermute | solution.py:544
  155.5 7.3 %collective-permute-start.33 = (f32[44,128]{1,0:T(8,128)S(1)}, f32[44,128]{1,0:T(8,128)S(1)}, u32[]{:S(2)}, u32[]{:S(2)}) collective-permute-start(f32[44,128]{1,0:T(8,128)S(1)} %shard_map.101.mine), channel_id=1, source_target_pairs={{0,1},{1,0},{2,3},{3,2},{4,5},{5,4},{6,7},{7,6},{8,9},{9,8},{10,11... | collective-permute-start | bytes 67592 | tf_op jit(solution)/shard_map/ppermute | solution.py:540
  155.6 6.5 %collective-permute-start.34 = (f32[8,128]{1,0:T(8,128)S(1)}, f32[8,128]{1,0:T(8,128)S(1)}, u32[]{:S(2)}, u32[]{:S(2)}) collective-permute-start(f32[8,128]{1,0:T(8,128)S(1)} %slice.46), channel_id=1, source_target_pairs={{0,2},{1,3},{2,0},{3,1},{4,6},{5,7},{6,4},{7,5},{8,10},{9,11},{10,... | collective-permute-start | bytes 12296 | tf_op jit(solution)/shard_map/ppermute | solution.py:544
  159.2 3.6 %collective-permute-start.35 = (f32[8,128]{1,0:T(8,128)S(1)}, f32[8,128]{1,0:T(8,128)S(1)}, u32[]{:S(2)}, u32[]{:S(2)}) collective-permute-start(f32[8,128]{1,0:T(8,128)S(1)} %slice.46), channel_id=1, source_target_pairs={{0,3},{1,2},{2,1},{3,0},{4,7},{5,6},{6,5},{7,4},{8,11},{9,10},{10,... | collective-permute-start | bytes 12296 | tf_op jit(solution)/shard_map/ppermute | solution.py:544
  160.6 9.7 %collective-permute-start.39 = (f32[44,128]{1,0:T(8,128)S(1)}, f32[44,128]{1,0:T(8,128)S(1)}, u32[]{:S(2)}, u32[]{:S(2)}) collective-permute-start(f32[44,128]{1,0:T(8,128)S(1)} %shard_map.101.mine), channel_id=1, source_target_pairs={{0,7},{1,2},{2,1},{3,4},{4,3},{5,6},{6,5},{7,0},{8,15},{9,10},{10,... | collective-permute-start | bytes 67592 | tf_op jit(solution)/shard_map/ppermute | solution.py:540
  162.8 20.6 %collective-permute-start.38 = (f32[8,128]{1,0:T(8,128)S(1)}, f32[8,128]{1,0:T(8,128)S(1)}, u32[]{:S(2)}, u32[]{:S(2)}) collective-permute-start(f32[8,128]{1,0:T(8,128)S(1)} %fusion.1), channel_id=1, source_target_pairs={{0,36},{1,37},{2,38},{3,39},{4,32},{5,33},{6,34},{7,35},{8,44},{9,... | collective-permute-start | bytes 12296 | tf_op jit(solution)/shard_map/ppermute | solution.py:706
  168.3 15.0 %collective-permute-start.37 = (f32[8,128]{1,0:T(8,128)S(1)}, f32[8,128]{1,0:T(8,128)S(1)}, u32[]{:S(2)}, u32[]{:S(2)}) collective-permute-start(f32[8,128]{1,0:T(8,128)S(1)} %fusion.1), channel_id=1, source_target_pairs={{0,4},{1,5},{2,6},{3,7},{4,0},{5,1},{6,2},{7,3},{8,12},{9,13},{10,... | collective-permute-start | bytes 12296 | tf_op jit(solution)/shard_map/ppermute | solution.py:706
  168.5 14.9 %collective-permute-start.36 = (f32[8,128]{1,0:T(8,128)S(1)}, f32[8,128]{1,0:T(8,128)S(1)}, u32[]{:S(2)}, u32[]{:S(2)}) collective-permute-start(f32[8,128]{1,0:T(8,128)S(1)} %fusion.1), channel_id=1, source_target_pairs={{0,32},{1,33},{2,34},{3,35},{4,36},{5,37},{6,38},{7,39},{8,40},{9,... | collective-permute-start | bytes 12296 | tf_op jit(solution)/shard_map/ppermute | solution.py:706

commit v4 on v3

--- a/solution.py
+++ b/solution.py
@@ -22,6 +22,8 @@
 TILES = SLOTS // LANES
 BRICK = 16
 PLANES = 26
+HALF = PLANES // 2
+EDGE = 10
 PAD = 8
 WIDE = 32
 INTERPRET = False
@@ -136,15 +138,15 @@
 
 
 def plan_kernel(rows, fields, *refs):
-    info, own = refs[:2]
-    sources = refs[2:5]
+    info, own, field = refs[:3]
+    sources = refs[3:6]
     if fields == 2:
         known = ()
-        listed, tiles, evolved, given, sums, active = refs[5:]
+        listed, tiles, evolved, given, sums, active = refs[6:]
     else:
-        known = refs[5:6]
-        given = refs[6]
-        listed, tiles, evolved, sums, active = refs[7:]
+        known = refs[6:7]
+        given = refs[7]
+        listed, tiles, evolved, sums, active = refs[8:]
     low, high = [], []
     for dim in range(3):
         living = own[28:32, :] > 0.0
@@ -161,10 +163,10 @@
     slots = (1, jnp.where(after_first, 2, 0), jnp.where(after_first, 0, 2))
     for source, slot, ok in zip(sources, slots, (None,) + valid):
 
-        def visit(cell, carry, source=source, slot=slot, ok=ok):
+        for cell in range(9):
             number = slot * 9 + cell
-            sides = (lax.rem(cell, 3) - 1, cell // 3 - 1, slot - 1)
-            block = source[pl.ds(pl.multiple_of(cell * rows, 8), rows), :]
+            sides = (cell % 3 - 1, cell // 3 - 1, slot - 1)
+            block = source[cell * rows : cell * rows + rows, :]
             if ok is not None:
                 block = block * ok
             if known:
@@ -195,10 +197,7 @@
                     gap = jnp.maximum(jnp.maximum(near_low[dim] - hi, lo - near_high[dim]), 0.0)
                     apart = apart + gap * gap
                 near = jnp.where(apart < CUTOFF * CUTOFF * 1.0001, 1.0, 0.0)
-                active[tile, pl.ds(4 * number, TILES), :] = near
-            return carry
-
-        lax.fori_loop(0, 9, visit, 0)
+                active[tile, pl.ds(pl.multiple_of(4 * number, TILES), TILES), :] = near
     row = lax.broadcasted_iota(jnp.int32, (LANES, LANES), 0)
     lane = lax.broadcasted_iota(jnp.int32, (LANES, LANES), 1)
     before = jnp.where(lane < row, 1.0, 0.0).astype(jnp.bfloat16)
@@ -222,13 +221,13 @@
     cross = squares
     target = squares
     adds = shift_masks(info, 2)
+    evolved[...] = field[0 : 8 * PLANES, :].reshape(PLANES, 8, LANES)
+    take_shares(2, adds, sources[1:], 9 * rows, evolved, 0)
+    if fields == 2:
+        given[...] = field[8 * PLANES : 16 * PLANES, :].reshape(PLANES, 8, LANES)
+        take_shares(2, adds, sources[1:], 9 * rows + 8 * HALF, given, 0)
     for plane in range(PLANES):
-        at = slice(9 * rows + 8 * plane, 9 * rows + 8 * plane + 8)
-        value = received(2, adds, sources, at)
-        evolved[plane] = value
-        if fields == 2:
-            at = slice(9 * rows + 8 * (PLANES + plane), 9 * rows + 8 * (PLANES + plane) + 8)
-            given[plane] = received(2, adds, sources, at)
+        value = evolved[plane]
         if 5 <= plane < 5 + BRICK:
             value = jnp.where(own_points, value, 0.0)
             wanted = jnp.where(own_points, given[plane], 0.0)
@@ -246,9 +245,13 @@
     return after_first, (1.0, jnp.where(info[7 + 2 * axis] > 0, 1.0, 0.0))
 
 
+def upper_half(axis):
+    lane = lax.broadcasted_iota(jnp.int32, (8, LANES), 1)
+    return (lane >= 64) if axis == 1 else ((lane & (WIDE - 1)) >= BRICK)
+
+
 def shift_masks(info, axis):
-    lane = lax.broadcasted_iota(jnp.int32, (8, LANES), 1)
-    upper = (lane >= 64) if axis == 1 else ((lane & (WIDE - 1)) >= BRICK)
+    upper = upper_half(axis)
     after_first, valid = arrivals(info, axis)
     after_one = jnp.where(after_first, 1.0, 0.0)
     masks = []
@@ -257,40 +260,57 @@
     return masks
 
 
-def received(axis, masks, sources, at):
-    value = sources[0][at, :]
-    for (from_after, from_before), source in zip(masks, sources[1:]):
-        other = source[at, :]
-        if axis == 1:
-            value = value + pltpu.roll(other, 64, 1) * (from_after + from_before)
-        else:
-            value = value + pltpu.roll(other, BRICK, 1) * from_after
-            value = value + pltpu.roll(other, LANES - BRICK, 1) * from_before
-    return value
-
-
-def merge_kernel(axis, count, rows, fields, info, mine, first, second, out):
+def half_steps(axis):
+    return (64, 64) if axis == 1 else (BRICK, LANES - BRICK)
+
+
+def take_shares(axis, masks, sources, base, into, first):
+    up, down = half_steps(axis)
+    for plane in range(HALF):
+        at = slice(base + 8 * plane, base + 8 * plane + 8)
+        low = into[first + plane]
+        high = into[first + HALF + plane]
+        for (from_after, from_before), source in zip(masks, sources):
+            share = source[at, :]
+            low = low + pltpu.roll(share, up, 1) * from_after + share * from_before
+            high = high + share * from_after + pltpu.roll(share, down, 1) * from_before
+        into[first + plane] = low
+        into[first + HALF + plane] = high
+
+
+def give_shares(info, axis, field, first, outs, base):
+    up, down = half_steps(axis)
+    upper = upper_half(axis)
+    after_first, _ = arrivals(info, axis)
+    for plane in range(HALF):
+        low, high = field[first + plane], field[first + HALF + plane]
+        after = jnp.where(upper, high, pltpu.roll(low, down, 1))
+        before = jnp.where(upper, pltpu.roll(high, up, 1), low)
+        at = slice(base + 8 * plane, base + 8 * plane + 8)
+        outs[0][at, :] = jnp.where(after_first, after, before)
+        outs[1][at, :] = jnp.where(after_first, before, after)
+
+
+def merge_kernel(axis, count, rows, fields, info, field, mine, first, second, merged, out_first, out_second):
     after_first, valid = arrivals(info, axis)
     span = count * rows
-    out[span : 2 * span, :] = mine[0:span, :]
     slots = (jnp.where(after_first, 2 * span, 0), jnp.where(after_first, 0, 2 * span))
-    for source, slot, ok in zip((first, second), slots, valid):
-        out[pl.ds(pl.multiple_of(slot, 8), span), :] = source[0:span, :] * ok
-    if axis == 0:
-        for field in range(fields):
-            base = 3 * span + field * 8 * PLANES
-            mine_base = span + field * 8 * PLANES
-            out[base : base + 8 * PLANES, :] = mine[mine_base : mine_base + 8 * PLANES, :]
+    for out in (out_first, out_second):
+        out[span : 2 * span, :] = mine[0:span, :]
+        for source, slot, ok in zip((first, second), slots, valid):
+            out[pl.ds(pl.multiple_of(slot, 8), span), :] = source[0:span, :] * ok
+    merged[...] = field[...].reshape(fields * PLANES, 8, LANES)
+    for number in range(fields):
+        if axis == 0:
             for source, slot, ok in zip((first, second), slots, valid):
-                to = pl.multiple_of(jnp.where(slot > 0, 8 * BRICK, 0), 8)
-                into = pl.ds(pl.multiple_of(base + to, 8), 80)
-                off = pl.ds(pl.multiple_of(mine_base + 8 * BRICK - to, 8), 80)
-                out[into, :] = out[into, :] + source[off, :] * ok
-        return
-    masks = shift_masks(info, axis)
-    for plane in range(PLANES * fields):
-        at = slice(span + 8 * plane, span + 8 * plane + 8)
-        out[3 * span + 8 * plane : 3 * span + 8 * plane + 8, :] = received(axis, masks, (mine, first, second), at)
+                into = pl.ds(number * PLANES + jnp.where(slot > 0, BRICK, 0), EDGE)
+                at = slice(span + 8 * EDGE * number, span + 8 * EDGE * (number + 1))
+                merged[into] = merged[into] + source[at, :].reshape(EDGE, 8, LANES) * ok
+        else:
+            base = span + 8 * HALF * number
+            take_shares(axis, shift_masks(info, axis), (first, second), base, merged, number * PLANES)
+        base = 3 * span + 8 * HALF * number
+        give_shares(info, axis + 1, merged, number * PLANES, (out_first, out_second), base)
 
 
 def radius_merge_kernel(axis, count, extra, info, mine, first, second, *refs):
@@ -438,8 +458,7 @@
 def splat_kernel(fields, rows, bounds, own, *refs):
     if fields == 2:
         given = refs[0]
-    out, px, left_hi, left_lo, right = refs[fields - 1 :]
-    out[0:rows, :] = own[0:rows, :]
+    field, out_first, out_second, px, left_hi, left_lo, right = refs[fields - 1 :]
     for tile in range(TILES):
         lanes = slice(tile * LANES, (tile + 1) * LANES)
         z = profiles(own[8 + tile : 9 + tile, :], 0, -PAD, WIDE, bounds[4], bounds[5], False)
@@ -462,13 +481,20 @@
     placed = placed.reshape(PLANES, 4, 8, WIDE)
     for plane in range(PLANES):
         parts = [placed[plane, k] for k in range(4)]
-        out[rows + 8 * plane : rows + 8 * plane + 8, :] = jnp.concatenate(parts, axis=1)
+        field[8 * plane : 8 * plane + 8, :] = jnp.concatenate(parts, axis=1)
     if fields == 2:
-        base = rows + 8 * PLANES
-        out[base : base + 8 * PLANES, :] = jnp.zeros((8 * PLANES, LANES), jnp.float32)
+        base = 8 * PLANES
+        field[base : base + 8 * PLANES, :] = jnp.zeros((8 * PLANES, LANES), jnp.float32)
         for plane in range(BRICK):
             value = pltpu.roll(given[plane, 0:8, :], WIDE + PAD, 1) + pltpu.roll(given[plane, 8:16, :], 2 * WIDE + PAD, 1)
-            out[base + 8 * (plane + 5) : base + 8 * (plane + 6), :] = value
+            field[base + 8 * (plane + 5) : base + 8 * (plane + 6), :] = value
+    after_first, _ = arrivals(bounds, 0)
+    starts = (jnp.where(after_first, 8 * BRICK, 0), jnp.where(after_first, 0, 8 * BRICK))
+    for out, start in zip((out_first, out_second), starts):
+        out[0:rows, :] = own[0:rows, :]
+        for number in range(fields):
+            off = pl.ds(pl.multiple_of(8 * PLANES * number + start, 8), 8 * EDGE)
+            out[rows + 8 * EDGE * number : rows + 8 * EDGE * (number + 1), :] = field[off, :]
 
 
 def fit_kernel(scale, parts, bounds, *refs):
@@ -535,9 +561,9 @@
     return even, odd
 
 
-def both_sides(block, axis):
+def both_sides(blocks, axis):
     even, odd = partners(axis)
-    return lax.ppermute(block, axis, even), lax.ppermute(block, axis, odd)
+    return lax.ppermute(blocks[0], axis, even), lax.ppermute(blocks[1], axis, odd)
 
 
 def across(block, axis, flip):
@@ -579,9 +605,9 @@
     for step in range(STEPS):
         fields, rows = (2, 24) if step == 0 else (1, 16)
         planes = 8 * PLANES * fields
-        message = call(
+        field, *mine = call(
             functools.partial(splat_kernel, fields, rows),
-            f32(rows + planes, LANES),
+            (f32(planes, LANES),) + (f32(rows + 8 * EDGE * fields, LANES),) * 2,
             1 << 26,
             scratch=[
                 pltpu.VMEM((WIDE, LANES), jnp.float32),
@@ -594,13 +620,13 @@
         )(*((info, own, given) if step == 0 else (info, own)))
         for number, axis in enumerate(AXES[:2]):
             count = 3**number
-            message = call(
+            field, *mine = call(
                 functools.partial(merge_kernel, number, count, rows, fields),
-                f32(3 * count * rows + planes, LANES),
+                (f32(fields * PLANES, 8, LANES),) + (f32(3 * count * rows + 8 * HALF * fields, LANES),) * 2,
                 1 << 20,
                 smem=1,
-                n_in=4,
-            )(info, message, *both_sides(message, axis))
+                n_in=5,
+            )(info, field.reshape(planes, LANES), mine[0], *both_sides(mine, axis))
         before = () if step == 0 else (tiles, exp_ext)
         planned = call(
             functools.partial(plan_kernel, rows, fields),
@@ -610,14 +636,13 @@
             1 << 22,
             scratch=[pltpu.VMEM((TILES, LANES, LANES), jnp.float32)],
             smem=1,
-            n_in=5 + len(before),
-        )(info, own, message, *both_sides(message, AXES[2]), *before)
+            n_in=6 + len(before),
+        )(info, own, field.reshape(planes, LANES), mine[0], *both_sides(mine, AXES[2]), *before)
         if step == 0:
             listed, tiles, evolved, exp_ext, sums = planned
         else:
             listed, tiles, evolved, sums = planned
-        if sizes[0] >= 4:
-            sums = sums + across(sums, AXES[0], 2)
+        far = [across(sums, AXES[0], flip) for flip in (2, 3)] if sizes[0] >= 4 else []
         radius = call(
             born_kernel,
             f32(TILES + 8, LANES),
@@ -632,8 +657,8 @@
             span = count * TILES
             flips = (2, 3) if number and sizes[number] >= 4 else ()
             here = line[span:]
-            others = [across(here, axis, flip) for flip in flips]
-            near = both_sides(line, axis)
+            others = [across(here, axis, flip) for flip in flips] if number else far
+            near = both_sides((line, line), axis)
             if number == 2:
                 sums = here + near[0][span:]
                 for other in others:

time: 187 us -> 171 us (0.914)
  waiting for transfers between devices: 59.4 us -> 41.3 us
  starting transfers between devices: 57.5 us -> 63.3 us
  Pallas kernels: 64.4 us -> 60.5 us
    ppermute x24, waiting for transfers between devices: 44.5 us -> 26.6 us  [the longest x12 21.3 us: both_sides(): lax.ppermute(blocks[1], axis, odd)]
    ppermute x10 -> x12, starting transfers between devices: 17.9 us -> 23.1 us  [across(): lax.ppermute(block, axis, [(i, i ^ flip) for i in range(lax.axis_size(axi...]
    pallas_call x2, Pallas kernels: 9.07 us -> 4.09 us  [on_device(): call(functools.partial(plan_kernel, rows, fields), (jax.ShapeDtypeStruct(...]
    ppermute x10 -> x12, waiting for transfers between devices: 14.8 us -> 14.7 us  [across(): lax.ppermute(block, axis, [(i, i ^ flip) for i in range(lax.axis_size(axi...]
  transfers between devices with their start and end apart: 40 -> 42, of which waited for: 19 -> 19; matrix products, arithmetic and copies ran while one was open for 1% -> 1% of each run, Pallas kernels for 14% -> 16%
where the time goes in v4:
time: 171 us
  starting transfers between devices  63.3 us (37%)
  Pallas kernels  60.5 us (35%)
  waiting for transfers between devices  41.3 us (24%)
  local copies, waits for them, and re-layouts  2.98 us (2%)
    pallas_call x2, Pallas kernels, on_device(): call(gb_kernel, f32(3 * TILES, LANES), 1 << 28, scratch=[pltpu.VMEM((5, S...  26.4 us
    ppermute x12, starting transfers between devices, across(): lax.ppermute(block, axis, [(i, i ^ flip) for i in range(lax.axis_size(axi...  23.1 us
    ppermute x12, waiting for transfers between devices, both_sides(): lax.ppermute(blocks[1], axis, odd)  21.3 us
    pallas_call x2, Pallas kernels, on_device(): call(born_kernel, f32(TILES + 8, LANES), 1 << 27, scratch=[pltpu.VMEM((3,...  15.6 us
    ppermute x12, starting transfers between devices, both_sides(): lax.ppermute(blocks[1], axis, odd)  15.3 us
    ppermute x6, starting transfers between devices, finished(): total = total + lax.ppermute(sums, tuple(far), pairs)  15.3 us
    ppermute x12, waiting for transfers between devices, across(): lax.ppermute(block, axis, [(i, i ^ flip) for i in range(lax.axis_size(axi...  14.7 us
    ppermute x12, starting transfers between devices, both_sides(): lax.ppermute(blocks[0], axis, even)  9.57 us
  transfers between devices with their start and end apart: 42, of which 19 were waited for; matrix products, arithmetic and copies ran while one was open for 1% of the time, Pallas kernels for 16%

profile of v4, /device:TPU:56, one launch (start us, length us, event | category | flops | bytes accessed | tf_op | source)
XLA Modules:
  0.0 170.5 jit_solution(17378491024453858719)
XLA Ops:
  1.3 0.7 reduce
  2.1 0.6 copy-done.1
  2.8 1.8 %shard_map.85 = (f32[32,128]{1,0:T(8,128)S(1)}, f32[4,128]{1,0:T(4,128)S(1)}) custom-call(f32[3,8]{1,0:T(4,128)S(1)} %copy-done, s32[1]{0:T(128)} %bitcast.23.live_count, f32[12,128]{1,0:T(8,128)S(1)} %reshape.42.pos, f32[4,128]{1,0:T(4,128)S(1)} %bitcast.28, s32[4,128]{1,0:T(4,128)S(1)} %bitcast.29), custom_call_target="tpu_custom_call" | custom-call | flops 4194304 | bytes 262144 | tf_op jit(solution)/shard_map/pallas_call | solution.py:589
  4.7 1.5 shard_map.86
  6.2 0.8 collective-permute-start.1
  7.0 0.7 collective-permute-start
  7.7 5.1 %collective-permute-done.1.second = f32[184,128]{1,0:T(8,128)S(1)} collective-permute-done((f32[184,128]{1,0:T(8,128)S(1)}, f32[184,128]{1,0:T(8,128)S(1)}, u32[]{:S(2)}, u32[]{:S(2)}) %collective-permute-start.1) | collective-permute-done | bytes 94240 | tf_op jit(solution)/shard_map/ppermute | solution.py:566
  12.8 0.7 shard_map.87
  13.6 3.0 %collective-permute-start.3 = (f32[280,128]{1,0:T(8,128)S(1)}, f32[280,128]{1,0:T(8,128)S(1)}, u32[]{:S(2)}, u32[]{:S(2)}) collective-permute-start(f32[280,128]{1,0:T(8,128)S(1)} %get-tuple-element.42), channel_id=1, source_target_pairs={{0,56},{8,16},{16,8},{24,32},{32,24},{40,48},{48,40},{56,0},{1,57}... | collective-permute-start | bytes 430088 | tf_op jit(solution)/shard_map/ppermute | solution.py:566
  16.6 4.9 %collective-permute-done.3.second = f32[280,128]{1,0:T(8,128)S(1)} collective-permute-done((f32[280,128]{1,0:T(8,128)S(1)}, f32[280,128]{1,0:T(8,128)S(1)}, u32[]{:S(2)}, u32[]{:S(2)}) %collective-permute-start.3) | collective-permute-done | bytes 143392 | tf_op jit(solution)/shard_map/ppermute | solution.py:566
  22.1 0.7 shard_map.88
  22.9 2.0 %collective-permute-start.5 = (f32[424,128]{1,0:T(8,128)S(1)}, f32[424,128]{1,0:T(8,128)S(1)}, u32[]{:S(2)}, u32[]{:S(2)}) collective-permute-start(f32[424,128]{1,0:T(8,128)S(1)} %get-tuple-element.45), channel_id=1, source_target_pairs={{0,7},{1,2},{2,1},{3,4},{4,3},{5,6},{6,5},{7,0},{8,15},{9,10},{10,... | collective-permute-start | bytes 651272 | tf_op jit(solution)/shard_map/ppermute | solution.py:566
  24.9 4.0 %collective-permute-start.4 = (f32[424,128]{1,0:T(8,128)S(1)}, f32[424,128]{1,0:T(8,128)S(1)}, u32[]{:S(2)}, u32[]{:S(2)}) collective-permute-start(f32[424,128]{1,0:T(8,128)S(1)} %get-tuple-element.44.refs_3_), channel_id=1, source_target_pairs={{0,1},{1,0},{2,3},{3,2},{4,5},{5,4},{6,7},{7,6},{8,9},{9,8},{10,11... | collective-permute-start | bytes 651272 | tf_op jit(solution)/shard_map/ppermute | solution.py:566
  29.3 3.8 %collective-permute-done.4.refs_4_ = f32[424,128]{1,0:T(8,128)S(1)} collective-permute-done((f32[424,128]{1,0:T(8,128)S(1)}, f32[424,128]{1,0:T(8,128)S(1)}, u32[]{:S(2)}, u32[]{:S(2)}) %collective-permute-start.4) | collective-permute-done | bytes 217120 | tf_op jit(solution)/shard_map/ppermute | solution.py:566
  33.1 2.1 %shard_map.89 = (s32[16,128]{1,0:T(8,128)S(1)}, f32[112,8,128]{2,1,0:T(8,128)S(1)}, f32[26,8,128]{2,1,0:T(8,128)S(1)}, f32[26,8,128]{2,1,0:T(8,128)S(1)}, f32[8,128]{1,0:T(8,128)S(1)}) custom-call(s32[12]{0:T(128)S(1)} %stack.63.bounds.info.refs_0_, f32[32,128]{1,0:T(8,128)S(1)} %get-tuple-element.36.own.refs_1_.refs_0_.start, f32[416,128]{1,0:T(8,128)S(1)} %bitcast.24, ...), custom_call_target="tpu_custom_call" | custom-call | flops 4194304 | bytes 262144 | tf_op jit(solution)/shard_map/pallas_call | solution.py:631
  35.2 7.8 %shard_map.90.mine.own_radius = f32[12,128]{1,0:T(8,128)S(1)} custom-call(s32[16,128]{1,0:T(8,128)S(1)} %get-tuple-element.48.listed, f32[112,8,128]{2,1,0:T(8,128)S(1)} %get-tuple-element.49.tiles.refs_6_, f32[32,128]{1,0:T(8,128)S(1)} %get-tuple-element.36.own.refs_1_.refs_0_.start, f32[8,128]{1,0:T(8,128)S(1)} %get-tuple-element.50.sums), custom_call_target="tpu_custom_call" | custom-call | flops 134217728 | bytes 262144 | tf_op jit(solution)/shard_map/pallas_call | solution.py:646
  43.2 3.1 %collective-permute-start.9 = (f32[8,128]{1,0:T(8,128)S(1)}, f32[8,128]{1,0:T(8,128)S(1)}, u32[]{:S(2)}, u32[]{:S(2)}) collective-permute-start(f32[8,128]{1,0:T(8,128)S(1)} %get-tuple-element.50.sums), channel_id=1, source_target_pairs={{0,192},{64,128},{128,64},{192,0},{1,193},{65,129},{129,65},{193,1... | collective-permute-start | bytes 12296 | tf_op jit(solution)/shard_map/ppermute | solution.py:570
  46.8 1.0 collective-permute-done.9.refs_1_
  47.8 3.6 %collective-permute-done.8.refs_0_ = f32[8,128]{1,0:T(8,128)S(1)} collective-permute-done((f32[8,128]{1,0:T(8,128)S(1)}, f32[8,128]{1,0:T(8,128)S(1)}, u32[]{:S(2)}, u32[]{:S(2)}) %collective-permute-start.8) | collective-permute-done | bytes 4128 | tf_op jit(solution)/shard_map/ppermute | solution.py:570
  51.4 0.5 shard_map.91.mine
  52.0 2.1 %collective-permute-start.11 = (f32[20,128]{1,0:T(8,128)S(1)}, f32[20,128]{1,0:T(8,128)S(1)}, u32[]{:S(2)}, u32[]{:S(2)}) collective-permute-start(f32[20,128]{1,0:T(8,128)S(1)} %shard_map.91.mine), channel_id=1, source_target_pairs={{0,56},{8,16},{16,8},{24,32},{32,24},{40,48},{48,40},{56,0},{1,57}... | collective-permute-start | bytes 30728 | tf_op jit(solution)/shard_map/ppermute | solution.py:566
  54.4 3.9 %collective-permute-start.12 = (f32[8,128]{1,0:T(8,128)S(1)}, f32[8,128]{1,0:T(8,128)S(1)}, u32[]{:S(2)}, u32[]{:S(2)}) collective-permute-start(f32[8,128]{1,0:T(8,128)S(1)} %slice.42), channel_id=1, source_target_pairs={{0,16},{8,24},{16,0},{24,8},{32,48},{40,56},{48,32},{56,40},{1,17}... | collective-permute-start | bytes 12296 | tf_op jit(solution)/shard_map/ppermute | solution.py:570
  58.2 0.7 collective-permute-done.13.refs_1_
  58.9 0.9 collective-permute-done.12.refs_0_
  60.7 3.1 %collective-permute-start.15 = (f32[8,128]{1,0:T(8,128)S(1)}, f32[8,128]{1,0:T(8,128)S(1)}, u32[]{:S(2)}, u32[]{:S(2)}) collective-permute-start(f32[8,128]{1,0:T(8,128)S(1)} %slice.43), channel_id=1, source_target_pairs={{0,2},{1,3},{2,0},{3,1},{4,6},{5,7},{6,4},{7,5},{8,10},{9,11},{10,... | collective-permute-start | bytes 12296 | tf_op jit(solution)/shard_map/ppermute | solution.py:570
  64.1 1.8 %collective-permute-start.20 = (f32[44,128]{1,0:T(8,128)S(1)}, f32[44,128]{1,0:T(8,128)S(1)}, u32[]{:S(2)}, u32[]{:S(2)}) collective-permute-start(f32[44,128]{1,0:T(8,128)S(1)} %shard_map.92.mine), channel_id=1, source_target_pairs={{0,7},{1,2},{2,1},{3,4},{4,3},{5,6},{6,5},{7,0},{8,15},{9,10},{10,... | collective-permute-start | bytes 67592 | tf_op jit(solution)/shard_map/ppermute | solution.py:566
  65.9 1.6 collective-permute-done.16
  67.5 4.0 %collective-permute-start.19 = (f32[8,128]{1,0:T(8,128)S(1)}, f32[8,128]{1,0:T(8,128)S(1)}, u32[]{:S(2)}, u32[]{:S(2)}) collective-permute-start(f32[8,128]{1,0:T(8,128)S(1)} %fusion.3), channel_id=1, source_target_pairs={{0,36},{1,37},{2,38},{3,39},{4,32},{5,33},{6,34},{7,35},{8,44},{9,... | collective-permute-start | bytes 12296 | tf_op jit(solution)/shard_map/ppermute | solution.py:731
  71.4 2.9 %collective-permute-start.18 = (f32[8,128]{1,0:T(8,128)S(1)}, f32[8,128]{1,0:T(8,128)S(1)}, u32[]{:S(2)}, u32[]{:S(2)}) collective-permute-start(f32[8,128]{1,0:T(8,128)S(1)} %fusion.3), channel_id=1, source_target_pairs={{0,4},{1,5},{2,6},{3,7},{4,0},{5,1},{6,2},{7,3},{8,12},{9,13},{10,... | collective-permute-start | bytes 12296 | tf_op jit(solution)/shard_map/ppermute | solution.py:731
  74.3 0.6 collective-permute-start.17
  75.0 13.2 %shard_map.93.refs_4_ = f32[12,128]{1,0:T(8,128)S(1)} custom-call(s32[12]{0:T(128)S(1)} %stack.63.bounds.info.refs_0_, s32[16,128]{1,0:T(8,128)S(1)} %get-tuple-element.48.listed, f32[112,8,128]{2,1,0:T(8,128)S(1)} %get-tuple-element.49.tiles.refs_6_, f32[32,128]{1,0:T(8,128)S(1)} %get-tuple-element.36.own.refs_1_.refs_0_.start, ...), custom_call_target="tpu_custom_call" | custom-call | flops 268435456 | bytes 262144 | tf_op jit(solution)/shard_map/pallas_call | solution.py:674
  88.2 2.4 %shard_map.94 = (f32[32,128]{1,0:T(8,128)S(1)}, f32[12,128]{1,0:T(8,128)}) custom-call(s32[12]{0:T(128)S(1)} %stack.63.bounds.info.refs_0_, f32[32,128]{1,0:T(8,128)S(1)} %get-tuple-element.36.own.refs_1_.refs_0_.start, f32[26,8,128]{2,1,0:T(8,128)S(1)} %get-tuple-element.46.refs_1_, f32[26,8,128]{2,1,0:T(8,128)S(1)} %get-tuple-element.47.refs_2_.refs_7_, ...), custom_call_target="tpu_custom_call" | custom-call | flops 67108864 | bytes 262144 | tf_op jit(solution)/shard_map/pallas_call | solution.py:687
  90.7 1.5 shard_map.95
  92.4 4.9 %collective-permute-done.22.second = f32[96,128]{1,0:T(8,128)S(1)} collective-permute-done((f32[96,128]{1,0:T(8,128)S(1)}, f32[96,128]{1,0:T(8,128)S(1)}, u32[]{:S(2)}, u32[]{:S(2)}) %collective-permute-start.22) | collective-permute-done | bytes 49184 | tf_op jit(solution)/shard_map/ppermute | solution.py:566
  97.3 0.7 shard_map.96
  97.9 1.0 collective-permute-start.24
  98.9 2.6 %collective-permute-start.23 = (f32[152,128]{1,0:T(8,128)S(1)}, f32[152,128]{1,0:T(8,128)S(1)}, u32[]{:S(2)}, u32[]{:S(2)}) collective-permute-start(f32[152,128]{1,0:T(8,128)S(1)} %get-tuple-element.56.mine), channel_id=1, source_target_pairs={{0,8},{8,0},{16,24},{24,16},{32,40},{40,32},{48,56},{56,48},{1,9},... | collective-permute-start | bytes 233480 | tf_op jit(solution)/shard_map/ppermute | solution.py:566
  101.5 3.0 %collective-permute-done.24.second = f32[152,128]{1,0:T(8,128)S(1)} collective-permute-done((f32[152,128]{1,0:T(8,128)S(1)}, f32[152,128]{1,0:T(8,128)S(1)}, u32[]{:S(2)}, u32[]{:S(2)}) %collective-permute-start.24) | collective-permute-done | bytes 77856 | tf_op jit(solution)/shard_map/ppermute | solution.py:566
  104.5 0.7 shard_map.97
  105.3 1.0 collective-permute-start.26
  106.3 1.1 collective-permute-start.25
  107.4 2.9 %collective-permute-done.26.refs_5_ = f32[248,128]{1,0:T(8,128)S(1)} collective-permute-done((f32[248,128]{1,0:T(8,128)S(1)}, f32[248,128]{1,0:T(8,128)S(1)}, u32[]{:S(2)}, u32[]{:S(2)}) %collective-permute-start.26) | collective-permute-done | bytes 127008 | tf_op jit(solution)/shard_map/ppermute | solution.py:566
  110.3 0.9 collective-permute-done.25.refs_4_
  111.2 2.0 %shard_map.98 = (s32[16,128]{1,0:T(8,128)S(1)}, f32[112,8,128]{2,1,0:T(8,128)S(1)}, f32[26,8,128]{2,1,0:T(8,128)S(1)}, f32[8,128]{1,0:T(8,128)S(1)}) custom-call(s32[12]{0:T(128)S(1)} %stack.63.bounds.info.refs_0_, f32[32,128]{1,0:T(8,128)S(1)} %get-tuple-element.51.own.refs_1_.refs_0_, f32[208,128]{1,0:T(8,128)S(1)} %bitcast.27, ...), custom_call_target="tpu_custom_call" | custom-call | flops 4194304 | bytes 262144 | tf_op jit(solution)/shard_map/pallas_call | solution.py:631
  113.2 7.8 %shard_map.99.mine.own_radius = f32[12,128]{1,0:T(8,128)S(1)} custom-call(s32[16,128]{1,0:T(8,128)S(1)} %get-tuple-element.62.listed, f32[112,8,128]{2,1,0:T(8,128)S(1)} %get-tuple-element.63.tiles, f32[32,128]{1,0:T(8,128)S(1)} %get-tuple-element.51.own.refs_1_.refs_0_, f32[8,128]{1,0:T(8,128)S(1)} %get-tuple-element.64.sums), custom_call_target="tpu_custom_call" | custom-call | flops 134217728 | bytes 262144 | tf_op jit(solution)/shard_map/pallas_call | solution.py:646
  121.5 2.9 %collective-permute-start.30 = (f32[8,128]{1,0:T(8,128)S(1)}, f32[8,128]{1,0:T(8,128)S(1)}, u32[]{:S(2)}, u32[]{:S(2)}) collective-permute-start(f32[8,128]{1,0:T(8,128)S(1)} %get-tuple-element.64.sums), channel_id=1, source_target_pairs={{0,192},{64,128},{128,64},{192,0},{1,193},{65,129},{129,65},{193,1... | collective-permute-start | bytes 12296 | tf_op jit(solution)/shard_map/ppermute | solution.py:570
  124.4 0.7 collective-permute-start.29
  125.1 1.0 collective-permute-done.30.refs_1_
  126.1 3.4 %collective-permute-done.29.refs_0_ = f32[8,128]{1,0:T(8,128)S(1)} collective-permute-done((f32[8,128]{1,0:T(8,128)S(1)}, f32[8,128]{1,0:T(8,128)S(1)}, u32[]{:S(2)}, u32[]{:S(2)}) %collective-permute-start.29) | collective-permute-done | bytes 4128 | tf_op jit(solution)/shard_map/ppermute | solution.py:570
  130.1 1.5 collective-permute-start.32
  131.6 0.9 collective-permute-start.34
  132.5 3.2 %collective-permute-start.33 = (f32[8,128]{1,0:T(8,128)S(1)}, f32[8,128]{1,0:T(8,128)S(1)}, u32[]{:S(2)}, u32[]{:S(2)}) collective-permute-start(f32[8,128]{1,0:T(8,128)S(1)} %slice.45), channel_id=1, source_target_pairs={{0,16},{8,24},{16,0},{24,8},{32,48},{40,56},{48,32},{56,40},{1,17}... | collective-permute-start | bytes 12296 | tf_op jit(solution)/shard_map/ppermute | solution.py:570
  135.7 0.7 collective-permute-done.34.refs_1_
  136.4 1.2 collective-permute-done.33.refs_0_
  138.4 4.1 %collective-permute-start.36 = (f32[8,128]{1,0:T(8,128)S(1)}, f32[8,128]{1,0:T(8,128)S(1)}, u32[]{:S(2)}, u32[]{:S(2)}) collective-permute-start(f32[8,128]{1,0:T(8,128)S(1)} %slice.46), channel_id=1, source_target_pairs={{0,2},{1,3},{2,0},{3,1},{4,6},{5,7},{6,4},{7,5},{8,10},{9,11},{10,... | collective-permute-start | bytes 12296 | tf_op jit(solution)/shard_map/ppermute | solution.py:570
  142.9 0.8 slice.50
  143.7 1.8 %collective-permute-start.41 = (f32[44,128]{1,0:T(8,128)S(1)}, f32[44,128]{1,0:T(8,128)S(1)}, u32[]{:S(2)}, u32[]{:S(2)}) collective-permute-start(f32[44,128]{1,0:T(8,128)S(1)} %shard_map.101.mine), channel_id=1, source_target_pairs={{0,7},{1,2},{2,1},{3,4},{4,3},{5,6},{6,5},{7,0},{8,15},{9,10},{10,... | collective-permute-start | bytes 67592 | tf_op jit(solution)/shard_map/ppermute | solution.py:566
  145.5 0.6 collective-permute-done.37
  146.1 4.1 %collective-permute-start.40 = (f32[8,128]{1,0:T(8,128)S(1)}, f32[8,128]{1,0:T(8,128)S(1)}, u32[]{:S(2)}, u32[]{:S(2)}) collective-permute-start(f32[8,128]{1,0:T(8,128)S(1)} %fusion.1), channel_id=1, source_target_pairs={{0,36},{1,37},{2,38},{3,39},{4,32},{5,33},{6,34},{7,35},{8,44},{9,... | collective-permute-start | bytes 12296 | tf_op jit(solution)/shard_map/ppermute | solution.py:731
  150.2 3.8 %collective-permute-start.39 = (f32[8,128]{1,0:T(8,128)S(1)}, f32[8,128]{1,0:T(8,128)S(1)}, u32[]{:S(2)}, u32[]{:S(2)}) collective-permute-start(f32[8,128]{1,0:T(8,128)S(1)} %fusion.1), channel_id=1, source_target_pairs={{0,4},{1,5},{2,6},{3,7},{4,0},{5,1},{6,2},{7,3},{8,12},{9,13},{10,... | collective-permute-start | bytes 12296 | tf_op jit(solution)/shard_map/ppermute | solution.py:731
  153.9 13.2 %shard_map.102.refs_4_ = f32[12,128]{1,0:T(8,128)S(1)} custom-call(s32[12]{0:T(128)S(1)} %stack.63.bounds.info.refs_0_, s32[16,128]{1,0:T(8,128)S(1)} %get-tuple-element.62.listed, f32[112,8,128]{2,1,0:T(8,128)S(1)} %get-tuple-element.63.tiles, f32[32,128]{1,0:T(8,128)S(1)} %get-tuple-element.51.own.refs_1_.refs_0_, ...), custom_call_target="tpu_custom_call" | custom-call | flops 268435456 | bytes 262144 | tf_op jit(solution)/shard_map/pallas_call | solution.py:674
  167.2 1.8 %shard_map.103 = (f32[32,128]{1,0:T(8,128)S(1)}, f32[12,128]{1,0:T(8,128)S(1)}) custom-call(s32[12]{0:T(128)S(1)} %stack.63.bounds.info.refs_0_, f32[32,128]{1,0:T(8,128)S(1)} %get-tuple-element.51.own.refs_1_.refs_0_, f32[26,8,128]{2,1,0:T(8,128)S(1)} %get-tuple-element.61.refs_1_, f32[26,8,128]{2,1,0:T(8,128)S(1)} %get-tuple-element.47.refs_2_.refs_7_, ...), custom_call_target="tpu_custom_call" | custom-call | flops 67108864 | bytes 262144 | tf_op jit(solution)/shard_map/pallas_call | solution.py:687
  169.3 0.6 squeeze.9
  169.9 0.6 squeeze.8
  (67 shorter events, 6.0 us)
Async XLA Ops:
  0.6 1.5 copy-start.3
  2.1 0.7 copy-start.1
  2.1 0.7 copy-start.2
  2.1 0.7 copy-start
  6.2 6.6 %collective-permute-start.1 = (f32[184,128]{1,0:T(8,128)S(1)}, f32[184,128]{1,0:T(8,128)S(1)}, u32[]{:S(2)}, u32[]{:S(2)}) collective-permute-start(f32[184,128]{1,0:T(8,128)S(1)} %get-tuple-element.39), channel_id=1, source_target_pairs={{0,192},{64,128},{128,64},{192,0},{1,193},{65,129},{129,65},{193,1... | collective-permute-start | bytes 282632 | tf_op jit(solution)/shard_map/ppermute | solution.py:566
  7.0 5.8 %collective-permute-start = (f32[184,128]{1,0:T(8,128)S(1)}, f32[184,128]{1,0:T(8,128)S(1)}, u32[]{:S(2)}, u32[]{:S(2)}) collective-permute-start(f32[184,128]{1,0:T(8,128)S(1)} %get-tuple-element.38.mine), channel_id=1, source_target_pairs={{0,64},{64,0},{128,192},{192,128},{1,65},{65,1},{129,193},{193,129... | collective-permute-start | bytes 282632 | tf_op jit(solution)/shard_map/ppermute | solution.py:566
  13.6 8.0 %collective-permute-start.3 = (f32[280,128]{1,0:T(8,128)S(1)}, f32[280,128]{1,0:T(8,128)S(1)}, u32[]{:S(2)}, u32[]{:S(2)}) collective-permute-start(f32[280,128]{1,0:T(8,128)S(1)} %get-tuple-element.42), channel_id=1, source_target_pairs={{0,56},{8,16},{16,8},{24,32},{32,24},{40,48},{48,40},{56,0},{1,57}... | collective-permute-start | bytes 430088 | tf_op jit(solution)/shard_map/ppermute | solution.py:566
  16.6 5.5 %collective-permute-start.2 = (f32[280,128]{1,0:T(8,128)S(1)}, f32[280,128]{1,0:T(8,128)S(1)}, u32[]{:S(2)}, u32[]{:S(2)}) collective-permute-start(f32[280,128]{1,0:T(8,128)S(1)} %get-tuple-element.41.mine), channel_id=1, source_target_pairs={{0,8},{8,0},{16,24},{24,16},{32,40},{40,32},{48,56},{56,48},{1,9},... | collective-permute-start | bytes 430088 | tf_op jit(solution)/shard_map/ppermute | solution.py:566
  22.9 6.5 %collective-permute-start.5 = (f32[424,128]{1,0:T(8,128)S(1)}, f32[424,128]{1,0:T(8,128)S(1)}, u32[]{:S(2)}, u32[]{:S(2)}) collective-permute-start(f32[424,128]{1,0:T(8,128)S(1)} %get-tuple-element.45), channel_id=1, source_target_pairs={{0,7},{1,2},{2,1},{3,4},{4,3},{5,6},{6,5},{7,0},{8,15},{9,10},{10,... | collective-permute-start | bytes 651272 | tf_op jit(solution)/shard_map/ppermute | solution.py:566
  24.9 8.2 %collective-permute-start.4 = (f32[424,128]{1,0:T(8,128)S(1)}, f32[424,128]{1,0:T(8,128)S(1)}, u32[]{:S(2)}, u32[]{:S(2)}) collective-permute-start(f32[424,128]{1,0:T(8,128)S(1)} %get-tuple-element.44.refs_3_), channel_id=1, source_target_pairs={{0,1},{1,0},{2,3},{3,2},{4,5},{5,4},{6,7},{7,6},{8,9},{9,8},{10,11... | collective-permute-start | bytes 651272 | tf_op jit(solution)/shard_map/ppermute | solution.py:566
  43.0 8.5 %collective-permute-start.7 = (f32[12,128]{1,0:T(8,128)S(1)}, f32[12,128]{1,0:T(8,128)S(1)}, u32[]{:S(2)}, u32[]{:S(2)}) collective-permute-start(f32[12,128]{1,0:T(8,128)S(1)} %shard_map.90.mine.own_radius), channel_id=1, source_target_pairs={{0,192},{64,128},{128,64},{192,0},{1,193},{65,129},{129,65},{193,1... | collective-permute-start | bytes 18440 | tf_op jit(solution)/shard_map/ppermute | solution.py:566
  43.1 8.4 %collective-permute-start.6 = (f32[12,128]{1,0:T(8,128)S(1)}, f32[12,128]{1,0:T(8,128)S(1)}, u32[]{:S(2)}, u32[]{:S(2)}) collective-permute-start(f32[12,128]{1,0:T(8,128)S(1)} %shard_map.90.mine.own_radius), channel_id=1, source_target_pairs={{0,64},{64,0},{128,192},{192,128},{1,65},{65,1},{129,193},{193,129... | collective-permute-start | bytes 18440 | tf_op jit(solution)/shard_map/ppermute | solution.py:566
  43.2 4.6 %collective-permute-start.9 = (f32[8,128]{1,0:T(8,128)S(1)}, f32[8,128]{1,0:T(8,128)S(1)}, u32[]{:S(2)}, u32[]{:S(2)}) collective-permute-start(f32[8,128]{1,0:T(8,128)S(1)} %get-tuple-element.50.sums), channel_id=1, source_target_pairs={{0,192},{64,128},{128,64},{192,0},{1,193},{65,129},{129,65},{193,1... | collective-permute-start | bytes 12296 | tf_op jit(solution)/shard_map/ppermute | solution.py:570
  46.3 5.1 %collective-permute-start.8 = (f32[8,128]{1,0:T(8,128)S(1)}, f32[8,128]{1,0:T(8,128)S(1)}, u32[]{:S(2)}, u32[]{:S(2)}) collective-permute-start(f32[8,128]{1,0:T(8,128)S(1)} %get-tuple-element.50.sums), channel_id=1, source_target_pairs={{0,128},{64,192},{128,0},{192,64},{1,129},{65,193},{129,1},{193,65... | collective-permute-start | bytes 12296 | tf_op jit(solution)/shard_map/ppermute | solution.py:570
  52.0 7.8 %collective-permute-start.11 = (f32[20,128]{1,0:T(8,128)S(1)}, f32[20,128]{1,0:T(8,128)S(1)}, u32[]{:S(2)}, u32[]{:S(2)}) collective-permute-start(f32[20,128]{1,0:T(8,128)S(1)} %shard_map.91.mine), channel_id=1, source_target_pairs={{0,56},{8,16},{16,8},{24,32},{32,24},{40,48},{48,40},{56,0},{1,57}... | collective-permute-start | bytes 30728 | tf_op jit(solution)/shard_map/ppermute | solution.py:566
  54.1 5.7 %collective-permute-start.10 = (f32[20,128]{1,0:T(8,128)S(1)}, f32[20,128]{1,0:T(8,128)S(1)}, u32[]{:S(2)}, u32[]{:S(2)}) collective-permute-start(f32[20,128]{1,0:T(8,128)S(1)} %shard_map.91.mine), channel_id=1, source_target_pairs={{0,8},{8,0},{16,24},{24,16},{32,40},{40,32},{48,56},{56,48},{1,9},... | collective-permute-start | bytes 30728 | tf_op jit(solution)/shard_map/ppermute | solution.py:566
  54.1 4.8 %collective-permute-start.13 = (f32[8,128]{1,0:T(8,128)S(1)}, f32[8,128]{1,0:T(8,128)S(1)}, u32[]{:S(2)}, u32[]{:S(2)}) collective-permute-start(f32[8,128]{1,0:T(8,128)S(1)} %slice.42), channel_id=1, source_target_pairs={{0,24},{8,16},{16,8},{24,0},{32,56},{40,48},{48,40},{56,32},{1,25}... | collective-permute-start | bytes 12296 | tf_op jit(solution)/shard_map/ppermute | solution.py:570
  54.4 5.4 %collective-permute-start.12 = (f32[8,128]{1,0:T(8,128)S(1)}, f32[8,128]{1,0:T(8,128)S(1)}, u32[]{:S(2)}, u32[]{:S(2)}) collective-permute-start(f32[8,128]{1,0:T(8,128)S(1)} %slice.42), channel_id=1, source_target_pairs={{0,16},{8,24},{16,0},{24,8},{32,48},{40,56},{48,32},{56,40},{1,17}... | collective-permute-start | bytes 12296 | tf_op jit(solution)/shard_map/ppermute | solution.py:570
  60.4 7.1 %collective-permute-start.14 = (f32[44,128]{1,0:T(8,128)S(1)}, f32[44,128]{1,0:T(8,128)S(1)}, u32[]{:S(2)}, u32[]{:S(2)}) collective-permute-start(f32[44,128]{1,0:T(8,128)S(1)} %shard_map.92.mine), channel_id=1, source_target_pairs={{0,1},{1,0},{2,3},{3,2},{4,5},{5,4},{6,7},{7,6},{8,9},{9,8},{10,11... | collective-permute-start | bytes 67592 | tf_op jit(solution)/shard_map/ppermute | solution.py:566
  60.7 5.2 %collective-permute-start.15 = (f32[8,128]{1,0:T(8,128)S(1)}, f32[8,128]{1,0:T(8,128)S(1)}, u32[]{:S(2)}, u32[]{:S(2)}) collective-permute-start(f32[8,128]{1,0:T(8,128)S(1)} %slice.43), channel_id=1, source_target_pairs={{0,2},{1,3},{2,0},{3,1},{4,6},{5,7},{6,4},{7,5},{8,10},{9,11},{10,... | collective-permute-start | bytes 12296 | tf_op jit(solution)/shard_map/ppermute | solution.py:570
  63.9 3.6 %collective-permute-start.16 = (f32[8,128]{1,0:T(8,128)S(1)}, f32[8,128]{1,0:T(8,128)S(1)}, u32[]{:S(2)}, u32[]{:S(2)}) collective-permute-start(f32[8,128]{1,0:T(8,128)S(1)} %slice.43), channel_id=1, source_target_pairs={{0,3},{1,2},{2,1},{3,0},{4,7},{5,6},{6,5},{7,4},{8,11},{9,10},{10,... | collective-permute-start | bytes 12296 | tf_op jit(solution)/shard_map/ppermute | solution.py:570
  64.1 10.8 %collective-permute-start.20 = (f32[44,128]{1,0:T(8,128)S(1)}, f32[44,128]{1,0:T(8,128)S(1)}, u32[]{:S(2)}, u32[]{:S(2)}) collective-permute-start(f32[44,128]{1,0:T(8,128)S(1)} %shard_map.92.mine), channel_id=1, source_target_pairs={{0,7},{1,2},{2,1},{3,4},{4,3},{5,6},{6,5},{7,0},{8,15},{9,10},{10,... | collective-permute-start | bytes 67592 | tf_op jit(solution)/shard_map/ppermute | solution.py:566
  67.5 20.7 %collective-permute-start.19 = (f32[8,128]{1,0:T(8,128)S(1)}, f32[8,128]{1,0:T(8,128)S(1)}, u32[]{:S(2)}, u32[]{:S(2)}) collective-permute-start(f32[8,128]{1,0:T(8,128)S(1)} %fusion.3), channel_id=1, source_target_pairs={{0,36},{1,37},{2,38},{3,39},{4,32},{5,33},{6,34},{7,35},{8,44},{9,... | collective-permute-start | bytes 12296 | tf_op jit(solution)/shard_map/ppermute | solution.py:731
  71.4 16.8 %collective-permute-start.18 = (f32[8,128]{1,0:T(8,128)S(1)}, f32[8,128]{1,0:T(8,128)S(1)}, u32[]{:S(2)}, u32[]{:S(2)}) collective-permute-start(f32[8,128]{1,0:T(8,128)S(1)} %fusion.3), channel_id=1, source_target_pairs={{0,4},{1,5},{2,6},{3,7},{4,0},{5,1},{6,2},{7,3},{8,12},{9,13},{10,... | collective-permute-start | bytes 12296 | tf_op jit(solution)/shard_map/ppermute | solution.py:731
  74.3 13.9 %collective-permute-start.17 = (f32[8,128]{1,0:T(8,128)S(1)}, f32[8,128]{1,0:T(8,128)S(1)}, u32[]{:S(2)}, u32[]{:S(2)}) collective-permute-start(f32[8,128]{1,0:T(8,128)S(1)} %fusion.3), channel_id=1, source_target_pairs={{0,32},{1,33},{2,34},{3,35},{4,36},{5,37},{6,38},{7,39},{8,40},{9,... | collective-permute-start | bytes 12296 | tf_op jit(solution)/shard_map/ppermute | solution.py:731
  92.2 5.1 %collective-permute-start.22 = (f32[96,128]{1,0:T(8,128)S(1)}, f32[96,128]{1,0:T(8,128)S(1)}, u32[]{:S(2)}, u32[]{:S(2)}) collective-permute-start(f32[96,128]{1,0:T(8,128)S(1)} %get-tuple-element.54), channel_id=1, source_target_pairs={{0,192},{64,128},{128,64},{192,0},{1,193},{65,129},{129,65},{193,1... | collective-permute-start | bytes 147464 | tf_op jit(solution)/shard_map/ppermute | solution.py:566
  92.3 5.0 %collective-permute-start.21 = (f32[96,128]{1,0:T(8,128)S(1)}, f32[96,128]{1,0:T(8,128)S(1)}, u32[]{:S(2)}, u32[]{:S(2)}) collective-permute-start(f32[96,128]{1,0:T(8,128)S(1)} %get-tuple-element.53.mine), channel_id=1, source_target_pairs={{0,64},{64,0},{128,192},{192,128},{1,65},{65,1},{129,193},{193,129... | collective-permute-start | bytes 147464 | tf_op jit(solution)/shard_map/ppermute | solution.py:566
  97.9 6.6 %collective-permute-start.24 = (f32[152,128]{1,0:T(8,128)S(1)}, f32[152,128]{1,0:T(8,128)S(1)}, u32[]{:S(2)}, u32[]{:S(2)}) collective-permute-start(f32[152,128]{1,0:T(8,128)S(1)} %get-tuple-element.57), channel_id=1, source_target_pairs={{0,56},{8,16},{16,8},{24,32},{32,24},{40,48},{48,40},{56,0},{1,57}... | collective-permute-start | bytes 233480 | tf_op jit(solution)/shard_map/ppermute | solution.py:566
  98.9 5.6 %collective-permute-start.23 = (f32[152,128]{1,0:T(8,128)S(1)}, f32[152,128]{1,0:T(8,128)S(1)}, u32[]{:S(2)}, u32[]{:S(2)}) collective-permute-start(f32[152,128]{1,0:T(8,128)S(1)} %get-tuple-element.56.mine), channel_id=1, source_target_pairs={{0,8},{8,0},{16,24},{24,16},{32,40},{40,32},{48,56},{56,48},{1,9},... | collective-permute-start | bytes 233480 | tf_op jit(solution)/shard_map/ppermute | solution.py:566
  105.3 5.0 %collective-permute-start.26 = (f32[248,128]{1,0:T(8,128)S(1)}, f32[248,128]{1,0:T(8,128)S(1)}, u32[]{:S(2)}, u32[]{:S(2)}) collective-permute-start(f32[248,128]{1,0:T(8,128)S(1)} %get-tuple-element.60), channel_id=1, source_target_pairs={{0,7},{1,2},{2,1},{3,4},{4,3},{5,6},{6,5},{7,0},{8,15},{9,10},{10,... | collective-permute-start | bytes 380936 | tf_op jit(solution)/shard_map/ppermute | solution.py:566
  106.3 4.9 %collective-permute-start.25 = (f32[248,128]{1,0:T(8,128)S(1)}, f32[248,128]{1,0:T(8,128)S(1)}, u32[]{:S(2)}, u32[]{:S(2)}) collective-permute-start(f32[248,128]{1,0:T(8,128)S(1)} %get-tuple-element.59.refs_3_), channel_id=1, source_target_pairs={{0,1},{1,0},{2,3},{3,2},{4,5},{5,4},{6,7},{7,6},{8,9},{9,8},{10,11... | collective-permute-start | bytes 380936 | tf_op jit(solution)/shard_map/ppermute | solution.py:566
  121.1 8.5 %collective-permute-start.28 = (f32[12,128]{1,0:T(8,128)S(1)}, f32[12,128]{1,0:T(8,128)S(1)}, u32[]{:S(2)}, u32[]{:S(2)}) collective-permute-start(f32[12,128]{1,0:T(8,128)S(1)} %shard_map.99.mine.own_radius), channel_id=1, source_target_pairs={{0,192},{64,128},{128,64},{192,0},{1,193},{65,129},{129,65},{193,1... | collective-permute-start | bytes 18440 | tf_op jit(solution)/shard_map/ppermute | solution.py:566
  121.2 8.4 %collective-permute-start.27 = (f32[12,128]{1,0:T(8,128)S(1)}, f32[12,128]{1,0:T(8,128)S(1)}, u32[]{:S(2)}, u32[]{:S(2)}) collective-permute-start(f32[12,128]{1,0:T(8,128)S(1)} %shard_map.99.mine.own_radius), channel_id=1, source_target_pairs={{0,64},{64,0},{128,192},{192,128},{1,65},{65,1},{129,193},{193,129... | collective-permute-start | bytes 18440 | tf_op jit(solution)/shard_map/ppermute | solution.py:566
  121.5 4.6 %collective-permute-start.30 = (f32[8,128]{1,0:T(8,128)S(1)}, f32[8,128]{1,0:T(8,128)S(1)}, u32[]{:S(2)}, u32[]{:S(2)}) collective-permute-start(f32[8,128]{1,0:T(8,128)S(1)} %get-tuple-element.64.sums), channel_id=1, source_target_pairs={{0,192},{64,128},{128,64},{192,0},{1,193},{65,129},{129,65},{193,1... | collective-permute-start | bytes 12296 | tf_op jit(solution)/shard_map/ppermute | solution.py:570
  124.4 5.1 %collective-permute-start.29 = (f32[8,128]{1,0:T(8,128)S(1)}, f32[8,128]{1,0:T(8,128)S(1)}, u32[]{:S(2)}, u32[]{:S(2)}) collective-permute-start(f32[8,128]{1,0:T(8,128)S(1)} %get-tuple-element.64.sums), channel_id=1, source_target_pairs={{0,128},{64,192},{128,0},{192,64},{1,129},{65,193},{129,1},{193,65... | collective-permute-start | bytes 12296 | tf_op jit(solution)/shard_map/ppermute | solution.py:570
  130.1 7.5 %collective-permute-start.32 = (f32[20,128]{1,0:T(8,128)S(1)}, f32[20,128]{1,0:T(8,128)S(1)}, u32[]{:S(2)}, u32[]{:S(2)}) collective-permute-start(f32[20,128]{1,0:T(8,128)S(1)} %shard_map.100.mine), channel_id=1, source_target_pairs={{0,56},{8,16},{16,8},{24,32},{32,24},{40,48},{48,40},{56,0},{1,57}... | collective-permute-start | bytes 30728 | tf_op jit(solution)/shard_map/ppermute | solution.py:566
  131.6 6.0 %collective-permute-start.31 = (f32[20,128]{1,0:T(8,128)S(1)}, f32[20,128]{1,0:T(8,128)S(1)}, u32[]{:S(2)}, u32[]{:S(2)}) collective-permute-start(f32[20,128]{1,0:T(8,128)S(1)} %shard_map.100.mine), channel_id=1, source_target_pairs={{0,8},{8,0},{16,24},{24,16},{32,40},{40,32},{48,56},{56,48},{1,9},... | collective-permute-start | bytes 30728 | tf_op jit(solution)/shard_map/ppermute | solution.py:566
  131.6 4.8 %collective-permute-start.34 = (f32[8,128]{1,0:T(8,128)S(1)}, f32[8,128]{1,0:T(8,128)S(1)}, u32[]{:S(2)}, u32[]{:S(2)}) collective-permute-start(f32[8,128]{1,0:T(8,128)S(1)} %slice.45), channel_id=1, source_target_pairs={{0,24},{8,16},{16,8},{24,0},{32,56},{40,48},{48,40},{56,32},{1,25}... | collective-permute-start | bytes 12296 | tf_op jit(solution)/shard_map/ppermute | solution.py:570
  132.5 5.1 %collective-permute-start.33 = (f32[8,128]{1,0:T(8,128)S(1)}, f32[8,128]{1,0:T(8,128)S(1)}, u32[]{:S(2)}, u32[]{:S(2)}) collective-permute-start(f32[8,128]{1,0:T(8,128)S(1)} %slice.45), channel_id=1, source_target_pairs={{0,16},{8,24},{16,0},{24,8},{32,48},{40,56},{48,32},{56,40},{1,17}... | collective-permute-start | bytes 12296 | tf_op jit(solution)/shard_map/ppermute | solution.py:570
  138.2 7.9 %collective-permute-start.35 = (f32[44,128]{1,0:T(8,128)S(1)}, f32[44,128]{1,0:T(8,128)S(1)}, u32[]{:S(2)}, u32[]{:S(2)}) collective-permute-start(f32[44,128]{1,0:T(8,128)S(1)} %shard_map.101.mine), channel_id=1, source_target_pairs={{0,1},{1,0},{2,3},{3,2},{4,5},{5,4},{6,7},{7,6},{8,9},{9,8},{10,11... | collective-permute-start | bytes 67592 | tf_op jit(solution)/shard_map/ppermute | solution.py:566
  138.4 7.0 %collective-permute-start.36 = (f32[8,128]{1,0:T(8,128)S(1)}, f32[8,128]{1,0:T(8,128)S(1)}, u32[]{:S(2)}, u32[]{:S(2)}) collective-permute-start(f32[8,128]{1,0:T(8,128)S(1)} %slice.46), channel_id=1, source_target_pairs={{0,2},{1,3},{2,0},{3,1},{4,6},{5,7},{6,4},{7,5},{8,10},{9,11},{10,... | collective-permute-start | bytes 12296 | tf_op jit(solution)/shard_map/ppermute | solution.py:570
  142.5 3.6 %collective-permute-start.37 = (f32[8,128]{1,0:T(8,128)S(1)}, f32[8,128]{1,0:T(8,128)S(1)}, u32[]{:S(2)}, u32[]{:S(2)}) collective-permute-start(f32[8,128]{1,0:T(8,128)S(1)} %slice.46), channel_id=1, source_target_pairs={{0,3},{1,2},{2,1},{3,0},{4,7},{5,6},{6,5},{7,4},{8,11},{9,10},{10,... | collective-permute-start | bytes 12296 | tf_op jit(solution)/shard_map/ppermute | solution.py:570
  143.7 10.3 %collective-permute-start.41 = (f32[44,128]{1,0:T(8,128)S(1)}, f32[44,128]{1,0:T(8,128)S(1)}, u32[]{:S(2)}, u32[]{:S(2)}) collective-permute-start(f32[44,128]{1,0:T(8,128)S(1)} %shard_map.101.mine), channel_id=1, source_target_pairs={{0,7},{1,2},{2,1},{3,4},{4,3},{5,6},{6,5},{7,0},{8,15},{9,10},{10,... | collective-permute-start | bytes 67592 | tf_op jit(solution)/shard_map/ppermute | solution.py:566
  146.1 21.1 %collective-permute-start.40 = (f32[8,128]{1,0:T(8,128)S(1)}, f32[8,128]{1,0:T(8,128)S(1)}, u32[]{:S(2)}, u32[]{:S(2)}) collective-permute-start(f32[8,128]{1,0:T(8,128)S(1)} %fusion.1), channel_id=1, source_target_pairs={{0,36},{1,37},{2,38},{3,39},{4,32},{5,33},{6,34},{7,35},{8,44},{9,... | collective-permute-start | bytes 12296 | tf_op jit(solution)/shard_map/ppermute | solution.py:731
  150.2 17.0 %collective-permute-start.39 = (f32[8,128]{1,0:T(8,128)S(1)}, f32[8,128]{1,0:T(8,128)S(1)}, u32[]{:S(2)}, u32[]{:S(2)}) collective-permute-start(f32[8,128]{1,0:T(8,128)S(1)} %fusion.1), channel_id=1, source_target_pairs={{0,4},{1,5},{2,6},{3,7},{4,0},{5,1},{6,2},{7,3},{8,12},{9,13},{10,... | collective-permute-start | bytes 12296 | tf_op jit(solution)/shard_map/ppermute | solution.py:731
  153.9 13.3 %collective-permute-start.38 = (f32[8,128]{1,0:T(8,128)S(1)}, f32[8,128]{1,0:T(8,128)S(1)}, u32[]{:S(2)}, u32[]{:S(2)}) collective-permute-start(f32[8,128]{1,0:T(8,128)S(1)} %fusion.1), channel_id=1, source_target_pairs={{0,32},{1,33},{2,34},{3,35},{4,36},{5,37},{6,38},{7,39},{8,40},{9,... | collective-permute-start | bytes 12296 | tf_op jit(solution)/shard_map/ppermute | solution.py:731

commit v5 on v4

--- a/solution.py
+++ b/solution.py
@@ -56,7 +56,8 @@
 
 BLOCK = 32
 BLOCKS = SLOTS // BLOCK
-UNROLL = 8
+MANY = 16
+FEW = 4
 CELLS = 27
 EMPTY = CELLS * TILES
 ROOM = EMPTY + 4
@@ -313,22 +314,24 @@
         give_shares(info, axis + 1, merged, number * PLANES, (out_first, out_second), base)
 
 
-def radius_merge_kernel(axis, count, extra, info, mine, first, second, *refs):
-    others, out = refs[:extra], refs[extra]
-    after_first, valid = arrivals(info, axis)
+def radius_merge_kernel(axis, count, info, mine, first, second, out):
+    after_first, _ = arrivals(info, axis)
     span = count * TILES
     out[span : 2 * span, :] = mine[0:span, :]
     slots = (jnp.where(after_first, 2 * span, 0), jnp.where(after_first, 0, 2 * span))
     for source, slot in zip((first, second), slots):
         out[pl.ds(pl.multiple_of(slot, 8), span), :] = source[0:span, :]
-    total = mine[span : span + 8, :] + first[span : span + 8, :]
-    for other in others:
-        total = total + other[...]
-    out[3 * span : 3 * span + 8, :] = total
-
-
-def born_kernel(listed, tiles, own, sums, out, col, acc):
-    out[TILES : TILES + 8, :] = sums[...]
+    out[3 * span : 3 * span + 8, :] = mine[span : span + 8, :] + first[span : span + 8, :]
+
+
+def over_tiles(count, some, carry):
+    whole = count // MANY
+    carry = lax.fori_loop(0, whole, lambda i, c: some(MANY, i * MANY, c), carry)
+    rest = (count - whole * MANY + FEW - 1) // FEW
+    return lax.fori_loop(0, rest, lambda i, c: some(FEW, whole * MANY + i * FEW, c), carry)
+
+
+def born_kernel(listed, tiles, own, out, col, acc):
     for channel in range(3):
         for tile in range(TILES):
             row = own[4 * channel + tile : 4 * channel + tile + 1, :] * (1.0 / CUTOFF)
@@ -338,20 +341,19 @@
         at = pl.ds(pl.multiple_of(ib * BLOCK, BLOCK), BLOCK)
         xi, yi, zi = col[0, at, :], col[1, at, :], col[2, at, :]
 
-        def some(chunk, total):
-            for k in range(UNROLL):
-                tile = listed[ib, chunk * UNROLL + k]
+        def some(width, start, total):
+            for k in range(width):
+                tile = listed[ib, start + k]
                 dx = xi - tiles[tile, 0:1, :]
                 dy = yi - tiles[tile, 1:2, :]
                 dz = zi - tiles[tile, 2:3, :]
                 u = dx * dx + dy * dy + dz * dz
                 s = jnp.maximum(1.0 - u, 0.0)
-                e = jnp.exp(u * (-CUTOFF * CUTOFF / 8.0))
+                e = jnp.exp2(u * (-CUTOFF * CUTOFF / 8.0 * math.log2(math.e)))
                 total = total + (e * s) * (s * tiles[tile, 3:4, :])
             return total
 
-        chunks = (listed[ib, LANES - 1] + UNROLL - 1) // UNROLL
-        acc[at, :] = lax.fori_loop(0, chunks, some, jnp.zeros((BLOCK, LANES), jnp.float32))
+        acc[at, :] = over_tiles(listed[ib, LANES - 1], some, jnp.zeros((BLOCK, LANES), jnp.float32))
         return carry
 
     lax.fori_loop(0, BLOCKS, block, 0)
@@ -368,7 +370,7 @@
             col[channel, at, :] = spread(row)
         radius = spread(own_radius[tile : tile + 1, :] * (1.0 / CUTOFF))
         col[3, at, :] = radius
-        col[4, at, :] = -0.5 / radius
+        col[4, at, :] = (-0.5 * math.log2(math.e)) / radius
     rows[EMPTY:ROOM] = jnp.ones((ROOM - EMPTY, 2, LANES), jnp.float32)
 
     after_first, _ = arrivals(info, 2)
@@ -386,16 +388,16 @@
         xi, yi, zi = col[0, at, :], col[1, at, :], col[2, at, :]
         ri, ai = col[3, at, :], col[4, at, :]
 
-        def some(chunk, force):
+        def some(width, start, force):
             fx, fy, fz = force
-            for k in range(UNROLL):
-                tile = listed[ib, chunk * UNROLL + k]
+            for k in range(width):
+                tile = listed[ib, start + k]
                 dx = xi - tiles[tile, 0:1, :]
                 dy = yi - tiles[tile, 1:2, :]
                 dz = zi - tiles[tile, 2:3, :]
                 u = dx * dx + dy * dy + dz * dz
                 s = jnp.maximum(1.0 - u, 0.0)
-                e = jnp.exp(u * (ai * rows[tile, 1:2, :]))
+                e = jnp.exp2(u * (ai * rows[tile, 1:2, :]))
                 inv = lax.rsqrt(u + (ri * rows[tile, 0:1, :]) * e)
                 t = s * inv
                 m = (tiles[tile, 4:5, :] * t) * (1.0 + (t * inv) * (0.25 - 0.0625 * e))
@@ -404,9 +406,8 @@
                 fz = fz + m * dz
             return fx, fy, fz
 
-        chunks = (listed[ib, LANES - 1] + UNROLL - 1) // UNROLL
         zero = jnp.zeros((BLOCK, LANES), jnp.float32)
-        force = lax.fori_loop(0, chunks, some, (zero, zero, zero))
+        force = over_tiles(listed[ib, LANES - 1], some, (zero, zero, zero))
         for channel in range(3):
             acc[channel, at, :] = force[channel]
         return carry
@@ -566,8 +567,28 @@
     return lax.ppermute(blocks[0], axis, even), lax.ppermute(blocks[1], axis, odd)
 
 
-def across(block, axis, flip):
-    return lax.ppermute(block, axis, [(i, i ^ flip) for i in range(lax.axis_size(axis))])
+def across(block, axes, flips):
+    counts = [lax.axis_size(axis) for axis in axes]
+    pairs = []
+    for source in range(math.prod(counts)):
+        target, rest, unit = 0, source, 1
+        for count, flip in reversed(list(zip(counts, flips))):
+            target += (rest % count ^ flip) * unit
+            rest //= count
+            unit *= count
+        pairs.append((source, target))
+    return lax.ppermute(block, tuple(axes), pairs)
+
+
+def from_all(block, steps):
+    found = []
+    for choice in range(1, 1 << len(steps)):
+        flips = {}
+        for k, (axis, flip) in enumerate(steps):
+            if choice >> k & 1:
+                flips[axis] = flips.get(axis, 0) | flip
+        found.append(across(block, list(flips), list(flips.values())))
+    return found
 
 
 def f32(*shape):
@@ -584,6 +605,7 @@
         odd = place % 2
         info += [odd, jnp.where(odd == 0, place > 0, place < size - 1).astype(jnp.int32)]
     info = jnp.stack(info).astype(jnp.int32)
+    assert sizes[0] in (2, 4) and all(size in (2, 4, 8) for size in sizes)
     scale = FIT_GAIN * float(BRICK**3 * sizes[0] * sizes[1] * sizes[2])
 
     atoms, order = call(
@@ -642,39 +664,37 @@
             listed, tiles, evolved, exp_ext, sums = planned
         else:
             listed, tiles, evolved, sums = planned
-        far = [across(sums, AXES[0], flip) for flip in (2, 3)] if sizes[0] >= 4 else []
+        early = from_all(sums, [(axis, 2) for axis, size in zip(AXES[:2], sizes) if size >= 4])
         radius = call(
             born_kernel,
-            f32(TILES + 8, LANES),
-            1 << 27,
+            f32(TILES, LANES),
+            1 << 33,
             scratch=[pltpu.VMEM((3, SLOTS, LANES), jnp.float32), pltpu.VMEM((SLOTS, LANES), jnp.float32)],
             smem=1,
-            n_in=4,
-        )(listed, tiles, own, sums)
-        line = radius
+            n_in=3,
+        )(listed, tiles, own)
+        line = jnp.concatenate([radius, functools.reduce(jnp.add, early, sums)])
         for number, axis in enumerate(AXES):
             count = 3**number
             span = count * TILES
-            flips = (2, 3) if number and sizes[number] >= 4 else ()
-            here = line[span:]
-            others = [across(here, axis, flip) for flip in flips] if number else far
             near = both_sides((line, line), axis)
             if number == 2:
+                here = line[span:]
                 sums = here + near[0][span:]
-                for other in others:
-                    sums = sums + other
+                if sizes[2] >= 4:
+                    sums = sums + across(here, [axis], [2]) + across(here, [axis], [3])
                 break
             line = call(
-                functools.partial(radius_merge_kernel, number, count, len(others)),
+                functools.partial(radius_merge_kernel, number, count),
                 f32(3 * span + 8, LANES),
                 1 << 20,
                 smem=1,
-                n_in=4 + len(others),
-            )(info, line, *near, *others)
+                n_in=4,
+            )(info, line, *near)
         pair = call(
             gb_kernel,
             f32(3 * TILES, LANES),
-            1 << 28,
+            1 << 34,
             scratch=[
                 pltpu.VMEM((5, SLOTS, LANES), jnp.float32),
                 pltpu.VMEM((3, SLOTS, LANES), jnp.float32),
@@ -683,7 +703,8 @@
             smem=2,
             n_in=8,
         )(info, listed, tiles, own, radius, line, *near)
-        sums = finished(sums, sizes)
+        far = [(axis, 4) for axis, size in zip(AXES, sizes) if size >= 8]
+        sums = functools.reduce(jnp.add, from_all(sums, far), sums)
         own, force = call(
             functools.partial(fit_kernel, scale, 1),
             (f32(32, LANES), f32(3 * TILES, LANES)),
@@ -711,27 +732,6 @@
     return results[0], results[1], model
 
 
-def finished(sums, sizes):
-    assert sizes[0] in (2, 4) and all(size in (2, 4, 8) for size in sizes)
-    far = [axis for axis, size in zip(AXES, sizes) if size == 8]
-    if not far:
-        return sums
-    counts = [lax.axis_size(axis) for axis in far]
-    total = sums
-    for choice in range(1, 1 << len(far)):
-        flips = [4 if choice >> k & 1 else 0 for k in range(len(far))]
-        pairs = []
-        for source in range(math.prod(counts)):
-            target, rest, unit = 0, source, 1
-            for count, flip in reversed(list(zip(counts, flips))):
-                target += (rest % count ^ flip) * unit
-                rest //= count
-                unit *= count
-            pairs.append((source, target))
-        total = total + lax.ppermute(sums, tuple(far), pairs)
-    return total
-
-
 def solution(mesh):
     placed = (
         P(None, *AXES, None),

time: 171 us -> 169 us (0.988); the launches traced: 171 us -> 166 us
  Pallas kernels: 60.5 us -> 53.8 us
  waiting for transfers between devices: 41.3 us -> 46.7 us
  starting transfers between devices: 63.3 us -> 59.9 us
    ppermute x12, waiting for transfers between devices: 21.3 us -> 37.6 us  [both_sides(): lax.ppermute(blocks[1], axis, odd)]
    ppermute x18 -> x16, waiting for transfers between devices: 14.7 us -> 2.23 us  [across(): return lax.ppermute(block, tuple(axes), pairs)]
    pallas_call x8, Pallas kernels: 44.2 us -> 37.5 us  [the longest x2 22.3 us: on_device(): call(gb_kernel, f32(3 * TILES, LANES), 1 << 34, scratch=[pltpu.VMEM((5, S...]
    ppermute x18 -> x16, starting transfers between devices: 38.4 us -> 35 us  [across(): return lax.ppermute(block, tuple(axes), pairs)]
    ppermute x12, starting transfers between devices: 15.3 us -> 18.2 us  [both_sides(): lax.ppermute(blocks[1], axis, odd)]
    ppermute x12, starting transfers between devices: 9.57 us -> 6.74 us  [both_sides(): lax.ppermute(blocks[0], axis, even)]
  transfers between devices with their start and end apart: 42 -> 40, of which waited for: 19 -> 16; matrix products, arithmetic and copies ran while one was open for 1% -> 1% of each run, Pallas kernels for 16% -> 21%
where the time goes in v5:
time: 169 us; the launch traced here: 166 us
  starting transfers between devices  59.9 us (35%)
  Pallas kernels  53.8 us (32%)
  waiting for transfers between devices  46.7 us (28%)
  local copies, waits for them, and re-layouts  2.97 us (2%)
  between operations  1.79 us (1%)
    ppermute x12, waiting for transfers between devices, both_sides(): lax.ppermute(blocks[1], axis, odd)  37.6 us
    ppermute x16, starting transfers between devices, across(): return lax.ppermute(block, tuple(axes), pairs)  35 us
    pallas_call x2, Pallas kernels, on_device(): call(gb_kernel, f32(3 * TILES, LANES), 1 << 34, scratch=[pltpu.VMEM((5, S...  22.3 us
    ppermute x12, starting transfers between devices, both_sides(): lax.ppermute(blocks[1], axis, odd)  18.2 us
    pallas_call x2, Pallas kernels, on_device(): call(born_kernel, f32(TILES, LANES), 1 << 33, scratch=[pltpu.VMEM((3, SLO...  13 us
    ppermute x12, waiting for transfers between devices, both_sides(): lax.ppermute(blocks[0], axis, even)  6.83 us
    ppermute x12, starting transfers between devices, both_sides(): lax.ppermute(blocks[0], axis, even)  6.74 us
    pallas_call x2, Pallas kernels, on_device(): call(functools.partial(fit_kernel, scale, 1), (f32(32, LANES), f32(3 * TI...  4.26 us
  transfers between devices with their start and end apart: 40, of which 16 were waited for; matrix products, arithmetic and copies ran while one was open for 1% of the time, Pallas kernels for 21%

profile of v5, /device:TPU:56, one launch (start us, length us, event | category | flops | bytes accessed | tf_op | source)
XLA Modules:
  0.0 165.9 jit_solution(17794850415129319199)
XLA Ops:
  1.3 0.7 reduce
  2.1 0.6 copy-done.1
  2.8 1.8 %shard_map.85 = (f32[32,128]{1,0:T(8,128)S(1)}, f32[4,128]{1,0:T(4,128)S(1)}) custom-call(f32[3,8]{1,0:T(4,128)S(1)} %copy-done, s32[1]{0:T(128)} %bitcast.23.live_count, f32[12,128]{1,0:T(8,128)S(1)} %reshape.42.pos, f32[4,128]{1,0:T(4,128)S(1)} %bitcast.28, s32[4,128]{1,0:T(4,128)S(1)} %bitcast.29), custom_call_target="tpu_custom_call" | custom-call | flops 4194304 | bytes 262144 | tf_op jit(solution)/shard_map/pallas_call | solution.py:611
  4.7 1.5 shard_map.86
  6.2 0.8 collective-permute-start.1
  7.0 0.7 collective-permute-start
  7.7 5.1 %collective-permute-done.1.second = f32[184,128]{1,0:T(8,128)S(1)} collective-permute-done((f32[184,128]{1,0:T(8,128)S(1)}, f32[184,128]{1,0:T(8,128)S(1)}, u32[]{:S(2)}, u32[]{:S(2)}) %collective-permute-start.1) | collective-permute-done | bytes 94240 | tf_op jit(solution)/shard_map/ppermute | solution.py:567
  12.8 0.7 shard_map.87
  13.6 3.0 %collective-permute-start.3 = (f32[280,128]{1,0:T(8,128)S(1)}, f32[280,128]{1,0:T(8,128)S(1)}, u32[]{:S(2)}, u32[]{:S(2)}) collective-permute-start(f32[280,128]{1,0:T(8,128)S(1)} %get-tuple-element.42), channel_id=1, source_target_pairs={{0,56},{8,16},{16,8},{24,32},{32,24},{40,48},{48,40},{56,0},{1,57}... | collective-permute-start | bytes 430088 | tf_op jit(solution)/shard_map/ppermute | solution.py:567
  16.6 4.9 %collective-permute-done.3.second = f32[280,128]{1,0:T(8,128)S(1)} collective-permute-done((f32[280,128]{1,0:T(8,128)S(1)}, f32[280,128]{1,0:T(8,128)S(1)}, u32[]{:S(2)}, u32[]{:S(2)}) %collective-permute-start.3) | collective-permute-done | bytes 143392 | tf_op jit(solution)/shard_map/ppermute | solution.py:567
  21.6 0.5 collective-permute-done.2.first
  22.1 0.7 shard_map.88
  22.9 2.0 %collective-permute-start.5 = (f32[424,128]{1,0:T(8,128)S(1)}, f32[424,128]{1,0:T(8,128)S(1)}, u32[]{:S(2)}, u32[]{:S(2)}) collective-permute-start(f32[424,128]{1,0:T(8,128)S(1)} %get-tuple-element.45), channel_id=1, source_target_pairs={{0,7},{1,2},{2,1},{3,4},{4,3},{5,6},{6,5},{7,0},{8,15},{9,10},{10,... | collective-permute-start | bytes 651272 | tf_op jit(solution)/shard_map/ppermute | solution.py:567
  24.9 4.0 %collective-permute-start.4 = (f32[424,128]{1,0:T(8,128)S(1)}, f32[424,128]{1,0:T(8,128)S(1)}, u32[]{:S(2)}, u32[]{:S(2)}) collective-permute-start(f32[424,128]{1,0:T(8,128)S(1)} %get-tuple-element.44.refs_3_), channel_id=1, source_target_pairs={{0,1},{1,0},{2,3},{3,2},{4,5},{5,4},{6,7},{7,6},{8,9},{9,8},{10,11... | collective-permute-start | bytes 651272 | tf_op jit(solution)/shard_map/ppermute | solution.py:567
  29.3 3.8 %collective-permute-done.4.refs_4_ = f32[424,128]{1,0:T(8,128)S(1)} collective-permute-done((f32[424,128]{1,0:T(8,128)S(1)}, f32[424,128]{1,0:T(8,128)S(1)}, u32[]{:S(2)}, u32[]{:S(2)}) %collective-permute-start.4) | collective-permute-done | bytes 217120 | tf_op jit(solution)/shard_map/ppermute | solution.py:567
  33.1 2.1 %shard_map.89 = (s32[16,128]{1,0:T(8,128)S(1)}, f32[112,8,128]{2,1,0:T(8,128)S(1)}, f32[26,8,128]{2,1,0:T(8,128)S(1)}, f32[26,8,128]{2,1,0:T(8,128)S(1)}, f32[8,128]{1,0:T(8,128)S(1)}) custom-call(s32[12]{0:T(128)S(1)} %stack.63.bounds.info.refs_0_, f32[32,128]{1,0:T(8,128)S(1)} %get-tuple-element.36.own.refs_1_.refs_0_.start, f32[416,128]{1,0:T(8,128)S(1)} %bitcast.24, ...), custom_call_target="tpu_custom_call" | custom-call | flops 4194304 | bytes 262144 | tf_op jit(solution)/shard_map/pallas_call | solution.py:653
  35.2 1.4 collective-permute-start.8
  36.6 2.6 %collective-permute-start.7 = (f32[8,128]{1,0:T(8,128)S(1)}, f32[8,128]{1,0:T(8,128)S(1)}, u32[]{:S(2)}, u32[]{:S(2)}) collective-permute-start(f32[8,128]{1,0:T(8,128)S(1)} %get-tuple-element.50), channel_id=1, source_target_pairs={{0,16},{8,24},{16,0},{24,8},{32,48},{40,56},{48,32},{56,40},{1,17}... | collective-permute-start | bytes 12296 | tf_op jit(solution)/shard_map/ppermute | solution.py:580
  39.2 2.5 %collective-permute-start.6 = (f32[8,128]{1,0:T(8,128)S(1)}, f32[8,128]{1,0:T(8,128)S(1)}, u32[]{:S(2)}, u32[]{:S(2)}) collective-permute-start(f32[8,128]{1,0:T(8,128)S(1)} %get-tuple-element.50), channel_id=1, source_target_pairs={{0,128},{64,192},{128,0},{192,64},{1,129},{65,193},{129,1},{193,65... | collective-permute-start | bytes 12296 | tf_op jit(solution)/shard_map/ppermute | solution.py:580
  41.7 6.4 %shard_map.90.own_radius = f32[4,128]{1,0:T(4,128)S(1)} custom-call(s32[16,128]{1,0:T(8,128)S(1)} %get-tuple-element.48.listed, f32[112,8,128]{2,1,0:T(8,128)S(1)} %get-tuple-element.49.tiles.refs_6_, f32[32,128]{1,0:T(8,128)S(1)} %get-tuple-element.36.own.refs_1_.refs_0_.start), custom_call_target="tpu_custom_call" | custom-call | flops 8589934592 | bytes 262144 | tf_op jit(solution)/shard_map/pallas_call | solution.py:668
  48.4 4.5 %collective-permute-done.10.second = f32[12,128]{1,0:T(8,128)S(1)} collective-permute-done((f32[12,128]{1,0:T(8,128)S(1)}, f32[12,128]{1,0:T(8,128)S(1)}, u32[]{:S(2)}, u32[]{:S(2)}) %collective-permute-start.10) | collective-permute-done | bytes 6176 | tf_op jit(solution)/shard_map/ppermute | solution.py:567
  52.9 0.5 shard_map.91.mine
  53.5 2.7 %collective-permute-start.12 = (f32[20,128]{1,0:T(8,128)S(1)}, f32[20,128]{1,0:T(8,128)S(1)}, u32[]{:S(2)}, u32[]{:S(2)}) collective-permute-start(f32[20,128]{1,0:T(8,128)S(1)} %shard_map.91.mine), channel_id=1, source_target_pairs={{0,56},{8,16},{16,8},{24,32},{32,24},{40,48},{48,40},{56,0},{1,57}... | collective-permute-start | bytes 30728 | tf_op jit(solution)/shard_map/ppermute | solution.py:567
  56.2 3.2 %collective-permute-done.12.second = f32[20,128]{1,0:T(8,128)S(1)} collective-permute-done((f32[20,128]{1,0:T(8,128)S(1)}, f32[20,128]{1,0:T(8,128)S(1)}, u32[]{:S(2)}, u32[]{:S(2)}) %collective-permute-start.12) | collective-permute-done | bytes 10272 | tf_op jit(solution)/shard_map/ppermute | solution.py:567
  59.9 0.5 shard_map.92.mine
  60.6 3.2 %collective-permute-start.14 = (f32[8,128]{1,0:T(8,128)S(1)}, f32[8,128]{1,0:T(8,128)S(1)}, u32[]{:S(2)}, u32[]{:S(2)}) collective-permute-start(f32[8,128]{1,0:T(8,128)S(1)} %slice.34), channel_id=1, source_target_pairs={{0,2},{1,3},{2,0},{3,1},{4,6},{5,7},{6,4},{7,5},{8,10},{9,11},{10,... | collective-permute-start | bytes 12296 | tf_op jit(solution)/shard_map/ppermute | solution.py:580
  64.0 1.8 %collective-permute-start.19 = (f32[44,128]{1,0:T(8,128)S(1)}, f32[44,128]{1,0:T(8,128)S(1)}, u32[]{:S(2)}, u32[]{:S(2)}) collective-permute-start(f32[44,128]{1,0:T(8,128)S(1)} %shard_map.92.mine), channel_id=1, source_target_pairs={{0,7},{1,2},{2,1},{3,4},{4,3},{5,6},{6,5},{7,0},{8,15},{9,10},{10,... | collective-permute-start | bytes 67592 | tf_op jit(solution)/shard_map/ppermute | solution.py:567
  65.8 1.6 collective-permute-done.15
  67.4 2.9 %collective-permute-start.18 = (f32[8,128]{1,0:T(8,128)S(1)}, f32[8,128]{1,0:T(8,128)S(1)}, u32[]{:S(2)}, u32[]{:S(2)}) collective-permute-start(f32[8,128]{1,0:T(8,128)S(1)} %fusion.3), channel_id=1, source_target_pairs={{0,36},{1,37},{2,38},{3,39},{4,32},{5,33},{6,34},{7,35},{8,44},{9,... | collective-permute-start | bytes 12296 | tf_op jit(solution)/shard_map/ppermute | solution.py:580
  70.3 2.5 %collective-permute-start.17 = (f32[8,128]{1,0:T(8,128)S(1)}, f32[8,128]{1,0:T(8,128)S(1)}, u32[]{:S(2)}, u32[]{:S(2)}) collective-permute-start(f32[8,128]{1,0:T(8,128)S(1)} %fusion.3), channel_id=1, source_target_pairs={{0,4},{1,5},{2,6},{3,7},{4,0},{5,1},{6,2},{7,3},{8,12},{9,13},{10,... | collective-permute-start | bytes 12296 | tf_op jit(solution)/shard_map/ppermute | solution.py:580
  72.9 2.0 %collective-permute-start.16 = (f32[8,128]{1,0:T(8,128)S(1)}, f32[8,128]{1,0:T(8,128)S(1)}, u32[]{:S(2)}, u32[]{:S(2)}) collective-permute-start(f32[8,128]{1,0:T(8,128)S(1)} %fusion.3), channel_id=1, source_target_pairs={{0,32},{8,40},{16,48},{24,56},{32,0},{40,8},{48,16},{56,24},{1,33}... | collective-permute-start | bytes 12296 | tf_op jit(solution)/shard_map/ppermute | solution.py:580
  74.9 11.0 %shard_map.93.refs_4_ = f32[12,128]{1,0:T(8,128)S(1)} custom-call(s32[12]{0:T(128)S(1)} %stack.63.bounds.info.refs_0_, s32[16,128]{1,0:T(8,128)S(1)} %get-tuple-element.48.listed, f32[112,8,128]{2,1,0:T(8,128)S(1)} %get-tuple-element.49.tiles.refs_6_, f32[32,128]{1,0:T(8,128)S(1)} %get-tuple-element.36.own.refs_1_.refs_0_.start, ...), custom_call_target="tpu_custom_call" | custom-call | flops 17179869184 | bytes 262144 | tf_op jit(solution)/shard_map/pallas_call | solution.py:694
  85.9 2.4 %shard_map.94 = (f32[32,128]{1,0:T(8,128)S(1)}, f32[12,128]{1,0:T(8,128)}) custom-call(s32[12]{0:T(128)S(1)} %stack.63.bounds.info.refs_0_, f32[32,128]{1,0:T(8,128)S(1)} %get-tuple-element.36.own.refs_1_.refs_0_.start, f32[26,8,128]{2,1,0:T(8,128)S(1)} %get-tuple-element.46.refs_1_, f32[26,8,128]{2,1,0:T(8,128)S(1)} %get-tuple-element.47.refs_2_.refs_7_, ...), custom_call_target="tpu_custom_call" | custom-call | flops 67108864 | bytes 262144 | tf_op jit(solution)/shard_map/pallas_call | solution.py:708
  88.4 1.5 shard_map.95
  90.1 4.9 %collective-permute-done.21.second = f32[96,128]{1,0:T(8,128)S(1)} collective-permute-done((f32[96,128]{1,0:T(8,128)S(1)}, f32[96,128]{1,0:T(8,128)S(1)}, u32[]{:S(2)}, u32[]{:S(2)}) %collective-permute-start.21) | collective-permute-done | bytes 49184 | tf_op jit(solution)/shard_map/ppermute | solution.py:567
  95.0 0.7 shard_map.96
  95.6 1.9 %collective-permute-start.23 = (f32[152,128]{1,0:T(8,128)S(1)}, f32[152,128]{1,0:T(8,128)S(1)}, u32[]{:S(2)}, u32[]{:S(2)}) collective-permute-start(f32[152,128]{1,0:T(8,128)S(1)} %get-tuple-element.57), channel_id=1, source_target_pairs={{0,56},{8,16},{16,8},{24,32},{32,24},{40,48},{48,40},{56,0},{1,57}... | collective-permute-start | bytes 233480 | tf_op jit(solution)/shard_map/ppermute | solution.py:567
  97.6 4.7 %collective-permute-done.23.second = f32[152,128]{1,0:T(8,128)S(1)} collective-permute-done((f32[152,128]{1,0:T(8,128)S(1)}, f32[152,128]{1,0:T(8,128)S(1)}, u32[]{:S(2)}, u32[]{:S(2)}) %collective-permute-start.23) | collective-permute-done | bytes 77856 | tf_op jit(solution)/shard_map/ppermute | solution.py:567
  102.2 0.7 shard_map.97
  103.0 2.3 %collective-permute-start.25 = (f32[248,128]{1,0:T(8,128)S(1)}, f32[248,128]{1,0:T(8,128)S(1)}, u32[]{:S(2)}, u32[]{:S(2)}) collective-permute-start(f32[248,128]{1,0:T(8,128)S(1)} %get-tuple-element.60), channel_id=1, source_target_pairs={{0,7},{1,2},{2,1},{3,4},{4,3},{5,6},{6,5},{7,0},{8,15},{9,10},{10,... | collective-permute-start | bytes 380936 | tf_op jit(solution)/shard_map/ppermute | solution.py:567
  105.3 1.4 collective-permute-start.24
  106.7 1.5 collective-permute-done.25.refs_5_
  108.2 2.0 %collective-permute-done.24.refs_4_ = f32[248,128]{1,0:T(8,128)S(1)} collective-permute-done((f32[248,128]{1,0:T(8,128)S(1)}, f32[248,128]{1,0:T(8,128)S(1)}, u32[]{:S(2)}, u32[]{:S(2)}) %collective-permute-start.24) | collective-permute-done | bytes 127008 | tf_op jit(solution)/shard_map/ppermute | solution.py:567
  110.2 2.0 %shard_map.98 = (s32[16,128]{1,0:T(8,128)S(1)}, f32[112,8,128]{2,1,0:T(8,128)S(1)}, f32[26,8,128]{2,1,0:T(8,128)S(1)}, f32[8,128]{1,0:T(8,128)S(1)}) custom-call(s32[12]{0:T(128)S(1)} %stack.63.bounds.info.refs_0_, f32[32,128]{1,0:T(8,128)S(1)} %get-tuple-element.51.own.refs_1_.refs_0_, f32[208,128]{1,0:T(8,128)S(1)} %bitcast.27, ...), custom_call_target="tpu_custom_call" | custom-call | flops 4194304 | bytes 262144 | tf_op jit(solution)/shard_map/pallas_call | solution.py:653
  112.3 3.5 %collective-permute-start.27 = (f32[8,128]{1,0:T(8,128)S(1)}, f32[8,128]{1,0:T(8,128)S(1)}, u32[]{:S(2)}, u32[]{:S(2)}) collective-permute-start(f32[8,128]{1,0:T(8,128)S(1)} %get-tuple-element.64), channel_id=1, source_target_pairs={{0,16},{8,24},{16,0},{24,8},{32,48},{40,56},{48,32},{56,40},{1,17}... | collective-permute-start | bytes 12296 | tf_op jit(solution)/shard_map/ppermute | solution.py:580
  115.9 2.9 %collective-permute-start.26 = (f32[8,128]{1,0:T(8,128)S(1)}, f32[8,128]{1,0:T(8,128)S(1)}, u32[]{:S(2)}, u32[]{:S(2)}) collective-permute-start(f32[8,128]{1,0:T(8,128)S(1)} %get-tuple-element.64), channel_id=1, source_target_pairs={{0,128},{64,192},{128,0},{192,64},{1,129},{65,193},{129,1},{193,65... | collective-permute-start | bytes 12296 | tf_op jit(solution)/shard_map/ppermute | solution.py:580
  118.8 6.6 %shard_map.99.own_radius = f32[4,128]{1,0:T(4,128)S(1)} custom-call(s32[16,128]{1,0:T(8,128)S(1)} %get-tuple-element.62.listed, f32[112,8,128]{2,1,0:T(8,128)S(1)} %get-tuple-element.63.tiles, f32[32,128]{1,0:T(8,128)S(1)} %get-tuple-element.51.own.refs_1_.refs_0_), custom_call_target="tpu_custom_call" | custom-call | flops 8589934592 | bytes 262144 | tf_op jit(solution)/shard_map/pallas_call | solution.py:668
  125.7 4.5 %collective-permute-done.30.second = f32[12,128]{1,0:T(8,128)S(1)} collective-permute-done((f32[12,128]{1,0:T(8,128)S(1)}, f32[12,128]{1,0:T(8,128)S(1)}, u32[]{:S(2)}, u32[]{:S(2)}) %collective-permute-start.30) | collective-permute-done | bytes 6176 | tf_op jit(solution)/shard_map/ppermute | solution.py:567
  130.1 0.5 shard_map.100.mine
  130.7 2.0 %collective-permute-start.32 = (f32[20,128]{1,0:T(8,128)S(1)}, f32[20,128]{1,0:T(8,128)S(1)}, u32[]{:S(2)}, u32[]{:S(2)}) collective-permute-start(f32[20,128]{1,0:T(8,128)S(1)} %shard_map.100.mine), channel_id=1, source_target_pairs={{0,56},{8,16},{16,8},{24,32},{32,24},{40,48},{48,40},{56,0},{1,57}... | collective-permute-start | bytes 30728 | tf_op jit(solution)/shard_map/ppermute | solution.py:567
  132.6 3.9 %collective-permute-done.32.second = f32[20,128]{1,0:T(8,128)S(1)} collective-permute-done((f32[20,128]{1,0:T(8,128)S(1)}, f32[20,128]{1,0:T(8,128)S(1)}, u32[]{:S(2)}, u32[]{:S(2)}) %collective-permute-start.32) | collective-permute-done | bytes 10272 | tf_op jit(solution)/shard_map/ppermute | solution.py:567
  136.6 0.5 shard_map.101.mine
  137.2 2.9 %collective-permute-start.34 = (f32[8,128]{1,0:T(8,128)S(1)}, f32[8,128]{1,0:T(8,128)S(1)}, u32[]{:S(2)}, u32[]{:S(2)}) collective-permute-start(f32[8,128]{1,0:T(8,128)S(1)} %slice.36), channel_id=1, source_target_pairs={{0,2},{1,3},{2,0},{3,1},{4,6},{5,7},{6,4},{7,5},{8,10},{9,11},{10,... | collective-permute-start | bytes 12296 | tf_op jit(solution)/shard_map/ppermute | solution.py:580
  140.2 0.5 collective-permute-start.35
  140.9 0.8 slice.40
  141.7 1.5 collective-permute-start.39
  143.2 0.6 collective-permute-done.35
  143.8 1.3 collective-permute-start.38
  145.1 2.0 %collective-permute-start.37 = (f32[8,128]{1,0:T(8,128)S(1)}, f32[8,128]{1,0:T(8,128)S(1)}, u32[]{:S(2)}, u32[]{:S(2)}) collective-permute-start(f32[8,128]{1,0:T(8,128)S(1)} %fusion.1), channel_id=1, source_target_pairs={{0,4},{1,5},{2,6},{3,7},{4,0},{5,1},{6,2},{7,3},{8,12},{9,13},{10,... | collective-permute-start | bytes 12296 | tf_op jit(solution)/shard_map/ppermute | solution.py:580
  147.2 4.1 %collective-permute-start.36 = (f32[8,128]{1,0:T(8,128)S(1)}, f32[8,128]{1,0:T(8,128)S(1)}, u32[]{:S(2)}, u32[]{:S(2)}) collective-permute-start(f32[8,128]{1,0:T(8,128)S(1)} %fusion.1), channel_id=1, source_target_pairs={{0,32},{8,40},{16,48},{24,56},{32,0},{40,8},{48,16},{56,24},{1,33}... | collective-permute-start | bytes 12296 | tf_op jit(solution)/shard_map/ppermute | solution.py:580
  151.3 11.3 %shard_map.102.refs_4_ = f32[12,128]{1,0:T(8,128)S(1)} custom-call(s32[12]{0:T(128)S(1)} %stack.63.bounds.info.refs_0_, s32[16,128]{1,0:T(8,128)S(1)} %get-tuple-element.62.listed, f32[112,8,128]{2,1,0:T(8,128)S(1)} %get-tuple-element.63.tiles, f32[32,128]{1,0:T(8,128)S(1)} %get-tuple-element.51.own.refs_1_.refs_0_, f32[4,128]{1,0:T(4,128)S(1)} %shard_map.99.own_radius, ...), custom_call_target="tpu_custom_call" | custom-call | flops 17179869184 | bytes 262144 | tf_op jit(solution)/shard_map/pallas_call | solution.py:694
  162.6 1.8 %shard_map.103 = (f32[32,128]{1,0:T(8,128)S(1)}, f32[12,128]{1,0:T(8,128)S(1)}) custom-call(s32[12]{0:T(128)S(1)} %stack.63.bounds.info.refs_0_, f32[32,128]{1,0:T(8,128)S(1)} %get-tuple-element.51.own.refs_1_.refs_0_, f32[26,8,128]{2,1,0:T(8,128)S(1)} %get-tuple-element.61.refs_1_, f32[26,8,128]{2,1,0:T(8,128)S(1)} %get-tuple-element.47.refs_2_.refs_7_, ...), custom_call_target="tpu_custom_call" | custom-call | flops 67108864 | bytes 262144 | tf_op jit(solution)/shard_map/pallas_call | solution.py:708
  164.7 0.6 squeeze.9
  165.3 0.6 squeeze.8
  (65 shorter events, 2.9 us)
Async XLA Ops:
  0.6 1.5 copy-start.3
  2.1 0.7 copy-start.1
  2.1 0.7 copy-start.2
  2.1 0.7 copy-start
  6.2 6.6 %collective-permute-start.1 = (f32[184,128]{1,0:T(8,128)S(1)}, f32[184,128]{1,0:T(8,128)S(1)}, u32[]{:S(2)}, u32[]{:S(2)}) collective-permute-start(f32[184,128]{1,0:T(8,128)S(1)} %get-tuple-element.39), channel_id=1, source_target_pairs={{0,192},{64,128},{128,64},{192,0},{1,193},{65,129},{129,65},{193,1... | collective-permute-start | bytes 282632 | tf_op jit(solution)/shard_map/ppermute | solution.py:567
  7.0 5.8 %collective-permute-start = (f32[184,128]{1,0:T(8,128)S(1)}, f32[184,128]{1,0:T(8,128)S(1)}, u32[]{:S(2)}, u32[]{:S(2)}) collective-permute-start(f32[184,128]{1,0:T(8,128)S(1)} %get-tuple-element.38.mine), channel_id=1, source_target_pairs={{0,64},{64,0},{128,192},{192,128},{1,65},{65,1},{129,193},{193,129... | collective-permute-start | bytes 282632 | tf_op jit(solution)/shard_map/ppermute | solution.py:567
  13.6 8.0 %collective-permute-start.3 = (f32[280,128]{1,0:T(8,128)S(1)}, f32[280,128]{1,0:T(8,128)S(1)}, u32[]{:S(2)}, u32[]{:S(2)}) collective-permute-start(f32[280,128]{1,0:T(8,128)S(1)} %get-tuple-element.42), channel_id=1, source_target_pairs={{0,56},{8,16},{16,8},{24,32},{32,24},{40,48},{48,40},{56,0},{1,57}... | collective-permute-start | bytes 430088 | tf_op jit(solution)/shard_map/ppermute | solution.py:567
  16.6 5.5 %collective-permute-start.2 = (f32[280,128]{1,0:T(8,128)S(1)}, f32[280,128]{1,0:T(8,128)S(1)}, u32[]{:S(2)}, u32[]{:S(2)}) collective-permute-start(f32[280,128]{1,0:T(8,128)S(1)} %get-tuple-element.41.mine), channel_id=1, source_target_pairs={{0,8},{8,0},{16,24},{24,16},{32,40},{40,32},{48,56},{56,48},{1,9},... | collective-permute-start | bytes 430088 | tf_op jit(solution)/shard_map/ppermute | solution.py:567
  22.9 6.5 %collective-permute-start.5 = (f32[424,128]{1,0:T(8,128)S(1)}, f32[424,128]{1,0:T(8,128)S(1)}, u32[]{:S(2)}, u32[]{:S(2)}) collective-permute-start(f32[424,128]{1,0:T(8,128)S(1)} %get-tuple-element.45), channel_id=1, source_target_pairs={{0,7},{1,2},{2,1},{3,4},{4,3},{5,6},{6,5},{7,0},{8,15},{9,10},{10,... | collective-permute-start | bytes 651272 | tf_op jit(solution)/shard_map/ppermute | solution.py:567
  24.9 8.2 %collective-permute-start.4 = (f32[424,128]{1,0:T(8,128)S(1)}, f32[424,128]{1,0:T(8,128)S(1)}, u32[]{:S(2)}, u32[]{:S(2)}) collective-permute-start(f32[424,128]{1,0:T(8,128)S(1)} %get-tuple-element.44.refs_3_), channel_id=1, source_target_pairs={{0,1},{1,0},{2,3},{3,2},{4,5},{5,4},{6,7},{7,6},{8,9},{9,8},{10,11... | collective-permute-start | bytes 651272 | tf_op jit(solution)/shard_map/ppermute | solution.py:567
  35.2 13.0 %collective-permute-start.8 = (f32[8,128]{1,0:T(8,128)S(1)}, f32[8,128]{1,0:T(8,128)S(1)}, u32[]{:S(2)}, u32[]{:S(2)}) collective-permute-start(f32[8,128]{1,0:T(8,128)S(1)} %get-tuple-element.50), channel_id=1, source_target_pairs={{0,144},{8,152},{16,128},{24,136},{32,176},{40,184},{48,160},{56,1... | collective-permute-start | bytes 12296 | tf_op jit(solution)/shard_map/ppermute | solution.py:580
  36.6 11.6 %collective-permute-start.7 = (f32[8,128]{1,0:T(8,128)S(1)}, f32[8,128]{1,0:T(8,128)S(1)}, u32[]{:S(2)}, u32[]{:S(2)}) collective-permute-start(f32[8,128]{1,0:T(8,128)S(1)} %get-tuple-element.50), channel_id=1, source_target_pairs={{0,16},{8,24},{16,0},{24,8},{32,48},{40,56},{48,32},{56,40},{1,17}... | collective-permute-start | bytes 12296 | tf_op jit(solution)/shard_map/ppermute | solution.py:580
  39.2 9.0 %collective-permute-start.6 = (f32[8,128]{1,0:T(8,128)S(1)}, f32[8,128]{1,0:T(8,128)S(1)}, u32[]{:S(2)}, u32[]{:S(2)}) collective-permute-start(f32[8,128]{1,0:T(8,128)S(1)} %get-tuple-element.50), channel_id=1, source_target_pairs={{0,128},{64,192},{128,0},{192,64},{1,129},{65,193},{129,1},{193,65... | collective-permute-start | bytes 12296 | tf_op jit(solution)/shard_map/ppermute | solution.py:580
  48.2 4.7 %collective-permute-start.10 = (f32[12,128]{1,0:T(8,128)S(1)}, f32[12,128]{1,0:T(8,128)S(1)}, u32[]{:S(2)}, u32[]{:S(2)}) collective-permute-start(f32[12,128]{1,0:T(8,128)S(1)} %pad_maximum_fusion.mine), channel_id=1, source_target_pairs={{0,192},{64,128},{128,64},{192,0},{1,193},{65,129},{129,65},{193,1... | collective-permute-start | bytes 18440 | tf_op jit(solution)/shard_map/ppermute | solution.py:567
  48.3 4.6 %collective-permute-start.9 = (f32[12,128]{1,0:T(8,128)S(1)}, f32[12,128]{1,0:T(8,128)S(1)}, u32[]{:S(2)}, u32[]{:S(2)}) collective-permute-start(f32[12,128]{1,0:T(8,128)S(1)} %pad_maximum_fusion.mine), channel_id=1, source_target_pairs={{0,64},{64,0},{128,192},{192,128},{1,65},{65,1},{129,193},{193,129... | collective-permute-start | bytes 18440 | tf_op jit(solution)/shard_map/ppermute | solution.py:567
  53.5 5.9 %collective-permute-start.12 = (f32[20,128]{1,0:T(8,128)S(1)}, f32[20,128]{1,0:T(8,128)S(1)}, u32[]{:S(2)}, u32[]{:S(2)}) collective-permute-start(f32[20,128]{1,0:T(8,128)S(1)} %shard_map.91.mine), channel_id=1, source_target_pairs={{0,56},{8,16},{16,8},{24,32},{32,24},{40,48},{48,40},{56,0},{1,57}... | collective-permute-start | bytes 30728 | tf_op jit(solution)/shard_map/ppermute | solution.py:567
  56.2 3.7 %collective-permute-start.11 = (f32[20,128]{1,0:T(8,128)S(1)}, f32[20,128]{1,0:T(8,128)S(1)}, u32[]{:S(2)}, u32[]{:S(2)}) collective-permute-start(f32[20,128]{1,0:T(8,128)S(1)} %shard_map.91.mine), channel_id=1, source_target_pairs={{0,8},{8,0},{16,24},{24,16},{32,40},{40,32},{48,56},{56,48},{1,9},... | collective-permute-start | bytes 30728 | tf_op jit(solution)/shard_map/ppermute | solution.py:567
  60.4 7.0 %collective-permute-start.13 = (f32[44,128]{1,0:T(8,128)S(1)}, f32[44,128]{1,0:T(8,128)S(1)}, u32[]{:S(2)}, u32[]{:S(2)}) collective-permute-start(f32[44,128]{1,0:T(8,128)S(1)} %shard_map.92.mine), channel_id=1, source_target_pairs={{0,1},{1,0},{2,3},{3,2},{4,5},{5,4},{6,7},{7,6},{8,9},{9,8},{10,11... | collective-permute-start | bytes 67592 | tf_op jit(solution)/shard_map/ppermute | solution.py:567
  60.6 5.2 %collective-permute-start.14 = (f32[8,128]{1,0:T(8,128)S(1)}, f32[8,128]{1,0:T(8,128)S(1)}, u32[]{:S(2)}, u32[]{:S(2)}) collective-permute-start(f32[8,128]{1,0:T(8,128)S(1)} %slice.34), channel_id=1, source_target_pairs={{0,2},{1,3},{2,0},{3,1},{4,6},{5,7},{6,4},{7,5},{8,10},{9,11},{10,... | collective-permute-start | bytes 12296 | tf_op jit(solution)/shard_map/ppermute | solution.py:580
  63.8 3.6 %collective-permute-start.15 = (f32[8,128]{1,0:T(8,128)S(1)}, f32[8,128]{1,0:T(8,128)S(1)}, u32[]{:S(2)}, u32[]{:S(2)}) collective-permute-start(f32[8,128]{1,0:T(8,128)S(1)} %slice.34), channel_id=1, source_target_pairs={{0,3},{1,2},{2,1},{3,0},{4,7},{5,6},{6,5},{7,4},{8,11},{9,10},{10,... | collective-permute-start | bytes 12296 | tf_op jit(solution)/shard_map/ppermute | solution.py:580
  64.0 10.9 %collective-permute-start.19 = (f32[44,128]{1,0:T(8,128)S(1)}, f32[44,128]{1,0:T(8,128)S(1)}, u32[]{:S(2)}, u32[]{:S(2)}) collective-permute-start(f32[44,128]{1,0:T(8,128)S(1)} %shard_map.92.mine), channel_id=1, source_target_pairs={{0,7},{1,2},{2,1},{3,4},{4,3},{5,6},{6,5},{7,0},{8,15},{9,10},{10,... | collective-permute-start | bytes 67592 | tf_op jit(solution)/shard_map/ppermute | solution.py:567
  67.4 18.5 %collective-permute-start.18 = (f32[8,128]{1,0:T(8,128)S(1)}, f32[8,128]{1,0:T(8,128)S(1)}, u32[]{:S(2)}, u32[]{:S(2)}) collective-permute-start(f32[8,128]{1,0:T(8,128)S(1)} %fusion.3), channel_id=1, source_target_pairs={{0,36},{1,37},{2,38},{3,39},{4,32},{5,33},{6,34},{7,35},{8,44},{9,... | collective-permute-start | bytes 12296 | tf_op jit(solution)/shard_map/ppermute | solution.py:580
  70.3 15.6 %collective-permute-start.17 = (f32[8,128]{1,0:T(8,128)S(1)}, f32[8,128]{1,0:T(8,128)S(1)}, u32[]{:S(2)}, u32[]{:S(2)}) collective-permute-start(f32[8,128]{1,0:T(8,128)S(1)} %fusion.3), channel_id=1, source_target_pairs={{0,4},{1,5},{2,6},{3,7},{4,0},{5,1},{6,2},{7,3},{8,12},{9,13},{10,... | collective-permute-start | bytes 12296 | tf_op jit(solution)/shard_map/ppermute | solution.py:580
  72.9 13.1 %collective-permute-start.16 = (f32[8,128]{1,0:T(8,128)S(1)}, f32[8,128]{1,0:T(8,128)S(1)}, u32[]{:S(2)}, u32[]{:S(2)}) collective-permute-start(f32[8,128]{1,0:T(8,128)S(1)} %fusion.3), channel_id=1, source_target_pairs={{0,32},{8,40},{16,48},{24,56},{32,0},{40,8},{48,16},{56,24},{1,33}... | collective-permute-start | bytes 12296 | tf_op jit(solution)/shard_map/ppermute | solution.py:580
  89.9 5.1 %collective-permute-start.21 = (f32[96,128]{1,0:T(8,128)S(1)}, f32[96,128]{1,0:T(8,128)S(1)}, u32[]{:S(2)}, u32[]{:S(2)}) collective-permute-start(f32[96,128]{1,0:T(8,128)S(1)} %get-tuple-element.54), channel_id=1, source_target_pairs={{0,192},{64,128},{128,64},{192,0},{1,193},{65,129},{129,65},{193,1... | collective-permute-start | bytes 147464 | tf_op jit(solution)/shard_map/ppermute | solution.py:567
  90.0 5.0 %collective-permute-start.20 = (f32[96,128]{1,0:T(8,128)S(1)}, f32[96,128]{1,0:T(8,128)S(1)}, u32[]{:S(2)}, u32[]{:S(2)}) collective-permute-start(f32[96,128]{1,0:T(8,128)S(1)} %get-tuple-element.53.mine), channel_id=1, source_target_pairs={{0,64},{64,0},{128,192},{192,128},{1,65},{65,1},{129,193},{193,129... | collective-permute-start | bytes 147464 | tf_op jit(solution)/shard_map/ppermute | solution.py:567
  95.6 6.6 %collective-permute-start.23 = (f32[152,128]{1,0:T(8,128)S(1)}, f32[152,128]{1,0:T(8,128)S(1)}, u32[]{:S(2)}, u32[]{:S(2)}) collective-permute-start(f32[152,128]{1,0:T(8,128)S(1)} %get-tuple-element.57), channel_id=1, source_target_pairs={{0,56},{8,16},{16,8},{24,32},{32,24},{40,48},{48,40},{56,0},{1,57}... | collective-permute-start | bytes 233480 | tf_op jit(solution)/shard_map/ppermute | solution.py:567
  97.5 4.7 %collective-permute-start.22 = (f32[152,128]{1,0:T(8,128)S(1)}, f32[152,128]{1,0:T(8,128)S(1)}, u32[]{:S(2)}, u32[]{:S(2)}) collective-permute-start(f32[152,128]{1,0:T(8,128)S(1)} %get-tuple-element.56.mine), channel_id=1, source_target_pairs={{0,8},{8,0},{16,24},{24,16},{32,40},{40,32},{48,56},{56,48},{1,9},... | collective-permute-start | bytes 233480 | tf_op jit(solution)/shard_map/ppermute | solution.py:567
  103.0 5.2 %collective-permute-start.25 = (f32[248,128]{1,0:T(8,128)S(1)}, f32[248,128]{1,0:T(8,128)S(1)}, u32[]{:S(2)}, u32[]{:S(2)}) collective-permute-start(f32[248,128]{1,0:T(8,128)S(1)} %get-tuple-element.60), channel_id=1, source_target_pairs={{0,7},{1,2},{2,1},{3,4},{4,3},{5,6},{6,5},{7,0},{8,15},{9,10},{10,... | collective-permute-start | bytes 380936 | tf_op jit(solution)/shard_map/ppermute | solution.py:567
  105.3 4.9 %collective-permute-start.24 = (f32[248,128]{1,0:T(8,128)S(1)}, f32[248,128]{1,0:T(8,128)S(1)}, u32[]{:S(2)}, u32[]{:S(2)}) collective-permute-start(f32[248,128]{1,0:T(8,128)S(1)} %get-tuple-element.59.refs_3_), channel_id=1, source_target_pairs={{0,1},{1,0},{2,3},{3,2},{4,5},{5,4},{6,7},{7,6},{8,9},{9,8},{10,11... | collective-permute-start | bytes 380936 | tf_op jit(solution)/shard_map/ppermute | solution.py:567
  112.2 13.2 %collective-permute-start.28 = (f32[8,128]{1,0:T(8,128)S(1)}, f32[8,128]{1,0:T(8,128)S(1)}, u32[]{:S(2)}, u32[]{:S(2)}) collective-permute-start(f32[8,128]{1,0:T(8,128)S(1)} %get-tuple-element.64), channel_id=1, source_target_pairs={{0,144},{8,152},{16,128},{24,136},{32,176},{40,184},{48,160},{56,1... | collective-permute-start | bytes 12296 | tf_op jit(solution)/shard_map/ppermute | solution.py:580
  112.3 13.1 %collective-permute-start.27 = (f32[8,128]{1,0:T(8,128)S(1)}, f32[8,128]{1,0:T(8,128)S(1)}, u32[]{:S(2)}, u32[]{:S(2)}) collective-permute-start(f32[8,128]{1,0:T(8,128)S(1)} %get-tuple-element.64), channel_id=1, source_target_pairs={{0,16},{8,24},{16,0},{24,8},{32,48},{40,56},{48,32},{56,40},{1,17}... | collective-permute-start | bytes 12296 | tf_op jit(solution)/shard_map/ppermute | solution.py:580
  115.9 9.6 %collective-permute-start.26 = (f32[8,128]{1,0:T(8,128)S(1)}, f32[8,128]{1,0:T(8,128)S(1)}, u32[]{:S(2)}, u32[]{:S(2)}) collective-permute-start(f32[8,128]{1,0:T(8,128)S(1)} %get-tuple-element.64), channel_id=1, source_target_pairs={{0,128},{64,192},{128,0},{192,64},{1,129},{65,193},{129,1},{193,65... | collective-permute-start | bytes 12296 | tf_op jit(solution)/shard_map/ppermute | solution.py:580
  125.5 4.7 %collective-permute-start.30 = (f32[12,128]{1,0:T(8,128)S(1)}, f32[12,128]{1,0:T(8,128)S(1)}, u32[]{:S(2)}, u32[]{:S(2)}) collective-permute-start(f32[12,128]{1,0:T(8,128)S(1)} %pad_maximum_fusion.1.mine), channel_id=1, source_target_pairs={{0,192},{64,128},{128,64},{192,0},{1,193},{65,129},{129,65},{193,1... | collective-permute-start | bytes 18440 | tf_op jit(solution)/shard_map/ppermute | solution.py:567
  125.6 4.6 %collective-permute-start.29 = (f32[12,128]{1,0:T(8,128)S(1)}, f32[12,128]{1,0:T(8,128)S(1)}, u32[]{:S(2)}, u32[]{:S(2)}) collective-permute-start(f32[12,128]{1,0:T(8,128)S(1)} %pad_maximum_fusion.1.mine), channel_id=1, source_target_pairs={{0,64},{64,0},{128,192},{192,128},{1,65},{65,1},{129,193},{193,129... | collective-permute-start | bytes 18440 | tf_op jit(solution)/shard_map/ppermute | solution.py:567
  130.7 5.9 %collective-permute-start.32 = (f32[20,128]{1,0:T(8,128)S(1)}, f32[20,128]{1,0:T(8,128)S(1)}, u32[]{:S(2)}, u32[]{:S(2)}) collective-permute-start(f32[20,128]{1,0:T(8,128)S(1)} %shard_map.100.mine), channel_id=1, source_target_pairs={{0,56},{8,16},{16,8},{24,32},{32,24},{40,48},{48,40},{56,0},{1,57}... | collective-permute-start | bytes 30728 | tf_op jit(solution)/shard_map/ppermute | solution.py:567
  132.6 3.9 %collective-permute-start.31 = (f32[20,128]{1,0:T(8,128)S(1)}, f32[20,128]{1,0:T(8,128)S(1)}, u32[]{:S(2)}, u32[]{:S(2)}) collective-permute-start(f32[20,128]{1,0:T(8,128)S(1)} %shard_map.100.mine), channel_id=1, source_target_pairs={{0,8},{8,0},{16,24},{24,16},{32,40},{40,32},{48,56},{56,48},{1,9},... | collective-permute-start | bytes 30728 | tf_op jit(solution)/shard_map/ppermute | solution.py:567
  137.1 6.7 %collective-permute-start.33 = (f32[44,128]{1,0:T(8,128)S(1)}, f32[44,128]{1,0:T(8,128)S(1)}, u32[]{:S(2)}, u32[]{:S(2)}) collective-permute-start(f32[44,128]{1,0:T(8,128)S(1)} %shard_map.101.mine), channel_id=1, source_target_pairs={{0,1},{1,0},{2,3},{3,2},{4,5},{5,4},{6,7},{7,6},{8,9},{9,8},{10,11... | collective-permute-start | bytes 67592 | tf_op jit(solution)/shard_map/ppermute | solution.py:567
  137.2 5.9 %collective-permute-start.34 = (f32[8,128]{1,0:T(8,128)S(1)}, f32[8,128]{1,0:T(8,128)S(1)}, u32[]{:S(2)}, u32[]{:S(2)}) collective-permute-start(f32[8,128]{1,0:T(8,128)S(1)} %slice.36), channel_id=1, source_target_pairs={{0,2},{1,3},{2,0},{3,1},{4,6},{5,7},{6,4},{7,5},{8,10},{9,11},{10,... | collective-permute-start | bytes 12296 | tf_op jit(solution)/shard_map/ppermute | solution.py:580
  140.2 3.6 %collective-permute-start.35 = (f32[8,128]{1,0:T(8,128)S(1)}, f32[8,128]{1,0:T(8,128)S(1)}, u32[]{:S(2)}, u32[]{:S(2)}) collective-permute-start(f32[8,128]{1,0:T(8,128)S(1)} %slice.36), channel_id=1, source_target_pairs={{0,3},{1,2},{2,1},{3,0},{4,7},{5,6},{6,5},{7,4},{8,11},{9,10},{10,... | collective-permute-start | bytes 12296 | tf_op jit(solution)/shard_map/ppermute | solution.py:580
  141.7 9.6 %collective-permute-start.39 = (f32[44,128]{1,0:T(8,128)S(1)}, f32[44,128]{1,0:T(8,128)S(1)}, u32[]{:S(2)}, u32[]{:S(2)}) collective-permute-start(f32[44,128]{1,0:T(8,128)S(1)} %shard_map.101.mine), channel_id=1, source_target_pairs={{0,7},{1,2},{2,1},{3,4},{4,3},{5,6},{6,5},{7,0},{8,15},{9,10},{10,... | collective-permute-start | bytes 67592 | tf_op jit(solution)/shard_map/ppermute | solution.py:567
  143.8 18.8 %collective-permute-start.38 = (f32[8,128]{1,0:T(8,128)S(1)}, f32[8,128]{1,0:T(8,128)S(1)}, u32[]{:S(2)}, u32[]{:S(2)}) collective-permute-start(f32[8,128]{1,0:T(8,128)S(1)} %fusion.1), channel_id=1, source_target_pairs={{0,36},{1,37},{2,38},{3,39},{4,32},{5,33},{6,34},{7,35},{8,44},{9,... | collective-permute-start | bytes 12296 | tf_op jit(solution)/shard_map/ppermute | solution.py:580
  145.1 17.4 %collective-permute-start.37 = (f32[8,128]{1,0:T(8,128)S(1)}, f32[8,128]{1,0:T(8,128)S(1)}, u32[]{:S(2)}, u32[]{:S(2)}) collective-permute-start(f32[8,128]{1,0:T(8,128)S(1)} %fusion.1), channel_id=1, source_target_pairs={{0,4},{1,5},{2,6},{3,7},{4,0},{5,1},{6,2},{7,3},{8,12},{9,13},{10,... | collective-permute-start | bytes 12296 | tf_op jit(solution)/shard_map/ppermute | solution.py:580
  147.2 15.4 %collective-permute-start.36 = (f32[8,128]{1,0:T(8,128)S(1)}, f32[8,128]{1,0:T(8,128)S(1)}, u32[]{:S(2)}, u32[]{:S(2)}) collective-permute-start(f32[8,128]{1,0:T(8,128)S(1)} %fusion.1), channel_id=1, source_target_pairs={{0,32},{8,40},{16,48},{24,56},{32,0},{40,8},{48,16},{56,24},{1,33}... | collective-permute-start | bytes 12296 | tf_op jit(solution)/shard_map/ppermute | solution.py:580

commit v6 on v5

--- a/solution.py
+++ b/solution.py
@@ -71,13 +71,19 @@
     return high, middle, (rest - middle.astype(jnp.float32)).astype(jnp.bfloat16)
 
 
-def arrange_kernel(table, live_count, pos, charges, types, out, order, col, left):
+def tiled(block, *index):
+    row = block[(*index, 0, 0)] if index else block[0, 0]
+    return jnp.concatenate([row[:, tile * LANES : (tile + 1) * LANES] for tile in range(TILES)], axis=0)
+
+
+def arrange_kernel(table, live_count, given, charges, types, out, order, col, left):
     count = live_count[0]
+    pos = jnp.concatenate([tiled(given, dim) for dim in range(3)], axis=0)
     slot = lax.broadcasted_iota(jnp.int32, (TILES, LANES), 0) * LANES
     slot = slot + lax.broadcasted_iota(jnp.int32, (TILES, LANES), 1)
     living = slot < count
     alive = jnp.where(living, 1.0, 0.0)
-    kinds = types[...]
+    kinds = tiled(types)
     props = []
     for row in range(3):
         value = jnp.zeros((TILES, LANES), jnp.float32)
@@ -100,7 +106,7 @@
         rank = jnp.concatenate(ranks, axis=0)
         group = jnp.floor(rank * (1.0 / size))
     order[...] = rank
-    values = [pos[0:4, :], pos[4:8, :], pos[8:12, :], charges[...] * alive]
+    values = [pos[0:4, :], pos[4:8, :], pos[8:12, :], tiled(charges) * alive]
     values += [props[1] * alive, props[2] * alive, props[0], alive]
     total = jnp.zeros((3 * len(values), SLOTS), jnp.float32)
     for tile in range(TILES):
@@ -117,7 +123,7 @@
             out[at, :] = total[channel : channel + 1, tile * LANES : (tile + 1) * LANES]
 
 
-def restore_kernel(order, moved, start, force, out, left):
+def restore_kernel(order, moved, start, force, displaced, final, left):
     values = [moved[4 * d : 4 * d + 4, :] - start[4 * d : 4 * d + 4, :] for d in range(3)]
     values += [force[4 * d : 4 * d + 4, :] for d in range(3)]
     values += [jnp.zeros((TILES, LANES), jnp.float32)] * 2
@@ -134,8 +140,8 @@
     for tile in range(TILES):
         total = totals[tile][0:8] + totals[tile][8:16] + totals[tile][16:24]
         for channel in range(6):
-            at = slice(4 * channel + tile, 4 * channel + tile + 1)
-            out[at, :] = total[channel : channel + 1, :]
+            out = displaced if channel < 3 else final
+            out[channel % 3, 0, 0, :, tile * LANES : (tile + 1) * LANES] = total[channel : channel + 1, :]
 
 
 def plan_kernel(rows, fields, *refs):
@@ -314,14 +320,19 @@
         give_shares(info, axis + 1, merged, number * PLANES, (out_first, out_second), base)
 
 
-def radius_merge_kernel(axis, count, info, mine, first, second, out):
+def radius_merge_kernel(axis, count, info, mine, first, second, *refs):
+    others, (out, sums) = refs[:-2], refs[-2:]
     after_first, _ = arrivals(info, axis)
     span = count * TILES
     out[span : 2 * span, :] = mine[0:span, :]
     slots = (jnp.where(after_first, 2 * span, 0), jnp.where(after_first, 0, 2 * span))
     for source, slot in zip((first, second), slots):
         out[pl.ds(pl.multiple_of(slot, 8), span), :] = source[0:span, :]
-    out[3 * span : 3 * span + 8, :] = mine[span : span + 8, :] + first[span : span + 8, :]
+    total = mine[span : span + 8, :] + first[span : span + 8, :]
+    for other in others:
+        total = total + other[...]
+    out[3 * span : 3 * span + 8, :] = total
+    sums[...] = total
 
 
 def over_tiles(count, some, carry):
@@ -580,17 +591,6 @@
     return lax.ppermute(block, tuple(axes), pairs)
 
 
-def from_all(block, steps):
-    found = []
-    for choice in range(1, 1 << len(steps)):
-        flips = {}
-        for k, (axis, flip) in enumerate(steps):
-            if choice >> k & 1:
-                flips[axis] = flips.get(axis, 0) | flip
-        found.append(across(block, list(flips), list(flips.values())))
-    return found
-
-
 def f32(*shape):
     return jax.ShapeDtypeStruct(shape, jnp.float32)
 
@@ -618,9 +618,9 @@
     )(
         type_table,
         live_count.reshape(1),
-        positions.reshape(3 * TILES, LANES),
-        charges.reshape(TILES, LANES),
-        atom_types.reshape(TILES, LANES),
+        positions,
+        charges,
+        atom_types,
     )
     given = jnp.pad(exp_map, ((0, 0), (0, 0), (0, LANES - BRICK)))
     own = atoms
@@ -664,7 +664,7 @@
             listed, tiles, evolved, exp_ext, sums = planned
         else:
             listed, tiles, evolved, sums = planned
-        early = from_all(sums, [(axis, 2) for axis, size in zip(AXES[:2], sizes) if size >= 4])
+        early = [across(sums, AXES[:1], [2])] if sizes[0] >= 4 else []
         radius = call(
             born_kernel,
             f32(TILES, LANES),
@@ -673,24 +673,28 @@
             smem=1,
             n_in=3,
         )(listed, tiles, own)
-        line = jnp.concatenate([radius, functools.reduce(jnp.add, early, sums)])
+        sums = functools.reduce(jnp.add, early, sums)
+        line = jnp.concatenate([radius, sums])
+        flips = (
+            [(("gy",), (2,)), (("gx", "gy"), (1, 2))] if sizes[1] >= 4 else [],
+            [(("gy",), (4,)), (("gy",), (5,))] if sizes[1] >= 8 else [],
+            [(("gz",), (2,)), (("gz",), (3,))] if sizes[2] >= 4 else [],
+        )
         for number, axis in enumerate(AXES):
             count = 3**number
             span = count * TILES
+            others = [across(sums, *flip) for flip in flips[number]]
             near = both_sides((line, line), axis)
             if number == 2:
-                here = line[span:]
-                sums = here + near[0][span:]
-                if sizes[2] >= 4:
-                    sums = sums + across(here, [axis], [2]) + across(here, [axis], [3])
+                sums = functools.reduce(jnp.add, others, sums + near[0][span:])
                 break
-            line = call(
+            line, sums = call(
                 functools.partial(radius_merge_kernel, number, count),
-                f32(3 * span + 8, LANES),
+                (f32(3 * span + 8, LANES), f32(8, LANES)),
                 1 << 20,
                 smem=1,
-                n_in=4,
-            )(info, line, *near)
+                n_in=4 + len(others),
+            )(info, line, *near, *others)
         pair = call(
             gb_kernel,
             f32(3 * TILES, LANES),
@@ -703,8 +707,8 @@
             smem=2,
             n_in=8,
         )(info, listed, tiles, own, radius, line, *near)
-        far = [(axis, 4) for axis, size in zip(AXES, sizes) if size >= 8]
-        sums = functools.reduce(jnp.add, from_all(sums, far), sums)
+        if sizes[2] >= 8:
+            sums = sums + across(sums, AXES[2:], [4])
         own, force = call(
             functools.partial(fit_kernel, scale, 1),
             (f32(32, LANES), f32(3 * TILES, LANES)),
@@ -719,17 +723,16 @@
             smem=1,
             n_in=6,
         )(info, own, evolved, exp_ext, sums, pair)
-    results = call(
+    displaced, final = call(
         restore_kernel,
-        f32(6 * TILES, LANES),
+        (f32(*positions.shape),) * 2,
         1 << 20,
         scratch=[pltpu.VMEM((24, LANES), jnp.float32)],
         n_in=4,
     )(order, own, atoms, force)
     model = evolved[5 : 5 + BRICK].reshape(BRICK, 8, 4, WIDE).transpose(0, 2, 1, 3).reshape(BRICK, WIDE, WIDE)
     model = model[:, PAD : PAD + BRICK, PAD : PAD + BRICK]
-    results = results.reshape((2,) + positions.shape)
-    return results[0], results[1], model
+    return displaced, final, model
 
 
 def solution(mesh):

time: 169 us -> 157 us (0.929); the launches traced: 166 us -> 157 us
  waiting for transfers between devices: 46.7 us -> 39.6 us
  starting transfers between devices: 59.9 us -> 55.7 us
  Pallas kernels: 53.8 us -> 57.7 us
    ppermute x12, waiting for transfers between devices: 37.6 us -> 23.6 us  [both_sides(): lax.ppermute(blocks[1], axis, odd)]
    ppermute x16, starting transfers between devices: 35 us -> 26.9 us  [across(): return lax.ppermute(block, tuple(axes), pairs)]
    ppermute x16, waiting for transfers between devices: 2.23 us -> 9.63 us  [across(): return lax.ppermute(block, tuple(axes), pairs)]
    ppermute x12, starting transfers between devices: 6.74 us -> 9.22 us  [both_sides(): lax.ppermute(blocks[0], axis, even)]
    pallas_call x2, Pallas kernels: 22.3 us -> 24.4 us  [on_device(): call(gb_kernel, f32(3 * TILES, LANES), 1 << 34, scratch=[pltpu.VMEM((5, S...]
  transfers between devices with their start and end apart: 40 -> 40, of which waited for: 16 -> 18; matrix products, arithmetic and copies ran while one was open for 1% -> 1% of each run, Pallas kernels for 21% -> 25%
where the time goes in v6:
time: 157 us
  Pallas kernels  57.7 us (37%)
  starting transfers between devices  55.7 us (35%)
  waiting for transfers between devices  39.6 us (25%)
  local copies, waits for them, and re-layouts  1.94 us (1%)
  between operations  1.65 us (1%)
    ppermute x16, starting transfers between devices, across(): return lax.ppermute(block, tuple(axes), pairs)  26.9 us
    pallas_call x2, Pallas kernels, on_device(): call(gb_kernel, f32(3 * TILES, LANES), 1 << 34, scratch=[pltpu.VMEM((5, S...  24.4 us
    ppermute x12, waiting for transfers between devices, both_sides(): lax.ppermute(blocks[1], axis, odd)  23.6 us
    ppermute x12, starting transfers between devices, both_sides(): lax.ppermute(blocks[1], axis, odd)  19.6 us
    pallas_call x2, Pallas kernels, on_device(): call(born_kernel, f32(TILES, LANES), 1 << 33, scratch=[pltpu.VMEM((3, SLO...  14.2 us
    ppermute x16, waiting for transfers between devices, across(): return lax.ppermute(block, tuple(axes), pairs)  9.63 us
    ppermute x12, starting transfers between devices, both_sides(): lax.ppermute(blocks[0], axis, even)  9.22 us
    ppermute x12, waiting for transfers between devices, both_sides(): lax.ppermute(blocks[0], axis, even)  6.35 us
  transfers between devices with their start and end apart: 40, of which 18 were waited for; matrix products, arithmetic and copies ran while one was open for 1% of the time, Pallas kernels for 25%

profile of v6, /device:TPU:56, one launch (start us, length us, event | category | flops | bytes accessed | tf_op | source)
XLA Modules:
  0.0 156.6 jit_solution(8327986279498643805)
XLA Ops:
  1.6 0.7 copy-done
  2.3 1.8 %shard_map.85 = (f32[32,128]{1,0:T(8,128)S(1)}, f32[4,128]{1,0:T(4,128)S(1)}) custom-call(f32[3,8]{1,0:T(4,128)S(1)} %copy-done.1, s32[1]{0:T(128)} %bitcast.21.live_count, f32[3,1,1,1,512]{4,3,2,1,0:T(1,128)S(1)} %copy-done, f32[1,1,1,512]{3,2,1,0:T(1,128)S(1)} %copy-done.2, s32[1,1,1,512]{3,2,1,0:T(1,128)S(1)} %copy-done.3), custom_call_target="tpu_custom_call" | custom-call | flops 4194304 | bytes 262144 | tf_op jit(solution)/shard_map/pallas_call | solution.py:611
  4.2 1.5 shard_map.86
  5.7 0.8 collective-permute-start.1
  6.4 0.7 collective-permute-start
  7.1 5.1 %collective-permute-done.1.second = f32[184,128]{1,0:T(8,128)S(1)} collective-permute-done((f32[184,128]{1,0:T(8,128)S(1)}, f32[184,128]{1,0:T(8,128)S(1)}, u32[]{:S(2)}, u32[]{:S(2)}) %collective-permute-start.1) | collective-permute-done | bytes 94240 | tf_op jit(solution)/shard_map/ppermute | solution.py:578
  12.3 0.7 shard_map.87
  13.0 3.0 %collective-permute-start.3 = (f32[280,128]{1,0:T(8,128)S(1)}, f32[280,128]{1,0:T(8,128)S(1)}, u32[]{:S(2)}, u32[]{:S(2)}) collective-permute-start(f32[280,128]{1,0:T(8,128)S(1)} %get-tuple-element.52), channel_id=1, source_target_pairs={{0,56},{8,16},{16,8},{24,32},{32,24},{40,48},{48,40},{56,0},{1,57}... | collective-permute-start | bytes 430088 | tf_op jit(solution)/shard_map/ppermute | solution.py:578
  16.1 4.9 %collective-permute-done.3.second = f32[280,128]{1,0:T(8,128)S(1)} collective-permute-done((f32[280,128]{1,0:T(8,128)S(1)}, f32[280,128]{1,0:T(8,128)S(1)}, u32[]{:S(2)}, u32[]{:S(2)}) %collective-permute-start.3) | collective-permute-done | bytes 143392 | tf_op jit(solution)/shard_map/ppermute | solution.py:578
  21.0 0.5 collective-permute-done.2.first
  21.5 0.7 shard_map.88
  22.3 2.0 %collective-permute-start.5 = (f32[424,128]{1,0:T(8,128)S(1)}, f32[424,128]{1,0:T(8,128)S(1)}, u32[]{:S(2)}, u32[]{:S(2)}) collective-permute-start(f32[424,128]{1,0:T(8,128)S(1)} %get-tuple-element.55), channel_id=1, source_target_pairs={{0,7},{1,2},{2,1},{3,4},{4,3},{5,6},{6,5},{7,0},{8,15},{9,10},{10,... | collective-permute-start | bytes 651272 | tf_op jit(solution)/shard_map/ppermute | solution.py:578
  24.3 4.0 %collective-permute-start.4 = (f32[424,128]{1,0:T(8,128)S(1)}, f32[424,128]{1,0:T(8,128)S(1)}, u32[]{:S(2)}, u32[]{:S(2)}) collective-permute-start(f32[424,128]{1,0:T(8,128)S(1)} %get-tuple-element.54.refs_3_), channel_id=1, source_target_pairs={{0,1},{1,0},{2,3},{3,2},{4,5},{5,4},{6,7},{7,6},{8,9},{9,8},{10,11... | collective-permute-start | bytes 651272 | tf_op jit(solution)/shard_map/ppermute | solution.py:578
  28.8 3.8 %collective-permute-done.4.refs_4_ = f32[424,128]{1,0:T(8,128)S(1)} collective-permute-done((f32[424,128]{1,0:T(8,128)S(1)}, f32[424,128]{1,0:T(8,128)S(1)}, u32[]{:S(2)}, u32[]{:S(2)}) %collective-permute-start.4) | collective-permute-done | bytes 217120 | tf_op jit(solution)/shard_map/ppermute | solution.py:578
  32.5 2.1 %shard_map.89 = (s32[16,128]{1,0:T(8,128)S(1)}, f32[112,8,128]{2,1,0:T(8,128)S(1)}, f32[26,8,128]{2,1,0:T(8,128)S(1)}, f32[26,8,128]{2,1,0:T(8,128)S(1)}, f32[8,128]{1,0:T(8,128)S(1)}) custom-call(s32[12]{0:T(128)S(1)} %stack.63.bounds.info.refs_0_, f32[32,128]{1,0:T(8,128)S(1)} %get-tuple-element.46.own.refs_1_.refs_0_.start, f32[416,128]{1,0:T(8,128)S(1)} %bitcast.22, ...), custom_call_target="tpu_custom_call" | custom-call | flops 4194304 | bytes 262144 | tf_op jit(solution)/shard_map/pallas_call | solution.py:653
  34.6 1.1 collective-permute-start.6
  35.7 7.0 %shard_map.90.own_radius = f32[4,128]{1,0:T(4,128)S(1)} custom-call(s32[16,128]{1,0:T(8,128)S(1)} %get-tuple-element.58.listed, f32[112,8,128]{2,1,0:T(8,128)S(1)} %get-tuple-element.59.tiles.refs_6_, f32[32,128]{1,0:T(8,128)S(1)} %get-tuple-element.46.own.refs_1_.refs_0_.start), custom_call_target="tpu_custom_call" | custom-call | flops 8589934592 | bytes 262144 | tf_op jit(solution)/shard_map/pallas_call | solution.py:668
  42.7 0.6 collective-permute-start.8
  43.3 0.7 collective-permute-start.7
  44.5 2.7 %collective-permute-start.9 = (f32[8,128]{1,0:T(8,128)S(1)}, f32[8,128]{1,0:T(8,128)S(1)}, u32[]{:S(2)}, u32[]{:S(2)}) collective-permute-start(f32[8,128]{1,0:T(8,128)S(1)} %add.45), channel_id=1, source_target_pairs={{0,16},{8,24},{16,0},{24,8},{32,48},{40,56},{48,32},{56,40},{1,17}... | collective-permute-start | bytes 12296 | tf_op jit(solution)/shard_map/ppermute | solution.py:591
  47.2 1.4 collective-permute-done.10.refs_1_
  48.6 1.1 collective-permute-done.9.refs_0_
  49.6 0.5 shard_map.91
  50.2 3.8 %collective-permute-start.12 = (f32[20,128]{1,0:T(8,128)S(1)}, f32[20,128]{1,0:T(8,128)S(1)}, u32[]{:S(2)}, u32[]{:S(2)}) collective-permute-start(f32[20,128]{1,0:T(8,128)S(1)} %get-tuple-element.61.mine), channel_id=1, source_target_pairs={{0,56},{8,16},{16,8},{24,32},{32,24},{40,48},{48,40},{56,0},{1,57}... | collective-permute-start | bytes 30728 | tf_op jit(solution)/shard_map/ppermute | solution.py:578
  54.0 1.7 %collective-permute-start.14 = (f32[8,128]{1,0:T(8,128)S(1)}, f32[8,128]{1,0:T(8,128)S(1)}, u32[]{:S(2)}, u32[]{:S(2)}) collective-permute-start(f32[8,128]{1,0:T(8,128)S(1)} %get-tuple-element.62), channel_id=1, source_target_pairs={{0,40},{8,32},{16,56},{24,48},{32,8},{40,0},{48,24},{56,16},{1,41}... | collective-permute-start | bytes 12296 | tf_op jit(solution)/shard_map/ppermute | solution.py:591
  55.7 1.8 %collective-permute-start.13 = (f32[8,128]{1,0:T(8,128)S(1)}, f32[8,128]{1,0:T(8,128)S(1)}, u32[]{:S(2)}, u32[]{:S(2)}) collective-permute-start(f32[8,128]{1,0:T(8,128)S(1)} %get-tuple-element.62), channel_id=1, source_target_pairs={{0,32},{8,40},{16,48},{24,56},{32,0},{40,8},{48,16},{56,24},{1,33}... | collective-permute-start | bytes 12296 | tf_op jit(solution)/shard_map/ppermute | solution.py:591
  57.5 1.0 collective-permute-done.14.refs_1_
  58.5 0.8 collective-permute-done.13.refs_0_
  60.3 2.0 %collective-permute-start.17 = (f32[8,128]{1,0:T(8,128)S(1)}, f32[8,128]{1,0:T(8,128)S(1)}, u32[]{:S(2)}, u32[]{:S(2)}) collective-permute-start(f32[8,128]{1,0:T(8,128)S(1)} %get-tuple-element.63), channel_id=1, source_target_pairs={{0,3},{1,2},{2,1},{3,0},{4,7},{5,6},{6,5},{7,4},{8,11},{9,10},{10,... | collective-permute-start | bytes 12296 | tf_op jit(solution)/shard_map/ppermute | solution.py:591
  62.3 2.1 %collective-permute-start.16 = (f32[8,128]{1,0:T(8,128)S(1)}, f32[8,128]{1,0:T(8,128)S(1)}, u32[]{:S(2)}, u32[]{:S(2)}) collective-permute-start(f32[8,128]{1,0:T(8,128)S(1)} %get-tuple-element.63), channel_id=1, source_target_pairs={{0,2},{1,3},{2,0},{3,1},{4,6},{5,7},{6,4},{7,5},{8,10},{9,11},{10,... | collective-permute-start | bytes 12296 | tf_op jit(solution)/shard_map/ppermute | solution.py:591
  64.4 1.5 collective-permute-start.19
  65.9 0.9 collective-permute-done.16
  66.8 2.3 %collective-permute-start.18 = (f32[8,128]{1,0:T(8,128)S(1)}, f32[8,128]{1,0:T(8,128)S(1)}, u32[]{:S(2)}, u32[]{:S(2)}) collective-permute-start(f32[8,128]{1,0:T(8,128)S(1)} %fusion.3), channel_id=1, source_target_pairs={{0,4},{1,5},{2,6},{3,7},{4,0},{5,1},{6,2},{7,3},{8,12},{9,13},{10,... | collective-permute-start | bytes 12296 | tf_op jit(solution)/shard_map/ppermute | solution.py:591
  69.2 12.0 %shard_map.93.refs_4_ = f32[12,128]{1,0:T(8,128)S(1)} custom-call(s32[12]{0:T(128)S(1)} %stack.63.bounds.info.refs_0_, s32[16,128]{1,0:T(8,128)S(1)} %get-tuple-element.58.listed, f32[112,8,128]{2,1,0:T(8,128)S(1)} %get-tuple-element.59.tiles.refs_6_, f32[32,128]{1,0:T(8,128)S(1)} %get-tuple-element.46.own.refs_1_.refs_0_.start, ...), custom_call_target="tpu_custom_call" | custom-call | flops 17179869184 | bytes 262144 | tf_op jit(solution)/shard_map/pallas_call | solution.py:698
  81.2 2.4 %shard_map.94 = (f32[32,128]{1,0:T(8,128)S(1)}, f32[12,128]{1,0:T(8,128)}) custom-call(s32[12]{0:T(128)S(1)} %stack.63.bounds.info.refs_0_, f32[32,128]{1,0:T(8,128)S(1)} %get-tuple-element.46.own.refs_1_.refs_0_.start, f32[26,8,128]{2,1,0:T(8,128)S(1)} %get-tuple-element.56.refs_1_, f32[26,8,128]{2,1,0:T(8,128)S(1)} %get-tuple-element.57.refs_2_.refs_7_, ...), custom_call_target="tpu_custom_call" | custom-call | flops 67108864 | bytes 262144 | tf_op jit(solution)/shard_map/pallas_call | solution.py:712
  83.6 1.5 shard_map.95
  85.3 4.9 %collective-permute-done.21.second = f32[96,128]{1,0:T(8,128)S(1)} collective-permute-done((f32[96,128]{1,0:T(8,128)S(1)}, f32[96,128]{1,0:T(8,128)S(1)}, u32[]{:S(2)}, u32[]{:S(2)}) %collective-permute-start.21) | collective-permute-done | bytes 49184 | tf_op jit(solution)/shard_map/ppermute | solution.py:578
  90.2 0.7 shard_map.96
  91.4 0.7 collective-permute-start.22
  92.1 5.4 %collective-permute-done.23.second = f32[152,128]{1,0:T(8,128)S(1)} collective-permute-done((f32[152,128]{1,0:T(8,128)S(1)}, f32[152,128]{1,0:T(8,128)S(1)}, u32[]{:S(2)}, u32[]{:S(2)}) %collective-permute-start.23) | collective-permute-done | bytes 77856 | tf_op jit(solution)/shard_map/ppermute | solution.py:578
  97.5 0.7 shard_map.97
  98.2 3.3 %collective-permute-start.25 = (f32[248,128]{1,0:T(8,128)S(1)}, f32[248,128]{1,0:T(8,128)S(1)}, u32[]{:S(2)}, u32[]{:S(2)}) collective-permute-start(f32[248,128]{1,0:T(8,128)S(1)} %get-tuple-element.74), channel_id=1, source_target_pairs={{0,7},{1,2},{2,1},{3,4},{4,3},{5,6},{6,5},{7,0},{8,15},{9,10},{10,... | collective-permute-start | bytes 380936 | tf_op jit(solution)/shard_map/ppermute | solution.py:578
  101.5 2.9 %collective-permute-done.25.refs_5_ = f32[248,128]{1,0:T(8,128)S(1)} collective-permute-done((f32[248,128]{1,0:T(8,128)S(1)}, f32[248,128]{1,0:T(8,128)S(1)}, u32[]{:S(2)}, u32[]{:S(2)}) %collective-permute-start.25) | collective-permute-done | bytes 127008 | tf_op jit(solution)/shard_map/ppermute | solution.py:578
  104.4 2.0 %collective-permute-done.24.refs_4_ = f32[248,128]{1,0:T(8,128)S(1)} collective-permute-done((f32[248,128]{1,0:T(8,128)S(1)}, f32[248,128]{1,0:T(8,128)S(1)}, u32[]{:S(2)}, u32[]{:S(2)}) %collective-permute-start.24) | collective-permute-done | bytes 127008 | tf_op jit(solution)/shard_map/ppermute | solution.py:578
  106.4 2.0 %shard_map.98 = (s32[16,128]{1,0:T(8,128)S(1)}, f32[112,8,128]{2,1,0:T(8,128)S(1)}, f32[26,8,128]{2,1,0:T(8,128)S(1)}, f32[8,128]{1,0:T(8,128)S(1)}) custom-call(s32[12]{0:T(128)S(1)} %stack.63.bounds.info.refs_0_, f32[32,128]{1,0:T(8,128)S(1)} %get-tuple-element.65.own.refs_1_.refs_0_, f32[208,128]{1,0:T(8,128)S(1)} %bitcast.25, ...), custom_call_target="tpu_custom_call" | custom-call | flops 4194304 | bytes 262144 | tf_op jit(solution)/shard_map/pallas_call | solution.py:653
  108.8 7.2 %shard_map.99.own_radius = f32[4,128]{1,0:T(4,128)S(1)} custom-call(s32[16,128]{1,0:T(8,128)S(1)} %get-tuple-element.76.listed, f32[112,8,128]{2,1,0:T(8,128)S(1)} %get-tuple-element.77.tiles, f32[32,128]{1,0:T(8,128)S(1)} %get-tuple-element.65.own.refs_1_.refs_0_), custom_call_target="tpu_custom_call" | custom-call | flops 8589934592 | bytes 262144 | tf_op jit(solution)/shard_map/pallas_call | solution.py:668
  116.4 1.7 %collective-permute-start.27 = (f32[12,128]{1,0:T(8,128)S(1)}, f32[12,128]{1,0:T(8,128)S(1)}, u32[]{:S(2)}, u32[]{:S(2)}) collective-permute-start(f32[12,128]{1,0:T(8,128)S(1)} %pad_maximum_fusion.1.mine), channel_id=1, source_target_pairs={{0,64},{64,0},{128,192},{192,128},{1,65},{65,1},{129,193},{193,129... | collective-permute-start | bytes 18440 | tf_op jit(solution)/shard_map/ppermute | solution.py:578
  118.5 2.7 %collective-permute-start.29 = (f32[8,128]{1,0:T(8,128)S(1)}, f32[8,128]{1,0:T(8,128)S(1)}, u32[]{:S(2)}, u32[]{:S(2)}) collective-permute-start(f32[8,128]{1,0:T(8,128)S(1)} %add.50), channel_id=1, source_target_pairs={{0,16},{8,24},{16,0},{24,8},{32,48},{40,56},{48,32},{56,40},{1,17}... | collective-permute-start | bytes 12296 | tf_op jit(solution)/shard_map/ppermute | solution.py:591
  121.2 1.4 collective-permute-done.30.refs_1_
  122.6 1.0 collective-permute-done.29.refs_0_
  124.2 2.0 %collective-permute-start.32 = (f32[20,128]{1,0:T(8,128)S(1)}, f32[20,128]{1,0:T(8,128)S(1)}, u32[]{:S(2)}, u32[]{:S(2)}) collective-permute-start(f32[20,128]{1,0:T(8,128)S(1)} %get-tuple-element.79.mine), channel_id=1, source_target_pairs={{0,56},{8,16},{16,8},{24,32},{32,24},{40,48},{48,40},{56,0},{1,57}... | collective-permute-start | bytes 30728 | tf_op jit(solution)/shard_map/ppermute | solution.py:578
  126.2 0.7 collective-permute-start.31
  126.9 0.9 collective-permute-start.34
  127.8 1.9 %collective-permute-start.33 = (f32[8,128]{1,0:T(8,128)S(1)}, f32[8,128]{1,0:T(8,128)S(1)}, u32[]{:S(2)}, u32[]{:S(2)}) collective-permute-start(f32[8,128]{1,0:T(8,128)S(1)} %get-tuple-element.80), channel_id=1, source_target_pairs={{0,32},{8,40},{16,48},{24,56},{32,0},{40,8},{48,16},{56,24},{1,33}... | collective-permute-start | bytes 12296 | tf_op jit(solution)/shard_map/ppermute | solution.py:591
  129.7 1.8 %collective-permute-done.34.refs_1_ = f32[8,128]{1,0:T(8,128)S(1)} collective-permute-done((f32[8,128]{1,0:T(8,128)S(1)}, f32[8,128]{1,0:T(8,128)S(1)}, u32[]{:S(2)}, u32[]{:S(2)}) %collective-permute-start.34) | collective-permute-done | bytes 4128 | tf_op jit(solution)/shard_map/ppermute | solution.py:591
  131.5 0.5 shard_map.101
  132.1 2.7 %collective-permute-start.37 = (f32[8,128]{1,0:T(8,128)S(1)}, f32[8,128]{1,0:T(8,128)S(1)}, u32[]{:S(2)}, u32[]{:S(2)}) collective-permute-start(f32[8,128]{1,0:T(8,128)S(1)} %get-tuple-element.81), channel_id=1, source_target_pairs={{0,3},{1,2},{2,1},{3,0},{4,7},{5,6},{6,5},{7,4},{8,11},{9,10},{10,... | collective-permute-start | bytes 12296 | tf_op jit(solution)/shard_map/ppermute | solution.py:591
  134.9 1.6 %collective-permute-start.36 = (f32[8,128]{1,0:T(8,128)S(1)}, f32[8,128]{1,0:T(8,128)S(1)}, u32[]{:S(2)}, u32[]{:S(2)}) collective-permute-start(f32[8,128]{1,0:T(8,128)S(1)} %get-tuple-element.81), channel_id=1, source_target_pairs={{0,2},{1,3},{2,0},{3,1},{4,6},{5,7},{6,4},{7,5},{8,10},{9,11},{10,... | collective-permute-start | bytes 12296 | tf_op jit(solution)/shard_map/ppermute | solution.py:591
  136.7 0.8 slice.18
  137.4 1.6 %collective-permute-start.39 = (f32[44,128]{1,0:T(8,128)S(1)}, f32[44,128]{1,0:T(8,128)S(1)}, u32[]{:S(2)}, u32[]{:S(2)}) collective-permute-start(f32[44,128]{1,0:T(8,128)S(1)} %get-tuple-element.82.mine), channel_id=1, source_target_pairs={{0,7},{1,2},{2,1},{3,4},{4,3},{5,6},{6,5},{7,0},{8,15},{9,10},{10,... | collective-permute-start | bytes 67592 | tf_op jit(solution)/shard_map/ppermute | solution.py:578
  139.4 2.1 %collective-permute-start.38 = (f32[8,128]{1,0:T(8,128)S(1)}, f32[8,128]{1,0:T(8,128)S(1)}, u32[]{:S(2)}, u32[]{:S(2)}) collective-permute-start(f32[8,128]{1,0:T(8,128)S(1)} %fusion.1), channel_id=1, source_target_pairs={{0,4},{1,5},{2,6},{3,7},{4,0},{5,1},{6,2},{7,3},{8,12},{9,13},{10,... | collective-permute-start | bytes 12296 | tf_op jit(solution)/shard_map/ppermute | solution.py:591
  141.5 12.4 %shard_map.102.refs_4_ = f32[12,128]{1,0:T(8,128)S(1)} custom-call(s32[12]{0:T(128)S(1)} %stack.63.bounds.info.refs_0_, s32[16,128]{1,0:T(8,128)S(1)} %get-tuple-element.76.listed, f32[112,8,128]{2,1,0:T(8,128)S(1)} %get-tuple-element.77.tiles, f32[32,128]{1,0:T(8,128)S(1)} %get-tuple-element.65.own.refs_1_.refs_0_, f32[4,128]{1,0:T(4,128)S(1)} %shard_map.99.own_radius, ...), custom_call_target="tpu_custom_call" | custom-call | flops 17179869184 | bytes 262144 | tf_op jit(solution)/shard_map/pallas_call | solution.py:698
  153.9 1.8 %shard_map.103 = (f32[32,128]{1,0:T(8,128)S(1)}, f32[12,128]{1,0:T(8,128)S(1)}) custom-call(s32[12]{0:T(128)S(1)} %stack.63.bounds.info.refs_0_, f32[32,128]{1,0:T(8,128)S(1)} %get-tuple-element.65.own.refs_1_.refs_0_, f32[26,8,128]{2,1,0:T(8,128)S(1)} %get-tuple-element.75.refs_1_, f32[26,8,128]{2,1,0:T(8,128)S(1)} %get-tuple-element.57.refs_2_.refs_7_, ...), custom_call_target="tpu_custom_call" | custom-call | flops 67108864 | bytes 262144 | tf_op jit(solution)/shard_map/pallas_call | solution.py:712
  155.8 0.9 shard_map.104
  (60 shorter events, 5.3 us)
Async XLA Ops:
  0.6 0.9 copy-start.4
  1.5 0.7 copy-start
  1.5 0.7 copy-start.1
  1.5 0.7 copy-start.2
  1.5 0.7 copy-start.3
  5.7 6.6 %collective-permute-start.1 = (f32[184,128]{1,0:T(8,128)S(1)}, f32[184,128]{1,0:T(8,128)S(1)}, u32[]{:S(2)}, u32[]{:S(2)}) collective-permute-start(f32[184,128]{1,0:T(8,128)S(1)} %get-tuple-element.49), channel_id=1, source_target_pairs={{0,192},{64,128},{128,64},{192,0},{1,193},{65,129},{129,65},{193,1... | collective-permute-start | bytes 282632 | tf_op jit(solution)/shard_map/ppermute | solution.py:578
  6.4 5.8 %collective-permute-start = (f32[184,128]{1,0:T(8,128)S(1)}, f32[184,128]{1,0:T(8,128)S(1)}, u32[]{:S(2)}, u32[]{:S(2)}) collective-permute-start(f32[184,128]{1,0:T(8,128)S(1)} %get-tuple-element.48.mine), channel_id=1, source_target_pairs={{0,64},{64,0},{128,192},{192,128},{1,65},{65,1},{129,193},{193,129... | collective-permute-start | bytes 282632 | tf_op jit(solution)/shard_map/ppermute | solution.py:578
  13.0 8.0 %collective-permute-start.3 = (f32[280,128]{1,0:T(8,128)S(1)}, f32[280,128]{1,0:T(8,128)S(1)}, u32[]{:S(2)}, u32[]{:S(2)}) collective-permute-start(f32[280,128]{1,0:T(8,128)S(1)} %get-tuple-element.52), channel_id=1, source_target_pairs={{0,56},{8,16},{16,8},{24,32},{32,24},{40,48},{48,40},{56,0},{1,57}... | collective-permute-start | bytes 430088 | tf_op jit(solution)/shard_map/ppermute | solution.py:578
  16.0 5.5 %collective-permute-start.2 = (f32[280,128]{1,0:T(8,128)S(1)}, f32[280,128]{1,0:T(8,128)S(1)}, u32[]{:S(2)}, u32[]{:S(2)}) collective-permute-start(f32[280,128]{1,0:T(8,128)S(1)} %get-tuple-element.51.mine), channel_id=1, source_target_pairs={{0,8},{8,0},{16,24},{24,16},{32,40},{40,32},{48,56},{56,48},{1,9},... | collective-permute-start | bytes 430088 | tf_op jit(solution)/shard_map/ppermute | solution.py:578
  22.3 6.5 %collective-permute-start.5 = (f32[424,128]{1,0:T(8,128)S(1)}, f32[424,128]{1,0:T(8,128)S(1)}, u32[]{:S(2)}, u32[]{:S(2)}) collective-permute-start(f32[424,128]{1,0:T(8,128)S(1)} %get-tuple-element.55), channel_id=1, source_target_pairs={{0,7},{1,2},{2,1},{3,4},{4,3},{5,6},{6,5},{7,0},{8,15},{9,10},{10,... | collective-permute-start | bytes 651272 | tf_op jit(solution)/shard_map/ppermute | solution.py:578
  24.3 8.2 %collective-permute-start.4 = (f32[424,128]{1,0:T(8,128)S(1)}, f32[424,128]{1,0:T(8,128)S(1)}, u32[]{:S(2)}, u32[]{:S(2)}) collective-permute-start(f32[424,128]{1,0:T(8,128)S(1)} %get-tuple-element.54.refs_3_), channel_id=1, source_target_pairs={{0,1},{1,0},{2,3},{3,2},{4,5},{5,4},{6,7},{7,6},{8,9},{9,8},{10,11... | collective-permute-start | bytes 651272 | tf_op jit(solution)/shard_map/ppermute | solution.py:578
  34.6 8.1 %collective-permute-start.6 = (f32[8,128]{1,0:T(8,128)S(1)}, f32[8,128]{1,0:T(8,128)S(1)}, u32[]{:S(2)}, u32[]{:S(2)}) collective-permute-start(f32[8,128]{1,0:T(8,128)S(1)} %get-tuple-element.60), channel_id=1, source_target_pairs={{0,128},{64,192},{128,0},{192,64},{1,129},{65,193},{129,1},{193,65... | collective-permute-start | bytes 12296 | tf_op jit(solution)/shard_map/ppermute | solution.py:591
  42.7 6.9 %collective-permute-start.8 = (f32[12,128]{1,0:T(8,128)S(1)}, f32[12,128]{1,0:T(8,128)S(1)}, u32[]{:S(2)}, u32[]{:S(2)}) collective-permute-start(f32[12,128]{1,0:T(8,128)S(1)} %pad_maximum_fusion.mine), channel_id=1, source_target_pairs={{0,192},{64,128},{128,64},{192,0},{1,193},{65,129},{129,65},{193,1... | collective-permute-start | bytes 18440 | tf_op jit(solution)/shard_map/ppermute | solution.py:578
  43.3 6.3 %collective-permute-start.7 = (f32[12,128]{1,0:T(8,128)S(1)}, f32[12,128]{1,0:T(8,128)S(1)}, u32[]{:S(2)}, u32[]{:S(2)}) collective-permute-start(f32[12,128]{1,0:T(8,128)S(1)} %pad_maximum_fusion.mine), channel_id=1, source_target_pairs={{0,64},{64,0},{128,192},{192,128},{1,65},{65,1},{129,193},{193,129... | collective-permute-start | bytes 18440 | tf_op jit(solution)/shard_map/ppermute | solution.py:578
  44.0 4.5 %collective-permute-start.10 = (f32[8,128]{1,0:T(8,128)S(1)}, f32[8,128]{1,0:T(8,128)S(1)}, u32[]{:S(2)}, u32[]{:S(2)}) collective-permute-start(f32[8,128]{1,0:T(8,128)S(1)} %add.45), channel_id=1, source_target_pairs={{0,80},{8,88},{16,64},{24,72},{32,112},{40,120},{48,96},{56,104},{... | collective-permute-start | bytes 12296 | tf_op jit(solution)/shard_map/ppermute | solution.py:591
  44.5 5.1 %collective-permute-start.9 = (f32[8,128]{1,0:T(8,128)S(1)}, f32[8,128]{1,0:T(8,128)S(1)}, u32[]{:S(2)}, u32[]{:S(2)}) collective-permute-start(f32[8,128]{1,0:T(8,128)S(1)} %add.45), channel_id=1, source_target_pairs={{0,16},{8,24},{16,0},{24,8},{32,48},{40,56},{48,32},{56,40},{1,17}... | collective-permute-start | bytes 12296 | tf_op jit(solution)/shard_map/ppermute | solution.py:591
  50.2 9.2 %collective-permute-start.12 = (f32[20,128]{1,0:T(8,128)S(1)}, f32[20,128]{1,0:T(8,128)S(1)}, u32[]{:S(2)}, u32[]{:S(2)}) collective-permute-start(f32[20,128]{1,0:T(8,128)S(1)} %get-tuple-element.61.mine), channel_id=1, source_target_pairs={{0,56},{8,16},{16,8},{24,32},{32,24},{40,48},{48,40},{56,0},{1,57}... | collective-permute-start | bytes 30728 | tf_op jit(solution)/shard_map/ppermute | solution.py:578
  54.0 5.3 %collective-permute-start.11 = (f32[20,128]{1,0:T(8,128)S(1)}, f32[20,128]{1,0:T(8,128)S(1)}, u32[]{:S(2)}, u32[]{:S(2)}) collective-permute-start(f32[20,128]{1,0:T(8,128)S(1)} %get-tuple-element.61.mine), channel_id=1, source_target_pairs={{0,8},{8,0},{16,24},{24,16},{32,40},{40,32},{48,56},{56,48},{1,9},... | collective-permute-start | bytes 30728 | tf_op jit(solution)/shard_map/ppermute | solution.py:578
  54.0 4.5 %collective-permute-start.14 = (f32[8,128]{1,0:T(8,128)S(1)}, f32[8,128]{1,0:T(8,128)S(1)}, u32[]{:S(2)}, u32[]{:S(2)}) collective-permute-start(f32[8,128]{1,0:T(8,128)S(1)} %get-tuple-element.62), channel_id=1, source_target_pairs={{0,40},{8,32},{16,56},{24,48},{32,8},{40,0},{48,24},{56,16},{1,41}... | collective-permute-start | bytes 12296 | tf_op jit(solution)/shard_map/ppermute | solution.py:591
  55.7 3.6 %collective-permute-start.13 = (f32[8,128]{1,0:T(8,128)S(1)}, f32[8,128]{1,0:T(8,128)S(1)}, u32[]{:S(2)}, u32[]{:S(2)}) collective-permute-start(f32[8,128]{1,0:T(8,128)S(1)} %get-tuple-element.62), channel_id=1, source_target_pairs={{0,32},{8,40},{16,48},{24,56},{32,0},{40,8},{48,16},{56,24},{1,33}... | collective-permute-start | bytes 12296 | tf_op jit(solution)/shard_map/ppermute | solution.py:591
  59.9 6.9 %collective-permute-start.15 = (f32[44,128]{1,0:T(8,128)S(1)}, f32[44,128]{1,0:T(8,128)S(1)}, u32[]{:S(2)}, u32[]{:S(2)}) collective-permute-start(f32[44,128]{1,0:T(8,128)S(1)} %get-tuple-element.64.mine), channel_id=1, source_target_pairs={{0,1},{1,0},{2,3},{3,2},{4,5},{5,4},{6,7},{7,6},{8,9},{9,8},{10,11... | collective-permute-start | bytes 67592 | tf_op jit(solution)/shard_map/ppermute | solution.py:578
  60.3 5.6 %collective-permute-start.17 = (f32[8,128]{1,0:T(8,128)S(1)}, f32[8,128]{1,0:T(8,128)S(1)}, u32[]{:S(2)}, u32[]{:S(2)}) collective-permute-start(f32[8,128]{1,0:T(8,128)S(1)} %get-tuple-element.63), channel_id=1, source_target_pairs={{0,3},{1,2},{2,1},{3,0},{4,7},{5,6},{6,5},{7,4},{8,11},{9,10},{10,... | collective-permute-start | bytes 12296 | tf_op jit(solution)/shard_map/ppermute | solution.py:591
  62.3 4.5 %collective-permute-start.16 = (f32[8,128]{1,0:T(8,128)S(1)}, f32[8,128]{1,0:T(8,128)S(1)}, u32[]{:S(2)}, u32[]{:S(2)}) collective-permute-start(f32[8,128]{1,0:T(8,128)S(1)} %get-tuple-element.63), channel_id=1, source_target_pairs={{0,2},{1,3},{2,0},{3,1},{4,6},{5,7},{6,4},{7,5},{8,10},{9,11},{10,... | collective-permute-start | bytes 12296 | tf_op jit(solution)/shard_map/ppermute | solution.py:591
  64.4 4.8 %collective-permute-start.19 = (f32[44,128]{1,0:T(8,128)S(1)}, f32[44,128]{1,0:T(8,128)S(1)}, u32[]{:S(2)}, u32[]{:S(2)}) collective-permute-start(f32[44,128]{1,0:T(8,128)S(1)} %get-tuple-element.64.mine), channel_id=1, source_target_pairs={{0,7},{1,2},{2,1},{3,4},{4,3},{5,6},{6,5},{7,0},{8,15},{9,10},{10,... | collective-permute-start | bytes 67592 | tf_op jit(solution)/shard_map/ppermute | solution.py:578
  66.8 14.3 %collective-permute-start.18 = (f32[8,128]{1,0:T(8,128)S(1)}, f32[8,128]{1,0:T(8,128)S(1)}, u32[]{:S(2)}, u32[]{:S(2)}) collective-permute-start(f32[8,128]{1,0:T(8,128)S(1)} %fusion.3), channel_id=1, source_target_pairs={{0,4},{1,5},{2,6},{3,7},{4,0},{5,1},{6,2},{7,3},{8,12},{9,13},{10,... | collective-permute-start | bytes 12296 | tf_op jit(solution)/shard_map/ppermute | solution.py:591
  85.1 5.1 %collective-permute-start.21 = (f32[96,128]{1,0:T(8,128)S(1)}, f32[96,128]{1,0:T(8,128)S(1)}, u32[]{:S(2)}, u32[]{:S(2)}) collective-permute-start(f32[96,128]{1,0:T(8,128)S(1)} %get-tuple-element.68), channel_id=1, source_target_pairs={{0,192},{64,128},{128,64},{192,0},{1,193},{65,129},{129,65},{193,1... | collective-permute-start | bytes 147464 | tf_op jit(solution)/shard_map/ppermute | solution.py:578
  85.2 5.0 %collective-permute-start.20 = (f32[96,128]{1,0:T(8,128)S(1)}, f32[96,128]{1,0:T(8,128)S(1)}, u32[]{:S(2)}, u32[]{:S(2)}) collective-permute-start(f32[96,128]{1,0:T(8,128)S(1)} %get-tuple-element.67.mine), channel_id=1, source_target_pairs={{0,64},{64,0},{128,192},{192,128},{1,65},{65,1},{129,193},{193,129... | collective-permute-start | bytes 147464 | tf_op jit(solution)/shard_map/ppermute | solution.py:578
  90.9 6.6 %collective-permute-start.23 = (f32[152,128]{1,0:T(8,128)S(1)}, f32[152,128]{1,0:T(8,128)S(1)}, u32[]{:S(2)}, u32[]{:S(2)}) collective-permute-start(f32[152,128]{1,0:T(8,128)S(1)} %get-tuple-element.71), channel_id=1, source_target_pairs={{0,56},{8,16},{16,8},{24,32},{32,24},{40,48},{48,40},{56,0},{1,57}... | collective-permute-start | bytes 233480 | tf_op jit(solution)/shard_map/ppermute | solution.py:578
  91.4 6.1 %collective-permute-start.22 = (f32[152,128]{1,0:T(8,128)S(1)}, f32[152,128]{1,0:T(8,128)S(1)}, u32[]{:S(2)}, u32[]{:S(2)}) collective-permute-start(f32[152,128]{1,0:T(8,128)S(1)} %get-tuple-element.70.mine), channel_id=1, source_target_pairs={{0,8},{8,0},{16,24},{24,16},{32,40},{40,32},{48,56},{56,48},{1,9},... | collective-permute-start | bytes 233480 | tf_op jit(solution)/shard_map/ppermute | solution.py:578
  98.2 6.2 %collective-permute-start.25 = (f32[248,128]{1,0:T(8,128)S(1)}, f32[248,128]{1,0:T(8,128)S(1)}, u32[]{:S(2)}, u32[]{:S(2)}) collective-permute-start(f32[248,128]{1,0:T(8,128)S(1)} %get-tuple-element.74), channel_id=1, source_target_pairs={{0,7},{1,2},{2,1},{3,4},{4,3},{5,6},{6,5},{7,0},{8,15},{9,10},{10,... | collective-permute-start | bytes 380936 | tf_op jit(solution)/shard_map/ppermute | solution.py:578
  101.4 4.9 %collective-permute-start.24 = (f32[248,128]{1,0:T(8,128)S(1)}, f32[248,128]{1,0:T(8,128)S(1)}, u32[]{:S(2)}, u32[]{:S(2)}) collective-permute-start(f32[248,128]{1,0:T(8,128)S(1)} %get-tuple-element.73.refs_3_), channel_id=1, source_target_pairs={{0,1},{1,0},{2,3},{3,2},{4,5},{5,4},{6,7},{7,6},{8,9},{9,8},{10,11... | collective-permute-start | bytes 380936 | tf_op jit(solution)/shard_map/ppermute | solution.py:578
  108.4 7.6 %collective-permute-start.26 = (f32[8,128]{1,0:T(8,128)S(1)}, f32[8,128]{1,0:T(8,128)S(1)}, u32[]{:S(2)}, u32[]{:S(2)}) collective-permute-start(f32[8,128]{1,0:T(8,128)S(1)} %get-tuple-element.78), channel_id=1, source_target_pairs={{0,128},{64,192},{128,0},{192,64},{1,129},{65,193},{129,1},{193,65... | collective-permute-start | bytes 12296 | tf_op jit(solution)/shard_map/ppermute | solution.py:591
  116.1 7.5 %collective-permute-start.28 = (f32[12,128]{1,0:T(8,128)S(1)}, f32[12,128]{1,0:T(8,128)S(1)}, u32[]{:S(2)}, u32[]{:S(2)}) collective-permute-start(f32[12,128]{1,0:T(8,128)S(1)} %pad_maximum_fusion.1.mine), channel_id=1, source_target_pairs={{0,192},{64,128},{128,64},{192,0},{1,193},{65,129},{129,65},{193,1... | collective-permute-start | bytes 18440 | tf_op jit(solution)/shard_map/ppermute | solution.py:578
  116.4 7.2 %collective-permute-start.27 = (f32[12,128]{1,0:T(8,128)S(1)}, f32[12,128]{1,0:T(8,128)S(1)}, u32[]{:S(2)}, u32[]{:S(2)}) collective-permute-start(f32[12,128]{1,0:T(8,128)S(1)} %pad_maximum_fusion.1.mine), channel_id=1, source_target_pairs={{0,64},{64,0},{128,192},{192,128},{1,65},{65,1},{129,193},{193,129... | collective-permute-start | bytes 18440 | tf_op jit(solution)/shard_map/ppermute | solution.py:578
  118.1 4.5 %collective-permute-start.30 = (f32[8,128]{1,0:T(8,128)S(1)}, f32[8,128]{1,0:T(8,128)S(1)}, u32[]{:S(2)}, u32[]{:S(2)}) collective-permute-start(f32[8,128]{1,0:T(8,128)S(1)} %add.50), channel_id=1, source_target_pairs={{0,80},{8,88},{16,64},{24,72},{32,112},{40,120},{48,96},{56,104},{... | collective-permute-start | bytes 12296 | tf_op jit(solution)/shard_map/ppermute | solution.py:591
  118.5 5.1 %collective-permute-start.29 = (f32[8,128]{1,0:T(8,128)S(1)}, f32[8,128]{1,0:T(8,128)S(1)}, u32[]{:S(2)}, u32[]{:S(2)}) collective-permute-start(f32[8,128]{1,0:T(8,128)S(1)} %add.50), channel_id=1, source_target_pairs={{0,16},{8,24},{16,0},{24,8},{32,48},{40,56},{48,32},{56,40},{1,17}... | collective-permute-start | bytes 12296 | tf_op jit(solution)/shard_map/ppermute | solution.py:591
  124.2 7.3 %collective-permute-start.32 = (f32[20,128]{1,0:T(8,128)S(1)}, f32[20,128]{1,0:T(8,128)S(1)}, u32[]{:S(2)}, u32[]{:S(2)}) collective-permute-start(f32[20,128]{1,0:T(8,128)S(1)} %get-tuple-element.79.mine), channel_id=1, source_target_pairs={{0,56},{8,16},{16,8},{24,32},{32,24},{40,48},{48,40},{56,0},{1,57}... | collective-permute-start | bytes 30728 | tf_op jit(solution)/shard_map/ppermute | solution.py:578
  126.2 5.3 %collective-permute-start.31 = (f32[20,128]{1,0:T(8,128)S(1)}, f32[20,128]{1,0:T(8,128)S(1)}, u32[]{:S(2)}, u32[]{:S(2)}) collective-permute-start(f32[20,128]{1,0:T(8,128)S(1)} %get-tuple-element.79.mine), channel_id=1, source_target_pairs={{0,8},{8,0},{16,24},{24,16},{32,40},{40,32},{48,56},{56,48},{1,9},... | collective-permute-start | bytes 30728 | tf_op jit(solution)/shard_map/ppermute | solution.py:578
  126.9 4.5 %collective-permute-start.34 = (f32[8,128]{1,0:T(8,128)S(1)}, f32[8,128]{1,0:T(8,128)S(1)}, u32[]{:S(2)}, u32[]{:S(2)}) collective-permute-start(f32[8,128]{1,0:T(8,128)S(1)} %get-tuple-element.80), channel_id=1, source_target_pairs={{0,40},{8,32},{16,56},{24,48},{32,8},{40,0},{48,24},{56,16},{1,41}... | collective-permute-start | bytes 12296 | tf_op jit(solution)/shard_map/ppermute | solution.py:591
  127.8 3.7 %collective-permute-start.33 = (f32[8,128]{1,0:T(8,128)S(1)}, f32[8,128]{1,0:T(8,128)S(1)}, u32[]{:S(2)}, u32[]{:S(2)}) collective-permute-start(f32[8,128]{1,0:T(8,128)S(1)} %get-tuple-element.80), channel_id=1, source_target_pairs={{0,32},{8,40},{16,48},{24,56},{32,0},{40,8},{48,16},{56,24},{1,33}... | collective-permute-start | bytes 12296 | tf_op jit(solution)/shard_map/ppermute | solution.py:591
  132.0 7.4 %collective-permute-start.35 = (f32[44,128]{1,0:T(8,128)S(1)}, f32[44,128]{1,0:T(8,128)S(1)}, u32[]{:S(2)}, u32[]{:S(2)}) collective-permute-start(f32[44,128]{1,0:T(8,128)S(1)} %get-tuple-element.82.mine), channel_id=1, source_target_pairs={{0,1},{1,0},{2,3},{3,2},{4,5},{5,4},{6,7},{7,6},{8,9},{9,8},{10,11... | collective-permute-start | bytes 67592 | tf_op jit(solution)/shard_map/ppermute | solution.py:578
  132.1 7.0 %collective-permute-start.37 = (f32[8,128]{1,0:T(8,128)S(1)}, f32[8,128]{1,0:T(8,128)S(1)}, u32[]{:S(2)}, u32[]{:S(2)}) collective-permute-start(f32[8,128]{1,0:T(8,128)S(1)} %get-tuple-element.81), channel_id=1, source_target_pairs={{0,3},{1,2},{2,1},{3,0},{4,7},{5,6},{6,5},{7,4},{8,11},{9,10},{10,... | collective-permute-start | bytes 12296 | tf_op jit(solution)/shard_map/ppermute | solution.py:591
  134.9 4.5 %collective-permute-start.36 = (f32[8,128]{1,0:T(8,128)S(1)}, f32[8,128]{1,0:T(8,128)S(1)}, u32[]{:S(2)}, u32[]{:S(2)}) collective-permute-start(f32[8,128]{1,0:T(8,128)S(1)} %get-tuple-element.81), channel_id=1, source_target_pairs={{0,2},{1,3},{2,0},{3,1},{4,6},{5,7},{6,4},{7,5},{8,10},{9,11},{10,... | collective-permute-start | bytes 12296 | tf_op jit(solution)/shard_map/ppermute | solution.py:591
  137.4 4.0 %collective-permute-start.39 = (f32[44,128]{1,0:T(8,128)S(1)}, f32[44,128]{1,0:T(8,128)S(1)}, u32[]{:S(2)}, u32[]{:S(2)}) collective-permute-start(f32[44,128]{1,0:T(8,128)S(1)} %get-tuple-element.82.mine), channel_id=1, source_target_pairs={{0,7},{1,2},{2,1},{3,4},{4,3},{5,6},{6,5},{7,0},{8,15},{9,10},{10,... | collective-permute-start | bytes 67592 | tf_op jit(solution)/shard_map/ppermute | solution.py:578
  139.4 14.5 %collective-permute-start.38 = (f32[8,128]{1,0:T(8,128)S(1)}, f32[8,128]{1,0:T(8,128)S(1)}, u32[]{:S(2)}, u32[]{:S(2)}) collective-permute-start(f32[8,128]{1,0:T(8,128)S(1)} %fusion.1), channel_id=1, source_target_pairs={{0,4},{1,5},{2,6},{3,7},{4,0},{5,1},{6,2},{7,3},{8,12},{9,13},{10,... | collective-permute-start | bytes 12296 | tf_op jit(solution)/shard_map/ppermute | solution.py:591

commit v7 on v6

--- a/solution.py
+++ b/solution.py
@@ -411,7 +411,7 @@
                 e = jnp.exp2(u * (ai * rows[tile, 1:2, :]))
                 inv = lax.rsqrt(u + (ri * rows[tile, 0:1, :]) * e)
                 t = s * inv
-                m = (tiles[tile, 4:5, :] * t) * (1.0 + (t * inv) * (0.25 - 0.0625 * e))
+                m = (tiles[tile, 4:5, :] * t) * (16.0 + (t * inv) * (4.0 - e))
                 fx = fx + m * dx
                 fy = fy + m * dy
                 fz = fz + m * dz
@@ -554,7 +554,7 @@
             plain = plain + at_x * part
             turned_z = turned_z + at_x * inner[rows, LANES : 2 * LANES]
         weight = scale * own[20 + tile : 21 + tile, :]
-        charge = -2.0 / (CUTOFF * CUTOFF) * own[12 + tile : 13 + tile, :]
+        charge = -2.0 / (16.0 * CUTOFF * CUTOFF) * own[12 + tile : 13 + tile, :]
         sides = (turned_x * y, plain * ys, turned_z * y)
         for channel in range(3):
             at = slice(4 * channel + tile, 4 * channel + tile + 1)
@@ -676,8 +676,8 @@
         sums = functools.reduce(jnp.add, early, sums)
         line = jnp.concatenate([radius, sums])
         flips = (
-            [(("gy",), (2,)), (("gx", "gy"), (1, 2))] if sizes[1] >= 4 else [],
-            [(("gy",), (4,)), (("gy",), (5,))] if sizes[1] >= 8 else [],
+            [(("gy",), (4,)), (("gx", "gy"), (1, 4))] if sizes[1] >= 8 else [],
+            [(("gy",), (2,)), (("gy",), (3,))] if sizes[1] >= 4 else [],
             [(("gz",), (2,)), (("gz",), (3,))] if sizes[2] >= 4 else [],
         )
         for number, axis in enumerate(AXES):
@@ -708,7 +708,7 @@
             n_in=8,
         )(info, listed, tiles, own, radius, line, *near)
         if sizes[2] >= 8:
-            sums = sums + across(sums, AXES[2:], [4])
+            sums = sums + across(sums, AXES[2:], [7])
         own, force = call(
             functools.partial(fit_kernel, scale, 1),
             (f32(32, LANES), f32(3 * TILES, LANES)),

time: 157 us -> 156 us (level)
  Pallas kernels: 57.7 us -> 55 us
    ppermute x12, starting transfers between devices: 19.6 us -> 16.7 us  [both_sides(): lax.ppermute(blocks[1], axis, odd)]
    ppermute x16, waiting for transfers between devices: 9.63 us -> 12.1 us  [across(): return lax.ppermute(block, tuple(axes), pairs)]
    ppermute x16, starting transfers between devices: 26.9 us -> 29.1 us  [across(): return lax.ppermute(block, tuple(axes), pairs)]
    ppermute x12, waiting for transfers between devices: 23.6 us -> 21.6 us  [both_sides(): lax.ppermute(blocks[1], axis, odd)]
    pallas_call x2, Pallas kernels: 24.4 us -> 22.5 us  [on_device(): call(gb_kernel, f32(3 * TILES, LANES), 1 << 34, scratch=[pltpu.VMEM((5, S...]
  transfers between devices with their start and end apart: 40 -> 40, of which waited for: 18 -> 20; matrix products, arithmetic and copies ran while one was open for 1% -> 1% of each run, Pallas kernels for 25% -> 23%
where the time goes in v7:
time: 156 us; the launch traced here: 155 us
  starting transfers between devices  56.2 us (36%)
  Pallas kernels  55 us (35%)
  waiting for transfers between devices  40.4 us (26%)
  local copies, waits for them, and re-layouts  1.94 us (1%)
  between operations  1.65 us (1%)
    ppermute x16, starting transfers between devices, across(): return lax.ppermute(block, tuple(axes), pairs)  29.1 us
    pallas_call x2, Pallas kernels, on_device(): call(gb_kernel, f32(3 * TILES, LANES), 1 << 34, scratch=[pltpu.VMEM((5, S...  22.5 us
    ppermute x12, waiting for transfers between devices, both_sides(): lax.ppermute(blocks[1], axis, odd)  21.6 us
    ppermute x12, starting transfers between devices, both_sides(): lax.ppermute(blocks[1], axis, odd)  16.7 us
    pallas_call x2, Pallas kernels, on_device(): call(born_kernel, f32(TILES, LANES), 1 << 33, scratch=[pltpu.VMEM((3, SLO...  13.4 us
    ppermute x16, waiting for transfers between devices, across(): return lax.ppermute(block, tuple(axes), pairs)  12.1 us
    ppermute x12, starting transfers between devices, both_sides(): lax.ppermute(blocks[0], axis, even)  10.4 us
    ppermute x12, waiting for transfers between devices, both_sides(): lax.ppermute(blocks[0], axis, even)  6.67 us
  transfers between devices with their start and end apart: 40, of which 20 were waited for; matrix products, arithmetic and copies ran while one was open for 1% of the time, Pallas kernels for 23%

profile of v7, /device:TPU:56, one launch (start us, length us, event | category | flops | bytes accessed | tf_op | source)
XLA Modules:
  0.0 155.2 jit_solution(10915582277007802263)
XLA Ops:
  1.6 0.7 copy-done
  2.3 1.8 %shard_map.85 = (f32[32,128]{1,0:T(8,128)S(1)}, f32[4,128]{1,0:T(4,128)S(1)}) custom-call(f32[3,8]{1,0:T(4,128)S(1)} %copy-done.1, s32[1]{0:T(128)} %bitcast.21.live_count, f32[3,1,1,1,512]{4,3,2,1,0:T(1,128)S(1)} %copy-done, f32[1,1,1,512]{3,2,1,0:T(1,128)S(1)} %copy-done.2, s32[1,1,1,512]{3,2,1,0:T(1,128)S(1)} %copy-done.3), custom_call_target="tpu_custom_call" | custom-call | flops 4194304 | bytes 262144 | tf_op jit(solution)/shard_map/pallas_call | solution.py:611
  4.2 1.5 shard_map.86
  5.7 0.8 collective-permute-start.1
  6.4 0.7 collective-permute-start
  7.1 5.1 %collective-permute-done.1.second = f32[184,128]{1,0:T(8,128)S(1)} collective-permute-done((f32[184,128]{1,0:T(8,128)S(1)}, f32[184,128]{1,0:T(8,128)S(1)}, u32[]{:S(2)}, u32[]{:S(2)}) %collective-permute-start.1) | collective-permute-done | bytes 94240 | tf_op jit(solution)/shard_map/ppermute | solution.py:578
  12.3 0.7 shard_map.87
  13.0 3.0 %collective-permute-start.3 = (f32[280,128]{1,0:T(8,128)S(1)}, f32[280,128]{1,0:T(8,128)S(1)}, u32[]{:S(2)}, u32[]{:S(2)}) collective-permute-start(f32[280,128]{1,0:T(8,128)S(1)} %get-tuple-element.52), channel_id=1, source_target_pairs={{0,56},{8,16},{16,8},{24,32},{32,24},{40,48},{48,40},{56,0},{1,57}... | collective-permute-start | bytes 430088 | tf_op jit(solution)/shard_map/ppermute | solution.py:578
  16.1 4.9 %collective-permute-done.3.second = f32[280,128]{1,0:T(8,128)S(1)} collective-permute-done((f32[280,128]{1,0:T(8,128)S(1)}, f32[280,128]{1,0:T(8,128)S(1)}, u32[]{:S(2)}, u32[]{:S(2)}) %collective-permute-start.3) | collective-permute-done | bytes 143392 | tf_op jit(solution)/shard_map/ppermute | solution.py:578
  21.5 0.7 shard_map.88
  22.3 2.0 %collective-permute-start.5 = (f32[424,128]{1,0:T(8,128)S(1)}, f32[424,128]{1,0:T(8,128)S(1)}, u32[]{:S(2)}, u32[]{:S(2)}) collective-permute-start(f32[424,128]{1,0:T(8,128)S(1)} %get-tuple-element.55), channel_id=1, source_target_pairs={{0,7},{1,2},{2,1},{3,4},{4,3},{5,6},{6,5},{7,0},{8,15},{9,10},{10,... | collective-permute-start | bytes 651272 | tf_op jit(solution)/shard_map/ppermute | solution.py:578
  24.3 4.0 %collective-permute-start.4 = (f32[424,128]{1,0:T(8,128)S(1)}, f32[424,128]{1,0:T(8,128)S(1)}, u32[]{:S(2)}, u32[]{:S(2)}) collective-permute-start(f32[424,128]{1,0:T(8,128)S(1)} %get-tuple-element.54.refs_3_), channel_id=1, source_target_pairs={{0,1},{1,0},{2,3},{3,2},{4,5},{5,4},{6,7},{7,6},{8,9},{9,8},{10,11... | collective-permute-start | bytes 651272 | tf_op jit(solution)/shard_map/ppermute | solution.py:578
  28.8 3.8 %collective-permute-done.4.refs_4_ = f32[424,128]{1,0:T(8,128)S(1)} collective-permute-done((f32[424,128]{1,0:T(8,128)S(1)}, f32[424,128]{1,0:T(8,128)S(1)}, u32[]{:S(2)}, u32[]{:S(2)}) %collective-permute-start.4) | collective-permute-done | bytes 217120 | tf_op jit(solution)/shard_map/ppermute | solution.py:578
  32.5 2.1 %shard_map.89 = (s32[16,128]{1,0:T(8,128)S(1)}, f32[112,8,128]{2,1,0:T(8,128)S(1)}, f32[26,8,128]{2,1,0:T(8,128)S(1)}, f32[26,8,128]{2,1,0:T(8,128)S(1)}, f32[8,128]{1,0:T(8,128)S(1)}) custom-call(s32[12]{0:T(128)S(1)} %stack.63.bounds.info.refs_0_, f32[32,128]{1,0:T(8,128)S(1)} %get-tuple-element.46.own.refs_1_.refs_0_.start, f32[416,128]{1,0:T(8,128)S(1)} %bitcast.22, ...), custom_call_target="tpu_custom_call" | custom-call | flops 4194304 | bytes 262144 | tf_op jit(solution)/shard_map/pallas_call | solution.py:653
  34.6 1.1 collective-permute-start.6
  35.7 6.7 %shard_map.90.own_radius = f32[4,128]{1,0:T(4,128)S(1)} custom-call(s32[16,128]{1,0:T(8,128)S(1)} %get-tuple-element.58.listed, f32[112,8,128]{2,1,0:T(8,128)S(1)} %get-tuple-element.59.tiles.refs_6_, f32[32,128]{1,0:T(8,128)S(1)} %get-tuple-element.46.own.refs_1_.refs_0_.start), custom_call_target="tpu_custom_call" | custom-call | flops 8589934592 | bytes 262144 | tf_op jit(solution)/shard_map/pallas_call | solution.py:668
  42.5 1.9 %collective-permute-start.7 = (f32[12,128]{1,0:T(8,128)S(1)}, f32[12,128]{1,0:T(8,128)S(1)}, u32[]{:S(2)}, u32[]{:S(2)}) collective-permute-start(f32[12,128]{1,0:T(8,128)S(1)} %pad_maximum_fusion.mine), channel_id=1, source_target_pairs={{0,64},{64,0},{128,192},{192,128},{1,65},{65,1},{129,193},{193,129... | collective-permute-start | bytes 18440 | tf_op jit(solution)/shard_map/ppermute | solution.py:578
  44.4 1.6 %collective-permute-start.9 = (f32[8,128]{1,0:T(8,128)S(1)}, f32[8,128]{1,0:T(8,128)S(1)}, u32[]{:S(2)}, u32[]{:S(2)}) collective-permute-start(f32[8,128]{1,0:T(8,128)S(1)} %add.45), channel_id=1, source_target_pairs={{0,32},{8,40},{16,48},{24,56},{32,0},{40,8},{48,16},{56,24},{1,33}... | collective-permute-start | bytes 12296 | tf_op jit(solution)/shard_map/ppermute | solution.py:591
  46.0 1.4 collective-permute-done.10.refs_1_
  47.4 0.6 collective-permute-done.9.refs_0_
  48.1 0.5 shard_map.91
  48.6 2.6 %collective-permute-start.12 = (f32[20,128]{1,0:T(8,128)S(1)}, f32[20,128]{1,0:T(8,128)S(1)}, u32[]{:S(2)}, u32[]{:S(2)}) collective-permute-start(f32[20,128]{1,0:T(8,128)S(1)} %get-tuple-element.61.mine), channel_id=1, source_target_pairs={{0,56},{8,16},{16,8},{24,32},{32,24},{40,48},{48,40},{56,0},{1,57}... | collective-permute-start | bytes 30728 | tf_op jit(solution)/shard_map/ppermute | solution.py:578
  51.2 1.8 %collective-permute-start.14 = (f32[8,128]{1,0:T(8,128)S(1)}, f32[8,128]{1,0:T(8,128)S(1)}, u32[]{:S(2)}, u32[]{:S(2)}) collective-permute-start(f32[8,128]{1,0:T(8,128)S(1)} %get-tuple-element.62), channel_id=1, source_target_pairs={{0,24},{8,16},{16,8},{24,0},{32,56},{40,48},{48,40},{56,32},{1,25}... | collective-permute-start | bytes 12296 | tf_op jit(solution)/shard_map/ppermute | solution.py:591
  53.0 2.3 %collective-permute-start.13 = (f32[8,128]{1,0:T(8,128)S(1)}, f32[8,128]{1,0:T(8,128)S(1)}, u32[]{:S(2)}, u32[]{:S(2)}) collective-permute-start(f32[8,128]{1,0:T(8,128)S(1)} %get-tuple-element.62), channel_id=1, source_target_pairs={{0,16},{8,24},{16,0},{24,8},{32,48},{40,56},{48,32},{56,40},{1,17}... | collective-permute-start | bytes 12296 | tf_op jit(solution)/shard_map/ppermute | solution.py:591
  55.3 0.7 collective-permute-done.14.refs_1_
  56.0 2.1 %collective-permute-done.13.refs_0_ = f32[8,128]{1,0:T(8,128)S(1)} collective-permute-done((f32[8,128]{1,0:T(8,128)S(1)}, f32[8,128]{1,0:T(8,128)S(1)}, u32[]{:S(2)}, u32[]{:S(2)}) %collective-permute-start.13) | collective-permute-done | bytes 4128 | tf_op jit(solution)/shard_map/ppermute | solution.py:591
  58.1 0.5 shard_map.92
  59.1 1.9 %collective-permute-start.17 = (f32[8,128]{1,0:T(8,128)S(1)}, f32[8,128]{1,0:T(8,128)S(1)}, u32[]{:S(2)}, u32[]{:S(2)}) collective-permute-start(f32[8,128]{1,0:T(8,128)S(1)} %get-tuple-element.63), channel_id=1, source_target_pairs={{0,3},{1,2},{2,1},{3,0},{4,7},{5,6},{6,5},{7,4},{8,11},{9,10},{10,... | collective-permute-start | bytes 12296 | tf_op jit(solution)/shard_map/ppermute | solution.py:591
  61.1 2.1 %collective-permute-start.16 = (f32[8,128]{1,0:T(8,128)S(1)}, f32[8,128]{1,0:T(8,128)S(1)}, u32[]{:S(2)}, u32[]{:S(2)}) collective-permute-start(f32[8,128]{1,0:T(8,128)S(1)} %get-tuple-element.63), channel_id=1, source_target_pairs={{0,2},{1,3},{2,0},{3,1},{4,6},{5,7},{6,4},{7,5},{8,10},{9,11},{10,... | collective-permute-start | bytes 12296 | tf_op jit(solution)/shard_map/ppermute | solution.py:591
  63.1 1.0 collective-permute-start.19
  64.1 1.5 collective-permute-done.16
  65.6 2.9 %collective-permute-start.18 = (f32[8,128]{1,0:T(8,128)S(1)}, f32[8,128]{1,0:T(8,128)S(1)}, u32[]{:S(2)}, u32[]{:S(2)}) collective-permute-start(f32[8,128]{1,0:T(8,128)S(1)} %fusion.3), channel_id=1, source_target_pairs={{0,7},{1,6},{2,5},{3,4},{4,3},{5,2},{6,1},{7,0},{8,15},{9,14},{10,... | collective-permute-start | bytes 12296 | tf_op jit(solution)/shard_map/ppermute | solution.py:591
  68.5 11.2 %shard_map.93.refs_4_ = f32[12,128]{1,0:T(8,128)S(1)} custom-call(s32[12]{0:T(128)S(1)} %stack.63.bounds.info.refs_0_, s32[16,128]{1,0:T(8,128)S(1)} %get-tuple-element.58.listed, f32[112,8,128]{2,1,0:T(8,128)S(1)} %get-tuple-element.59.tiles.refs_6_, f32[32,128]{1,0:T(8,128)S(1)} %get-tuple-element.46.own.refs_1_.refs_0_.start, ...), custom_call_target="tpu_custom_call" | custom-call | flops 17179869184 | bytes 262144 | tf_op jit(solution)/shard_map/pallas_call | solution.py:698
  79.7 2.4 %shard_map.94 = (f32[32,128]{1,0:T(8,128)S(1)}, f32[12,128]{1,0:T(8,128)}) custom-call(s32[12]{0:T(128)S(1)} %stack.63.bounds.info.refs_0_, f32[32,128]{1,0:T(8,128)S(1)} %get-tuple-element.46.own.refs_1_.refs_0_.start, f32[26,8,128]{2,1,0:T(8,128)S(1)} %get-tuple-element.56.refs_1_, f32[26,8,128]{2,1,0:T(8,128)S(1)} %get-tuple-element.57.refs_2_.refs_7_, ...), custom_call_target="tpu_custom_call" | custom-call | flops 67108864 | bytes 262144 | tf_op jit(solution)/shard_map/pallas_call | solution.py:712
  82.2 1.5 shard_map.95
  83.7 0.9 collective-permute-start.20
  84.6 4.1 %collective-permute-done.21.second = f32[96,128]{1,0:T(8,128)S(1)} collective-permute-done((f32[96,128]{1,0:T(8,128)S(1)}, f32[96,128]{1,0:T(8,128)S(1)}, u32[]{:S(2)}, u32[]{:S(2)}) %collective-permute-start.21) | collective-permute-done | bytes 49184 | tf_op jit(solution)/shard_map/ppermute | solution.py:578
  88.7 0.7 shard_map.96
  89.4 2.8 %collective-permute-start.23 = (f32[152,128]{1,0:T(8,128)S(1)}, f32[152,128]{1,0:T(8,128)S(1)}, u32[]{:S(2)}, u32[]{:S(2)}) collective-permute-start(f32[152,128]{1,0:T(8,128)S(1)} %get-tuple-element.71), channel_id=1, source_target_pairs={{0,56},{8,16},{16,8},{24,32},{32,24},{40,48},{48,40},{56,0},{1,57}... | collective-permute-start | bytes 233480 | tf_op jit(solution)/shard_map/ppermute | solution.py:578
  92.3 3.7 %collective-permute-done.23.second = f32[152,128]{1,0:T(8,128)S(1)} collective-permute-done((f32[152,128]{1,0:T(8,128)S(1)}, f32[152,128]{1,0:T(8,128)S(1)}, u32[]{:S(2)}, u32[]{:S(2)}) %collective-permute-start.23) | collective-permute-done | bytes 77856 | tf_op jit(solution)/shard_map/ppermute | solution.py:578
  96.0 0.6 collective-permute-done.22.first
  96.7 0.7 shard_map.97
  97.4 1.8 %collective-permute-start.25 = (f32[248,128]{1,0:T(8,128)S(1)}, f32[248,128]{1,0:T(8,128)S(1)}, u32[]{:S(2)}, u32[]{:S(2)}) collective-permute-start(f32[248,128]{1,0:T(8,128)S(1)} %get-tuple-element.74), channel_id=1, source_target_pairs={{0,7},{1,2},{2,1},{3,4},{4,3},{5,6},{6,5},{7,0},{8,15},{9,10},{10,... | collective-permute-start | bytes 380936 | tf_op jit(solution)/shard_map/ppermute | solution.py:578
  99.2 3.2 %collective-permute-done.25.refs_5_ = f32[248,128]{1,0:T(8,128)S(1)} collective-permute-done((f32[248,128]{1,0:T(8,128)S(1)}, f32[248,128]{1,0:T(8,128)S(1)}, u32[]{:S(2)}, u32[]{:S(2)}) %collective-permute-start.25) | collective-permute-done | bytes 127008 | tf_op jit(solution)/shard_map/ppermute | solution.py:578
  102.4 1.7 %collective-permute-done.24.refs_4_ = f32[248,128]{1,0:T(8,128)S(1)} collective-permute-done((f32[248,128]{1,0:T(8,128)S(1)}, f32[248,128]{1,0:T(8,128)S(1)}, u32[]{:S(2)}, u32[]{:S(2)}) %collective-permute-start.24) | collective-permute-done | bytes 127008 | tf_op jit(solution)/shard_map/ppermute | solution.py:578
  104.1 2.0 %shard_map.98 = (s32[16,128]{1,0:T(8,128)S(1)}, f32[112,8,128]{2,1,0:T(8,128)S(1)}, f32[26,8,128]{2,1,0:T(8,128)S(1)}, f32[8,128]{1,0:T(8,128)S(1)}) custom-call(s32[12]{0:T(128)S(1)} %stack.63.bounds.info.refs_0_, f32[32,128]{1,0:T(8,128)S(1)} %get-tuple-element.65.own.refs_1_.refs_0_, f32[208,128]{1,0:T(8,128)S(1)} %bitcast.25, ...), custom_call_target="tpu_custom_call" | custom-call | flops 4194304 | bytes 262144 | tf_op jit(solution)/shard_map/pallas_call | solution.py:653
  106.1 0.7 collective-permute-start.26
  106.8 6.7 %shard_map.99.own_radius = f32[4,128]{1,0:T(4,128)S(1)} custom-call(s32[16,128]{1,0:T(8,128)S(1)} %get-tuple-element.76.listed, f32[112,8,128]{2,1,0:T(8,128)S(1)} %get-tuple-element.77.tiles, f32[32,128]{1,0:T(8,128)S(1)} %get-tuple-element.65.own.refs_1_.refs_0_), custom_call_target="tpu_custom_call" | custom-call | flops 8589934592 | bytes 262144 | tf_op jit(solution)/shard_map/pallas_call | solution.py:668
  113.9 2.3 %collective-permute-start.27 = (f32[12,128]{1,0:T(8,128)S(1)}, f32[12,128]{1,0:T(8,128)S(1)}, u32[]{:S(2)}, u32[]{:S(2)}) collective-permute-start(f32[12,128]{1,0:T(8,128)S(1)} %pad_maximum_fusion.1.mine), channel_id=1, source_target_pairs={{0,64},{64,0},{128,192},{192,128},{1,65},{65,1},{129,193},{193,129... | collective-permute-start | bytes 18440 | tf_op jit(solution)/shard_map/ppermute | solution.py:578
  116.3 1.6 %collective-permute-start.29 = (f32[8,128]{1,0:T(8,128)S(1)}, f32[8,128]{1,0:T(8,128)S(1)}, u32[]{:S(2)}, u32[]{:S(2)}) collective-permute-start(f32[8,128]{1,0:T(8,128)S(1)} %add.50), channel_id=1, source_target_pairs={{0,32},{8,40},{16,48},{24,56},{32,0},{40,8},{48,16},{56,24},{1,33}... | collective-permute-start | bytes 12296 | tf_op jit(solution)/shard_map/ppermute | solution.py:591
  117.9 1.4 collective-permute-done.30.refs_1_
  119.3 0.6 collective-permute-done.29.refs_0_
  120.5 1.9 %collective-permute-start.32 = (f32[20,128]{1,0:T(8,128)S(1)}, f32[20,128]{1,0:T(8,128)S(1)}, u32[]{:S(2)}, u32[]{:S(2)}) collective-permute-start(f32[20,128]{1,0:T(8,128)S(1)} %get-tuple-element.79.mine), channel_id=1, source_target_pairs={{0,56},{8,16},{16,8},{24,32},{32,24},{40,48},{48,40},{56,0},{1,57}... | collective-permute-start | bytes 30728 | tf_op jit(solution)/shard_map/ppermute | solution.py:578
  122.4 2.4 %collective-permute-start.34 = (f32[8,128]{1,0:T(8,128)S(1)}, f32[8,128]{1,0:T(8,128)S(1)}, u32[]{:S(2)}, u32[]{:S(2)}) collective-permute-start(f32[8,128]{1,0:T(8,128)S(1)} %get-tuple-element.80), channel_id=1, source_target_pairs={{0,24},{8,16},{16,8},{24,0},{32,56},{40,48},{48,40},{56,32},{1,25}... | collective-permute-start | bytes 12296 | tf_op jit(solution)/shard_map/ppermute | solution.py:591
  124.8 1.7 %collective-permute-start.33 = (f32[8,128]{1,0:T(8,128)S(1)}, f32[8,128]{1,0:T(8,128)S(1)}, u32[]{:S(2)}, u32[]{:S(2)}) collective-permute-start(f32[8,128]{1,0:T(8,128)S(1)} %get-tuple-element.80), channel_id=1, source_target_pairs={{0,16},{8,24},{16,0},{24,8},{32,48},{40,56},{48,32},{56,40},{1,17}... | collective-permute-start | bytes 12296 | tf_op jit(solution)/shard_map/ppermute | solution.py:591
  126.5 0.7 collective-permute-done.34.refs_1_
  127.2 2.7 %collective-permute-done.33.refs_0_ = f32[8,128]{1,0:T(8,128)S(1)} collective-permute-done((f32[8,128]{1,0:T(8,128)S(1)}, f32[8,128]{1,0:T(8,128)S(1)}, u32[]{:S(2)}, u32[]{:S(2)}) %collective-permute-start.33) | collective-permute-done | bytes 4128 | tf_op jit(solution)/shard_map/ppermute | solution.py:591
  130.6 1.3 collective-permute-start.37
  131.9 3.1 %collective-permute-start.36 = (f32[8,128]{1,0:T(8,128)S(1)}, f32[8,128]{1,0:T(8,128)S(1)}, u32[]{:S(2)}, u32[]{:S(2)}) collective-permute-start(f32[8,128]{1,0:T(8,128)S(1)} %get-tuple-element.81), channel_id=1, source_target_pairs={{0,2},{1,3},{2,0},{3,1},{4,6},{5,7},{6,4},{7,5},{8,10},{9,11},{10,... | collective-permute-start | bytes 12296 | tf_op jit(solution)/shard_map/ppermute | solution.py:591
  135.2 0.8 slice.18
  136.6 4.6 %collective-permute-start.38 = (f32[8,128]{1,0:T(8,128)S(1)}, f32[8,128]{1,0:T(8,128)S(1)}, u32[]{:S(2)}, u32[]{:S(2)}) collective-permute-start(f32[8,128]{1,0:T(8,128)S(1)} %fusion.1), channel_id=1, source_target_pairs={{0,7},{1,6},{2,5},{3,4},{4,3},{5,2},{6,1},{7,0},{8,15},{9,14},{10,... | collective-permute-start | bytes 12296 | tf_op jit(solution)/shard_map/ppermute | solution.py:591
  141.2 11.3 %shard_map.102.refs_4_ = f32[12,128]{1,0:T(8,128)S(1)} custom-call(s32[12]{0:T(128)S(1)} %stack.63.bounds.info.refs_0_, s32[16,128]{1,0:T(8,128)S(1)} %get-tuple-element.76.listed, f32[112,8,128]{2,1,0:T(8,128)S(1)} %get-tuple-element.77.tiles, f32[32,128]{1,0:T(8,128)S(1)} %get-tuple-element.65.own.refs_1_.refs_0_, f32[4,128]{1,0:T(4,128)S(1)} %shard_map.99.own_radius, ...), custom_call_target="tpu_custom_call" | custom-call | flops 17179869184 | bytes 262144 | tf_op jit(solution)/shard_map/pallas_call | solution.py:698
  152.5 1.8 %shard_map.103 = (f32[32,128]{1,0:T(8,128)S(1)}, f32[12,128]{1,0:T(8,128)S(1)}) custom-call(s32[12]{0:T(128)S(1)} %stack.63.bounds.info.refs_0_, f32[32,128]{1,0:T(8,128)S(1)} %get-tuple-element.65.own.refs_1_.refs_0_, f32[26,8,128]{2,1,0:T(8,128)S(1)} %get-tuple-element.75.refs_1_, f32[26,8,128]{2,1,0:T(8,128)S(1)} %get-tuple-element.57.refs_2_.refs_7_, ...), custom_call_target="tpu_custom_call" | custom-call | flops 67108864 | bytes 262144 | tf_op jit(solution)/shard_map/pallas_call | solution.py:712
  154.3 0.9 shard_map.104
  (60 shorter events, 4.5 us)
Async XLA Ops:
  0.6 0.9 copy-start.4
  1.5 0.7 copy-start
  1.5 0.7 copy-start.1
  1.5 0.7 copy-start.2
  1.5 0.7 copy-start.3
  5.7 6.6 %collective-permute-start.1 = (f32[184,128]{1,0:T(8,128)S(1)}, f32[184,128]{1,0:T(8,128)S(1)}, u32[]{:S(2)}, u32[]{:S(2)}) collective-permute-start(f32[184,128]{1,0:T(8,128)S(1)} %get-tuple-element.49), channel_id=1, source_target_pairs={{0,192},{64,128},{128,64},{192,0},{1,193},{65,129},{129,65},{193,1... | collective-permute-start | bytes 282632 | tf_op jit(solution)/shard_map/ppermute | solution.py:578
  6.4 5.8 %collective-permute-start = (f32[184,128]{1,0:T(8,128)S(1)}, f32[184,128]{1,0:T(8,128)S(1)}, u32[]{:S(2)}, u32[]{:S(2)}) collective-permute-start(f32[184,128]{1,0:T(8,128)S(1)} %get-tuple-element.48.mine), channel_id=1, source_target_pairs={{0,64},{64,0},{128,192},{192,128},{1,65},{65,1},{129,193},{193,129... | collective-permute-start | bytes 282632 | tf_op jit(solution)/shard_map/ppermute | solution.py:578
  13.0 8.0 %collective-permute-start.3 = (f32[280,128]{1,0:T(8,128)S(1)}, f32[280,128]{1,0:T(8,128)S(1)}, u32[]{:S(2)}, u32[]{:S(2)}) collective-permute-start(f32[280,128]{1,0:T(8,128)S(1)} %get-tuple-element.52), channel_id=1, source_target_pairs={{0,56},{8,16},{16,8},{24,32},{32,24},{40,48},{48,40},{56,0},{1,57}... | collective-permute-start | bytes 430088 | tf_op jit(solution)/shard_map/ppermute | solution.py:578
  16.0 5.5 %collective-permute-start.2 = (f32[280,128]{1,0:T(8,128)S(1)}, f32[280,128]{1,0:T(8,128)S(1)}, u32[]{:S(2)}, u32[]{:S(2)}) collective-permute-start(f32[280,128]{1,0:T(8,128)S(1)} %get-tuple-element.51.mine), channel_id=1, source_target_pairs={{0,8},{8,0},{16,24},{24,16},{32,40},{40,32},{48,56},{56,48},{1,9},... | collective-permute-start | bytes 430088 | tf_op jit(solution)/shard_map/ppermute | solution.py:578
  22.3 6.5 %collective-permute-start.5 = (f32[424,128]{1,0:T(8,128)S(1)}, f32[424,128]{1,0:T(8,128)S(1)}, u32[]{:S(2)}, u32[]{:S(2)}) collective-permute-start(f32[424,128]{1,0:T(8,128)S(1)} %get-tuple-element.55), channel_id=1, source_target_pairs={{0,7},{1,2},{2,1},{3,4},{4,3},{5,6},{6,5},{7,0},{8,15},{9,10},{10,... | collective-permute-start | bytes 651272 | tf_op jit(solution)/shard_map/ppermute | solution.py:578
  24.3 8.2 %collective-permute-start.4 = (f32[424,128]{1,0:T(8,128)S(1)}, f32[424,128]{1,0:T(8,128)S(1)}, u32[]{:S(2)}, u32[]{:S(2)}) collective-permute-start(f32[424,128]{1,0:T(8,128)S(1)} %get-tuple-element.54.refs_3_), channel_id=1, source_target_pairs={{0,1},{1,0},{2,3},{3,2},{4,5},{5,4},{6,7},{7,6},{8,9},{9,8},{10,11... | collective-permute-start | bytes 651272 | tf_op jit(solution)/shard_map/ppermute | solution.py:578
  34.6 7.8 %collective-permute-start.6 = (f32[8,128]{1,0:T(8,128)S(1)}, f32[8,128]{1,0:T(8,128)S(1)}, u32[]{:S(2)}, u32[]{:S(2)}) collective-permute-start(f32[8,128]{1,0:T(8,128)S(1)} %get-tuple-element.60), channel_id=1, source_target_pairs={{0,128},{64,192},{128,0},{192,64},{1,129},{65,193},{129,1},{193,65... | collective-permute-start | bytes 12296 | tf_op jit(solution)/shard_map/ppermute | solution.py:591
  42.4 5.6 %collective-permute-start.8 = (f32[12,128]{1,0:T(8,128)S(1)}, f32[12,128]{1,0:T(8,128)S(1)}, u32[]{:S(2)}, u32[]{:S(2)}) collective-permute-start(f32[12,128]{1,0:T(8,128)S(1)} %pad_maximum_fusion.mine), channel_id=1, source_target_pairs={{0,192},{64,128},{128,64},{192,0},{1,193},{65,129},{129,65},{193,1... | collective-permute-start | bytes 18440 | tf_op jit(solution)/shard_map/ppermute | solution.py:578
  42.5 5.5 %collective-permute-start.7 = (f32[12,128]{1,0:T(8,128)S(1)}, f32[12,128]{1,0:T(8,128)S(1)}, u32[]{:S(2)}, u32[]{:S(2)}) collective-permute-start(f32[12,128]{1,0:T(8,128)S(1)} %pad_maximum_fusion.mine), channel_id=1, source_target_pairs={{0,64},{64,0},{128,192},{192,128},{1,65},{65,1},{129,193},{193,129... | collective-permute-start | bytes 18440 | tf_op jit(solution)/shard_map/ppermute | solution.py:578
  44.4 3.0 %collective-permute-start.10 = (f32[8,128]{1,0:T(8,128)S(1)}, f32[8,128]{1,0:T(8,128)S(1)}, u32[]{:S(2)}, u32[]{:S(2)}) collective-permute-start(f32[8,128]{1,0:T(8,128)S(1)} %add.45), channel_id=1, source_target_pairs={{0,96},{8,104},{16,112},{24,120},{32,64},{40,72},{48,80},{56,88},{... | collective-permute-start | bytes 12296 | tf_op jit(solution)/shard_map/ppermute | solution.py:591
  44.4 3.6 %collective-permute-start.9 = (f32[8,128]{1,0:T(8,128)S(1)}, f32[8,128]{1,0:T(8,128)S(1)}, u32[]{:S(2)}, u32[]{:S(2)}) collective-permute-start(f32[8,128]{1,0:T(8,128)S(1)} %add.45), channel_id=1, source_target_pairs={{0,32},{8,40},{16,48},{24,56},{32,0},{40,8},{48,16},{56,24},{1,33}... | collective-permute-start | bytes 12296 | tf_op jit(solution)/shard_map/ppermute | solution.py:591
  48.6 9.5 %collective-permute-start.12 = (f32[20,128]{1,0:T(8,128)S(1)}, f32[20,128]{1,0:T(8,128)S(1)}, u32[]{:S(2)}, u32[]{:S(2)}) collective-permute-start(f32[20,128]{1,0:T(8,128)S(1)} %get-tuple-element.61.mine), channel_id=1, source_target_pairs={{0,56},{8,16},{16,8},{24,32},{32,24},{40,48},{48,40},{56,0},{1,57}... | collective-permute-start | bytes 30728 | tf_op jit(solution)/shard_map/ppermute | solution.py:578
  51.2 6.9 %collective-permute-start.11 = (f32[20,128]{1,0:T(8,128)S(1)}, f32[20,128]{1,0:T(8,128)S(1)}, u32[]{:S(2)}, u32[]{:S(2)}) collective-permute-start(f32[20,128]{1,0:T(8,128)S(1)} %get-tuple-element.61.mine), channel_id=1, source_target_pairs={{0,8},{8,0},{16,24},{24,16},{32,40},{40,32},{48,56},{56,48},{1,9},... | collective-permute-start | bytes 30728 | tf_op jit(solution)/shard_map/ppermute | solution.py:578
  51.2 4.8 %collective-permute-start.14 = (f32[8,128]{1,0:T(8,128)S(1)}, f32[8,128]{1,0:T(8,128)S(1)}, u32[]{:S(2)}, u32[]{:S(2)}) collective-permute-start(f32[8,128]{1,0:T(8,128)S(1)} %get-tuple-element.62), channel_id=1, source_target_pairs={{0,24},{8,16},{16,8},{24,0},{32,56},{40,48},{48,40},{56,32},{1,25}... | collective-permute-start | bytes 12296 | tf_op jit(solution)/shard_map/ppermute | solution.py:591
  53.0 5.1 %collective-permute-start.13 = (f32[8,128]{1,0:T(8,128)S(1)}, f32[8,128]{1,0:T(8,128)S(1)}, u32[]{:S(2)}, u32[]{:S(2)}) collective-permute-start(f32[8,128]{1,0:T(8,128)S(1)} %get-tuple-element.62), channel_id=1, source_target_pairs={{0,16},{8,24},{16,0},{24,8},{32,48},{40,56},{48,32},{56,40},{1,17}... | collective-permute-start | bytes 12296 | tf_op jit(solution)/shard_map/ppermute | solution.py:591
  58.7 6.9 %collective-permute-start.15 = (f32[44,128]{1,0:T(8,128)S(1)}, f32[44,128]{1,0:T(8,128)S(1)}, u32[]{:S(2)}, u32[]{:S(2)}) collective-permute-start(f32[44,128]{1,0:T(8,128)S(1)} %get-tuple-element.64.mine), channel_id=1, source_target_pairs={{0,1},{1,0},{2,3},{3,2},{4,5},{5,4},{6,7},{7,6},{8,9},{9,8},{10,11... | collective-permute-start | bytes 67592 | tf_op jit(solution)/shard_map/ppermute | solution.py:578
  59.1 5.0 %collective-permute-start.17 = (f32[8,128]{1,0:T(8,128)S(1)}, f32[8,128]{1,0:T(8,128)S(1)}, u32[]{:S(2)}, u32[]{:S(2)}) collective-permute-start(f32[8,128]{1,0:T(8,128)S(1)} %get-tuple-element.63), channel_id=1, source_target_pairs={{0,3},{1,2},{2,1},{3,0},{4,7},{5,6},{6,5},{7,4},{8,11},{9,10},{10,... | collective-permute-start | bytes 12296 | tf_op jit(solution)/shard_map/ppermute | solution.py:591
  61.1 4.5 %collective-permute-start.16 = (f32[8,128]{1,0:T(8,128)S(1)}, f32[8,128]{1,0:T(8,128)S(1)}, u32[]{:S(2)}, u32[]{:S(2)}) collective-permute-start(f32[8,128]{1,0:T(8,128)S(1)} %get-tuple-element.63), channel_id=1, source_target_pairs={{0,2},{1,3},{2,0},{3,1},{4,6},{5,7},{6,4},{7,5},{8,10},{9,11},{10,... | collective-permute-start | bytes 12296 | tf_op jit(solution)/shard_map/ppermute | solution.py:591
  63.1 5.4 %collective-permute-start.19 = (f32[44,128]{1,0:T(8,128)S(1)}, f32[44,128]{1,0:T(8,128)S(1)}, u32[]{:S(2)}, u32[]{:S(2)}) collective-permute-start(f32[44,128]{1,0:T(8,128)S(1)} %get-tuple-element.64.mine), channel_id=1, source_target_pairs={{0,7},{1,2},{2,1},{3,4},{4,3},{5,6},{6,5},{7,0},{8,15},{9,10},{10,... | collective-permute-start | bytes 67592 | tf_op jit(solution)/shard_map/ppermute | solution.py:578
  65.6 14.1 %collective-permute-start.18 = (f32[8,128]{1,0:T(8,128)S(1)}, f32[8,128]{1,0:T(8,128)S(1)}, u32[]{:S(2)}, u32[]{:S(2)}) collective-permute-start(f32[8,128]{1,0:T(8,128)S(1)} %fusion.3), channel_id=1, source_target_pairs={{0,7},{1,6},{2,5},{3,4},{4,3},{5,2},{6,1},{7,0},{8,15},{9,14},{10,... | collective-permute-start | bytes 12296 | tf_op jit(solution)/shard_map/ppermute | solution.py:591
  83.6 5.1 %collective-permute-start.21 = (f32[96,128]{1,0:T(8,128)S(1)}, f32[96,128]{1,0:T(8,128)S(1)}, u32[]{:S(2)}, u32[]{:S(2)}) collective-permute-start(f32[96,128]{1,0:T(8,128)S(1)} %get-tuple-element.68), channel_id=1, source_target_pairs={{0,192},{64,128},{128,64},{192,0},{1,193},{65,129},{129,65},{193,1... | collective-permute-start | bytes 147464 | tf_op jit(solution)/shard_map/ppermute | solution.py:578
  83.7 5.0 %collective-permute-start.20 = (f32[96,128]{1,0:T(8,128)S(1)}, f32[96,128]{1,0:T(8,128)S(1)}, u32[]{:S(2)}, u32[]{:S(2)}) collective-permute-start(f32[96,128]{1,0:T(8,128)S(1)} %get-tuple-element.67.mine), channel_id=1, source_target_pairs={{0,64},{64,0},{128,192},{192,128},{1,65},{65,1},{129,193},{193,129... | collective-permute-start | bytes 147464 | tf_op jit(solution)/shard_map/ppermute | solution.py:578
  89.4 6.6 %collective-permute-start.23 = (f32[152,128]{1,0:T(8,128)S(1)}, f32[152,128]{1,0:T(8,128)S(1)}, u32[]{:S(2)}, u32[]{:S(2)}) collective-permute-start(f32[152,128]{1,0:T(8,128)S(1)} %get-tuple-element.71), channel_id=1, source_target_pairs={{0,56},{8,16},{16,8},{24,32},{32,24},{40,48},{48,40},{56,0},{1,57}... | collective-permute-start | bytes 233480 | tf_op jit(solution)/shard_map/ppermute | solution.py:578
  92.3 4.4 %collective-permute-start.22 = (f32[152,128]{1,0:T(8,128)S(1)}, f32[152,128]{1,0:T(8,128)S(1)}, u32[]{:S(2)}, u32[]{:S(2)}) collective-permute-start(f32[152,128]{1,0:T(8,128)S(1)} %get-tuple-element.70.mine), channel_id=1, source_target_pairs={{0,8},{8,0},{16,24},{24,16},{32,40},{40,32},{48,56},{56,48},{1,9},... | collective-permute-start | bytes 233480 | tf_op jit(solution)/shard_map/ppermute | solution.py:578
  97.4 5.0 %collective-permute-start.25 = (f32[248,128]{1,0:T(8,128)S(1)}, f32[248,128]{1,0:T(8,128)S(1)}, u32[]{:S(2)}, u32[]{:S(2)}) collective-permute-start(f32[248,128]{1,0:T(8,128)S(1)} %get-tuple-element.74), channel_id=1, source_target_pairs={{0,7},{1,2},{2,1},{3,4},{4,3},{5,6},{6,5},{7,0},{8,15},{9,10},{10,... | collective-permute-start | bytes 380936 | tf_op jit(solution)/shard_map/ppermute | solution.py:578
  99.2 4.9 %collective-permute-start.24 = (f32[248,128]{1,0:T(8,128)S(1)}, f32[248,128]{1,0:T(8,128)S(1)}, u32[]{:S(2)}, u32[]{:S(2)}) collective-permute-start(f32[248,128]{1,0:T(8,128)S(1)} %get-tuple-element.73.refs_3_), channel_id=1, source_target_pairs={{0,1},{1,0},{2,3},{3,2},{4,5},{5,4},{6,7},{7,6},{8,9},{9,8},{10,11... | collective-permute-start | bytes 380936 | tf_op jit(solution)/shard_map/ppermute | solution.py:578
  106.1 7.4 %collective-permute-start.26 = (f32[8,128]{1,0:T(8,128)S(1)}, f32[8,128]{1,0:T(8,128)S(1)}, u32[]{:S(2)}, u32[]{:S(2)}) collective-permute-start(f32[8,128]{1,0:T(8,128)S(1)} %get-tuple-element.78), channel_id=1, source_target_pairs={{0,128},{64,192},{128,0},{192,64},{1,129},{65,193},{129,1},{193,65... | collective-permute-start | bytes 12296 | tf_op jit(solution)/shard_map/ppermute | solution.py:591
  113.6 6.3 %collective-permute-start.28 = (f32[12,128]{1,0:T(8,128)S(1)}, f32[12,128]{1,0:T(8,128)S(1)}, u32[]{:S(2)}, u32[]{:S(2)}) collective-permute-start(f32[12,128]{1,0:T(8,128)S(1)} %pad_maximum_fusion.1.mine), channel_id=1, source_target_pairs={{0,192},{64,128},{128,64},{192,0},{1,193},{65,129},{129,65},{193,1... | collective-permute-start | bytes 18440 | tf_op jit(solution)/shard_map/ppermute | solution.py:578
  113.9 6.0 %collective-permute-start.27 = (f32[12,128]{1,0:T(8,128)S(1)}, f32[12,128]{1,0:T(8,128)S(1)}, u32[]{:S(2)}, u32[]{:S(2)}) collective-permute-start(f32[12,128]{1,0:T(8,128)S(1)} %pad_maximum_fusion.1.mine), channel_id=1, source_target_pairs={{0,64},{64,0},{128,192},{192,128},{1,65},{65,1},{129,193},{193,129... | collective-permute-start | bytes 18440 | tf_op jit(solution)/shard_map/ppermute | solution.py:578
  116.3 3.0 %collective-permute-start.30 = (f32[8,128]{1,0:T(8,128)S(1)}, f32[8,128]{1,0:T(8,128)S(1)}, u32[]{:S(2)}, u32[]{:S(2)}) collective-permute-start(f32[8,128]{1,0:T(8,128)S(1)} %add.50), channel_id=1, source_target_pairs={{0,96},{8,104},{16,112},{24,120},{32,64},{40,72},{48,80},{56,88},{... | collective-permute-start | bytes 12296 | tf_op jit(solution)/shard_map/ppermute | solution.py:591
  116.3 3.6 %collective-permute-start.29 = (f32[8,128]{1,0:T(8,128)S(1)}, f32[8,128]{1,0:T(8,128)S(1)}, u32[]{:S(2)}, u32[]{:S(2)}) collective-permute-start(f32[8,128]{1,0:T(8,128)S(1)} %add.50), channel_id=1, source_target_pairs={{0,32},{8,40},{16,48},{24,56},{32,0},{40,8},{48,16},{56,24},{1,33}... | collective-permute-start | bytes 12296 | tf_op jit(solution)/shard_map/ppermute | solution.py:591
  120.5 9.5 %collective-permute-start.32 = (f32[20,128]{1,0:T(8,128)S(1)}, f32[20,128]{1,0:T(8,128)S(1)}, u32[]{:S(2)}, u32[]{:S(2)}) collective-permute-start(f32[20,128]{1,0:T(8,128)S(1)} %get-tuple-element.79.mine), channel_id=1, source_target_pairs={{0,56},{8,16},{16,8},{24,32},{32,24},{40,48},{48,40},{56,0},{1,57}... | collective-permute-start | bytes 30728 | tf_op jit(solution)/shard_map/ppermute | solution.py:578
  122.4 7.5 %collective-permute-start.31 = (f32[20,128]{1,0:T(8,128)S(1)}, f32[20,128]{1,0:T(8,128)S(1)}, u32[]{:S(2)}, u32[]{:S(2)}) collective-permute-start(f32[20,128]{1,0:T(8,128)S(1)} %get-tuple-element.79.mine), channel_id=1, source_target_pairs={{0,8},{8,0},{16,24},{24,16},{32,40},{40,32},{48,56},{56,48},{1,9},... | collective-permute-start | bytes 30728 | tf_op jit(solution)/shard_map/ppermute | solution.py:578
  122.4 4.8 %collective-permute-start.34 = (f32[8,128]{1,0:T(8,128)S(1)}, f32[8,128]{1,0:T(8,128)S(1)}, u32[]{:S(2)}, u32[]{:S(2)}) collective-permute-start(f32[8,128]{1,0:T(8,128)S(1)} %get-tuple-element.80), channel_id=1, source_target_pairs={{0,24},{8,16},{16,8},{24,0},{32,56},{40,48},{48,40},{56,32},{1,25}... | collective-permute-start | bytes 12296 | tf_op jit(solution)/shard_map/ppermute | solution.py:591
  124.8 5.1 %collective-permute-start.33 = (f32[8,128]{1,0:T(8,128)S(1)}, f32[8,128]{1,0:T(8,128)S(1)}, u32[]{:S(2)}, u32[]{:S(2)}) collective-permute-start(f32[8,128]{1,0:T(8,128)S(1)} %get-tuple-element.80), channel_id=1, source_target_pairs={{0,16},{8,24},{16,0},{24,8},{32,48},{40,56},{48,32},{56,40},{1,17}... | collective-permute-start | bytes 12296 | tf_op jit(solution)/shard_map/ppermute | solution.py:591
  130.5 6.1 %collective-permute-start.35 = (f32[44,128]{1,0:T(8,128)S(1)}, f32[44,128]{1,0:T(8,128)S(1)}, u32[]{:S(2)}, u32[]{:S(2)}) collective-permute-start(f32[44,128]{1,0:T(8,128)S(1)} %get-tuple-element.82.mine), channel_id=1, source_target_pairs={{0,1},{1,0},{2,3},{3,2},{4,5},{5,4},{6,7},{7,6},{8,9},{9,8},{10,11... | collective-permute-start | bytes 67592 | tf_op jit(solution)/shard_map/ppermute | solution.py:578
  130.6 5.6 %collective-permute-start.37 = (f32[8,128]{1,0:T(8,128)S(1)}, f32[8,128]{1,0:T(8,128)S(1)}, u32[]{:S(2)}, u32[]{:S(2)}) collective-permute-start(f32[8,128]{1,0:T(8,128)S(1)} %get-tuple-element.81), channel_id=1, source_target_pairs={{0,3},{1,2},{2,1},{3,0},{4,7},{5,6},{6,5},{7,4},{8,11},{9,10},{10,... | collective-permute-start | bytes 12296 | tf_op jit(solution)/shard_map/ppermute | solution.py:591
  131.9 4.7 %collective-permute-start.36 = (f32[8,128]{1,0:T(8,128)S(1)}, f32[8,128]{1,0:T(8,128)S(1)}, u32[]{:S(2)}, u32[]{:S(2)}) collective-permute-start(f32[8,128]{1,0:T(8,128)S(1)} %get-tuple-element.81), channel_id=1, source_target_pairs={{0,2},{1,3},{2,0},{3,1},{4,6},{5,7},{6,4},{7,5},{8,10},{9,11},{10,... | collective-permute-start | bytes 12296 | tf_op jit(solution)/shard_map/ppermute | solution.py:591
  135.9 5.2 %collective-permute-start.39 = (f32[44,128]{1,0:T(8,128)S(1)}, f32[44,128]{1,0:T(8,128)S(1)}, u32[]{:S(2)}, u32[]{:S(2)}) collective-permute-start(f32[44,128]{1,0:T(8,128)S(1)} %get-tuple-element.82.mine), channel_id=1, source_target_pairs={{0,7},{1,2},{2,1},{3,4},{4,3},{5,6},{6,5},{7,0},{8,15},{9,10},{10,... | collective-permute-start | bytes 67592 | tf_op jit(solution)/shard_map/ppermute | solution.py:578
  136.6 15.8 %collective-permute-start.38 = (f32[8,128]{1,0:T(8,128)S(1)}, f32[8,128]{1,0:T(8,128)S(1)}, u32[]{:S(2)}, u32[]{:S(2)}) collective-permute-start(f32[8,128]{1,0:T(8,128)S(1)} %fusion.1), channel_id=1, source_target_pairs={{0,7},{1,6},{2,5},{3,4},{4,3},{5,2},{6,1},{7,0},{8,15},{9,14},{10,... | collective-permute-start | bytes 12296 | tf_op jit(solution)/shard_map/ppermute | solution.py:591

commit v8 on v7

--- a/solution.py
+++ b/solution.py
@@ -24,6 +24,7 @@
 PLANES = 26
 HALF = PLANES // 2
 EDGE = 10
+GIVEN_EDGE = 5
 PAD = 8
 WIDE = 32
 INTERPRET = False
@@ -153,7 +154,7 @@
     else:
         known = refs[6:7]
         given = refs[7]
-        listed, tiles, evolved, sums, active = refs[8:]
+        listed, tiles, evolved, sums, model, active = refs[8:]
     low, high = [], []
     for dim in range(3):
         living = own[28:32, :] > 0.0
@@ -235,6 +236,10 @@
         take_shares(2, adds, sources[1:], 9 * rows + 8 * HALF, given, 0)
     for plane in range(PLANES):
         value = evolved[plane]
+        if fields == 1 and 5 <= plane < 5 + BRICK:
+            for block in (1, 2):
+                moved = pltpu.roll(value, LANES - WIDE * block - PAD, 1)
+                model[plane - 5, 8 * block - 8 : 8 * block, :] = moved[:, 0:BRICK]
         if 5 <= plane < 5 + BRICK:
             value = jnp.where(own_points, value, 0.0)
             wanted = jnp.where(own_points, given[plane], 0.0)
@@ -310,9 +315,10 @@
     for number in range(fields):
         if axis == 0:
             for source, slot, ok in zip((first, second), slots, valid):
-                into = pl.ds(number * PLANES + jnp.where(slot > 0, BRICK, 0), EDGE)
-                at = slice(span + 8 * EDGE * number, span + 8 * EDGE * (number + 1))
-                merged[into] = merged[into] + source[at, :].reshape(EDGE, 8, LANES) * ok
+                width = GIVEN_EDGE if number else EDGE
+                into = pl.ds(number * PLANES + jnp.where(slot > 0, PLANES - width, 0), width)
+                at = slice(span + 8 * EDGE * number, span + 8 * EDGE * number + 8 * width)
+                merged[into] = merged[into] + source[at, :].reshape(width, 8, LANES) * ok
         else:
             base = span + 8 * HALF * number
             take_shares(axis, shift_masks(info, axis), (first, second), base, merged, number * PLANES)
@@ -501,12 +507,14 @@
             value = pltpu.roll(given[plane, 0:8, :], WIDE + PAD, 1) + pltpu.roll(given[plane, 8:16, :], 2 * WIDE + PAD, 1)
             field[base + 8 * (plane + 5) : base + 8 * (plane + 6), :] = value
     after_first, _ = arrivals(bounds, 0)
-    starts = (jnp.where(after_first, 8 * BRICK, 0), jnp.where(after_first, 0, 8 * BRICK))
-    for out, start in zip((out_first, out_second), starts):
+    for out, after in ((out_first, after_first), (out_second, jnp.logical_not(after_first))):
         out[0:rows, :] = own[0:rows, :]
-        for number in range(fields):
-            off = pl.ds(pl.multiple_of(8 * PLANES * number + start, 8), 8 * EDGE)
-            out[rows + 8 * EDGE * number : rows + 8 * EDGE * (number + 1), :] = field[off, :]
+        off = pl.ds(pl.multiple_of(jnp.where(after, 8 * BRICK, 0), 8), 8 * EDGE)
+        out[rows : rows + 8 * EDGE, :] = field[off, :]
+        if fields == 2:
+            start = 8 * PLANES + jnp.where(after, 8 * BRICK, 8 * GIVEN_EDGE)
+            off = pl.ds(pl.multiple_of(start, 8), 8 * GIVEN_EDGE)
+            out[rows + 8 * EDGE :, :] = field[off, :]
 
 
 def fit_kernel(scale, parts, bounds, *refs):
@@ -629,7 +637,7 @@
         planes = 8 * PLANES * fields
         field, *mine = call(
             functools.partial(splat_kernel, fields, rows),
-            (f32(planes, LANES),) + (f32(rows + 8 * EDGE * fields, LANES),) * 2,
+            (f32(planes, LANES),) + (f32(rows + 8 * EDGE + 8 * GIVEN_EDGE * (fields - 1), LANES),) * 2,
             1 << 26,
             scratch=[
                 pltpu.VMEM((WIDE, LANES), jnp.float32),
@@ -654,7 +662,8 @@
             functools.partial(plan_kernel, rows, fields),
             (jax.ShapeDtypeStruct((BLOCKS, LANES), jnp.int32), f32(ROOM, 8, LANES))
             + (f32(PLANES, 8, LANES),) * fields
-            + (f32(8, LANES),),
+            + (f32(8, LANES),)
+            + (() if step == 0 else (f32(BRICK, BRICK, BRICK),)),
             1 << 22,
             scratch=[pltpu.VMEM((TILES, LANES, LANES), jnp.float32)],
             smem=1,
@@ -663,7 +672,7 @@
         if step == 0:
             listed, tiles, evolved, exp_ext, sums = planned
         else:
-            listed, tiles, evolved, sums = planned
+            listed, tiles, evolved, sums, model = planned
         early = [across(sums, AXES[:1], [2])] if sizes[0] >= 4 else []
         radius = call(
             born_kernel,
@@ -730,8 +739,6 @@
         scratch=[pltpu.VMEM((24, LANES), jnp.float32)],
         n_in=4,
     )(order, own, atoms, force)
-    model = evolved[5 : 5 + BRICK].reshape(BRICK, 8, 4, WIDE).transpose(0, 2, 1, 3).reshape(BRICK, WIDE, WIDE)
-    model = model[:, PAD : PAD + BRICK, PAD : PAD + BRICK]
     return displaced, final, model
 
 

time: 156 us -> 155 us (level)
  Pallas kernels: 55 us -> 52.9 us
    ppermute x12, starting transfers between devices: 16.7 us -> 19.9 us  [both_sides(): lax.ppermute(blocks[1], axis, odd)]
    pallas_call x2, Pallas kernels: 22.5 us -> 20.7 us  [on_device(): call(gb_kernel, f32(3 * TILES, LANES), 1 << 34, scratch=[pltpu.VMEM((5, S...]
  transfers between devices with their start and end apart: 40 -> 40, of which waited for: 20 -> 20; matrix products, arithmetic and copies ran while one was open for 1% -> 0% of each run, Pallas kernels for 23% -> 22%
where the time goes in v8:
time: 155 us; the launch traced here: 153 us
  starting transfers between devices  57.3 us (37%)
  Pallas kernels  52.9 us (34%)
  waiting for transfers between devices  40.6 us (26%)
  between operations  1.62 us (1%)
    ppermute x16, starting transfers between devices, across(): return lax.ppermute(block, tuple(axes), pairs)  28.1 us
    ppermute x12, waiting for transfers between devices, both_sides(): lax.ppermute(blocks[1], axis, odd)  21.3 us
    pallas_call x2, Pallas kernels, on_device(): call(gb_kernel, f32(3 * TILES, LANES), 1 << 34, scratch=[pltpu.VMEM((5, S...  20.7 us
    ppermute x12, starting transfers between devices, both_sides(): lax.ppermute(blocks[1], axis, odd)  19.9 us
    ppermute x16, waiting for transfers between devices, across(): return lax.ppermute(block, tuple(axes), pairs)  13.3 us
    pallas_call x2, Pallas kernels, on_device(): call(born_kernel, f32(TILES, LANES), 1 << 33, scratch=[pltpu.VMEM((3, SLO...  12.4 us
    ppermute x12, starting transfers between devices, both_sides(): lax.ppermute(blocks[0], axis, even)  9.29 us
    ppermute x12, waiting for transfers between devices, both_sides(): lax.ppermute(blocks[0], axis, even)  6.06 us
  transfers between devices with their start and end apart: 40, of which 20 were waited for; matrix products, arithmetic and copies ran while one was open for 0% of the time, Pallas kernels for 22%

profile of v8, /device:TPU:56, one launch (start us, length us, event | category | flops | bytes accessed | tf_op | source)
XLA Modules:
  0.0 153.5 jit_solution(10703120140706524217)
XLA Ops:
  1.6 0.7 copy-done
  2.3 1.8 %shard_map.85 = (f32[32,128]{1,0:T(8,128)S(1)}, f32[4,128]{1,0:T(4,128)S(1)}) custom-call(f32[3,8]{1,0:T(4,128)S(1)} %copy-done.1, s32[1]{0:T(128)} %bitcast.17.live_count, f32[3,1,1,1,512]{4,3,2,1,0:T(1,128)S(1)} %copy-done, f32[1,1,1,512]{3,2,1,0:T(1,128)S(1)} %copy-done.2, s32[1,1,1,512]{3,2,1,0:T(1,128)S(1)} %copy-done.3), custom_call_target="tpu_custom_call" | custom-call | flops 4194304 | bytes 262144 | tf_op jit(solution)/shard_map/pallas_call | solution.py:619
  4.2 1.5 shard_map.86
  5.7 0.8 collective-permute-start.1
  6.4 0.7 collective-permute-start
  7.1 4.7 %collective-permute-done.1.second = f32[144,128]{1,0:T(8,128)S(1)} collective-permute-done((f32[144,128]{1,0:T(8,128)S(1)}, f32[144,128]{1,0:T(8,128)S(1)}, u32[]{:S(2)}, u32[]{:S(2)}) %collective-permute-start.1) | collective-permute-done | bytes 73760 | tf_op jit(solution)/shard_map/ppermute | solution.py:586
  11.8 0.7 shard_map.87
  12.5 3.0 %collective-permute-start.3 = (f32[280,128]{1,0:T(8,128)S(1)}, f32[280,128]{1,0:T(8,128)S(1)}, u32[]{:S(2)}, u32[]{:S(2)}) collective-permute-start(f32[280,128]{1,0:T(8,128)S(1)} %get-tuple-element.53), channel_id=1, source_target_pairs={{0,56},{8,16},{16,8},{24,32},{32,24},{40,48},{48,40},{56,0},{1,57}... | collective-permute-start | bytes 430088 | tf_op jit(solution)/shard_map/ppermute | solution.py:586
  15.6 4.9 %collective-permute-done.3.second = f32[280,128]{1,0:T(8,128)S(1)} collective-permute-done((f32[280,128]{1,0:T(8,128)S(1)}, f32[280,128]{1,0:T(8,128)S(1)}, u32[]{:S(2)}, u32[]{:S(2)}) %collective-permute-start.3) | collective-permute-done | bytes 143392 | tf_op jit(solution)/shard_map/ppermute | solution.py:586
  21.1 0.7 shard_map.88
  21.8 2.0 %collective-permute-start.5 = (f32[424,128]{1,0:T(8,128)S(1)}, f32[424,128]{1,0:T(8,128)S(1)}, u32[]{:S(2)}, u32[]{:S(2)}) collective-permute-start(f32[424,128]{1,0:T(8,128)S(1)} %get-tuple-element.56), channel_id=1, source_target_pairs={{0,7},{1,2},{2,1},{3,4},{4,3},{5,6},{6,5},{7,0},{8,15},{9,10},{10,... | collective-permute-start | bytes 651272 | tf_op jit(solution)/shard_map/ppermute | solution.py:586
  23.8 4.0 %collective-permute-start.4 = (f32[424,128]{1,0:T(8,128)S(1)}, f32[424,128]{1,0:T(8,128)S(1)}, u32[]{:S(2)}, u32[]{:S(2)}) collective-permute-start(f32[424,128]{1,0:T(8,128)S(1)} %get-tuple-element.55.refs_3_), channel_id=1, source_target_pairs={{0,1},{1,0},{2,3},{3,2},{4,5},{5,4},{6,7},{7,6},{8,9},{9,8},{10,11... | collective-permute-start | bytes 651272 | tf_op jit(solution)/shard_map/ppermute | solution.py:586
  28.3 3.8 %collective-permute-done.4.refs_4_ = f32[424,128]{1,0:T(8,128)S(1)} collective-permute-done((f32[424,128]{1,0:T(8,128)S(1)}, f32[424,128]{1,0:T(8,128)S(1)}, u32[]{:S(2)}, u32[]{:S(2)}) %collective-permute-start.4) | collective-permute-done | bytes 217120 | tf_op jit(solution)/shard_map/ppermute | solution.py:586
  32.1 2.1 %shard_map.89 = (s32[16,128]{1,0:T(8,128)S(1)}, f32[112,8,128]{2,1,0:T(8,128)S(1)}, f32[26,8,128]{2,1,0:T(8,128)S(1)}, f32[26,8,128]{2,1,0:T(8,128)S(1)}, f32[8,128]{1,0:T(8,128)S(1)}) custom-call(s32[12]{0:T(128)S(1)} %stack.63.bounds.info.refs_0_, f32[32,128]{1,0:T(8,128)S(1)} %get-tuple-element.47.own.refs_1_.refs_0_.start, f32[416,128]{1,0:T(8,128)S(1)} %bitcast.18, ...), custom_call_target="tpu_custom_call" | custom-call | flops 4194304 | bytes 262144 | tf_op jit(solution)/shard_map/pallas_call | solution.py:661
  34.1 1.1 collective-permute-start.6
  35.2 6.2 %shard_map.90.own_radius = f32[4,128]{1,0:T(4,128)S(1)} custom-call(s32[16,128]{1,0:T(8,128)S(1)} %get-tuple-element.59.listed, f32[112,8,128]{2,1,0:T(8,128)S(1)} %get-tuple-element.60.tiles.refs_6_, f32[32,128]{1,0:T(8,128)S(1)} %get-tuple-element.47.own.refs_1_.refs_0_.start), custom_call_target="tpu_custom_call" | custom-call | flops 8589934592 | bytes 262144 | tf_op jit(solution)/shard_map/pallas_call | solution.py:677
  41.5 1.1 collective-permute-start.8
  42.6 0.9 collective-permute-start.7
  43.6 1.6 %collective-permute-start.9 = (f32[8,128]{1,0:T(8,128)S(1)}, f32[8,128]{1,0:T(8,128)S(1)}, u32[]{:S(2)}, u32[]{:S(2)}) collective-permute-start(f32[8,128]{1,0:T(8,128)S(1)} %add.45), channel_id=1, source_target_pairs={{0,32},{8,40},{16,48},{24,56},{32,0},{40,8},{48,16},{56,24},{1,33}... | collective-permute-start | bytes 12296 | tf_op jit(solution)/shard_map/ppermute | solution.py:599
  45.2 1.4 collective-permute-done.10.refs_1_
  46.6 0.6 collective-permute-done.9.refs_0_
  47.8 3.2 %collective-permute-start.12 = (f32[20,128]{1,0:T(8,128)S(1)}, f32[20,128]{1,0:T(8,128)S(1)}, u32[]{:S(2)}, u32[]{:S(2)}) collective-permute-start(f32[20,128]{1,0:T(8,128)S(1)} %get-tuple-element.62.mine), channel_id=1, source_target_pairs={{0,56},{8,16},{16,8},{24,32},{32,24},{40,48},{48,40},{56,0},{1,57}... | collective-permute-start | bytes 30728 | tf_op jit(solution)/shard_map/ppermute | solution.py:586
  51.0 1.1 collective-permute-start.14
  52.1 3.0 %collective-permute-start.13 = (f32[8,128]{1,0:T(8,128)S(1)}, f32[8,128]{1,0:T(8,128)S(1)}, u32[]{:S(2)}, u32[]{:S(2)}) collective-permute-start(f32[8,128]{1,0:T(8,128)S(1)} %get-tuple-element.63), channel_id=1, source_target_pairs={{0,16},{8,24},{16,0},{24,8},{32,48},{40,56},{48,32},{56,40},{1,17}... | collective-permute-start | bytes 12296 | tf_op jit(solution)/shard_map/ppermute | solution.py:599
  55.1 0.7 collective-permute-done.14.refs_1_
  55.8 1.4 collective-permute-done.13.refs_0_
  57.8 0.8 collective-permute-start.15
  58.7 1.8 %collective-permute-start.17 = (f32[8,128]{1,0:T(8,128)S(1)}, f32[8,128]{1,0:T(8,128)S(1)}, u32[]{:S(2)}, u32[]{:S(2)}) collective-permute-start(f32[8,128]{1,0:T(8,128)S(1)} %get-tuple-element.64), channel_id=1, source_target_pairs={{0,3},{1,2},{2,1},{3,0},{4,7},{5,6},{6,5},{7,4},{8,11},{9,10},{10,... | collective-permute-start | bytes 12296 | tf_op jit(solution)/shard_map/ppermute | solution.py:599
  60.4 1.8 %collective-permute-start.16 = (f32[8,128]{1,0:T(8,128)S(1)}, f32[8,128]{1,0:T(8,128)S(1)}, u32[]{:S(2)}, u32[]{:S(2)}) collective-permute-start(f32[8,128]{1,0:T(8,128)S(1)} %get-tuple-element.64), channel_id=1, source_target_pairs={{0,2},{1,3},{2,0},{3,1},{4,6},{5,7},{6,4},{7,5},{8,10},{9,11},{10,... | collective-permute-start | bytes 12296 | tf_op jit(solution)/shard_map/ppermute | solution.py:599
  62.3 0.9 collective-permute-start.19
  63.2 1.8 %collective-permute-done.16 = f32[8,128]{1,0:T(8,128)S(1)} collective-permute-done((f32[8,128]{1,0:T(8,128)S(1)}, f32[8,128]{1,0:T(8,128)S(1)}, u32[]{:S(2)}, u32[]{:S(2)}) %collective-permute-start.16) | collective-permute-done | bytes 4128 | tf_op jit(solution)/shard_map/ppermute | solution.py:599
  65.0 3.0 %collective-permute-start.18 = (f32[8,128]{1,0:T(8,128)S(1)}, f32[8,128]{1,0:T(8,128)S(1)}, u32[]{:S(2)}, u32[]{:S(2)}) collective-permute-start(f32[8,128]{1,0:T(8,128)S(1)} %fusion.3), channel_id=1, source_target_pairs={{0,7},{1,6},{2,5},{3,4},{4,3},{5,2},{6,1},{7,0},{8,15},{9,14},{10,... | collective-permute-start | bytes 12296 | tf_op jit(solution)/shard_map/ppermute | solution.py:599
  68.0 10.3 %shard_map.93.refs_4_ = f32[12,128]{1,0:T(8,128)S(1)} custom-call(s32[12]{0:T(128)S(1)} %stack.63.bounds.info.refs_0_, s32[16,128]{1,0:T(8,128)S(1)} %get-tuple-element.59.listed, f32[112,8,128]{2,1,0:T(8,128)S(1)} %get-tuple-element.60.tiles.refs_6_, f32[32,128]{1,0:T(8,128)S(1)} %get-tuple-element.47.own.refs_1_.refs_0_.start, ...), custom_call_target="tpu_custom_call" | custom-call | flops 17179869184 | bytes 262144 | tf_op jit(solution)/shard_map/pallas_call | solution.py:707
  78.3 2.4 %shard_map.94 = (f32[32,128]{1,0:T(8,128)S(1)}, f32[12,128]{1,0:T(8,128)}) custom-call(s32[12]{0:T(128)S(1)} %stack.63.bounds.info.refs_0_, f32[32,128]{1,0:T(8,128)S(1)} %get-tuple-element.47.own.refs_1_.refs_0_.start, f32[26,8,128]{2,1,0:T(8,128)S(1)} %get-tuple-element.57.refs_1_, f32[26,8,128]{2,1,0:T(8,128)S(1)} %get-tuple-element.58.refs_2_.refs_7_, ...), custom_call_target="tpu_custom_call" | custom-call | flops 67108864 | bytes 262144 | tf_op jit(solution)/shard_map/pallas_call | solution.py:721
  80.8 1.5 shard_map.95
  82.4 1.1 collective-permute-start.20
  83.4 3.9 %collective-permute-done.21.second = f32[96,128]{1,0:T(8,128)S(1)} collective-permute-done((f32[96,128]{1,0:T(8,128)S(1)}, f32[96,128]{1,0:T(8,128)S(1)}, u32[]{:S(2)}, u32[]{:S(2)}) %collective-permute-start.21) | collective-permute-done | bytes 49184 | tf_op jit(solution)/shard_map/ppermute | solution.py:586
  87.4 0.7 shard_map.96
  88.1 3.2 %collective-permute-start.23 = (f32[152,128]{1,0:T(8,128)S(1)}, f32[152,128]{1,0:T(8,128)S(1)}, u32[]{:S(2)}, u32[]{:S(2)}) collective-permute-start(f32[152,128]{1,0:T(8,128)S(1)} %get-tuple-element.72), channel_id=1, source_target_pairs={{0,56},{8,16},{16,8},{24,32},{32,24},{40,48},{48,40},{56,0},{1,57}... | collective-permute-start | bytes 233480 | tf_op jit(solution)/shard_map/ppermute | solution.py:586
  91.3 3.4 %collective-permute-done.23.second = f32[152,128]{1,0:T(8,128)S(1)} collective-permute-done((f32[152,128]{1,0:T(8,128)S(1)}, f32[152,128]{1,0:T(8,128)S(1)}, u32[]{:S(2)}, u32[]{:S(2)}) %collective-permute-start.23) | collective-permute-done | bytes 77856 | tf_op jit(solution)/shard_map/ppermute | solution.py:586
  94.6 1.0 collective-permute-done.22.first
  95.7 0.7 shard_map.97
  96.4 0.8 collective-permute-start.25
  97.5 3.9 %collective-permute-done.25.refs_5_ = f32[248,128]{1,0:T(8,128)S(1)} collective-permute-done((f32[248,128]{1,0:T(8,128)S(1)}, f32[248,128]{1,0:T(8,128)S(1)}, u32[]{:S(2)}, u32[]{:S(2)}) %collective-permute-start.25) | collective-permute-done | bytes 127008 | tf_op jit(solution)/shard_map/ppermute | solution.py:586
  101.4 0.7 collective-permute-done.24.refs_4_
  102.1 2.8 %shard_map.98 = (s32[16,128]{1,0:T(8,128)S(1)}, f32[112,8,128]{2,1,0:T(8,128)S(1)}, f32[26,8,128]{2,1,0:T(8,128)S(1)}, f32[8,128]{1,0:T(8,128)S(1)}, f32[16,16,16]{2,1,0:T(8,128)}) custom-call(s32[12]{0:T(128)S(1)} %stack.63.bounds.info.refs_0_, f32[32,128]{1,0:T(8,128)S(1)} %get-tuple-element.66.own.refs_1_.refs_0_, f32[208,128]{1,0:T(8,128)S(1)} %bitcast.21, ...), custom_call_target="tpu_custom_call" | custom-call | flops 4194304 | bytes 262144 | tf_op jit(solution)/shard_map/pallas_call | solution.py:661
  104.9 1.7 %collective-permute-start.26 = (f32[8,128]{1,0:T(8,128)S(1)}, f32[8,128]{1,0:T(8,128)S(1)}, u32[]{:S(2)}, u32[]{:S(2)}) collective-permute-start(f32[8,128]{1,0:T(8,128)S(1)} %get-tuple-element.79), channel_id=1, source_target_pairs={{0,128},{64,192},{128,0},{192,64},{1,129},{65,193},{129,1},{193,65... | collective-permute-start | bytes 12296 | tf_op jit(solution)/shard_map/ppermute | solution.py:599
  106.6 6.2 %shard_map.99.own_radius = f32[4,128]{1,0:T(4,128)S(1)} custom-call(s32[16,128]{1,0:T(8,128)S(1)} %get-tuple-element.77.listed, f32[112,8,128]{2,1,0:T(8,128)S(1)} %get-tuple-element.78.tiles, f32[32,128]{1,0:T(8,128)S(1)} %get-tuple-element.66.own.refs_1_.refs_0_), custom_call_target="tpu_custom_call" | custom-call | flops 8589934592 | bytes 262144 | tf_op jit(solution)/shard_map/pallas_call | solution.py:677
  113.2 1.3 collective-permute-start.27
  114.5 1.6 %collective-permute-start.29 = (f32[8,128]{1,0:T(8,128)S(1)}, f32[8,128]{1,0:T(8,128)S(1)}, u32[]{:S(2)}, u32[]{:S(2)}) collective-permute-start(f32[8,128]{1,0:T(8,128)S(1)} %add.50), channel_id=1, source_target_pairs={{0,32},{8,40},{16,48},{24,56},{32,0},{40,8},{48,16},{56,24},{1,33}... | collective-permute-start | bytes 12296 | tf_op jit(solution)/shard_map/ppermute | solution.py:599
  116.1 1.4 collective-permute-done.30.refs_1_
  117.5 0.6 collective-permute-done.29.refs_0_
  118.7 2.1 %collective-permute-start.32 = (f32[20,128]{1,0:T(8,128)S(1)}, f32[20,128]{1,0:T(8,128)S(1)}, u32[]{:S(2)}, u32[]{:S(2)}) collective-permute-start(f32[20,128]{1,0:T(8,128)S(1)} %get-tuple-element.80.mine), channel_id=1, source_target_pairs={{0,56},{8,16},{16,8},{24,32},{32,24},{40,48},{48,40},{56,0},{1,57}... | collective-permute-start | bytes 30728 | tf_op jit(solution)/shard_map/ppermute | solution.py:586
  120.8 2.2 %collective-permute-start.34 = (f32[8,128]{1,0:T(8,128)S(1)}, f32[8,128]{1,0:T(8,128)S(1)}, u32[]{:S(2)}, u32[]{:S(2)}) collective-permute-start(f32[8,128]{1,0:T(8,128)S(1)} %get-tuple-element.81), channel_id=1, source_target_pairs={{0,24},{8,16},{16,8},{24,0},{32,56},{40,48},{48,40},{56,32},{1,25}... | collective-permute-start | bytes 12296 | tf_op jit(solution)/shard_map/ppermute | solution.py:599
  123.0 1.8 %collective-permute-start.33 = (f32[8,128]{1,0:T(8,128)S(1)}, f32[8,128]{1,0:T(8,128)S(1)}, u32[]{:S(2)}, u32[]{:S(2)}) collective-permute-start(f32[8,128]{1,0:T(8,128)S(1)} %get-tuple-element.81), channel_id=1, source_target_pairs={{0,16},{8,24},{16,0},{24,8},{32,48},{40,56},{48,32},{56,40},{1,17}... | collective-permute-start | bytes 12296 | tf_op jit(solution)/shard_map/ppermute | solution.py:599
  124.9 0.7 collective-permute-done.34.refs_1_
  125.6 2.5 %collective-permute-done.33.refs_0_ = f32[8,128]{1,0:T(8,128)S(1)} collective-permute-done((f32[8,128]{1,0:T(8,128)S(1)}, f32[8,128]{1,0:T(8,128)S(1)}, u32[]{:S(2)}, u32[]{:S(2)}) %collective-permute-start.33) | collective-permute-done | bytes 4128 | tf_op jit(solution)/shard_map/ppermute | solution.py:599
  128.8 4.2 %collective-permute-start.37 = (f32[8,128]{1,0:T(8,128)S(1)}, f32[8,128]{1,0:T(8,128)S(1)}, u32[]{:S(2)}, u32[]{:S(2)}) collective-permute-start(f32[8,128]{1,0:T(8,128)S(1)} %get-tuple-element.82), channel_id=1, source_target_pairs={{0,3},{1,2},{2,1},{3,0},{4,7},{5,6},{6,5},{7,4},{8,11},{9,10},{10,... | collective-permute-start | bytes 12296 | tf_op jit(solution)/shard_map/ppermute | solution.py:599
  133.2 2.3 %collective-permute-start.39 = (f32[44,128]{1,0:T(8,128)S(1)}, f32[44,128]{1,0:T(8,128)S(1)}, u32[]{:S(2)}, u32[]{:S(2)}) collective-permute-start(f32[44,128]{1,0:T(8,128)S(1)} %get-tuple-element.83.mine), channel_id=1, source_target_pairs={{0,7},{1,2},{2,1},{3,4},{4,3},{5,6},{6,5},{7,0},{8,15},{9,10},{10,... | collective-permute-start | bytes 67592 | tf_op jit(solution)/shard_map/ppermute | solution.py:586
  135.5 2.0 %collective-permute-done.36 = f32[8,128]{1,0:T(8,128)S(1)} collective-permute-done((f32[8,128]{1,0:T(8,128)S(1)}, f32[8,128]{1,0:T(8,128)S(1)}, u32[]{:S(2)}, u32[]{:S(2)}) %collective-permute-start.36) | collective-permute-done | bytes 4128 | tf_op jit(solution)/shard_map/ppermute | solution.py:599
  137.5 2.8 %collective-permute-start.38 = (f32[8,128]{1,0:T(8,128)S(1)}, f32[8,128]{1,0:T(8,128)S(1)}, u32[]{:S(2)}, u32[]{:S(2)}) collective-permute-start(f32[8,128]{1,0:T(8,128)S(1)} %fusion.1), channel_id=1, source_target_pairs={{0,7},{1,6},{2,5},{3,4},{4,3},{5,2},{6,1},{7,0},{8,15},{9,14},{10,... | collective-permute-start | bytes 12296 | tf_op jit(solution)/shard_map/ppermute | solution.py:599
  140.4 10.3 %shard_map.102.refs_4_ = f32[12,128]{1,0:T(8,128)S(1)} custom-call(s32[12]{0:T(128)S(1)} %stack.63.bounds.info.refs_0_, s32[16,128]{1,0:T(8,128)S(1)} %get-tuple-element.77.listed, f32[112,8,128]{2,1,0:T(8,128)S(1)} %get-tuple-element.78.tiles, f32[32,128]{1,0:T(8,128)S(1)} %get-tuple-element.66.own.refs_1_.refs_0_, f32[4,128]{1,0:T(4,128)S(1)} %shard_map.99.own_radius, ...), custom_call_target="tpu_custom_call" | custom-call | flops 17179869184 | bytes 262144 | tf_op jit(solution)/shard_map/pallas_call | solution.py:707
  150.7 1.8 %shard_map.103 = (f32[32,128]{1,0:T(8,128)S(1)}, f32[12,128]{1,0:T(8,128)S(1)}) custom-call(s32[12]{0:T(128)S(1)} %stack.63.bounds.info.refs_0_, f32[32,128]{1,0:T(8,128)S(1)} %get-tuple-element.66.own.refs_1_.refs_0_, f32[26,8,128]{2,1,0:T(8,128)S(1)} %get-tuple-element.76.refs_1_, f32[26,8,128]{2,1,0:T(8,128)S(1)} %get-tuple-element.58.refs_2_.refs_7_, ...), custom_call_target="tpu_custom_call" | custom-call | flops 67108864 | bytes 262144 | tf_op jit(solution)/shard_map/pallas_call | solution.py:721
  152.6 0.9 shard_map.104
  (56 shorter events, 4.6 us)
Async XLA Ops:
  0.6 0.9 copy-start.4
  1.5 0.7 copy-start
  1.5 0.7 copy-start.1
  1.5 0.7 copy-start.2
  1.5 0.7 copy-start.3
  5.7 6.1 %collective-permute-start.1 = (f32[144,128]{1,0:T(8,128)S(1)}, f32[144,128]{1,0:T(8,128)S(1)}, u32[]{:S(2)}, u32[]{:S(2)}) collective-permute-start(f32[144,128]{1,0:T(8,128)S(1)} %get-tuple-element.50), channel_id=1, source_target_pairs={{0,192},{64,128},{128,64},{192,0},{1,193},{65,129},{129,65},{193,1... | collective-permute-start | bytes 221192 | tf_op jit(solution)/shard_map/ppermute | solution.py:586
  6.4 5.4 %collective-permute-start = (f32[144,128]{1,0:T(8,128)S(1)}, f32[144,128]{1,0:T(8,128)S(1)}, u32[]{:S(2)}, u32[]{:S(2)}) collective-permute-start(f32[144,128]{1,0:T(8,128)S(1)} %get-tuple-element.49.mine), channel_id=1, source_target_pairs={{0,64},{64,0},{128,192},{192,128},{1,65},{65,1},{129,193},{193,129... | collective-permute-start | bytes 221192 | tf_op jit(solution)/shard_map/ppermute | solution.py:586
  12.5 8.0 %collective-permute-start.3 = (f32[280,128]{1,0:T(8,128)S(1)}, f32[280,128]{1,0:T(8,128)S(1)}, u32[]{:S(2)}, u32[]{:S(2)}) collective-permute-start(f32[280,128]{1,0:T(8,128)S(1)} %get-tuple-element.53), channel_id=1, source_target_pairs={{0,56},{8,16},{16,8},{24,32},{32,24},{40,48},{48,40},{56,0},{1,57}... | collective-permute-start | bytes 430088 | tf_op jit(solution)/shard_map/ppermute | solution.py:586
  15.6 5.5 %collective-permute-start.2 = (f32[280,128]{1,0:T(8,128)S(1)}, f32[280,128]{1,0:T(8,128)S(1)}, u32[]{:S(2)}, u32[]{:S(2)}) collective-permute-start(f32[280,128]{1,0:T(8,128)S(1)} %get-tuple-element.52.mine), channel_id=1, source_target_pairs={{0,8},{8,0},{16,24},{24,16},{32,40},{40,32},{48,56},{56,48},{1,9},... | collective-permute-start | bytes 430088 | tf_op jit(solution)/shard_map/ppermute | solution.py:586
  21.8 6.5 %collective-permute-start.5 = (f32[424,128]{1,0:T(8,128)S(1)}, f32[424,128]{1,0:T(8,128)S(1)}, u32[]{:S(2)}, u32[]{:S(2)}) collective-permute-start(f32[424,128]{1,0:T(8,128)S(1)} %get-tuple-element.56), channel_id=1, source_target_pairs={{0,7},{1,2},{2,1},{3,4},{4,3},{5,6},{6,5},{7,0},{8,15},{9,10},{10,... | collective-permute-start | bytes 651272 | tf_op jit(solution)/shard_map/ppermute | solution.py:586
  23.8 8.2 %collective-permute-start.4 = (f32[424,128]{1,0:T(8,128)S(1)}, f32[424,128]{1,0:T(8,128)S(1)}, u32[]{:S(2)}, u32[]{:S(2)}) collective-permute-start(f32[424,128]{1,0:T(8,128)S(1)} %get-tuple-element.55.refs_3_), channel_id=1, source_target_pairs={{0,1},{1,0},{2,3},{3,2},{4,5},{5,4},{6,7},{7,6},{8,9},{9,8},{10,11... | collective-permute-start | bytes 651272 | tf_op jit(solution)/shard_map/ppermute | solution.py:586
  34.1 7.3 %collective-permute-start.6 = (f32[8,128]{1,0:T(8,128)S(1)}, f32[8,128]{1,0:T(8,128)S(1)}, u32[]{:S(2)}, u32[]{:S(2)}) collective-permute-start(f32[8,128]{1,0:T(8,128)S(1)} %get-tuple-element.61), channel_id=1, source_target_pairs={{0,128},{64,192},{128,0},{192,64},{1,129},{65,193},{129,1},{193,65... | collective-permute-start | bytes 12296 | tf_op jit(solution)/shard_map/ppermute | solution.py:599
  41.5 5.7 %collective-permute-start.8 = (f32[12,128]{1,0:T(8,128)S(1)}, f32[12,128]{1,0:T(8,128)S(1)}, u32[]{:S(2)}, u32[]{:S(2)}) collective-permute-start(f32[12,128]{1,0:T(8,128)S(1)} %pad_maximum_fusion.mine), channel_id=1, source_target_pairs={{0,192},{64,128},{128,64},{192,0},{1,193},{65,129},{129,65},{193,1... | collective-permute-start | bytes 18440 | tf_op jit(solution)/shard_map/ppermute | solution.py:586
  42.6 4.6 %collective-permute-start.7 = (f32[12,128]{1,0:T(8,128)S(1)}, f32[12,128]{1,0:T(8,128)S(1)}, u32[]{:S(2)}, u32[]{:S(2)}) collective-permute-start(f32[12,128]{1,0:T(8,128)S(1)} %pad_maximum_fusion.mine), channel_id=1, source_target_pairs={{0,64},{64,0},{128,192},{192,128},{1,65},{65,1},{129,193},{193,129... | collective-permute-start | bytes 18440 | tf_op jit(solution)/shard_map/ppermute | solution.py:586
  43.6 3.0 %collective-permute-start.10 = (f32[8,128]{1,0:T(8,128)S(1)}, f32[8,128]{1,0:T(8,128)S(1)}, u32[]{:S(2)}, u32[]{:S(2)}) collective-permute-start(f32[8,128]{1,0:T(8,128)S(1)} %add.45), channel_id=1, source_target_pairs={{0,96},{8,104},{16,112},{24,120},{32,64},{40,72},{48,80},{56,88},{... | collective-permute-start | bytes 12296 | tf_op jit(solution)/shard_map/ppermute | solution.py:599
  43.6 3.6 %collective-permute-start.9 = (f32[8,128]{1,0:T(8,128)S(1)}, f32[8,128]{1,0:T(8,128)S(1)}, u32[]{:S(2)}, u32[]{:S(2)}) collective-permute-start(f32[8,128]{1,0:T(8,128)S(1)} %add.45), channel_id=1, source_target_pairs={{0,32},{8,40},{16,48},{24,56},{32,0},{40,8},{48,16},{56,24},{1,33}... | collective-permute-start | bytes 12296 | tf_op jit(solution)/shard_map/ppermute | solution.py:599
  47.8 9.5 %collective-permute-start.12 = (f32[20,128]{1,0:T(8,128)S(1)}, f32[20,128]{1,0:T(8,128)S(1)}, u32[]{:S(2)}, u32[]{:S(2)}) collective-permute-start(f32[20,128]{1,0:T(8,128)S(1)} %get-tuple-element.62.mine), channel_id=1, source_target_pairs={{0,56},{8,16},{16,8},{24,32},{32,24},{40,48},{48,40},{56,0},{1,57}... | collective-permute-start | bytes 30728 | tf_op jit(solution)/shard_map/ppermute | solution.py:586
  51.0 6.3 %collective-permute-start.11 = (f32[20,128]{1,0:T(8,128)S(1)}, f32[20,128]{1,0:T(8,128)S(1)}, u32[]{:S(2)}, u32[]{:S(2)}) collective-permute-start(f32[20,128]{1,0:T(8,128)S(1)} %get-tuple-element.62.mine), channel_id=1, source_target_pairs={{0,8},{8,0},{16,24},{24,16},{32,40},{40,32},{48,56},{56,48},{1,9},... | collective-permute-start | bytes 30728 | tf_op jit(solution)/shard_map/ppermute | solution.py:586
  51.0 4.8 %collective-permute-start.14 = (f32[8,128]{1,0:T(8,128)S(1)}, f32[8,128]{1,0:T(8,128)S(1)}, u32[]{:S(2)}, u32[]{:S(2)}) collective-permute-start(f32[8,128]{1,0:T(8,128)S(1)} %get-tuple-element.63), channel_id=1, source_target_pairs={{0,24},{8,16},{16,8},{24,0},{32,56},{40,48},{48,40},{56,32},{1,25}... | collective-permute-start | bytes 12296 | tf_op jit(solution)/shard_map/ppermute | solution.py:599
  52.1 5.1 %collective-permute-start.13 = (f32[8,128]{1,0:T(8,128)S(1)}, f32[8,128]{1,0:T(8,128)S(1)}, u32[]{:S(2)}, u32[]{:S(2)}) collective-permute-start(f32[8,128]{1,0:T(8,128)S(1)} %get-tuple-element.63), channel_id=1, source_target_pairs={{0,16},{8,24},{16,0},{24,8},{32,48},{40,56},{48,32},{56,40},{1,17}... | collective-permute-start | bytes 12296 | tf_op jit(solution)/shard_map/ppermute | solution.py:599
  57.8 7.2 %collective-permute-start.15 = (f32[44,128]{1,0:T(8,128)S(1)}, f32[44,128]{1,0:T(8,128)S(1)}, u32[]{:S(2)}, u32[]{:S(2)}) collective-permute-start(f32[44,128]{1,0:T(8,128)S(1)} %get-tuple-element.65.mine), channel_id=1, source_target_pairs={{0,1},{1,0},{2,3},{3,2},{4,5},{5,4},{6,7},{7,6},{8,9},{9,8},{10,11... | collective-permute-start | bytes 67592 | tf_op jit(solution)/shard_map/ppermute | solution.py:586
  58.7 4.5 %collective-permute-start.17 = (f32[8,128]{1,0:T(8,128)S(1)}, f32[8,128]{1,0:T(8,128)S(1)}, u32[]{:S(2)}, u32[]{:S(2)}) collective-permute-start(f32[8,128]{1,0:T(8,128)S(1)} %get-tuple-element.64), channel_id=1, source_target_pairs={{0,3},{1,2},{2,1},{3,0},{4,7},{5,6},{6,5},{7,4},{8,11},{9,10},{10,... | collective-permute-start | bytes 12296 | tf_op jit(solution)/shard_map/ppermute | solution.py:599
  60.4 4.5 %collective-permute-start.16 = (f32[8,128]{1,0:T(8,128)S(1)}, f32[8,128]{1,0:T(8,128)S(1)}, u32[]{:S(2)}, u32[]{:S(2)}) collective-permute-start(f32[8,128]{1,0:T(8,128)S(1)} %get-tuple-element.64), channel_id=1, source_target_pairs={{0,2},{1,3},{2,0},{3,1},{4,6},{5,7},{6,4},{7,5},{8,10},{9,11},{10,... | collective-permute-start | bytes 12296 | tf_op jit(solution)/shard_map/ppermute | solution.py:599
  62.3 5.7 %collective-permute-start.19 = (f32[44,128]{1,0:T(8,128)S(1)}, f32[44,128]{1,0:T(8,128)S(1)}, u32[]{:S(2)}, u32[]{:S(2)}) collective-permute-start(f32[44,128]{1,0:T(8,128)S(1)} %get-tuple-element.65.mine), channel_id=1, source_target_pairs={{0,7},{1,2},{2,1},{3,4},{4,3},{5,6},{6,5},{7,0},{8,15},{9,10},{10,... | collective-permute-start | bytes 67592 | tf_op jit(solution)/shard_map/ppermute | solution.py:586
  65.0 13.4 %collective-permute-start.18 = (f32[8,128]{1,0:T(8,128)S(1)}, f32[8,128]{1,0:T(8,128)S(1)}, u32[]{:S(2)}, u32[]{:S(2)}) collective-permute-start(f32[8,128]{1,0:T(8,128)S(1)} %fusion.3), channel_id=1, source_target_pairs={{0,7},{1,6},{2,5},{3,4},{4,3},{5,2},{6,1},{7,0},{8,15},{9,14},{10,... | collective-permute-start | bytes 12296 | tf_op jit(solution)/shard_map/ppermute | solution.py:599
  82.3 5.1 %collective-permute-start.21 = (f32[96,128]{1,0:T(8,128)S(1)}, f32[96,128]{1,0:T(8,128)S(1)}, u32[]{:S(2)}, u32[]{:S(2)}) collective-permute-start(f32[96,128]{1,0:T(8,128)S(1)} %get-tuple-element.69), channel_id=1, source_target_pairs={{0,192},{64,128},{128,64},{192,0},{1,193},{65,129},{129,65},{193,1... | collective-permute-start | bytes 147464 | tf_op jit(solution)/shard_map/ppermute | solution.py:586
  82.4 5.0 %collective-permute-start.20 = (f32[96,128]{1,0:T(8,128)S(1)}, f32[96,128]{1,0:T(8,128)S(1)}, u32[]{:S(2)}, u32[]{:S(2)}) collective-permute-start(f32[96,128]{1,0:T(8,128)S(1)} %get-tuple-element.68.mine), channel_id=1, source_target_pairs={{0,64},{64,0},{128,192},{192,128},{1,65},{65,1},{129,193},{193,129... | collective-permute-start | bytes 147464 | tf_op jit(solution)/shard_map/ppermute | solution.py:586
  88.1 6.6 %collective-permute-start.23 = (f32[152,128]{1,0:T(8,128)S(1)}, f32[152,128]{1,0:T(8,128)S(1)}, u32[]{:S(2)}, u32[]{:S(2)}) collective-permute-start(f32[152,128]{1,0:T(8,128)S(1)} %get-tuple-element.72), channel_id=1, source_target_pairs={{0,56},{8,16},{16,8},{24,32},{32,24},{40,48},{48,40},{56,0},{1,57}... | collective-permute-start | bytes 233480 | tf_op jit(solution)/shard_map/ppermute | solution.py:586
  91.3 4.4 %collective-permute-start.22 = (f32[152,128]{1,0:T(8,128)S(1)}, f32[152,128]{1,0:T(8,128)S(1)}, u32[]{:S(2)}, u32[]{:S(2)}) collective-permute-start(f32[152,128]{1,0:T(8,128)S(1)} %get-tuple-element.71.mine), channel_id=1, source_target_pairs={{0,8},{8,0},{16,24},{24,16},{32,40},{40,32},{48,56},{56,48},{1,9},... | collective-permute-start | bytes 233480 | tf_op jit(solution)/shard_map/ppermute | solution.py:586
  96.4 5.0 %collective-permute-start.25 = (f32[248,128]{1,0:T(8,128)S(1)}, f32[248,128]{1,0:T(8,128)S(1)}, u32[]{:S(2)}, u32[]{:S(2)}) collective-permute-start(f32[248,128]{1,0:T(8,128)S(1)} %get-tuple-element.75), channel_id=1, source_target_pairs={{0,7},{1,2},{2,1},{3,4},{4,3},{5,6},{6,5},{7,0},{8,15},{9,10},{10,... | collective-permute-start | bytes 380936 | tf_op jit(solution)/shard_map/ppermute | solution.py:586
  97.2 4.9 %collective-permute-start.24 = (f32[248,128]{1,0:T(8,128)S(1)}, f32[248,128]{1,0:T(8,128)S(1)}, u32[]{:S(2)}, u32[]{:S(2)}) collective-permute-start(f32[248,128]{1,0:T(8,128)S(1)} %get-tuple-element.74.refs_3_), channel_id=1, source_target_pairs={{0,1},{1,0},{2,3},{3,2},{4,5},{5,4},{6,7},{7,6},{8,9},{9,8},{10,11... | collective-permute-start | bytes 380936 | tf_op jit(solution)/shard_map/ppermute | solution.py:586
  104.9 7.9 %collective-permute-start.26 = (f32[8,128]{1,0:T(8,128)S(1)}, f32[8,128]{1,0:T(8,128)S(1)}, u32[]{:S(2)}, u32[]{:S(2)}) collective-permute-start(f32[8,128]{1,0:T(8,128)S(1)} %get-tuple-element.79), channel_id=1, source_target_pairs={{0,128},{64,192},{128,0},{192,64},{1,129},{65,193},{129,1},{193,65... | collective-permute-start | bytes 12296 | tf_op jit(solution)/shard_map/ppermute | solution.py:599
  112.9 5.2 %collective-permute-start.28 = (f32[12,128]{1,0:T(8,128)S(1)}, f32[12,128]{1,0:T(8,128)S(1)}, u32[]{:S(2)}, u32[]{:S(2)}) collective-permute-start(f32[12,128]{1,0:T(8,128)S(1)} %pad_maximum_fusion.1.mine), channel_id=1, source_target_pairs={{0,192},{64,128},{128,64},{192,0},{1,193},{65,129},{129,65},{193,1... | collective-permute-start | bytes 18440 | tf_op jit(solution)/shard_map/ppermute | solution.py:586
  113.2 4.9 %collective-permute-start.27 = (f32[12,128]{1,0:T(8,128)S(1)}, f32[12,128]{1,0:T(8,128)S(1)}, u32[]{:S(2)}, u32[]{:S(2)}) collective-permute-start(f32[12,128]{1,0:T(8,128)S(1)} %pad_maximum_fusion.1.mine), channel_id=1, source_target_pairs={{0,64},{64,0},{128,192},{192,128},{1,65},{65,1},{129,193},{193,129... | collective-permute-start | bytes 18440 | tf_op jit(solution)/shard_map/ppermute | solution.py:586
  114.4 3.0 %collective-permute-start.30 = (f32[8,128]{1,0:T(8,128)S(1)}, f32[8,128]{1,0:T(8,128)S(1)}, u32[]{:S(2)}, u32[]{:S(2)}) collective-permute-start(f32[8,128]{1,0:T(8,128)S(1)} %add.50), channel_id=1, source_target_pairs={{0,96},{8,104},{16,112},{24,120},{32,64},{40,72},{48,80},{56,88},{... | collective-permute-start | bytes 12296 | tf_op jit(solution)/shard_map/ppermute | solution.py:599
  114.5 3.6 %collective-permute-start.29 = (f32[8,128]{1,0:T(8,128)S(1)}, f32[8,128]{1,0:T(8,128)S(1)}, u32[]{:S(2)}, u32[]{:S(2)}) collective-permute-start(f32[8,128]{1,0:T(8,128)S(1)} %add.50), channel_id=1, source_target_pairs={{0,32},{8,40},{16,48},{24,56},{32,0},{40,8},{48,16},{56,24},{1,33}... | collective-permute-start | bytes 12296 | tf_op jit(solution)/shard_map/ppermute | solution.py:599
  118.7 9.5 %collective-permute-start.32 = (f32[20,128]{1,0:T(8,128)S(1)}, f32[20,128]{1,0:T(8,128)S(1)}, u32[]{:S(2)}, u32[]{:S(2)}) collective-permute-start(f32[20,128]{1,0:T(8,128)S(1)} %get-tuple-element.80.mine), channel_id=1, source_target_pairs={{0,56},{8,16},{16,8},{24,32},{32,24},{40,48},{48,40},{56,0},{1,57}... | collective-permute-start | bytes 30728 | tf_op jit(solution)/shard_map/ppermute | solution.py:586
  120.8 7.4 %collective-permute-start.31 = (f32[20,128]{1,0:T(8,128)S(1)}, f32[20,128]{1,0:T(8,128)S(1)}, u32[]{:S(2)}, u32[]{:S(2)}) collective-permute-start(f32[20,128]{1,0:T(8,128)S(1)} %get-tuple-element.80.mine), channel_id=1, source_target_pairs={{0,8},{8,0},{16,24},{24,16},{32,40},{40,32},{48,56},{56,48},{1,9},... | collective-permute-start | bytes 30728 | tf_op jit(solution)/shard_map/ppermute | solution.py:586
  120.8 4.8 %collective-permute-start.34 = (f32[8,128]{1,0:T(8,128)S(1)}, f32[8,128]{1,0:T(8,128)S(1)}, u32[]{:S(2)}, u32[]{:S(2)}) collective-permute-start(f32[8,128]{1,0:T(8,128)S(1)} %get-tuple-element.81), channel_id=1, source_target_pairs={{0,24},{8,16},{16,8},{24,0},{32,56},{40,48},{48,40},{56,32},{1,25}... | collective-permute-start | bytes 12296 | tf_op jit(solution)/shard_map/ppermute | solution.py:599
  123.0 5.1 %collective-permute-start.33 = (f32[8,128]{1,0:T(8,128)S(1)}, f32[8,128]{1,0:T(8,128)S(1)}, u32[]{:S(2)}, u32[]{:S(2)}) collective-permute-start(f32[8,128]{1,0:T(8,128)S(1)} %get-tuple-element.81), channel_id=1, source_target_pairs={{0,16},{8,24},{16,0},{24,8},{32,48},{40,56},{48,32},{56,40},{1,17}... | collective-permute-start | bytes 12296 | tf_op jit(solution)/shard_map/ppermute | solution.py:599
  128.7 8.8 %collective-permute-start.35 = (f32[44,128]{1,0:T(8,128)S(1)}, f32[44,128]{1,0:T(8,128)S(1)}, u32[]{:S(2)}, u32[]{:S(2)}) collective-permute-start(f32[44,128]{1,0:T(8,128)S(1)} %get-tuple-element.83.mine), channel_id=1, source_target_pairs={{0,1},{1,0},{2,3},{3,2},{4,5},{5,4},{6,7},{7,6},{8,9},{9,8},{10,11... | collective-permute-start | bytes 67592 | tf_op jit(solution)/shard_map/ppermute | solution.py:586
  128.8 6.7 %collective-permute-start.37 = (f32[8,128]{1,0:T(8,128)S(1)}, f32[8,128]{1,0:T(8,128)S(1)}, u32[]{:S(2)}, u32[]{:S(2)}) collective-permute-start(f32[8,128]{1,0:T(8,128)S(1)} %get-tuple-element.82), channel_id=1, source_target_pairs={{0,3},{1,2},{2,1},{3,0},{4,7},{5,6},{6,5},{7,4},{8,11},{9,10},{10,... | collective-permute-start | bytes 12296 | tf_op jit(solution)/shard_map/ppermute | solution.py:599
  133.0 4.5 %collective-permute-start.36 = (f32[8,128]{1,0:T(8,128)S(1)}, f32[8,128]{1,0:T(8,128)S(1)}, u32[]{:S(2)}, u32[]{:S(2)}) collective-permute-start(f32[8,128]{1,0:T(8,128)S(1)} %get-tuple-element.82), channel_id=1, source_target_pairs={{0,2},{1,3},{2,0},{3,1},{4,6},{5,7},{6,4},{7,5},{8,10},{9,11},{10,... | collective-permute-start | bytes 12296 | tf_op jit(solution)/shard_map/ppermute | solution.py:599
  133.2 7.2 %collective-permute-start.39 = (f32[44,128]{1,0:T(8,128)S(1)}, f32[44,128]{1,0:T(8,128)S(1)}, u32[]{:S(2)}, u32[]{:S(2)}) collective-permute-start(f32[44,128]{1,0:T(8,128)S(1)} %get-tuple-element.83.mine), channel_id=1, source_target_pairs={{0,7},{1,2},{2,1},{3,4},{4,3},{5,6},{6,5},{7,0},{8,15},{9,10},{10,... | collective-permute-start | bytes 67592 | tf_op jit(solution)/shard_map/ppermute | solution.py:586
  137.5 13.2 %collective-permute-start.38 = (f32[8,128]{1,0:T(8,128)S(1)}, f32[8,128]{1,0:T(8,128)S(1)}, u32[]{:S(2)}, u32[]{:S(2)}) collective-permute-start(f32[8,128]{1,0:T(8,128)S(1)} %fusion.1), channel_id=1, source_target_pairs={{0,7},{1,6},{2,5},{3,4},{4,3},{5,2},{6,1},{7,0},{8,15},{9,14},{10,... | collective-permute-start | bytes 12296 | tf_op jit(solution)/shard_map/ppermute | solution.py:599

commit v9 on v8

--- a/solution.py
+++ b/solution.py
@@ -633,7 +633,7 @@
     given = jnp.pad(exp_map, ((0, 0), (0, 0), (0, LANES - BRICK)))
     own = atoms
     for step in range(STEPS):
-        fields, rows = (2, 24) if step == 0 else (1, 16)
+        fields, rows = (2, 20) if step == 0 else (1, 12)
         planes = 8 * PLANES * fields
         field, *mine = call(
             functools.partial(splat_kernel, fields, rows),

time: 155 us -> 156 us (level)
  Pallas kernels: 52.9 us -> 59.5 us
  starting transfers between devices: 57.3 us -> 52.2 us
    pallas_call x2, Pallas kernels: 20.7 us -> 24.9 us  [on_device(): call(gb_kernel, f32(3 * TILES, LANES), 1 << 34, scratch=[pltpu.VMEM((5, S...]
    ppermute x16, starting transfers between devices: 28.1 us -> 24.9 us  [across(): return lax.ppermute(block, tuple(axes), pairs)]
    pallas_call x2, Pallas kernels: 12.4 us -> 14.8 us  [on_device(): call(born_kernel, f32(TILES, LANES), 1 << 33, scratch=[pltpu.VMEM((3, SLO...]
  transfers between devices with their start and end apart: 40 -> 40, of which waited for: 20 -> 19; matrix products, arithmetic and copies ran while one was open for 0% -> 0% of each run, Pallas kernels for 22% -> 26%
where the time goes in v9:
time: 156 us; the launch traced here: 155 us
  Pallas kernels  59.5 us (38%)
  starting transfers between devices  52.2 us (33%)
  waiting for transfers between devices  40.9 us (26%)
  between operations  1.63 us (1%)
    ppermute x16, starting transfers between devices, across(): return lax.ppermute(block, tuple(axes), pairs)  24.9 us
    pallas_call x2, Pallas kernels, on_device(): call(gb_kernel, f32(3 * TILES, LANES), 1 << 34, scratch=[pltpu.VMEM((5, S...  24.9 us
    ppermute x12, waiting for transfers between devices, both_sides(): lax.ppermute(blocks[1], axis, odd)  22.8 us
    ppermute x12, starting transfers between devices, both_sides(): lax.ppermute(blocks[1], axis, odd)  19.3 us
    pallas_call x2, Pallas kernels, on_device(): call(born_kernel, f32(TILES, LANES), 1 << 33, scratch=[pltpu.VMEM((3, SLO...  14.8 us
    ppermute x16, waiting for transfers between devices, across(): return lax.ppermute(block, tuple(axes), pairs)  12.7 us
    ppermute x12, starting transfers between devices, both_sides(): lax.ppermute(blocks[0], axis, even)  7.96 us
    ppermute x12, waiting for transfers between devices, both_sides(): lax.ppermute(blocks[0], axis, even)  5.45 us
  transfers between devices with their start and end apart: 40, of which 19 were waited for; matrix products, arithmetic and copies ran while one was open for 0% of the time, Pallas kernels for 26%

profile of v9, /device:TPU:56, one launch (start us, length us, event | category | flops | bytes accessed | tf_op | source)
XLA Modules:
  0.0 155.3 jit_solution(4645599414914869146)
XLA Ops:
  1.6 0.7 copy-done
  2.3 1.8 %shard_map.85 = (f32[32,128]{1,0:T(8,128)S(1)}, f32[4,128]{1,0:T(4,128)S(1)}) custom-call(f32[3,8]{1,0:T(4,128)S(1)} %copy-done.1, s32[1]{0:T(128)} %bitcast.17.live_count, f32[3,1,1,1,512]{4,3,2,1,0:T(1,128)S(1)} %copy-done, f32[1,1,1,512]{3,2,1,0:T(1,128)S(1)} %copy-done.2, s32[1,1,1,512]{3,2,1,0:T(1,128)S(1)} %copy-done.3), custom_call_target="tpu_custom_call" | custom-call | flops 4194304 | bytes 262144 | tf_op jit(solution)/shard_map/pallas_call | solution.py:619
  4.2 1.5 shard_map.86
  5.7 0.8 collective-permute-start.1
  6.4 0.7 collective-permute-start
  7.1 4.7 %collective-permute-done.1.second = f32[140,128]{1,0:T(8,128)S(1)} collective-permute-done((f32[140,128]{1,0:T(8,128)S(1)}, f32[140,128]{1,0:T(8,128)S(1)}, u32[]{:S(2)}, u32[]{:S(2)}) %collective-permute-start.1) | collective-permute-done | bytes 71712 | tf_op jit(solution)/shard_map/ppermute | solution.py:586
  11.8 0.7 shard_map.87
  12.5 3.0 %collective-permute-start.3 = (f32[268,128]{1,0:T(8,128)S(1)}, f32[268,128]{1,0:T(8,128)S(1)}, u32[]{:S(2)}, u32[]{:S(2)}) collective-permute-start(f32[268,128]{1,0:T(8,128)S(1)} %get-tuple-element.53), channel_id=1, source_target_pairs={{0,56},{8,16},{16,8},{24,32},{32,24},{40,48},{48,40},{56,0},{1,57}... | collective-permute-start | bytes 411656 | tf_op jit(solution)/shard_map/ppermute | solution.py:586
  15.6 4.8 %collective-permute-done.3.second = f32[268,128]{1,0:T(8,128)S(1)} collective-permute-done((f32[268,128]{1,0:T(8,128)S(1)}, f32[268,128]{1,0:T(8,128)S(1)}, u32[]{:S(2)}, u32[]{:S(2)}) %collective-permute-start.3) | collective-permute-done | bytes 137248 | tf_op jit(solution)/shard_map/ppermute | solution.py:586
  20.4 0.5 collective-permute-done.2.first
  21.0 0.7 shard_map.88
  21.7 2.0 %collective-permute-start.5 = (f32[388,128]{1,0:T(8,128)S(1)}, f32[388,128]{1,0:T(8,128)S(1)}, u32[]{:S(2)}, u32[]{:S(2)}) collective-permute-start(f32[388,128]{1,0:T(8,128)S(1)} %get-tuple-element.56), channel_id=1, source_target_pairs={{0,7},{1,2},{2,1},{3,4},{4,3},{5,6},{6,5},{7,0},{8,15},{9,10},{10,... | collective-permute-start | bytes 595976 | tf_op jit(solution)/shard_map/ppermute | solution.py:586
  23.8 4.0 %collective-permute-start.4 = (f32[388,128]{1,0:T(8,128)S(1)}, f32[388,128]{1,0:T(8,128)S(1)}, u32[]{:S(2)}, u32[]{:S(2)}) collective-permute-start(f32[388,128]{1,0:T(8,128)S(1)} %get-tuple-element.55.refs_3_), channel_id=1, source_target_pairs={{0,1},{1,0},{2,3},{3,2},{4,5},{5,4},{6,7},{7,6},{8,9},{9,8},{10,11... | collective-permute-start | bytes 595976 | tf_op jit(solution)/shard_map/ppermute | solution.py:586
  27.9 3.8 %collective-permute-done.4.refs_4_ = f32[388,128]{1,0:T(8,128)S(1)} collective-permute-done((f32[388,128]{1,0:T(8,128)S(1)}, f32[388,128]{1,0:T(8,128)S(1)}, u32[]{:S(2)}, u32[]{:S(2)}) %collective-permute-start.4) | collective-permute-done | bytes 198688 | tf_op jit(solution)/shard_map/ppermute | solution.py:586
  31.6 2.1 %shard_map.89 = (s32[16,128]{1,0:T(8,128)S(1)}, f32[112,8,128]{2,1,0:T(8,128)S(1)}, f32[26,8,128]{2,1,0:T(8,128)S(1)}, f32[26,8,128]{2,1,0:T(8,128)S(1)}, f32[8,128]{1,0:T(8,128)S(1)}) custom-call(s32[12]{0:T(128)S(1)} %stack.63.bounds.info.refs_0_, f32[32,128]{1,0:T(8,128)S(1)} %get-tuple-element.47.own.refs_1_.refs_0_.start, f32[416,128]{1,0:T(8,128)S(1)} %bitcast.18, ...), custom_call_target="tpu_custom_call" | custom-call | flops 4194304 | bytes 262144 | tf_op jit(solution)/shard_map/pallas_call | solution.py:661
  33.7 1.1 collective-permute-start.6
  34.8 7.4 %shard_map.90.own_radius = f32[4,128]{1,0:T(4,128)S(1)} custom-call(s32[16,128]{1,0:T(8,128)S(1)} %get-tuple-element.59.listed, f32[112,8,128]{2,1,0:T(8,128)S(1)} %get-tuple-element.60.tiles.refs_6_, f32[32,128]{1,0:T(8,128)S(1)} %get-tuple-element.47.own.refs_1_.refs_0_.start), custom_call_target="tpu_custom_call" | custom-call | flops 8589934592 | bytes 262144 | tf_op jit(solution)/shard_map/pallas_call | solution.py:677
  42.3 0.8 collective-permute-start.7
  43.2 1.4 collective-permute-start.9
  44.7 1.4 collective-permute-done.10.refs_1_
  46.1 0.8 collective-permute-done.9.refs_0_
  46.8 0.5 shard_map.91
  47.4 3.4 %collective-permute-start.12 = (f32[20,128]{1,0:T(8,128)S(1)}, f32[20,128]{1,0:T(8,128)S(1)}, u32[]{:S(2)}, u32[]{:S(2)}) collective-permute-start(f32[20,128]{1,0:T(8,128)S(1)} %get-tuple-element.62.mine), channel_id=1, source_target_pairs={{0,56},{8,16},{16,8},{24,32},{32,24},{40,48},{48,40},{56,0},{1,57}... | collective-permute-start | bytes 30728 | tf_op jit(solution)/shard_map/ppermute | solution.py:586
  50.8 0.9 collective-permute-start.14
  51.7 3.2 %collective-permute-start.13 = (f32[8,128]{1,0:T(8,128)S(1)}, f32[8,128]{1,0:T(8,128)S(1)}, u32[]{:S(2)}, u32[]{:S(2)}) collective-permute-start(f32[8,128]{1,0:T(8,128)S(1)} %get-tuple-element.63), channel_id=1, source_target_pairs={{0,16},{8,24},{16,0},{24,8},{32,48},{40,56},{48,32},{56,40},{1,17}... | collective-permute-start | bytes 12296 | tf_op jit(solution)/shard_map/ppermute | solution.py:599
  54.9 0.7 collective-permute-done.14.refs_1_
  55.6 1.2 collective-permute-done.13.refs_0_
  56.8 0.5 shard_map.92
  57.4 1.0 collective-permute-start.15
  58.3 2.5 %collective-permute-start.17 = (f32[8,128]{1,0:T(8,128)S(1)}, f32[8,128]{1,0:T(8,128)S(1)}, u32[]{:S(2)}, u32[]{:S(2)}) collective-permute-start(f32[8,128]{1,0:T(8,128)S(1)} %get-tuple-element.64), channel_id=1, source_target_pairs={{0,3},{1,2},{2,1},{3,0},{4,7},{5,6},{6,5},{7,4},{8,11},{9,10},{10,... | collective-permute-start | bytes 12296 | tf_op jit(solution)/shard_map/ppermute | solution.py:599
  60.8 1.0 collective-permute-start.16
  61.8 1.5 collective-permute-start.19
  63.3 2.0 %collective-permute-done.16 = f32[8,128]{1,0:T(8,128)S(1)} collective-permute-done((f32[8,128]{1,0:T(8,128)S(1)}, f32[8,128]{1,0:T(8,128)S(1)}, u32[]{:S(2)}, u32[]{:S(2)}) %collective-permute-start.16) | collective-permute-done | bytes 4128 | tf_op jit(solution)/shard_map/ppermute | solution.py:599
  65.4 2.0 %collective-permute-start.18 = (f32[8,128]{1,0:T(8,128)S(1)}, f32[8,128]{1,0:T(8,128)S(1)}, u32[]{:S(2)}, u32[]{:S(2)}) collective-permute-start(f32[8,128]{1,0:T(8,128)S(1)} %fusion.3), channel_id=1, source_target_pairs={{0,7},{1,6},{2,5},{3,4},{4,3},{5,2},{6,1},{7,0},{8,15},{9,14},{10,... | collective-permute-start | bytes 12296 | tf_op jit(solution)/shard_map/ppermute | solution.py:599
  67.4 12.4 %shard_map.93.refs_4_ = f32[12,128]{1,0:T(8,128)S(1)} custom-call(s32[12]{0:T(128)S(1)} %stack.63.bounds.info.refs_0_, s32[16,128]{1,0:T(8,128)S(1)} %get-tuple-element.59.listed, f32[112,8,128]{2,1,0:T(8,128)S(1)} %get-tuple-element.60.tiles.refs_6_, f32[32,128]{1,0:T(8,128)S(1)} %get-tuple-element.47.own.refs_1_.refs_0_.start, ...), custom_call_target="tpu_custom_call" | custom-call | flops 17179869184 | bytes 262144 | tf_op jit(solution)/shard_map/pallas_call | solution.py:707
  79.8 2.4 %shard_map.94 = (f32[32,128]{1,0:T(8,128)S(1)}, f32[12,128]{1,0:T(8,128)}) custom-call(s32[12]{0:T(128)S(1)} %stack.63.bounds.info.refs_0_, f32[32,128]{1,0:T(8,128)S(1)} %get-tuple-element.47.own.refs_1_.refs_0_.start, f32[26,8,128]{2,1,0:T(8,128)S(1)} %get-tuple-element.57.refs_1_, f32[26,8,128]{2,1,0:T(8,128)S(1)} %get-tuple-element.58.refs_2_.refs_7_, ...), custom_call_target="tpu_custom_call" | custom-call | flops 67108864 | bytes 262144 | tf_op jit(solution)/shard_map/pallas_call | solution.py:721
  82.2 1.5 shard_map.95
  83.9 4.9 %collective-permute-done.21.second = f32[92,128]{1,0:T(8,128)S(1)} collective-permute-done((f32[92,128]{1,0:T(8,128)S(1)}, f32[92,128]{1,0:T(8,128)S(1)}, u32[]{:S(2)}, u32[]{:S(2)}) %collective-permute-start.21) | collective-permute-done | bytes 47136 | tf_op jit(solution)/shard_map/ppermute | solution.py:586
  88.8 0.7 shard_map.96
  89.5 1.9 %collective-permute-start.23 = (f32[140,128]{1,0:T(8,128)S(1)}, f32[140,128]{1,0:T(8,128)S(1)}, u32[]{:S(2)}, u32[]{:S(2)}) collective-permute-start(f32[140,128]{1,0:T(8,128)S(1)} %get-tuple-element.72), channel_id=1, source_target_pairs={{0,56},{8,16},{16,8},{24,32},{32,24},{40,48},{48,40},{56,0},{1,57}... | collective-permute-start | bytes 215048 | tf_op jit(solution)/shard_map/ppermute | solution.py:586
  91.4 4.6 %collective-permute-done.23.second = f32[140,128]{1,0:T(8,128)S(1)} collective-permute-done((f32[140,128]{1,0:T(8,128)S(1)}, f32[140,128]{1,0:T(8,128)S(1)}, u32[]{:S(2)}, u32[]{:S(2)}) %collective-permute-start.23) | collective-permute-done | bytes 71712 | tf_op jit(solution)/shard_map/ppermute | solution.py:586
  96.0 0.7 shard_map.97
  96.8 1.2 collective-permute-start.25
  98.0 3.6 %collective-permute-done.25.refs_5_ = f32[212,128]{1,0:T(8,128)S(1)} collective-permute-done((f32[212,128]{1,0:T(8,128)S(1)}, f32[212,128]{1,0:T(8,128)S(1)}, u32[]{:S(2)}, u32[]{:S(2)}) %collective-permute-start.25) | collective-permute-done | bytes 108576 | tf_op jit(solution)/shard_map/ppermute | solution.py:586
  101.6 1.1 collective-permute-done.24.refs_4_
  102.7 2.8 %shard_map.98 = (s32[16,128]{1,0:T(8,128)S(1)}, f32[112,8,128]{2,1,0:T(8,128)S(1)}, f32[26,8,128]{2,1,0:T(8,128)S(1)}, f32[8,128]{1,0:T(8,128)S(1)}, f32[16,16,16]{2,1,0:T(8,128)}) custom-call(s32[12]{0:T(128)S(1)} %stack.63.bounds.info.refs_0_, f32[32,128]{1,0:T(8,128)S(1)} %get-tuple-element.66.own.refs_1_.refs_0_, f32[208,128]{1,0:T(8,128)S(1)} %bitcast.20, ...), custom_call_target="tpu_custom_call" | custom-call | flops 4194304 | bytes 262144 | tf_op jit(solution)/shard_map/pallas_call | solution.py:661
  105.9 7.4 %shard_map.99.own_radius = f32[4,128]{1,0:T(4,128)S(1)} custom-call(s32[16,128]{1,0:T(8,128)S(1)} %get-tuple-element.77.listed, f32[112,8,128]{2,1,0:T(8,128)S(1)} %get-tuple-element.78.tiles, f32[32,128]{1,0:T(8,128)S(1)} %get-tuple-element.66.own.refs_1_.refs_0_), custom_call_target="tpu_custom_call" | custom-call | flops 8589934592 | bytes 262144 | tf_op jit(solution)/shard_map/pallas_call | solution.py:677
  113.7 1.3 collective-permute-start.27
  115.0 1.6 %collective-permute-start.29 = (f32[8,128]{1,0:T(8,128)S(1)}, f32[8,128]{1,0:T(8,128)S(1)}, u32[]{:S(2)}, u32[]{:S(2)}) collective-permute-start(f32[8,128]{1,0:T(8,128)S(1)} %add.50), channel_id=1, source_target_pairs={{0,32},{8,40},{16,48},{24,56},{32,0},{40,8},{48,16},{56,24},{1,33}... | collective-permute-start | bytes 12296 | tf_op jit(solution)/shard_map/ppermute | solution.py:599
  116.6 1.4 collective-permute-done.30.refs_1_
  118.0 0.6 collective-permute-done.29.refs_0_
  119.2 2.9 %collective-permute-start.32 = (f32[20,128]{1,0:T(8,128)S(1)}, f32[20,128]{1,0:T(8,128)S(1)}, u32[]{:S(2)}, u32[]{:S(2)}) collective-permute-start(f32[20,128]{1,0:T(8,128)S(1)} %get-tuple-element.80.mine), channel_id=1, source_target_pairs={{0,56},{8,16},{16,8},{24,32},{32,24},{40,48},{48,40},{56,0},{1,57}... | collective-permute-start | bytes 30728 | tf_op jit(solution)/shard_map/ppermute | solution.py:586
  122.1 1.5 collective-permute-start.34
  123.6 2.6 %collective-permute-start.33 = (f32[8,128]{1,0:T(8,128)S(1)}, f32[8,128]{1,0:T(8,128)S(1)}, u32[]{:S(2)}, u32[]{:S(2)}) collective-permute-start(f32[8,128]{1,0:T(8,128)S(1)} %get-tuple-element.81), channel_id=1, source_target_pairs={{0,16},{8,24},{16,0},{24,8},{32,48},{40,56},{48,32},{56,40},{1,17}... | collective-permute-start | bytes 12296 | tf_op jit(solution)/shard_map/ppermute | solution.py:599
  126.2 0.7 collective-permute-done.34.refs_1_
  126.9 1.8 %collective-permute-done.33.refs_0_ = f32[8,128]{1,0:T(8,128)S(1)} collective-permute-done((f32[8,128]{1,0:T(8,128)S(1)}, f32[8,128]{1,0:T(8,128)S(1)}, u32[]{:S(2)}, u32[]{:S(2)}) %collective-permute-start.33) | collective-permute-done | bytes 4128 | tf_op jit(solution)/shard_map/ppermute | solution.py:599
  128.7 0.5 shard_map.101
  129.3 4.0 %collective-permute-start.37 = (f32[8,128]{1,0:T(8,128)S(1)}, f32[8,128]{1,0:T(8,128)S(1)}, u32[]{:S(2)}, u32[]{:S(2)}) collective-permute-start(f32[8,128]{1,0:T(8,128)S(1)} %get-tuple-element.82), channel_id=1, source_target_pairs={{0,3},{1,2},{2,1},{3,0},{4,7},{5,6},{6,5},{7,4},{8,11},{9,10},{10,... | collective-permute-start | bytes 12296 | tf_op jit(solution)/shard_map/ppermute | solution.py:599
  133.7 2.1 %collective-permute-start.39 = (f32[44,128]{1,0:T(8,128)S(1)}, f32[44,128]{1,0:T(8,128)S(1)}, u32[]{:S(2)}, u32[]{:S(2)}) collective-permute-start(f32[44,128]{1,0:T(8,128)S(1)} %get-tuple-element.83.mine), channel_id=1, source_target_pairs={{0,7},{1,2},{2,1},{3,4},{4,3},{5,6},{6,5},{7,0},{8,15},{9,10},{10,... | collective-permute-start | bytes 67592 | tf_op jit(solution)/shard_map/ppermute | solution.py:586
  135.8 2.0 %collective-permute-done.36 = f32[8,128]{1,0:T(8,128)S(1)} collective-permute-done((f32[8,128]{1,0:T(8,128)S(1)}, f32[8,128]{1,0:T(8,128)S(1)}, u32[]{:S(2)}, u32[]{:S(2)}) %collective-permute-start.36) | collective-permute-done | bytes 4128 | tf_op jit(solution)/shard_map/ppermute | solution.py:599
  137.9 2.1 %collective-permute-start.38 = (f32[8,128]{1,0:T(8,128)S(1)}, f32[8,128]{1,0:T(8,128)S(1)}, u32[]{:S(2)}, u32[]{:S(2)}) collective-permute-start(f32[8,128]{1,0:T(8,128)S(1)} %fusion.1), channel_id=1, source_target_pairs={{0,7},{1,6},{2,5},{3,4},{4,3},{5,2},{6,1},{7,0},{8,15},{9,14},{10,... | collective-permute-start | bytes 12296 | tf_op jit(solution)/shard_map/ppermute | solution.py:599
  140.0 12.5 %shard_map.102.refs_4_ = f32[12,128]{1,0:T(8,128)S(1)} custom-call(s32[12]{0:T(128)S(1)} %stack.63.bounds.info.refs_0_, s32[16,128]{1,0:T(8,128)S(1)} %get-tuple-element.77.listed, f32[112,8,128]{2,1,0:T(8,128)S(1)} %get-tuple-element.78.tiles, f32[32,128]{1,0:T(8,128)S(1)} %get-tuple-element.66.own.refs_1_.refs_0_, f32[4,128]{1,0:T(4,128)S(1)} %shard_map.99.own_radius, ...), custom_call_target="tpu_custom_call" | custom-call | flops 17179869184 | bytes 262144 | tf_op jit(solution)/shard_map/pallas_call | solution.py:707
  152.6 1.8 %shard_map.103 = (f32[32,128]{1,0:T(8,128)S(1)}, f32[12,128]{1,0:T(8,128)S(1)}) custom-call(s32[12]{0:T(128)S(1)} %stack.63.bounds.info.refs_0_, f32[32,128]{1,0:T(8,128)S(1)} %get-tuple-element.66.own.refs_1_.refs_0_, f32[26,8,128]{2,1,0:T(8,128)S(1)} %get-tuple-element.76.refs_1_, f32[26,8,128]{2,1,0:T(8,128)S(1)} %get-tuple-element.58.refs_2_.refs_7_, ...), custom_call_target="tpu_custom_call" | custom-call | flops 67108864 | bytes 262144 | tf_op jit(solution)/shard_map/pallas_call | solution.py:721
  154.4 0.9 shard_map.104
  (56 shorter events, 2.7 us)
Async XLA Ops:
  0.6 0.9 copy-start.4
  1.5 0.7 copy-start
  1.5 0.7 copy-start.1
  1.5 0.7 copy-start.2
  1.5 0.7 copy-start.3
  5.7 6.1 %collective-permute-start.1 = (f32[140,128]{1,0:T(8,128)S(1)}, f32[140,128]{1,0:T(8,128)S(1)}, u32[]{:S(2)}, u32[]{:S(2)}) collective-permute-start(f32[140,128]{1,0:T(8,128)S(1)} %get-tuple-element.50), channel_id=1, source_target_pairs={{0,192},{64,128},{128,64},{192,0},{1,193},{65,129},{129,65},{193,1... | collective-permute-start | bytes 215048 | tf_op jit(solution)/shard_map/ppermute | solution.py:586
  6.4 5.4 %collective-permute-start = (f32[140,128]{1,0:T(8,128)S(1)}, f32[140,128]{1,0:T(8,128)S(1)}, u32[]{:S(2)}, u32[]{:S(2)}) collective-permute-start(f32[140,128]{1,0:T(8,128)S(1)} %get-tuple-element.49.mine), channel_id=1, source_target_pairs={{0,64},{64,0},{128,192},{192,128},{1,65},{65,1},{129,193},{193,129... | collective-permute-start | bytes 215048 | tf_op jit(solution)/shard_map/ppermute | solution.py:586
  12.5 7.9 %collective-permute-start.3 = (f32[268,128]{1,0:T(8,128)S(1)}, f32[268,128]{1,0:T(8,128)S(1)}, u32[]{:S(2)}, u32[]{:S(2)}) collective-permute-start(f32[268,128]{1,0:T(8,128)S(1)} %get-tuple-element.53), channel_id=1, source_target_pairs={{0,56},{8,16},{16,8},{24,32},{32,24},{40,48},{48,40},{56,0},{1,57}... | collective-permute-start | bytes 411656 | tf_op jit(solution)/shard_map/ppermute | solution.py:586
  15.6 5.4 %collective-permute-start.2 = (f32[268,128]{1,0:T(8,128)S(1)}, f32[268,128]{1,0:T(8,128)S(1)}, u32[]{:S(2)}, u32[]{:S(2)}) collective-permute-start(f32[268,128]{1,0:T(8,128)S(1)} %get-tuple-element.52.mine), channel_id=1, source_target_pairs={{0,8},{8,0},{16,24},{24,16},{32,40},{40,32},{48,56},{56,48},{1,9},... | collective-permute-start | bytes 411656 | tf_op jit(solution)/shard_map/ppermute | solution.py:586
  21.7 6.1 %collective-permute-start.5 = (f32[388,128]{1,0:T(8,128)S(1)}, f32[388,128]{1,0:T(8,128)S(1)}, u32[]{:S(2)}, u32[]{:S(2)}) collective-permute-start(f32[388,128]{1,0:T(8,128)S(1)} %get-tuple-element.56), channel_id=1, source_target_pairs={{0,7},{1,2},{2,1},{3,4},{4,3},{5,6},{6,5},{7,0},{8,15},{9,10},{10,... | collective-permute-start | bytes 595976 | tf_op jit(solution)/shard_map/ppermute | solution.py:586
  23.8 7.9 %collective-permute-start.4 = (f32[388,128]{1,0:T(8,128)S(1)}, f32[388,128]{1,0:T(8,128)S(1)}, u32[]{:S(2)}, u32[]{:S(2)}) collective-permute-start(f32[388,128]{1,0:T(8,128)S(1)} %get-tuple-element.55.refs_3_), channel_id=1, source_target_pairs={{0,1},{1,0},{2,3},{3,2},{4,5},{5,4},{6,7},{7,6},{8,9},{9,8},{10,11... | collective-permute-start | bytes 595976 | tf_op jit(solution)/shard_map/ppermute | solution.py:586
  33.7 8.5 %collective-permute-start.6 = (f32[8,128]{1,0:T(8,128)S(1)}, f32[8,128]{1,0:T(8,128)S(1)}, u32[]{:S(2)}, u32[]{:S(2)}) collective-permute-start(f32[8,128]{1,0:T(8,128)S(1)} %get-tuple-element.61), channel_id=1, source_target_pairs={{0,128},{64,192},{128,0},{192,64},{1,129},{65,193},{129,1},{193,65... | collective-permute-start | bytes 12296 | tf_op jit(solution)/shard_map/ppermute | solution.py:599
  42.2 4.7 %collective-permute-start.8 = (f32[12,128]{1,0:T(8,128)S(1)}, f32[12,128]{1,0:T(8,128)S(1)}, u32[]{:S(2)}, u32[]{:S(2)}) collective-permute-start(f32[12,128]{1,0:T(8,128)S(1)} %pad_maximum_fusion.mine), channel_id=1, source_target_pairs={{0,192},{64,128},{128,64},{192,0},{1,193},{65,129},{129,65},{193,1... | collective-permute-start | bytes 18440 | tf_op jit(solution)/shard_map/ppermute | solution.py:586
  42.3 4.6 %collective-permute-start.7 = (f32[12,128]{1,0:T(8,128)S(1)}, f32[12,128]{1,0:T(8,128)S(1)}, u32[]{:S(2)}, u32[]{:S(2)}) collective-permute-start(f32[12,128]{1,0:T(8,128)S(1)} %pad_maximum_fusion.mine), channel_id=1, source_target_pairs={{0,64},{64,0},{128,192},{192,128},{1,65},{65,1},{129,193},{193,129... | collective-permute-start | bytes 18440 | tf_op jit(solution)/shard_map/ppermute | solution.py:586
  43.0 3.0 %collective-permute-start.10 = (f32[8,128]{1,0:T(8,128)S(1)}, f32[8,128]{1,0:T(8,128)S(1)}, u32[]{:S(2)}, u32[]{:S(2)}) collective-permute-start(f32[8,128]{1,0:T(8,128)S(1)} %add.45), channel_id=1, source_target_pairs={{0,96},{8,104},{16,112},{24,120},{32,64},{40,72},{48,80},{56,88},{... | collective-permute-start | bytes 12296 | tf_op jit(solution)/shard_map/ppermute | solution.py:599
  43.2 3.6 %collective-permute-start.9 = (f32[8,128]{1,0:T(8,128)S(1)}, f32[8,128]{1,0:T(8,128)S(1)}, u32[]{:S(2)}, u32[]{:S(2)}) collective-permute-start(f32[8,128]{1,0:T(8,128)S(1)} %add.45), channel_id=1, source_target_pairs={{0,32},{8,40},{16,48},{24,56},{32,0},{40,8},{48,16},{56,24},{1,33}... | collective-permute-start | bytes 12296 | tf_op jit(solution)/shard_map/ppermute | solution.py:599
  47.4 9.4 %collective-permute-start.12 = (f32[20,128]{1,0:T(8,128)S(1)}, f32[20,128]{1,0:T(8,128)S(1)}, u32[]{:S(2)}, u32[]{:S(2)}) collective-permute-start(f32[20,128]{1,0:T(8,128)S(1)} %get-tuple-element.62.mine), channel_id=1, source_target_pairs={{0,56},{8,16},{16,8},{24,32},{32,24},{40,48},{48,40},{56,0},{1,57}... | collective-permute-start | bytes 30728 | tf_op jit(solution)/shard_map/ppermute | solution.py:586
  50.8 6.0 %collective-permute-start.11 = (f32[20,128]{1,0:T(8,128)S(1)}, f32[20,128]{1,0:T(8,128)S(1)}, u32[]{:S(2)}, u32[]{:S(2)}) collective-permute-start(f32[20,128]{1,0:T(8,128)S(1)} %get-tuple-element.62.mine), channel_id=1, source_target_pairs={{0,8},{8,0},{16,24},{24,16},{32,40},{40,32},{48,56},{56,48},{1,9},... | collective-permute-start | bytes 30728 | tf_op jit(solution)/shard_map/ppermute | solution.py:586
  50.8 4.8 %collective-permute-start.14 = (f32[8,128]{1,0:T(8,128)S(1)}, f32[8,128]{1,0:T(8,128)S(1)}, u32[]{:S(2)}, u32[]{:S(2)}) collective-permute-start(f32[8,128]{1,0:T(8,128)S(1)} %get-tuple-element.63), channel_id=1, source_target_pairs={{0,24},{8,16},{16,8},{24,0},{32,56},{40,48},{48,40},{56,32},{1,25}... | collective-permute-start | bytes 12296 | tf_op jit(solution)/shard_map/ppermute | solution.py:599
  51.7 5.1 %collective-permute-start.13 = (f32[8,128]{1,0:T(8,128)S(1)}, f32[8,128]{1,0:T(8,128)S(1)}, u32[]{:S(2)}, u32[]{:S(2)}) collective-permute-start(f32[8,128]{1,0:T(8,128)S(1)} %get-tuple-element.63), channel_id=1, source_target_pairs={{0,16},{8,24},{16,0},{24,8},{32,48},{40,56},{48,32},{56,40},{1,17}... | collective-permute-start | bytes 12296 | tf_op jit(solution)/shard_map/ppermute | solution.py:599
  57.4 8.0 %collective-permute-start.15 = (f32[44,128]{1,0:T(8,128)S(1)}, f32[44,128]{1,0:T(8,128)S(1)}, u32[]{:S(2)}, u32[]{:S(2)}) collective-permute-start(f32[44,128]{1,0:T(8,128)S(1)} %get-tuple-element.65.mine), channel_id=1, source_target_pairs={{0,1},{1,0},{2,3},{3,2},{4,5},{5,4},{6,7},{7,6},{8,9},{9,8},{10,11... | collective-permute-start | bytes 67592 | tf_op jit(solution)/shard_map/ppermute | solution.py:586
  58.3 5.0 %collective-permute-start.17 = (f32[8,128]{1,0:T(8,128)S(1)}, f32[8,128]{1,0:T(8,128)S(1)}, u32[]{:S(2)}, u32[]{:S(2)}) collective-permute-start(f32[8,128]{1,0:T(8,128)S(1)} %get-tuple-element.64), channel_id=1, source_target_pairs={{0,3},{1,2},{2,1},{3,0},{4,7},{5,6},{6,5},{7,4},{8,11},{9,10},{10,... | collective-permute-start | bytes 12296 | tf_op jit(solution)/shard_map/ppermute | solution.py:599
  60.8 4.5 %collective-permute-start.16 = (f32[8,128]{1,0:T(8,128)S(1)}, f32[8,128]{1,0:T(8,128)S(1)}, u32[]{:S(2)}, u32[]{:S(2)}) collective-permute-start(f32[8,128]{1,0:T(8,128)S(1)} %get-tuple-element.64), channel_id=1, source_target_pairs={{0,2},{1,3},{2,0},{3,1},{4,6},{5,7},{6,4},{7,5},{8,10},{9,11},{10,... | collective-permute-start | bytes 12296 | tf_op jit(solution)/shard_map/ppermute | solution.py:599
  61.8 5.6 %collective-permute-start.19 = (f32[44,128]{1,0:T(8,128)S(1)}, f32[44,128]{1,0:T(8,128)S(1)}, u32[]{:S(2)}, u32[]{:S(2)}) collective-permute-start(f32[44,128]{1,0:T(8,128)S(1)} %get-tuple-element.65.mine), channel_id=1, source_target_pairs={{0,7},{1,2},{2,1},{3,4},{4,3},{5,6},{6,5},{7,0},{8,15},{9,10},{10,... | collective-permute-start | bytes 67592 | tf_op jit(solution)/shard_map/ppermute | solution.py:586
  65.4 14.4 %collective-permute-start.18 = (f32[8,128]{1,0:T(8,128)S(1)}, f32[8,128]{1,0:T(8,128)S(1)}, u32[]{:S(2)}, u32[]{:S(2)}) collective-permute-start(f32[8,128]{1,0:T(8,128)S(1)} %fusion.3), channel_id=1, source_target_pairs={{0,7},{1,6},{2,5},{3,4},{4,3},{5,2},{6,1},{7,0},{8,15},{9,14},{10,... | collective-permute-start | bytes 12296 | tf_op jit(solution)/shard_map/ppermute | solution.py:599
  83.7 5.1 %collective-permute-start.21 = (f32[92,128]{1,0:T(8,128)S(1)}, f32[92,128]{1,0:T(8,128)S(1)}, u32[]{:S(2)}, u32[]{:S(2)}) collective-permute-start(f32[92,128]{1,0:T(8,128)S(1)} %get-tuple-element.69), channel_id=1, source_target_pairs={{0,192},{64,128},{128,64},{192,0},{1,193},{65,129},{129,65},{193,1... | collective-permute-start | bytes 141320 | tf_op jit(solution)/shard_map/ppermute | solution.py:586
  83.8 5.0 %collective-permute-start.20 = (f32[92,128]{1,0:T(8,128)S(1)}, f32[92,128]{1,0:T(8,128)S(1)}, u32[]{:S(2)}, u32[]{:S(2)}) collective-permute-start(f32[92,128]{1,0:T(8,128)S(1)} %get-tuple-element.68.mine), channel_id=1, source_target_pairs={{0,64},{64,0},{128,192},{192,128},{1,65},{65,1},{129,193},{193,129... | collective-permute-start | bytes 141320 | tf_op jit(solution)/shard_map/ppermute | solution.py:586
  89.5 6.5 %collective-permute-start.23 = (f32[140,128]{1,0:T(8,128)S(1)}, f32[140,128]{1,0:T(8,128)S(1)}, u32[]{:S(2)}, u32[]{:S(2)}) collective-permute-start(f32[140,128]{1,0:T(8,128)S(1)} %get-tuple-element.72), channel_id=1, source_target_pairs={{0,56},{8,16},{16,8},{24,32},{32,24},{40,48},{48,40},{56,0},{1,57}... | collective-permute-start | bytes 215048 | tf_op jit(solution)/shard_map/ppermute | solution.py:586
  91.4 4.7 %collective-permute-start.22 = (f32[140,128]{1,0:T(8,128)S(1)}, f32[140,128]{1,0:T(8,128)S(1)}, u32[]{:S(2)}, u32[]{:S(2)}) collective-permute-start(f32[140,128]{1,0:T(8,128)S(1)} %get-tuple-element.71.mine), channel_id=1, source_target_pairs={{0,8},{8,0},{16,24},{24,16},{32,40},{40,32},{48,56},{56,48},{1,9},... | collective-permute-start | bytes 215048 | tf_op jit(solution)/shard_map/ppermute | solution.py:586
  96.8 4.8 %collective-permute-start.25 = (f32[212,128]{1,0:T(8,128)S(1)}, f32[212,128]{1,0:T(8,128)S(1)}, u32[]{:S(2)}, u32[]{:S(2)}) collective-permute-start(f32[212,128]{1,0:T(8,128)S(1)} %get-tuple-element.75), channel_id=1, source_target_pairs={{0,7},{1,2},{2,1},{3,4},{4,3},{5,6},{6,5},{7,0},{8,15},{9,10},{10,... | collective-permute-start | bytes 325640 | tf_op jit(solution)/shard_map/ppermute | solution.py:586
  98.0 4.7 %collective-permute-start.24 = (f32[212,128]{1,0:T(8,128)S(1)}, f32[212,128]{1,0:T(8,128)S(1)}, u32[]{:S(2)}, u32[]{:S(2)}) collective-permute-start(f32[212,128]{1,0:T(8,128)S(1)} %get-tuple-element.74.refs_3_), channel_id=1, source_target_pairs={{0,1},{1,0},{2,3},{3,2},{4,5},{5,4},{6,7},{7,6},{8,9},{9,8},{10,11... | collective-permute-start | bytes 325640 | tf_op jit(solution)/shard_map/ppermute | solution.py:586
  105.5 7.8 %collective-permute-start.26 = (f32[8,128]{1,0:T(8,128)S(1)}, f32[8,128]{1,0:T(8,128)S(1)}, u32[]{:S(2)}, u32[]{:S(2)}) collective-permute-start(f32[8,128]{1,0:T(8,128)S(1)} %get-tuple-element.79), channel_id=1, source_target_pairs={{0,128},{64,192},{128,0},{192,64},{1,129},{65,193},{129,1},{193,65... | collective-permute-start | bytes 12296 | tf_op jit(solution)/shard_map/ppermute | solution.py:599
  113.4 5.3 %collective-permute-start.28 = (f32[12,128]{1,0:T(8,128)S(1)}, f32[12,128]{1,0:T(8,128)S(1)}, u32[]{:S(2)}, u32[]{:S(2)}) collective-permute-start(f32[12,128]{1,0:T(8,128)S(1)} %pad_maximum_fusion.1.mine), channel_id=1, source_target_pairs={{0,192},{64,128},{128,64},{192,0},{1,193},{65,129},{129,65},{193,1... | collective-permute-start | bytes 18440 | tf_op jit(solution)/shard_map/ppermute | solution.py:586
  113.7 4.9 %collective-permute-start.27 = (f32[12,128]{1,0:T(8,128)S(1)}, f32[12,128]{1,0:T(8,128)S(1)}, u32[]{:S(2)}, u32[]{:S(2)}) collective-permute-start(f32[12,128]{1,0:T(8,128)S(1)} %pad_maximum_fusion.1.mine), channel_id=1, source_target_pairs={{0,64},{64,0},{128,192},{192,128},{1,65},{65,1},{129,193},{193,129... | collective-permute-start | bytes 18440 | tf_op jit(solution)/shard_map/ppermute | solution.py:586
  115.0 3.0 %collective-permute-start.30 = (f32[8,128]{1,0:T(8,128)S(1)}, f32[8,128]{1,0:T(8,128)S(1)}, u32[]{:S(2)}, u32[]{:S(2)}) collective-permute-start(f32[8,128]{1,0:T(8,128)S(1)} %add.50), channel_id=1, source_target_pairs={{0,96},{8,104},{16,112},{24,120},{32,64},{40,72},{48,80},{56,88},{... | collective-permute-start | bytes 12296 | tf_op jit(solution)/shard_map/ppermute | solution.py:599
  115.0 3.6 %collective-permute-start.29 = (f32[8,128]{1,0:T(8,128)S(1)}, f32[8,128]{1,0:T(8,128)S(1)}, u32[]{:S(2)}, u32[]{:S(2)}) collective-permute-start(f32[8,128]{1,0:T(8,128)S(1)} %add.50), channel_id=1, source_target_pairs={{0,32},{8,40},{16,48},{24,56},{32,0},{40,8},{48,16},{56,24},{1,33}... | collective-permute-start | bytes 12296 | tf_op jit(solution)/shard_map/ppermute | solution.py:599
  119.2 9.5 %collective-permute-start.32 = (f32[20,128]{1,0:T(8,128)S(1)}, f32[20,128]{1,0:T(8,128)S(1)}, u32[]{:S(2)}, u32[]{:S(2)}) collective-permute-start(f32[20,128]{1,0:T(8,128)S(1)} %get-tuple-element.80.mine), channel_id=1, source_target_pairs={{0,56},{8,16},{16,8},{24,32},{32,24},{40,48},{48,40},{56,0},{1,57}... | collective-permute-start | bytes 30728 | tf_op jit(solution)/shard_map/ppermute | solution.py:586
  122.1 6.6 %collective-permute-start.31 = (f32[20,128]{1,0:T(8,128)S(1)}, f32[20,128]{1,0:T(8,128)S(1)}, u32[]{:S(2)}, u32[]{:S(2)}) collective-permute-start(f32[20,128]{1,0:T(8,128)S(1)} %get-tuple-element.80.mine), channel_id=1, source_target_pairs={{0,8},{8,0},{16,24},{24,16},{32,40},{40,32},{48,56},{56,48},{1,9},... | collective-permute-start | bytes 30728 | tf_op jit(solution)/shard_map/ppermute | solution.py:586
  122.1 4.8 %collective-permute-start.34 = (f32[8,128]{1,0:T(8,128)S(1)}, f32[8,128]{1,0:T(8,128)S(1)}, u32[]{:S(2)}, u32[]{:S(2)}) collective-permute-start(f32[8,128]{1,0:T(8,128)S(1)} %get-tuple-element.81), channel_id=1, source_target_pairs={{0,24},{8,16},{16,8},{24,0},{32,56},{40,48},{48,40},{56,32},{1,25}... | collective-permute-start | bytes 12296 | tf_op jit(solution)/shard_map/ppermute | solution.py:599
  123.6 5.1 %collective-permute-start.33 = (f32[8,128]{1,0:T(8,128)S(1)}, f32[8,128]{1,0:T(8,128)S(1)}, u32[]{:S(2)}, u32[]{:S(2)}) collective-permute-start(f32[8,128]{1,0:T(8,128)S(1)} %get-tuple-element.81), channel_id=1, source_target_pairs={{0,16},{8,24},{16,0},{24,8},{32,48},{40,56},{48,32},{56,40},{1,17}... | collective-permute-start | bytes 12296 | tf_op jit(solution)/shard_map/ppermute | solution.py:599
  129.2 8.7 %collective-permute-start.35 = (f32[44,128]{1,0:T(8,128)S(1)}, f32[44,128]{1,0:T(8,128)S(1)}, u32[]{:S(2)}, u32[]{:S(2)}) collective-permute-start(f32[44,128]{1,0:T(8,128)S(1)} %get-tuple-element.83.mine), channel_id=1, source_target_pairs={{0,1},{1,0},{2,3},{3,2},{4,5},{5,4},{6,7},{7,6},{8,9},{9,8},{10,11... | collective-permute-start | bytes 67592 | tf_op jit(solution)/shard_map/ppermute | solution.py:586
  129.3 6.5 %collective-permute-start.37 = (f32[8,128]{1,0:T(8,128)S(1)}, f32[8,128]{1,0:T(8,128)S(1)}, u32[]{:S(2)}, u32[]{:S(2)}) collective-permute-start(f32[8,128]{1,0:T(8,128)S(1)} %get-tuple-element.82), channel_id=1, source_target_pairs={{0,3},{1,2},{2,1},{3,0},{4,7},{5,6},{6,5},{7,4},{8,11},{9,10},{10,... | collective-permute-start | bytes 12296 | tf_op jit(solution)/shard_map/ppermute | solution.py:599
  133.4 4.5 %collective-permute-start.36 = (f32[8,128]{1,0:T(8,128)S(1)}, f32[8,128]{1,0:T(8,128)S(1)}, u32[]{:S(2)}, u32[]{:S(2)}) collective-permute-start(f32[8,128]{1,0:T(8,128)S(1)} %get-tuple-element.82), channel_id=1, source_target_pairs={{0,2},{1,3},{2,0},{3,1},{4,6},{5,7},{6,4},{7,5},{8,10},{9,11},{10,... | collective-permute-start | bytes 12296 | tf_op jit(solution)/shard_map/ppermute | solution.py:599
  133.7 6.3 %collective-permute-start.39 = (f32[44,128]{1,0:T(8,128)S(1)}, f32[44,128]{1,0:T(8,128)S(1)}, u32[]{:S(2)}, u32[]{:S(2)}) collective-permute-start(f32[44,128]{1,0:T(8,128)S(1)} %get-tuple-element.83.mine), channel_id=1, source_target_pairs={{0,7},{1,2},{2,1},{3,4},{4,3},{5,6},{6,5},{7,0},{8,15},{9,10},{10,... | collective-permute-start | bytes 67592 | tf_op jit(solution)/shard_map/ppermute | solution.py:586
  137.9 14.7 %collective-permute-start.38 = (f32[8,128]{1,0:T(8,128)S(1)}, f32[8,128]{1,0:T(8,128)S(1)}, u32[]{:S(2)}, u32[]{:S(2)}) collective-permute-start(f32[8,128]{1,0:T(8,128)S(1)} %fusion.1), channel_id=1, source_target_pairs={{0,7},{1,6},{2,5},{3,4},{4,3},{5,2},{6,1},{7,0},{8,15},{9,14},{10,... | collective-permute-start | bytes 12296 | tf_op jit(solution)/shard_map/ppermute | solution.py:599
